TPU v7x, 128 devices: a whole 4x4x4 slice. The times are simulated.
128 devices in a mesh: lat: 8 (over y, core), lon: 16 (over x, z).
Axes of the slice: x: 4, y: 4, z: 4, core: 2. Of those that a mesh axis runs over, the one named last changes fastest.
Arguments:
- transport: float32 [4, 36, 256, 2048], P(None, None, 'lat', 'lon'), may hold values from 0.03 to 0.24
- mixing: float32 [35, 256, 2048], P(None, 'lat', 'lon'), may hold values from 0.05 to 5
- trajectory: bfloat16 [4, 3, 36, 256, 2048], P(None, None, None, 'lat', 'lon'), may hold values from -6 to 6
- kernel_table: float32 [64, 36], replicated, may hold values from 0 to 0.5
- track_tile: int32 [4, 65536, 1], P(None, ('lat', 'lon')), may hold values from 0 to 127; in each aligned block of 512 rows (0 to 511, 512 to 1023, ..., all dimensions but the last counted through in order) at most 8 rows name the same one
- sound_cell: int32 [4, 65536], P(None, ('lat', 'lon')), may hold values from 0 to 4095
- kernel_index: int32 [4, 65536], P(None, ('lat', 'lon')), may hold values from 0 to 63
- observed: float32 [4, 3, 65536], P(None, None, ('lat', 'lon')), may hold values from -8 to 8
- precision: float32 [4, 65536], P(None, ('lat', 'lon')), may hold values from 0.3 to 3
Outputs:
- adjoint_field: float32 [3, 36, 256, 2048], P(None, None, 'lat', 'lon')
- flux_grad: float32 [3, 256, 2048], P(None, 'lat', 'lon')
Inputs may be any that keep to these rules, and one draw needn't show every extreme that they name: `track_tile`: within one step, the soundings held by one device name any one tile at most 8 times, and some device names some tile exactly 8 times.
All inputs are finite; a program needn't handle non-finite values.
Results may differ from a plain program's by a relative error of at most 0.0003.
Values may be sent and summed in bfloat16 or wider, within the bound.
No kernel may reach another device: no remote copies, remote signals or barrier semaphores. Data moves between devices by JAX's collectives and lax.ppermute only.
A program may use at most 128 MiB of HBM per device.

v0:
```python
import functools

import jax
import jax.numpy as jnp
from jax import lax
from jax.experimental import pallas as pl
from jax.experimental.pallas import tpu as pltpu
from jax.sharding import PartitionSpec as P

CAP = 8
WORDS = 5
F32 = jnp.float32
BF16 = jnp.bfloat16


def split3(x):
    hi = x.astype(BF16)
    rest = x - hi.astype(F32)
    mid = rest.astype(BF16)
    return hi, mid, (rest - mid.astype(F32)).astype(BF16)


def split2(x):
    hi = x.astype(BF16)
    return hi, (x - hi.astype(F32)).astype(BF16)


def dot(a, b):
    return jnp.dot(a, b, preferred_element_type=F32)


def dot_t(a, b):
    return lax.dot_general(a, b, (((1,), (1,)), ((), ())), preferred_element_type=F32)


def call(kernel, outs, *args, scratch=(), vmem=24 << 20):
    return pl.pallas_call(
        kernel,
        out_shape=outs,
        in_specs=[pl.BlockSpec(memory_space=pltpu.VMEM)] * len(args),
        out_specs=jax.tree.map(lambda _: pl.BlockSpec(memory_space=pltpu.VMEM), outs),
        scratch_shapes=list(scratch),
        compiler_params=pltpu.CompilerParams(vmem_limit_bytes=vmem),
    )(*args)


def sds(*shape, dtype=F32):
    return jax.ShapeDtypeStruct(shape, dtype)


def route_kernel(tile_ref, cell_ref, index_ref, obs_ref, prec_ref, out_ref):
    steps, count = tile_ref.shape
    ntiles = out_ref.shape[0]
    tile_ids = lax.broadcasted_iota(jnp.int32, (ntiles, count), 0)
    before = (
        lax.broadcasted_iota(jnp.int32, (count, count), 0)
        < lax.broadcasted_iota(jnp.int32, (count, count), 1)
    ).astype(F32).astype(BF16)
    rank_ids = lax.broadcasted_iota(jnp.int32, (CAP, count), 0)
    pad = jnp.zeros((64 - CAP * WORDS, count), F32)
    half = jnp.zeros((64, count), F32)
    for pair in range(steps // 2):
        total = None
        for side in range(2):
            s = 2 * pair + side
            mine = tile_ids == tile_ref[s : s + 1, :]
            mine_f = mine.astype(F32)
            mine_b = mine_f.astype(BF16)
            seen = dot(mine_b, before)
            rank = jnp.sum(mine_f * seen, axis=0, keepdims=True).astype(jnp.int32)
            at_rank = rank_ids == rank
            code = (index_ref[s : s + 1, :] * 4096 + cell_ref[s : s + 1, :]).astype(F32)
            words = [code] + [obs_ref[s, t : t + 1, :] for t in range(3)] + [prec_ref[s : s + 1, :]]
            rows = [jnp.where(at_rank, w, 0.0) for w in words]
            block = jnp.concatenate(rows + [pad] + [half], axis=0)
            if side == 1:
                block = jnp.concatenate([half] + rows + [pad], axis=0)
            for part in split3(block):
                term = dot_t(mine_b, part)
                total = term if total is None else total + term
        out_ref[:, pair, :] = total


def unpack_kernel(got_ref, out_ref):
    ntiles = got_ref.shape[0]
    for pair in range(2):
        turned = got_ref[:, pair, :].T
        for side in range(2):
            s = 2 * pair + side
            base = 64 * side
            code = turned[base : base + CAP, :].astype(jnp.int32)
            kidx = code // 4096
            cell = code - kidx * 4096
            row = cell // 128
            col = cell - row * 128
            hi = row // 16
            fields = [hi * 128 + col, row - hi * 16, kidx]
            fields = [f.astype(F32) for f in fields]
            fields += [turned[base + CAP * w : base + CAP * (w + 1), :] for w in range(1, WORDS)]
            for f, value in enumerate(fields):
                for r in range(CAP):
                    out_ref[s, f : f + 1, r * ntiles : (r + 1) * ntiles] = value[r : r + 1, :]
            out_ref[s, 7:8, :] = jnp.zeros((1, CAP * ntiles), F32)


def forcing_kernel(s, chunk, snd_ref, traj_ref, table_ref, out_ref, pick, weight, scaled):
    tracers, layers = out_ref.shape[:2]
    slots = snd_ref.shape[2]
    nker = table_ref.shape[1]
    cell_ids = lax.broadcasted_iota(jnp.int32, (256, chunk), 0).astype(F32)
    low_ids = lax.broadcasted_iota(jnp.int32, (16, chunk), 0).astype(F32)
    ker_ids = lax.broadcasted_iota(jnp.int32, (nker, chunk), 0).astype(F32)
    table = split3(table_ref[...])
    for c in range(slots // chunk):
        at = pl.ds(c * chunk, chunk)
        pick[:, at] = jnp.where(cell_ids == snd_ref[s, 0:1, at], 1.0, 0.0).astype(BF16)
        low = jnp.where(low_ids == snd_ref[s, 1:2, at], 1.0, 0.0)
        ker = jnp.where(ker_ids == snd_ref[s, 2:3, at], 1.0, 0.0).astype(BF16)
        w = dot(table[0], ker) + dot(table[1], ker) + dot(table[2], ker)
        for k in range(layers):
            weight[k, :, at] = w[k : k + 1, :] * low

    def per_tracer(t, _):
        lhs = jnp.concatenate(
            [
                traj_ref[s, t, :, 0:16, :].reshape(layers * 16, 128),
                traj_ref[s, t, :, 16:32, :].reshape(layers * 16, 128),
            ],
            axis=1,
        )
        force = None
        for c in range(slots // chunk):
            at = pl.ds(c * chunk, chunk)
            sampled = dot(lhs, pick[:, at]).reshape(layers, 16, chunk)
            model = jnp.sum(jnp.sum(sampled * weight[:, :, at], axis=0), axis=0, keepdims=True)
            sc = (model - snd_ref[s, pl.ds(3 + t, 1), at]) * snd_ref[s, 6:7, at]
            hi, lo = split2((weight[:, :, at] * sc).reshape(layers * 16, chunk))
            term = dot_t(hi, pick[:, at]) + dot_t(lo, pick[:, at])
            force = term if force is None else force + term
        out_ref[t, :, 0:16, :] = force[:, 0:128].reshape(layers, 16, 128)
        out_ref[t, :, 16:32, :] = force[:, 128:256].reshape(layers, 16, 128)
        return 0

    lax.fori_loop(0, tracers, per_tracer, 0)


def setup_kernel(mix_ref, inv_ref, up_ref):
    layers = inv_ref.shape[0]
    for k in range(layers):
        diag = jnp.ones_like(mix_ref[0])
        if k > 0:
            diag = diag + mix_ref[k - 1]
        if k < layers - 1:
            diag = diag + mix_ref[k]
        if k > 0:
            diag = diag + mix_ref[k - 1] * up
        inv = 1.0 / diag
        inv_ref[k] = inv
        if k < layers - 1:
            up = -mix_ref[k] * inv
            up_ref[k] = up


def halo_add(value, t, k, layers, lon, north_ref, south_ref):
    lane = lax.broadcasted_iota(jnp.int32, value.shape, 1)
    turned = pltpu.roll(lon[t], lax.rem(255 - 2 * k, 128), axis=1)
    value = value + jnp.where((lane == 0) | (lane == 127), turned, 0.0)
    row = lax.broadcasted_iota(jnp.int32, (8, 128), 0)
    at = pl.ds(t * layers + k, 1)
    top = value[0:8] + jnp.where(row == 0, north_ref[at, :], 0.0)
    low = value[24:32] + jnp.where(row == 7, south_ref[at, :], 0.0)
    return jnp.concatenate([top, value[8:24], low], axis=0)


def lon_merge(east_ref, west_ref, lon):
    lane = lax.broadcasted_iota(jnp.int32, east_ref.shape, 2)
    lon[...] = jnp.where(lane % 2 == 0, east_ref[...], west_ref[...])


def step_body(base, force_ref, mix_ref, inv_ref, up_ref, tr_ref, mask_ref, outs, v):
    w_out, lon_out, north_out, south_out = outs
    tracers, layers = force_ref.shape[:2]
    d = tuple((force_ref[t, 0] + base(t, 0)) * inv_ref[0] for t in range(tracers))
    for t in range(tracers):
        v[t, 0] = d[t]

    def forward(k, d):
        m, inv = mix_ref[k - 1], inv_ref[k]
        d = tuple((force_ref[t, k] + base(t, k) + m * d[t]) * inv for t in range(tracers))
        for t in range(tracers):
            v[t, k] = d[t]
        return d

    d = lax.fori_loop(1, layers, forward, d, unroll=5)

    def backward(i, x):
        k = layers - 2 - i
        u = up_ref[k]
        x = tuple(v[t, k] - u * x[t] for t in range(tracers))
        for t in range(tracers):
            v[t, k] = x[t]
        return x

    lax.fori_loop(0, layers - 1, backward, d, unroll=5)

    lane = lax.broadcasted_iota(jnp.int32, (32, 128), 1)
    row = lax.broadcasted_iota(jnp.int32, (32, 128), 0)
    lon_out[...] = jnp.zeros(lon_out.shape, F32)

    def across(k, _):
        te, tw, tn, ts = (tr_ref[i, k] for i in range(4))
        center = 1.0 - te - tw - tn - ts
        pair = (lane == 2 * k) | (lane == 2 * k + 1)
        for t in range(tracers):
            x = v[t, k]
            east = pltpu.roll(te * x, 1, axis=1)
            west = pltpu.roll(tw * x, 127, axis=1)
            north = pltpu.roll(tn * x, 1, axis=0)
            south = pltpu.roll(ts * x, 31, axis=0)
            out = center * x + jnp.where(lane == 0, west, jnp.where(lane == 127, east, east + west))
            w_out[t, k] = out + jnp.where(row == 0, 0.0, north) + jnp.where(row == 31, 0.0, south)
            ends = pltpu.roll(jnp.where(lane == 0, east, west), 2 * k + 1, axis=1)
            lon_out[t] = jnp.where(pair, ends, lon_out[t])
        return 0

    lax.fori_loop(0, layers, across, 0, unroll=2)

    for t in range(tracers):
        at = slice(t * layers, (t + 1) * layers)
        north_out[at, :] = v[t, :, 0, :] * tr_ref[3, :, 0, :] * mask_ref[0:1, :]
        south_out[at, :] = v[t, :, 31, :] * tr_ref[2, :, 31, :] * mask_ref[1:2, :]


def first_step_kernel(f, mix, inv, up, tr, mask, w_out, lon_out, north_out, south_out, v):
    step_body(lambda t, k: 0.0, f, mix, inv, up, tr, mask, (w_out, lon_out, north_out, south_out), v)


def step_kernel(
    w_in, east_in, west_in, north_in, south_in, flux_in, f, mix, inv, up, tr, mask,
    w_out, lon_out, north_out, south_out, flux_out, v, lon,
):
    tracers, layers = f.shape[:2]
    lon_merge(east_in, west_in, lon)

    def base(t, k):
        value = halo_add(w_in[t, k], t, k, layers, lon, north_in, south_in)
        if isinstance(k, int):
            flux_out[t] = flux_in[t] + value
        return value

    step_body(base, f, mix, inv, up, tr, mask, (w_out, lon_out, north_out, south_out), v)


def last_kernel(w_in, east_in, west_in, north_in, south_in, flux_in, adj_out, flux_out, lon):
    tracers, layers = w_in.shape[:2]
    lon_merge(east_in, west_in, lon)

    def finish(k, _):
        for t in range(tracers):
            adj_out[t, k] = halo_add(w_in[t, k], t, k, layers, lon, north_in, south_in)
        return 0

    lax.fori_loop(0, layers, finish, 0, unroll=2)
    flux_out[...] = flux_in[...] + adj_out[:, 0]


def shifts(axis):
    peers = lax.axis_size(axis)
    up = [(i, (i + 1) % peers) for i in range(peers)]
    return up, [(b, a) for a, b in up]


def exchange(lon, north, south):
    lat_up, lat_down = shifts("lat")
    lon_up, lon_down = shifts("lon")
    from_north = lax.ppermute(south, "lat", lat_up)
    from_south = lax.ppermute(north, "lat", lat_down)
    from_west = lax.ppermute(lon, "lon", lon_up)
    from_east = lax.ppermute(lon, "lon", lon_down)
    return from_east, from_west, from_north, from_south


def body(
    transport, mixing, trajectory, kernel_table, track_tile, sound_cell, kernel_index, observed, precision
):
    ntiles = lax.axis_size(("lat", "lon"))
    steps, tracers, layers, rows, cols = trajectory.shape
    field = sds(tracers, layers, rows, cols)
    plane = sds(tracers, rows, cols)
    edge = sds(tracers * layers, cols)
    slots = ntiles * CAP
    outgoing = call(
        route_kernel,
        sds(ntiles, 2, 128),
        track_tile[:, :, 0],
        sound_cell,
        kernel_index,
        observed,
        precision,
    )
    got = lax.all_to_all(outgoing, ("lat", "lon"), split_axis=0, concat_axis=0, tiled=True)
    inverse, upper = call(
        setup_kernel, (sds(layers, rows, cols), sds(layers - 1, rows, cols)), mixing
    )
    lat = lax.axis_index("lat")
    mask = jnp.stack([lat > 0, lat < lax.axis_size("lat") - 1]).astype(F32)
    mask = jnp.broadcast_to(mask[:, None], (2, cols))
    snd = call(unpack_kernel, sds(steps, 8, slots), got)
    table = kernel_table.T
    chunk = 256

    def forcing(s):
        return call(
            functools.partial(forcing_kernel, s, chunk),
            field,
            snd,
            trajectory,
            table,
            scratch=(
                pltpu.VMEM((256, slots), BF16),
                pltpu.VMEM((layers, 16, slots), F32),
                pltpu.VMEM((8, slots), F32),
            ),
        )

    fixed = (mixing, inverse, upper, transport, mask)
    v = pltpu.VMEM((tracers, layers, rows, cols), F32)
    lon = pltpu.VMEM((tracers, rows, cols), F32)
    moved = (field, plane, edge, edge)
    w, *edges = call(first_step_kernel, moved, forcing(steps - 1), *fixed, scratch=(v,))
    flux = jnp.zeros((tracers, rows, cols), F32)
    for s in range(steps - 2, -1, -1):
        halos = exchange(*edges)
        w, *edges, flux = call(
            step_kernel, moved + (plane,), w, *halos, flux, forcing(s), *fixed, scratch=(v, lon)
        )
    return call(last_kernel, (field, plane), w, *exchange(*edges), flux, scratch=(lon,))


def solution(mesh):
    return jax.shard_map(
        body,
        mesh=mesh,
        in_specs=(
            P(None, None, "lat", "lon"),
            P(None, "lat", "lon"),
            P(None, None, None, "lat", "lon"),
            P(),
            P(None, ("lat", "lon"), None),
            P(None, ("lat", "lon")),
            P(None, ("lat", "lon")),
            P(None, None, ("lat", "lon")),
            P(None, ("lat", "lon")),
        ),
        out_specs=(P(None, None, "lat", "lon"), P(None, "lat", "lon")),
        check_vma=False,
    )
```

profile of v0, /device:TPU:0, one launch (start us, length us, event | category | flops | bytes accessed | tf_op | source)
XLA Modules:
  0.0 113.9 jit_solution(11838106175819322525)
XLA Ops:
  4.2 2.0 %shard_map.104 = f32[128,2,128]{2,1,0:T(2,128)} custom-call(s32[4,512]{1,0:T(4,128)S(1)} %bitcast.10, s32[4,512]{1,0:T(4,128)S(1)} %copy-done.6, s32[4,512]{1,0:T(4,128)S(1)} %copy-done.7, f32[4,3,512]{2,1,0:T(4,128)S(1)} %copy.11.obs_ref, f32[4,512]{1,0:T(4,128)S(1)} %copy-done.8), custom_call_target="tpu_custom_call" | custom-call | tf_op jit(solution)/shard_map/pallas_call | solution.py:37
  6.1 11.1 %all-to-all-start = ((f32[128,2,128]{2,1,0:T(2,128)}), f32[128,2,128]{2,1,0:T(2,128)S(1)}, u32[]{:S(2)}, u32[]{:S(2)}) async-start(f32[128,2,128]{2,1,0:T(2,128)} %shard_map.104), calls=%async_computation | async-start | bytes 262144 | tf_op jit(solution)/shard_map/all_to_all | solution.py:301
  17.3 1.1 copy-done.3
  18.8 8.1 %all-to-all-done.got_ref = f32[128,2,128]{2,1,0:T(2,128)S(1)} async-done(((f32[128,2,128]{2,1,0:T(2,128)}), f32[128,2,128]{2,1,0:T(2,128)S(1)}, u32[]{:S(2)}, u32[]{:S(2)}) %all-to-all-start) | async-done | bytes 131104 | tf_op jit(solution)/shard_map/all_to_all | solution.py:301
  27.1 2.0 %copy-done = bf16[4,3,36,32,128]{4,3,2,1,0:T(8,128)(2,1)S(1)} copy-done((bf16[4,3,36,32,128]{4,3,2,1,0:T(8,128)(2,1)S(1)}, bf16[4,3,36,32,128]{4,3,2,1,0:T(8,128)(2,1)}, u32[]{:S(2)}) %copy-start) | copy-done | bytes 3538968
  29.8 6.4 %shard_map.106.f = f32[3,36,32,128]{3,2,1,0:T(8,128)S(1)} custom-call(f32[4,8,1024]{2,1,0:T(8,128)S(1)} %shard_map.105.snd_ref, bf16[4,3,36,32,128]{4,3,2,1,0:T(8,128)(2,1)S(1)} %copy-done, f32[36,64]{1,0:T(8,128)S(1)} %bitcast.6), custom_call_target="tpu_custom_call" | custom-call | tf_op jit(solution)/shard_map/pallas_call | solution.py:37
  36.3 4.0 %shard_map.108 = (f32[3,36,32,128]{3,2,1,0:T(8,128)S(1)}, f32[3,32,128]{2,1,0:T(8,128)S(1)}, f32[108,128]{1,0:T(8,128)S(1)}, f32[108,128]{1,0:T(8,128)S(1)}) custom-call(f32[3,36,32,128]{3,2,1,0:T(8,128)S(1)} %shard_map.106.f, f32[35,32,128]{2,1,0:T(8,128)S(1)} %copy-done.4, f32[36,32,128]{2,1,0:T(8,128)S(1)} %get-tuple-element.23.inv, ...), custom_call_target="tpu_custom_call" | custom-call | tf_op jit(solution)/shard_map/pallas_call | solution.py:37
  40.3 2.9 %collective-permute-start.3 = (f32[108,128]{1,0:T(8,128)S(1)}, f32[108,128]{1,0:T(8,128)S(1)}, u32[]{:S(2)}, u32[]{:S(2)}) collective-permute-start(f32[108,128]{1,0:T(8,128)S(1)} %get-tuple-element.28), channel_id=1, source_target_pairs={{16,0},{32,16},{48,32},{64,48},{80,64},{96,80},{112,96},{0,112},{1... | collective-permute-start | bytes 165896 | tf_op jit(solution)/shard_map/ppermute | solution.py:277
  43.3 1.3 %collective-permute-start = (f32[3,32,128]{2,1,0:T(8,128)S(1)}, f32[3,32,128]{2,1,0:T(8,128)S(1)}, u32[]{:S(2)}, u32[]{:S(2)}) collective-permute-start(f32[3,32,128]{2,1,0:T(8,128)S(1)} %get-tuple-element.26), channel_id=1, source_target_pairs={{1,0},{2,1},{3,2},{4,3},{5,4},{6,5},{7,6},{8,7},{9,8},{10,9},{11,1... | collective-permute-start | bytes 147464 | tf_op jit(solution)/shard_map/ppermute | solution.py:279
  45.3 6.4 %shard_map.109.f = f32[3,36,32,128]{3,2,1,0:T(8,128)S(1)} custom-call(f32[4,8,1024]{2,1,0:T(8,128)S(1)} %shard_map.105.snd_ref, bf16[4,3,36,32,128]{4,3,2,1,0:T(8,128)(2,1)S(1)} %copy-done.1, f32[36,64]{1,0:T(8,128)S(1)} %bitcast.7), custom_call_target="tpu_custom_call" | custom-call | tf_op jit(solution)/shard_map/pallas_call | solution.py:37
  52.0 4.9 %shard_map.110 = (f32[3,36,32,128]{3,2,1,0:T(8,128)S(1)}, f32[3,32,128]{2,1,0:T(8,128)S(1)}, f32[108,128]{1,0:T(8,128)S(1)}, f32[108,128]{1,0:T(8,128)S(1)}, f32[3,32,128]{2,1,0:T(8,128)S(1)}) custom-call(f32[3,36,32,128]{3,2,1,0:T(8,128)S(1)} %get-tuple-element.25.w_in, f32[3,32,128]{2,1,0:T(8,128)S(1)} %collective-permute-done.east_in, ...), custom_call_target="tpu_custom_call" | custom-call | tf_op jit(solution)/shard_map/pallas_call | solution.py:37
  56.9 2.9 %collective-permute-start.7 = (f32[108,128]{1,0:T(8,128)S(1)}, f32[108,128]{1,0:T(8,128)S(1)}, u32[]{:S(2)}, u32[]{:S(2)}) collective-permute-start(f32[108,128]{1,0:T(8,128)S(1)} %get-tuple-element.32), channel_id=1, source_target_pairs={{16,0},{32,16},{48,32},{64,48},{80,64},{96,80},{112,96},{0,112},{1... | collective-permute-start | bytes 165896 | tf_op jit(solution)/shard_map/ppermute | solution.py:277
  59.8 4.4 %collective-permute-start.4 = (f32[3,32,128]{2,1,0:T(8,128)S(1)}, f32[3,32,128]{2,1,0:T(8,128)S(1)}, u32[]{:S(2)}, u32[]{:S(2)}) collective-permute-start(f32[3,32,128]{2,1,0:T(8,128)S(1)} %get-tuple-element.30), channel_id=1, source_target_pairs={{1,0},{2,1},{3,2},{4,3},{5,4},{6,5},{7,6},{8,7},{9,8},{10,9},{11,1... | collective-permute-start | bytes 147464 | tf_op jit(solution)/shard_map/ppermute | solution.py:279
  64.2 6.4 %shard_map.111.f = f32[3,36,32,128]{3,2,1,0:T(8,128)S(1)} custom-call(f32[4,8,1024]{2,1,0:T(8,128)S(1)} %shard_map.105.snd_ref, bf16[4,3,36,32,128]{4,3,2,1,0:T(8,128)(2,1)S(1)} %copy-done.1, f32[36,64]{1,0:T(8,128)S(1)} %bitcast.8), custom_call_target="tpu_custom_call" | custom-call | tf_op jit(solution)/shard_map/pallas_call | solution.py:37
  71.6 4.9 %shard_map.112 = (f32[3,36,32,128]{3,2,1,0:T(8,128)S(1)}, f32[3,32,128]{2,1,0:T(8,128)S(1)}, f32[108,128]{1,0:T(8,128)S(1)}, f32[108,128]{1,0:T(8,128)S(1)}, f32[3,32,128]{2,1,0:T(8,128)S(1)}) custom-call(f32[3,36,32,128]{3,2,1,0:T(8,128)S(1)} %get-tuple-element.29.w_in, f32[3,32,128]{2,1,0:T(8,128)S(1)} %collective-permute-done.4.east_in, ...), custom_call_target="tpu_custom_call" | custom-call | tf_op jit(solution)/shard_map/pallas_call | solution.py:37
  76.5 2.9 %collective-permute-start.11 = (f32[108,128]{1,0:T(8,128)S(1)}, f32[108,128]{1,0:T(8,128)S(1)}, u32[]{:S(2)}, u32[]{:S(2)}) collective-permute-start(f32[108,128]{1,0:T(8,128)S(1)} %get-tuple-element.37), channel_id=1, source_target_pairs={{16,0},{32,16},{48,32},{64,48},{80,64},{96,80},{112,96},{0,112},{1... | collective-permute-start | bytes 165896 | tf_op jit(solution)/shard_map/ppermute | solution.py:277
  79.5 4.4 %collective-permute-start.8 = (f32[3,32,128]{2,1,0:T(8,128)S(1)}, f32[3,32,128]{2,1,0:T(8,128)S(1)}, u32[]{:S(2)}, u32[]{:S(2)}) collective-permute-start(f32[3,32,128]{2,1,0:T(8,128)S(1)} %get-tuple-element.35), channel_id=1, source_target_pairs={{1,0},{2,1},{3,2},{4,3},{5,4},{6,5},{7,6},{8,7},{9,8},{10,9},{11,1... | collective-permute-start | bytes 147464 | tf_op jit(solution)/shard_map/ppermute | solution.py:279
  83.9 6.4 %shard_map.113.f = f32[3,36,32,128]{3,2,1,0:T(8,128)S(1)} custom-call(f32[4,8,1024]{2,1,0:T(8,128)S(1)} %shard_map.105.snd_ref, bf16[4,3,36,32,128]{4,3,2,1,0:T(8,128)(2,1)S(1)} %copy-done.1, f32[36,64]{1,0:T(8,128)S(1)} %bitcast.9), custom_call_target="tpu_custom_call" | custom-call | tf_op jit(solution)/shard_map/pallas_call | solution.py:37
  91.3 4.9 %shard_map.114 = (f32[3,36,32,128]{3,2,1,0:T(8,128)S(1)}, f32[3,32,128]{2,1,0:T(8,128)S(1)}, f32[108,128]{1,0:T(8,128)S(1)}, f32[108,128]{1,0:T(8,128)S(1)}, f32[3,32,128]{2,1,0:T(8,128)S(1)}) custom-call(f32[3,36,32,128]{3,2,1,0:T(8,128)S(1)} %get-tuple-element.34.w_in, f32[3,32,128]{2,1,0:T(8,128)S(1)} %collective-permute-done.8.east_in, ...), custom_call_target="tpu_custom_call" | custom-call | tf_op jit(solution)/shard_map/pallas_call | solution.py:37
  96.2 2.9 %collective-permute-start.15 = (f32[108,128]{1,0:T(8,128)S(1)}, f32[108,128]{1,0:T(8,128)S(1)}, u32[]{:S(2)}, u32[]{:S(2)}) collective-permute-start(f32[108,128]{1,0:T(8,128)S(1)} %get-tuple-element.42), channel_id=1, source_target_pairs={{16,0},{32,16},{48,32},{64,48},{80,64},{96,80},{112,96},{0,112},{1... | collective-permute-start | bytes 165896 | tf_op jit(solution)/shard_map/ppermute | solution.py:277
  99.1 4.4 %collective-permute-start.12 = (f32[3,32,128]{2,1,0:T(8,128)S(1)}, f32[3,32,128]{2,1,0:T(8,128)S(1)}, u32[]{:S(2)}, u32[]{:S(2)}) collective-permute-start(f32[3,32,128]{2,1,0:T(8,128)S(1)} %get-tuple-element.40), channel_id=1, source_target_pairs={{1,0},{2,1},{3,2},{4,3},{5,4},{6,5},{7,6},{8,7},{9,8},{10,9},{11,1... | collective-permute-start | bytes 147464 | tf_op jit(solution)/shard_map/ppermute | solution.py:279
  103.5 1.7 %collective-permute-done.12.east_in = f32[3,32,128]{2,1,0:T(8,128)S(1)} collective-permute-done((f32[3,32,128]{2,1,0:T(8,128)S(1)}, f32[3,32,128]{2,1,0:T(8,128)S(1)}, u32[]{:S(2)}, u32[]{:S(2)}) %collective-permute-start.12) | collective-permute-done | bytes 49184 | tf_op jit(solution)/shard_map/ppermute | solution.py:279
  105.3 5.7 %collective-permute-done.13.west_in = f32[3,32,128]{2,1,0:T(8,128)S(1)} collective-permute-done((f32[3,32,128]{2,1,0:T(8,128)S(1)}, f32[3,32,128]{2,1,0:T(8,128)S(1)}, u32[]{:S(2)}, u32[]{:S(2)}) %collective-permute-start.13) | collective-permute-done | bytes 49184 | tf_op jit(solution)/shard_map/ppermute | solution.py:278
  110.9 3.0 %shard_map.115 = (f32[3,36,32,128]{3,2,1,0:T(8,128)}, f32[3,32,128]{2,1,0:T(8,128)}) custom-call(f32[3,36,32,128]{3,2,1,0:T(8,128)S(1)} %get-tuple-element.39.w_in, f32[3,32,128]{2,1,0:T(8,128)S(1)} %collective-permute-done.12.east_in, f32[3,32,128]{2,1,0:T(8,128)S(1)} %collective-permute-done.13.west_in, f32[108,128]{1,0:T(8,128)S(1)} %collective-permute-done.14.north_in, ...), custom_call_target="tpu_custom_call" | custom-call | tf_op jit(solution)/shard_map/pallas_call | solution.py:37
  (45 shorter events, 8.0 us)
Async XLA Ops:
  2.1 0.7 copy-start.6
  6.1 20.8 %all-to-all-start = ((f32[128,2,128]{2,1,0:T(2,128)}), f32[128,2,128]{2,1,0:T(2,128)S(1)}, u32[]{:S(2)}, u32[]{:S(2)}) async-start(f32[128,2,128]{2,1,0:T(2,128)} %shard_map.104), calls=%async_computation | async-start | bytes 262144 | tf_op jit(solution)/shard_map/all_to_all | solution.py:301
  17.3 1.1 copy-start.3
  27.1 2.0 %copy-start = (bf16[4,3,36,32,128]{4,3,2,1,0:T(8,128)(2,1)S(1)}, bf16[4,3,36,32,128]{4,3,2,1,0:T(8,128)(2,1)}, u32[]{:S(2)}) copy-start(bf16[4,3,36,32,128]{4,3,2,1,0:T(8,128)(2,1)} %traj_ref.7) | copy-start | bytes 10616836
  29.1 0.7 copy-start.5
  29.8 6.5 %copy-start.2 = (f32[4,36,32,128]{3,2,1,0:T(8,128)S(1)}, f32[4,36,32,128]{3,2,1,0:T(8,128)}, u32[]{:S(2)}) copy-start(f32[4,36,32,128]{3,2,1,0:T(8,128)} %tr.7) | copy-start | bytes 7077892
  29.8 6.5 %copy-start.4 = (f32[35,32,128]{2,1,0:T(8,128)S(1)}, f32[35,32,128]{2,1,0:T(8,128)}, u32[]{:S(2)}) copy-start(f32[35,32,128]{2,1,0:T(8,128)} %mix.7) | copy-start | bytes 1720324
  36.3 9.0 %copy-start.1 = (bf16[4,3,36,32,128]{4,3,2,1,0:T(8,128)(2,1)S(1)}, bf16[4,3,36,32,128]{4,3,2,1,0:T(8,128)(2,1)}, u32[]{:S(2)}) copy-start(bf16[4,3,36,32,128]{4,3,2,1,0:T(8,128)(2,1)} %traj_ref.7) | copy-start | bytes 10616836
  40.3 11.7 %collective-permute-start.2 = (f32[108,128]{1,0:T(8,128)S(1)}, f32[108,128]{1,0:T(8,128)S(1)}, u32[]{:S(2)}, u32[]{:S(2)}) collective-permute-start(f32[108,128]{1,0:T(8,128)S(1)} %get-tuple-element.27), channel_id=1, source_target_pairs={{0,16},{16,32},{32,48},{48,64},{64,80},{80,96},{96,112},{112,0},{1... | collective-permute-start | bytes 165896 | tf_op jit(solution)/shard_map/ppermute | solution.py:276
  40.3 11.6 %collective-permute-start.3 = (f32[108,128]{1,0:T(8,128)S(1)}, f32[108,128]{1,0:T(8,128)S(1)}, u32[]{:S(2)}, u32[]{:S(2)}) collective-permute-start(f32[108,128]{1,0:T(8,128)S(1)} %get-tuple-element.28), channel_id=1, source_target_pairs={{16,0},{32,16},{48,32},{64,48},{80,64},{96,80},{112,96},{0,112},{1... | collective-permute-start | bytes 165896 | tf_op jit(solution)/shard_map/ppermute | solution.py:277
  43.3 8.4 %collective-permute-start = (f32[3,32,128]{2,1,0:T(8,128)S(1)}, f32[3,32,128]{2,1,0:T(8,128)S(1)}, u32[]{:S(2)}, u32[]{:S(2)}) collective-permute-start(f32[3,32,128]{2,1,0:T(8,128)S(1)} %get-tuple-element.26), channel_id=1, source_target_pairs={{1,0},{2,1},{3,2},{4,3},{5,4},{6,5},{7,6},{8,7},{9,8},{10,9},{11,1... | collective-permute-start | bytes 147464 | tf_op jit(solution)/shard_map/ppermute | solution.py:279
  44.6 7.4 %collective-permute-start.1 = (f32[3,32,128]{2,1,0:T(8,128)S(1)}, f32[3,32,128]{2,1,0:T(8,128)S(1)}, u32[]{:S(2)}, u32[]{:S(2)}) collective-permute-start(f32[3,32,128]{2,1,0:T(8,128)S(1)} %get-tuple-element.26), channel_id=1, source_target_pairs={{0,1},{1,2},{2,3},{3,4},{4,5},{5,6},{6,7},{7,8},{8,9},{9,10},{10,1... | collective-permute-start | bytes 147464 | tf_op jit(solution)/shard_map/ppermute | solution.py:278
  56.9 14.8 %collective-permute-start.6 = (f32[108,128]{1,0:T(8,128)S(1)}, f32[108,128]{1,0:T(8,128)S(1)}, u32[]{:S(2)}, u32[]{:S(2)}) collective-permute-start(f32[108,128]{1,0:T(8,128)S(1)} %get-tuple-element.31), channel_id=1, source_target_pairs={{0,16},{16,32},{32,48},{48,64},{64,80},{80,96},{96,112},{112,0},{1... | collective-permute-start | bytes 165896 | tf_op jit(solution)/shard_map/ppermute | solution.py:276
  56.9 14.8 %collective-permute-start.7 = (f32[108,128]{1,0:T(8,128)S(1)}, f32[108,128]{1,0:T(8,128)S(1)}, u32[]{:S(2)}, u32[]{:S(2)}) collective-permute-start(f32[108,128]{1,0:T(8,128)S(1)} %get-tuple-element.32), channel_id=1, source_target_pairs={{16,0},{32,16},{48,32},{64,48},{80,64},{96,80},{112,96},{0,112},{1... | collective-permute-start | bytes 165896 | tf_op jit(solution)/shard_map/ppermute | solution.py:277
  59.8 10.8 %collective-permute-start.4 = (f32[3,32,128]{2,1,0:T(8,128)S(1)}, f32[3,32,128]{2,1,0:T(8,128)S(1)}, u32[]{:S(2)}, u32[]{:S(2)}) collective-permute-start(f32[3,32,128]{2,1,0:T(8,128)S(1)} %get-tuple-element.30), channel_id=1, source_target_pairs={{1,0},{2,1},{3,2},{4,3},{5,4},{6,5},{7,6},{8,7},{9,8},{10,9},{11,1... | collective-permute-start | bytes 147464 | tf_op jit(solution)/shard_map/ppermute | solution.py:279
  64.2 7.4 %collective-permute-start.5 = (f32[3,32,128]{2,1,0:T(8,128)S(1)}, f32[3,32,128]{2,1,0:T(8,128)S(1)}, u32[]{:S(2)}, u32[]{:S(2)}) collective-permute-start(f32[3,32,128]{2,1,0:T(8,128)S(1)} %get-tuple-element.30), channel_id=1, source_target_pairs={{0,1},{1,2},{2,3},{3,4},{4,5},{5,6},{6,7},{7,8},{8,9},{9,10},{10,1... | collective-permute-start | bytes 147464 | tf_op jit(solution)/shard_map/ppermute | solution.py:278
  76.5 14.8 %collective-permute-start.10 = (f32[108,128]{1,0:T(8,128)S(1)}, f32[108,128]{1,0:T(8,128)S(1)}, u32[]{:S(2)}, u32[]{:S(2)}) collective-permute-start(f32[108,128]{1,0:T(8,128)S(1)} %get-tuple-element.36), channel_id=1, source_target_pairs={{0,16},{16,32},{32,48},{48,64},{64,80},{80,96},{96,112},{112,0},{1... | collective-permute-start | bytes 165896 | tf_op jit(solution)/shard_map/ppermute | solution.py:276
  76.5 14.8 %collective-permute-start.11 = (f32[108,128]{1,0:T(8,128)S(1)}, f32[108,128]{1,0:T(8,128)S(1)}, u32[]{:S(2)}, u32[]{:S(2)}) collective-permute-start(f32[108,128]{1,0:T(8,128)S(1)} %get-tuple-element.37), channel_id=1, source_target_pairs={{16,0},{32,16},{48,32},{64,48},{80,64},{96,80},{112,96},{0,112},{1... | collective-permute-start | bytes 165896 | tf_op jit(solution)/shard_map/ppermute | solution.py:277
  79.5 10.8 %collective-permute-start.8 = (f32[3,32,128]{2,1,0:T(8,128)S(1)}, f32[3,32,128]{2,1,0:T(8,128)S(1)}, u32[]{:S(2)}, u32[]{:S(2)}) collective-permute-start(f32[3,32,128]{2,1,0:T(8,128)S(1)} %get-tuple-element.35), channel_id=1, source_target_pairs={{1,0},{2,1},{3,2},{4,3},{5,4},{6,5},{7,6},{8,7},{9,8},{10,9},{11,1... | collective-permute-start | bytes 147464 | tf_op jit(solution)/shard_map/ppermute | solution.py:279
  83.9 7.4 %collective-permute-start.9 = (f32[3,32,128]{2,1,0:T(8,128)S(1)}, f32[3,32,128]{2,1,0:T(8,128)S(1)}, u32[]{:S(2)}, u32[]{:S(2)}) collective-permute-start(f32[3,32,128]{2,1,0:T(8,128)S(1)} %get-tuple-element.35), channel_id=1, source_target_pairs={{0,1},{1,2},{2,3},{3,4},{4,5},{5,6},{6,7},{7,8},{8,9},{9,10},{10,1... | collective-permute-start | bytes 147464 | tf_op jit(solution)/shard_map/ppermute | solution.py:278
  96.2 14.8 %collective-permute-start.14 = (f32[108,128]{1,0:T(8,128)S(1)}, f32[108,128]{1,0:T(8,128)S(1)}, u32[]{:S(2)}, u32[]{:S(2)}) collective-permute-start(f32[108,128]{1,0:T(8,128)S(1)} %get-tuple-element.41), channel_id=1, source_target_pairs={{0,16},{16,32},{32,48},{48,64},{64,80},{80,96},{96,112},{112,0},{1... | collective-permute-start | bytes 165896 | tf_op jit(solution)/shard_map/ppermute | solution.py:276
  96.2 14.8 %collective-permute-start.15 = (f32[108,128]{1,0:T(8,128)S(1)}, f32[108,128]{1,0:T(8,128)S(1)}, u32[]{:S(2)}, u32[]{:S(2)}) collective-permute-start(f32[108,128]{1,0:T(8,128)S(1)} %get-tuple-element.42), channel_id=1, source_target_pairs={{16,0},{32,16},{48,32},{64,48},{80,64},{96,80},{112,96},{0,112},{1... | collective-permute-start | bytes 165896 | tf_op jit(solution)/shard_map/ppermute | solution.py:277
  99.1 6.1 %collective-permute-start.12 = (f32[3,32,128]{2,1,0:T(8,128)S(1)}, f32[3,32,128]{2,1,0:T(8,128)S(1)}, u32[]{:S(2)}, u32[]{:S(2)}) collective-permute-start(f32[3,32,128]{2,1,0:T(8,128)S(1)} %get-tuple-element.40), channel_id=1, source_target_pairs={{1,0},{2,1},{3,2},{4,3},{5,4},{6,5},{7,6},{8,7},{9,8},{10,9},{11,1... | collective-permute-start | bytes 147464 | tf_op jit(solution)/shard_map/ppermute | solution.py:279
  103.5 7.4 %collective-permute-start.13 = (f32[3,32,128]{2,1,0:T(8,128)S(1)}, f32[3,32,128]{2,1,0:T(8,128)S(1)}, u32[]{:S(2)}, u32[]{:S(2)}) collective-permute-start(f32[3,32,128]{2,1,0:T(8,128)S(1)} %get-tuple-element.40), channel_id=1, source_target_pairs={{0,1},{1,2},{2,3},{3,4},{4,5},{5,6},{6,7},{7,8},{8,9},{9,10},{10,1... | collective-permute-start | bytes 147464 | tf_op jit(solution)/shard_map/ppermute | solution.py:278
  (2 other events, 1.4 us)
where the time goes:
time: 114 us
  Pallas kernels  49.7 us (44%)
  starting transfers between devices  38.2 us (34%)
  waiting for transfers between devices  17.8 us (16%)
  local copies, waits for them, and re-layouts  7.41 us (6%)
    pallas_call x12, Pallas kernels, call(): pl.pallas_call(kernel, out_shape=outs, in_specs=[pl.BlockSpec(memory_spac...  49.7 us
    ppermute x4, starting transfers between devices, exchange(): from_east = lax.ppermute(lon, 'lon', lon_down)  14.4 us
    ppermute x4, starting transfers between devices, exchange(): from_south = lax.ppermute(north, 'lat', lat_down)  11.8 us
    all_to_all x1, starting transfers between devices, body(): lax.all_to_all(outgoing, ('lat', 'lon'), split_axis=0, concat_axis=0, til...  11.1 us
    all_to_all x1, waiting for transfers between devices, body(): lax.all_to_all(outgoing, ('lat', 'lon'), split_axis=0, concat_axis=0, til...  8.13 us
    ppermute x4, waiting for transfers between devices, exchange(): from_west = lax.ppermute(lon, 'lon', lon_up)  7.85 us
    unnamed x20, local copies, waits for them, and re-layouts  7.33 us
  transfers between devices with their start and end apart: 17, of which 6 were waited for; matrix products, arithmetic and copies ran while one was open for 0% of the time, Pallas kernels for 17%

commit v1 on v0

v1 whole, which is shorter than its diff:
```python
import functools

import jax
import jax.numpy as jnp
from jax import lax
from jax.experimental import pallas as pl
from jax.experimental.pallas import tpu as pltpu
from jax.sharding import PartitionSpec as P

CAP = 8
WORDS = 5
F32 = jnp.float32
BF16 = jnp.bfloat16


def split3(x):
    hi = x.astype(BF16)
    rest = x - hi.astype(F32)
    mid = rest.astype(BF16)
    return hi, mid, (rest - mid.astype(F32)).astype(BF16)


def split2(x):
    hi = x.astype(BF16)
    return hi, (x - hi.astype(F32)).astype(BF16)


def dot(a, b):
    return jnp.dot(a, b, preferred_element_type=F32)


def dot_t(a, b):
    return lax.dot_general(a, b, (((1,), (1,)), ((), ())), preferred_element_type=F32)


VMEM = pl.BlockSpec(memory_space=pltpu.VMEM)
HBM = pl.BlockSpec(memory_space=pltpu.HBM)


def call(kernel, outs, *args, scratch=(), vmem=12 << 20, hbm=(), hbm_out=()):
    outs = tuple(outs) if isinstance(outs, (tuple, list)) else (outs,)
    args = [pltpu.with_memory_space_constraint(a, pltpu.HBM) if i in hbm else a for i, a in enumerate(args)]
    done = pl.pallas_call(
        kernel,
        out_shape=outs,
        in_specs=[HBM if i in hbm else VMEM for i in range(len(args))],
        out_specs=tuple(HBM if i in hbm_out else VMEM for i in range(len(outs))),
        scratch_shapes=list(scratch),
        compiler_params=pltpu.CompilerParams(vmem_limit_bytes=vmem),
    )(*args)
    return done if len(outs) > 1 else done[0]


def sds(*shape, dtype=F32):
    return jax.ShapeDtypeStruct(shape, dtype)


def route_kernel(
    tile_in, cell_in, index_in, obs_in, prec_in, out_ref, tile_ref, cell_ref, index_ref, obs_ref, prec_ref, sems
):
    copies = [
        pltpu.make_async_copy(src, dst, sems.at[i])
        for i, (src, dst) in enumerate(
            (
                (tile_in, tile_ref),
                (cell_in, cell_ref),
                (index_in, index_ref),
                (obs_in, obs_ref),
                (prec_in, prec_ref),
            )
        )
    ]
    for copy in copies:
        copy.start()
    steps, count = cell_ref.shape
    ntiles = out_ref.shape[0]
    tile_ids = lax.broadcasted_iota(jnp.int32, (ntiles, count), 0)
    before = (
        lax.broadcasted_iota(jnp.int32, (count, count), 0)
        < lax.broadcasted_iota(jnp.int32, (count, count), 1)
    ).astype(F32).astype(BF16)
    rank_ids = lax.broadcasted_iota(jnp.int32, (CAP, count), 0)
    pad = jnp.zeros((64 - CAP * WORDS, count), F32)
    half = jnp.zeros((64, count), F32)
    for copy in copies:
        copy.wait()
    for pair in range(steps // 2):
        total = None
        for side in range(2):
            s = 2 * pair + side
            mine = tile_ids == tile_ref[s]
            mine_f = mine.astype(F32)
            mine_b = mine_f.astype(BF16)
            seen = dot(mine_b, before)
            rank = jnp.sum(mine_f * seen, axis=0, keepdims=True).astype(jnp.int32)
            at_rank = rank_ids == rank
            code = (index_ref[s : s + 1, :] * 4096 + cell_ref[s : s + 1, :]).astype(F32)
            words = [code] + [obs_ref[t, s : s + 1, :] for t in range(3)] + [prec_ref[s : s + 1, :]]
            rows = [jnp.where(at_rank, w, 0.0) for w in words]
            block = jnp.concatenate(rows + [pad] + [half], axis=0)
            if side == 1:
                block = jnp.concatenate([half] + rows + [pad], axis=0)
            for part in split3(block):
                term = dot_t(mine_b, part)
                total = term if total is None else total + term
        out_ref[:, pair, :] = total


def unpack_kernel(got_ref, out_ref):
    ntiles = got_ref.shape[0]
    for pair in range(2):
        turned = got_ref[:, pair, :].T
        for side in range(2):
            s = 2 * pair + side
            base = 64 * side
            code = turned[base : base + CAP, :].astype(jnp.int32)
            kidx = code // 4096
            cell = code - kidx * 4096
            row = cell // 128
            col = cell - row * 128
            hi = row // 16
            fields = [hi * 128 + col, row - hi * 16, kidx]
            fields = [f.astype(F32) for f in fields]
            fields += [turned[base + CAP * w : base + CAP * (w + 1), :] for w in range(1, WORDS)]
            for f, value in enumerate(fields):
                for r in range(CAP):
                    out_ref[s, f : f + 1, r * ntiles : (r + 1) * ntiles] = value[r : r + 1, :]
            out_ref[s, 7:8, :] = jnp.zeros((1, CAP * ntiles), F32)


def forcing_kernel(s, chunk, snd_ref, traj_ref, table_ref, out_ref, pick, weight):
    tracers, layers = out_ref.shape[:2]
    slots = snd_ref.shape[2]
    nker = table_ref.shape[2]
    cell_ids = lax.broadcasted_iota(jnp.int32, (256, chunk), 0).astype(F32)
    low_ids = lax.broadcasted_iota(jnp.int32, (16, chunk), 0).astype(F32)
    ker_ids = lax.broadcasted_iota(jnp.int32, (nker, chunk), 0).astype(F32)
    for c in range(slots // chunk):
        at = pl.ds(c * chunk, chunk)
        pick[:, at] = jnp.where(cell_ids == snd_ref[s, 0:1, at], 1.0, 0.0).astype(BF16)
        low = jnp.where(low_ids == snd_ref[s, 1:2, at], 1.0, 0.0)
        ker = jnp.where(ker_ids == snd_ref[s, 2:3, at], 1.0, 0.0).astype(BF16)
        w = dot(table_ref[0], ker) + dot(table_ref[1], ker) + dot(table_ref[2], ker)
        for k in range(layers):
            weight[k, :, at] = w[k : k + 1, :] * low
    for t in range(tracers):
        lhs = jnp.concatenate(
            [
                traj_ref[s, t, :, 0:16, :].reshape(layers * 16, 128),
                traj_ref[s, t, :, 16:32, :].reshape(layers * 16, 128),
            ],
            axis=1,
        )
        force = None
        for c in range(slots // chunk):
            at = pl.ds(c * chunk, chunk)
            sampled = dot(lhs, pick[:, at]).reshape(layers, 16, chunk)
            model = jnp.sum(jnp.sum(sampled * weight[:, :, at], axis=0), axis=0, keepdims=True)
            sc = (model - snd_ref[s, 3 + t : 4 + t, at]) * snd_ref[s, 6:7, at]
            hi, lo = split2((weight[:, :, at] * sc).reshape(layers * 16, chunk))
            term = dot_t(hi, pick[:, at]) + dot_t(lo, pick[:, at])
            force = term if force is None else force + term
        out_ref[t, :, 0:16, :] = force[:, 0:128].reshape(layers, 16, 128)
        out_ref[t, :, 16:32, :] = force[:, 128:256].reshape(layers, 16, 128)


def setup_kernel(
    mask_ref, mix_in, tr_in, traj_in, table_in,
    mix_ref, inv_ref, up_ref, coef_ref, lat_w, lon_w, shift_ref, ends_ref, traj_ref, parts_ref, tr_ref, table_ref, sems,
):
    layers = inv_ref.shape[0]
    copies = [
        pltpu.make_async_copy(src, dst, sems.at[i])
        for i, (src, dst) in enumerate(
            ((mix_in, mix_ref), (tr_in, tr_ref), (table_in, table_ref), (traj_in, traj_ref))
        )
    ]
    for copy in copies:
        copy.start()
    src = lax.broadcasted_iota(jnp.int32, (256, 256), 0) % 128
    dst = lax.broadcasted_iota(jnp.int32, (256, 256), 1)
    dst = jnp.where(dst < 128, dst - 1, dst - 127)
    shift_ref[...] = jnp.where(src == dst, 1.0, 0.0).astype(BF16)
    end_row = lax.broadcasted_iota(jnp.int32, (8, 256), 0)
    end_lane = lax.broadcasted_iota(jnp.int32, (8, 256), 1) % 128
    ends = ((end_row == 0) & (end_lane == 127)) | ((end_row == 1) & (end_lane == 0))
    ends = jnp.where(ends, 1.0, 0.0).astype(BF16)
    ends_ref[...] = ends
    copies[0].wait()
    for k in range(layers):
        diag = jnp.ones_like(mix_ref[0])
        if k > 0:
            diag = diag + mix_ref[k - 1]
        if k < layers - 1:
            diag = diag + mix_ref[k]
        if k > 0:
            diag = diag + mix_ref[k - 1] * up
        inv = 1.0 / diag
        inv_ref[k] = inv
        if k < layers - 1:
            up = -mix_ref[k] * inv
            up_ref[k] = up
    copies[1].wait()
    lane = lax.broadcasted_iota(jnp.int32, (32, 128), 1)
    row = lax.broadcasted_iota(jnp.int32, (32, 128), 0)

    def coefs(k, _):
        te, tw, tn, ts = (tr_ref[i, k] for i in range(4))
        coef_ref[0, k] = jnp.where(lane == 0, 0.0, pltpu.roll(te, 1, axis=1))
        coef_ref[1, k] = jnp.where(lane == 127, 0.0, pltpu.roll(tw, 127, axis=1))
        coef_ref[2, k] = jnp.where(row == 0, 0.0, pltpu.roll(tn, 1, axis=0))
        coef_ref[3, k] = jnp.where(row == 31, 0.0, pltpu.roll(ts, 31, axis=0))
        coef_ref[4, k] = 1.0 - te - tw - tn - ts
        return 0

    lax.fori_loop(0, layers, coefs, 0, unroll=4)
    lat_w[0] = tr_ref[3, :, 0, :] * mask_ref[0:1, :]
    lat_w[1] = tr_ref[2, :, 31, :] * mask_ref[1:2, :]
    for side in range(2):
        flat = None
        for part in split3(tr_ref[side].reshape(layers * 32, 128)):
            term = dot_t(ends[:, 0:128], part)
            flat = term if flat is None else flat + term
        lon_w[side] = flat[side : side + 1, :]
    copies[2].wait()
    for i, part in enumerate(split3(table_ref[...])):
        parts_ref[i] = part
    copies[3].wait()


def spread(west_ref, east_ref, halo):
    tracers, layers, rows, cols = halo.shape
    size = layers * rows
    row = lax.broadcasted_iota(jnp.int32, (4, cols), 0)
    lane = lax.broadcasted_iota(jnp.int32, (4, cols), 1)
    place = ((row % 2 == 0) & (lane == 0)) | ((row % 2 == 1) & (lane == cols - 1))
    place = jnp.where(place, 1.0, 0.0).astype(BF16)
    for t in range(tracers):
        at = slice(t * size, (t + 1) * size)
        hi, lo = split2(jnp.concatenate([west_ref[:, at], east_ref[:, at]], axis=0))
        both = jnp.concatenate([hi, lo], axis=0)
        spot = lax.dot_general(both, place, (((0,), (0,)), ((), ())), preferred_element_type=F32)
        halo[t] = spot.reshape(layers, rows, cols)


def received(w_ref, halo, north_ref, south_ref, t, k):
    value = w_ref[t, k] + halo[t, k]
    row = lax.broadcasted_iota(jnp.int32, (8, 128), 0)
    at = pl.ds(t * w_ref.shape[1] + k, 1)
    top = value[0:8] + jnp.where(row == 0, north_ref[at, :], 0.0)
    low = value[24:32] + jnp.where(row == 7, south_ref[at, :], 0.0)
    return jnp.concatenate([top, value[8:24], low], axis=0)


def step_body(base, force_ref, fixed, outs, v):
    mix_ref, inv_ref, up_ref, coef_ref, lat_w, lon_w, shift_ref, ends_ref = fixed
    w_out, east_out, west_out, north_out, south_out = outs
    tracers, layers, rows, cols = force_ref.shape
    d = tuple((force_ref[t, 0] + base(t, 0)) * inv_ref[0] for t in range(tracers))
    for t in range(tracers):
        v[t, 0] = d[t]

    def forward(k, d):
        m, inv = mix_ref[k - 1], inv_ref[k]
        d = tuple((force_ref[t, k] + base(t, k) + m * d[t]) * inv for t in range(tracers))
        for t in range(tracers):
            v[t, k] = d[t]
        return d

    d = lax.fori_loop(1, layers, forward, d, unroll=5)

    def backward(i, x):
        k = layers - 2 - i
        u = up_ref[k]
        x = tuple(v[t, k] - u * x[t] for t in range(tracers))
        for t in range(tracers):
            v[t, k] = x[t]
        return x

    lax.fori_loop(0, layers - 1, backward, d, unroll=5)

    group = 12
    size = group * rows
    for t in range(tracers):
        for g in range(0, layers, group):
            x = v[t, g : g + group]
            hi, lo = split2(x.reshape(size, cols))
            both = jnp.concatenate([hi, lo], axis=1)
            moved = dot(both, shift_ref[...])
            ends = dot_t(ends_ref[...], both)
            to = pl.ds((t * layers + g) * rows, size)
            at = pl.ds(g * rows, size)
            east_out[:, to] = ends[0:1, :] * lon_w[0, :, at]
            west_out[:, to] = ends[1:2, :] * lon_w[1, :, at]
            c = [coef_ref[i, g : g + group].reshape(size, cols) for i in range(5)]
            down = jnp.stack([pltpu.roll(x[i], 1, axis=0) for i in range(group)])
            up = jnp.stack([pltpu.roll(x[i], rows - 1, axis=0) for i in range(group)])
            out = c[4] * x.reshape(size, cols) + c[0] * moved[:, :cols] + c[1] * moved[:, cols:]
            out = out + c[2] * down.reshape(size, cols) + c[3] * up.reshape(size, cols)
            w_out[t, g : g + group] = out.reshape(group, rows, cols)

    for t in range(tracers):
        at = slice(t * layers, (t + 1) * layers)
        north_out[at, :] = v[t, :, 0, :] * lat_w[0]
        south_out[at, :] = v[t, :, rows - 1, :] * lat_w[1]


def first_step_kernel(*refs):
    step_body(lambda t, k: 0.0, refs[0], refs[1:9], refs[9:14], refs[14])


def step_kernel(w_in, west_in, east_in, north_in, south_in, flux_in, *refs):
    force_ref, fixed, outs, (flux_out, v, halo) = refs[0], refs[1:9], refs[9:14], refs[14:]
    spread(west_in, east_in, halo)

    def base(t, k):
        value = received(w_in, halo, north_in, south_in, t, k)
        if isinstance(k, int):
            flux_out[t] = flux_in[t] + value
        return value

    step_body(base, force_ref, fixed, outs, v)


def last_kernel(w_in, west_in, east_in, north_in, south_in, flux_in, adj_out, flux_out, halo, done, sems):
    tracers, layers = w_in.shape[:2]
    spread(west_in, east_in, halo)
    copies = []
    for t in range(tracers):

        def finish(k, _):
            done[t, k] = received(w_in, halo, north_in, south_in, t, k)
            return 0

        lax.fori_loop(0, layers, finish, 0, unroll=4)
        copies.append(pltpu.make_async_copy(done.at[t], adj_out.at[t], sems.at[t]))
        copies[-1].start()
    flux_out[...] = flux_in[...] + done[:, 0]
    for copy in copies:
        copy.wait()


def shifts(axis):
    peers = lax.axis_size(axis)
    up = [(i, (i + 1) % peers) for i in range(peers)]
    return up, [(b, a) for a, b in up]


def exchange(east, west, north, south):
    lat_up, lat_down = shifts("lat")
    lon_up, lon_down = shifts("lon")
    from_north = lax.ppermute(south, "lat", lat_up)
    from_south = lax.ppermute(north, "lat", lat_down)
    from_west = lax.ppermute(east, "lon", lon_up)
    from_east = lax.ppermute(west, "lon", lon_down)
    return from_west, from_east, from_north, from_south


def body(
    transport, mixing, trajectory, kernel_table, track_tile, sound_cell, kernel_index, observed, precision
):
    ntiles = lax.axis_size(("lat", "lon"))
    steps, tracers, layers, rows, cols = trajectory.shape
    count = sound_cell.shape[1]
    field = sds(tracers, layers, rows, cols)
    plane = sds(tracers, rows, cols)
    lat_edge = sds(tracers * layers, cols)
    lon_edge = sds(1, tracers * layers * rows)
    slots = ntiles * CAP
    outgoing = call(
        route_kernel,
        sds(ntiles, 2, 128),
        track_tile.transpose(0, 2, 1),
        sound_cell,
        kernel_index,
        observed.transpose(1, 0, 2),
        precision,
        hbm=range(5),
        scratch=(
            pltpu.VMEM((steps, 1, count), jnp.int32),
            pltpu.VMEM((steps, count), jnp.int32),
            pltpu.VMEM((steps, count), jnp.int32),
            pltpu.VMEM((tracers, steps, count), F32),
            pltpu.VMEM((steps, count), F32),
            pltpu.SemaphoreType.DMA((5,)),
        ),
    )
    got = lax.all_to_all(outgoing, ("lat", "lon"), split_axis=0, concat_axis=0, tiled=True)
    lat = lax.axis_index("lat")
    mask = jnp.stack([lat > 0, lat < lax.axis_size("lat") - 1]).astype(F32)
    mask = jnp.broadcast_to(mask[:, None], (2, cols))
    *fixed, local, table = call(
        setup_kernel,
        (
            sds(*mixing.shape),
            sds(layers, rows, cols),
            sds(*mixing.shape),
            sds(5, layers, rows, cols),
            sds(2, layers, cols),
            sds(2, 1, layers * rows),
            sds(256, 256, dtype=BF16),
            sds(8, 256, dtype=BF16),
            sds(*trajectory.shape, dtype=BF16),
            sds(3, layers, kernel_table.shape[0], dtype=BF16),
        ),
        mask,
        mixing,
        transport,
        trajectory,
        kernel_table.T,
        hbm=(1, 2, 3, 4),
        scratch=(
            pltpu.VMEM(transport.shape, F32),
            pltpu.VMEM(kernel_table.shape[::-1], F32),
            pltpu.SemaphoreType.DMA((4,)),
        ),
    )
    snd = call(unpack_kernel, sds(steps, 8, slots), got)

    def forcing(s):
        return call(
            functools.partial(forcing_kernel, s, 512),
            field,
            snd,
            local,
            table,
            scratch=(pltpu.VMEM((256, slots), BF16), pltpu.VMEM((layers, 16, slots), F32)),
        )

    v = pltpu.VMEM(field.shape, F32)
    moved = (field, lon_edge, lon_edge, lat_edge, lat_edge)
    w, *edges = call(first_step_kernel, moved, forcing(steps - 1), *fixed, scratch=(v,))
    flux = jnp.zeros((tracers, rows, cols), F32)
    for s in range(steps - 2, -1, -1):
        halos = exchange(*edges)
        w, *edges, flux = call(
            step_kernel, moved + (plane,), w, *halos, flux, forcing(s), *fixed, scratch=(v, v)
        )
    return call(
        last_kernel,
        (field, plane),
        w,
        *exchange(*edges),
        flux,
        hbm_out=(0,),
        scratch=(v, v, pltpu.SemaphoreType.DMA((tracers,))),
    )


def solution(mesh):
    return jax.shard_map(
        body,
        mesh=mesh,
        in_specs=(
            P(None, None, "lat", "lon"),
            P(None, "lat", "lon"),
            P(None, None, None, "lat", "lon"),
            P(),
            P(None, ("lat", "lon"), None),
            P(None, ("lat", "lon")),
            P(None, ("lat", "lon")),
            P(None, None, ("lat", "lon")),
            P(None, ("lat", "lon")),
        ),
        out_specs=(P(None, None, "lat", "lon"), P(None, "lat", "lon")),
        check_vma=False,
    )
```

time: 114 us -> 89.6 us (0.79)
  waiting for transfers between devices: 17.8 us -> 1.73 us
  Pallas kernels: 49.7 us -> 34.7 us
  starting transfers between devices: 38.2 us -> 44.9 us
    pallas_call x12, Pallas kernels: 49.7 us -> 34.7 us  [call(): pl.pallas_call(kernel, out_shape=outs, in_specs=[HBM if i in hbm else VME...]
    all_to_all x1, waiting for transfers between devices: 8.13 us -> 0.01 us  [body(): lax.all_to_all(outgoing, ('lat', 'lon'), split_axis=0, concat_axis=0, til...]
    ppermute x8, waiting for transfers between devices: 9.61 us -> 1.7 us  [the longest x4 1.69 us: exchange(): from_west = lax.ppermute(east, 'lon', lon_up)]
    ppermute x8, starting transfers between devices: 15.2 us -> 21.4 us  [the longest x4 20.4 us: exchange(): from_east = lax.ppermute(west, 'lon', lon_down)]
    unnamed x20 -> x28, local copies, waits for them, and re-layouts: 7.33 us -> 6.66 us
  transfers between devices with their start and end apart: 17 -> 17, of which waited for: 6 -> 1; matrix products, arithmetic and copies ran while one was open for 0% -> 0% of each run, Pallas kernels for 17% -> 17%
where the time goes in v1:
time: 89.6 us; the launch traced here: 89.3 us
  starting transfers between devices  44.9 us (50%)
  Pallas kernels  34.7 us (39%)
  local copies, waits for them, and re-layouts  6.74 us (8%)
  waiting for transfers between devices  1.73 us (2%)
  between operations  1.13 us (1%)
    pallas_call x12, Pallas kernels, call(): pl.pallas_call(kernel, out_shape=outs, in_specs=[HBM if i in hbm else VME...  34.7 us
    ppermute x4, starting transfers between devices, exchange(): from_east = lax.ppermute(west, 'lon', lon_down)  20.4 us
    ppermute x4, starting transfers between devices, exchange(): from_south = lax.ppermute(north, 'lat', lat_down)  11.8 us
    all_to_all x1, starting transfers between devices, body(): lax.all_to_all(outgoing, ('lat', 'lon'), split_axis=0, concat_axis=0, til...  11.7 us
    unnamed x28, local copies, waits for them, and re-layouts  6.66 us
  transfers between devices with their start and end apart: 17, of which 1 were waited for; matrix products, arithmetic and copies ran while one was open for 0% of the time, Pallas kernels for 17%

profile of v1, /device:TPU:0, one launch (start us, length us, event | category | flops | bytes accessed | tf_op | source)
XLA Modules:
  0.0 89.3 jit_solution(4902204858586373805)
XLA Ops:
  0.6 2.8 %shard_map.104 = f32[128,2,128]{2,1,0:T(2,128)} custom-call(s32[4,1,512]{2,1,0:T(1,128)} %bitcast.7, s32[4,512]{1,0:T(4,128)} %cell_in.1, s32[4,512]{1,0:T(4,128)} %index_in.1, f32[3,4,512]{2,1,0:T(4,128)} %bitcast.5, f32[4,512]{1,0:T(4,128)} %prec_in.1), custom_call_target="tpu_custom_call" | custom-call | tf_op jit(solution)/shard_map/pallas_call | solution.py:43
  3.5 11.7 %all-to-all-start = ((f32[128,2,128]{2,1,0:T(2,128)}), f32[128,2,128]{2,1,0:T(2,128)}, u32[]{:S(2)}, u32[]{:S(2)}) async-start(f32[128,2,128]{2,1,0:T(2,128)} %shard_map.104), calls=%async_computation | async-start | bytes 262144 | tf_op jit(solution)/shard_map/all_to_all | solution.py:388
  15.3 3.5 %shard_map.106 = (f32[35,32,128]{2,1,0:T(8,128)S(1)}, f32[36,32,128]{2,1,0:T(8,128)S(1)}, f32[35,32,128]{2,1,0:T(8,128)S(1)}, f32[5,36,32,128]{3,2,1,0:T(8,128)S...) custom-call(f32[2,128]{1,0:T(2,128)S(1)} %broadcast_in_dim.4.mask_re, ...), custom_call_target="tpu_custom_call" | custom-call | tf_op jit(solution)/shard_map/pallas_call | solution.py:43
  18.8 1.6 %copy-done = f32[5,36,32,128]{3,2,1,0:T(8,128)} copy-done((f32[5,36,32,128]{3,2,1,0:T(8,128)}, f32[5,36,32,128]{3,2,1,0:T(8,128)S(1)}, u32[]{:S(2)}) %copy-start) | copy-done | bytes 2949144
  24.7 1.1 %shard_map.105.snd_ref = f32[4,8,1024]{2,1,0:T(8,128)S(1)} custom-call(f32[128,2,128]{2,1,0:T(2,128)} %all-to-all-done.got_ref), custom_call_target="tpu_custom_call" | custom-call | tf_op jit(solution)/shard_map/pallas_call | solution.py:43
  26.6 3.8 %shard_map.107.refs_0_ = f32[3,36,32,128]{3,2,1,0:T(8,128)S(1)} custom-call(f32[4,8,1024]{2,1,0:T(8,128)S(1)} %shard_map.105.snd_ref, bf16[4,3,36,32,128]{4,3,2,1,0:T(8,128)(2,1)S(1)} %get-tuple-element.35.traj_ref, bf16[3,36,64]{2,1,0:T(8,128)(2,1)S(1)} %copy-done.13), custom_call_target="tpu_custom_call" | custom-call | tf_op jit(solution)/shard_map/pallas_call | solution.py:43
  30.5 2.0 %shard_map.108 = (f32[3,36,32,128]{3,2,1,0:T(8,128)S(1)}, f32[1,3456]{1,0:T(1,128)S(1)}, f32[1,3456]{1,0:T(1,128)S(1)}, f32[108,128]{1,0:T(8,128)S(1)}, f32[108,128]{1,0:T(8,128)S(1)}) custom-call(f32[3,36,32,128]{3,2,1,0:T(8,128)S(1)} %shard_map.107.refs_0_, f32[35,32,128]{2,1,0:T(8,128)S(1)} %copy-done.5, f32[36,32,128]{2,1,0:T(8,128)S(1)} %copy-done.3, ...), custom_call_target="tpu_custom_call" | custom-call | tf_op jit(solution)/shard_map/pallas_call | solution.py:43
  32.5 2.9 %collective-permute-start.3 = (f32[108,128]{1,0:T(8,128)S(1)}, f32[108,128]{1,0:T(8,128)S(1)}, u32[]{:S(2)}, u32[]{:S(2)}) collective-permute-start(f32[108,128]{1,0:T(8,128)S(1)} %get-tuple-element.49), channel_id=1, source_target_pairs={{16,0},{32,16},{48,32},{64,48},{80,64},{96,80},{112,96},{0,112},{1... | collective-permute-start | bytes 165896 | tf_op jit(solution)/shard_map/ppermute | solution.py:353
  35.4 1.0 %collective-permute-start = (f32[1,3456]{1,0:T(1,128)S(1)}, f32[1,3456]{1,0:T(1,128)S(1)}, u32[]{:S(2)}, u32[]{:S(2)}) collective-permute-start(f32[1,3456]{1,0:T(1,128)S(1)} %get-tuple-element.46), channel_id=1, source_target_pairs={{0,1},{1,2},{2,3},{3,4},{4,5},{5,6},{6,7},{7,8},{8,9},{9,10},{10,1... | collective-permute-start | bytes 41480 | tf_op jit(solution)/shard_map/ppermute | solution.py:354
  36.5 4.3 %collective-permute-start.1 = (f32[1,3456]{1,0:T(1,128)S(1)}, f32[1,3456]{1,0:T(1,128)S(1)}, u32[]{:S(2)}, u32[]{:S(2)}) collective-permute-start(f32[1,3456]{1,0:T(1,128)S(1)} %get-tuple-element.47), channel_id=1, source_target_pairs={{1,0},{2,1},{3,2},{4,3},{5,4},{6,5},{7,6},{8,7},{9,8},{10,9},{11,1... | collective-permute-start | bytes 41480 | tf_op jit(solution)/shard_map/ppermute | solution.py:355
  40.8 3.8 %shard_map.109.refs_0_ = f32[3,36,32,128]{3,2,1,0:T(8,128)S(1)} custom-call(f32[4,8,1024]{2,1,0:T(8,128)S(1)} %shard_map.105.snd_ref, bf16[4,3,36,32,128]{4,3,2,1,0:T(8,128)(2,1)S(1)} %get-tuple-element.35.traj_ref, bf16[3,36,64]{2,1,0:T(8,128)(2,1)S(1)} %copy-done.13), custom_call_target="tpu_custom_call" | custom-call | tf_op jit(solution)/shard_map/pallas_call | solution.py:43
  44.7 2.5 %shard_map.110 = (f32[3,36,32,128]{3,2,1,0:T(8,128)S(1)}, f32[1,3456]{1,0:T(1,128)S(1)}, f32[1,3456]{1,0:T(1,128)S(1)}, f32[108,128]{1,0:T(8,128)S(1)}, f32[108,...) custom-call(f32[3,36,32,128]{3,2,1,0:T(8,128)S(1)} %get-tuple-element.45.w_in, f32[1,3456]{1,0:T(1,128)S(1)} %collective-permute-done.west_in, ...), custom_call_target="tpu_custom_call" | custom-call | tf_op jit(solution)/shard_map/pallas_call | solution.py:43
  47.2 2.9 %collective-permute-start.7 = (f32[108,128]{1,0:T(8,128)S(1)}, f32[108,128]{1,0:T(8,128)S(1)}, u32[]{:S(2)}, u32[]{:S(2)}) collective-permute-start(f32[108,128]{1,0:T(8,128)S(1)} %get-tuple-element.54), channel_id=1, source_target_pairs={{16,0},{32,16},{48,32},{64,48},{80,64},{96,80},{112,96},{0,112},{1... | collective-permute-start | bytes 165896 | tf_op jit(solution)/shard_map/ppermute | solution.py:353
  50.2 5.3 %collective-permute-start.5 = (f32[1,3456]{1,0:T(1,128)S(1)}, f32[1,3456]{1,0:T(1,128)S(1)}, u32[]{:S(2)}, u32[]{:S(2)}) collective-permute-start(f32[1,3456]{1,0:T(1,128)S(1)} %get-tuple-element.52), channel_id=1, source_target_pairs={{1,0},{2,1},{3,2},{4,3},{5,4},{6,5},{7,6},{8,7},{9,8},{10,9},{11,1... | collective-permute-start | bytes 41480 | tf_op jit(solution)/shard_map/ppermute | solution.py:355
  55.5 3.8 %shard_map.111.refs_0_ = f32[3,36,32,128]{3,2,1,0:T(8,128)S(1)} custom-call(f32[4,8,1024]{2,1,0:T(8,128)S(1)} %shard_map.105.snd_ref, bf16[4,3,36,32,128]{4,3,2,1,0:T(8,128)(2,1)S(1)} %get-tuple-element.35.traj_ref, bf16[3,36,64]{2,1,0:T(8,128)(2,1)S(1)} %copy-done.13), custom_call_target="tpu_custom_call" | custom-call | tf_op jit(solution)/shard_map/pallas_call | solution.py:43
  59.4 2.5 %shard_map.112 = (f32[3,36,32,128]{3,2,1,0:T(8,128)S(1)}, f32[1,3456]{1,0:T(1,128)S(1)}, f32[1,3456]{1,0:T(1,128)S(1)}, f32[108,128]{1,0:T(8,128)S(1)}, f32[108,...) custom-call(f32[3,36,32,128]{3,2,1,0:T(8,128)S(1)} %get-tuple-element.50.w_in, f32[1,3456]{1,0:T(1,128)S(1)} %collective-permute-done.4.west_in, ...), custom_call_target="tpu_custom_call" | custom-call | tf_op jit(solution)/shard_map/pallas_call | solution.py:43
  62.0 2.9 %collective-permute-start.11 = (f32[108,128]{1,0:T(8,128)S(1)}, f32[108,128]{1,0:T(8,128)S(1)}, u32[]{:S(2)}, u32[]{:S(2)}) collective-permute-start(f32[108,128]{1,0:T(8,128)S(1)} %get-tuple-element.60), channel_id=1, source_target_pairs={{16,0},{32,16},{48,32},{64,48},{80,64},{96,80},{112,96},{0,112},{1... | collective-permute-start | bytes 165896 | tf_op jit(solution)/shard_map/ppermute | solution.py:353
  64.9 5.3 %collective-permute-start.9 = (f32[1,3456]{1,0:T(1,128)S(1)}, f32[1,3456]{1,0:T(1,128)S(1)}, u32[]{:S(2)}, u32[]{:S(2)}) collective-permute-start(f32[1,3456]{1,0:T(1,128)S(1)} %get-tuple-element.58), channel_id=1, source_target_pairs={{1,0},{2,1},{3,2},{4,3},{5,4},{6,5},{7,6},{8,7},{9,8},{10,9},{11,1... | collective-permute-start | bytes 41480 | tf_op jit(solution)/shard_map/ppermute | solution.py:355
  70.3 3.8 %shard_map.113.refs_0_ = f32[3,36,32,128]{3,2,1,0:T(8,128)S(1)} custom-call(f32[4,8,1024]{2,1,0:T(8,128)S(1)} %shard_map.105.snd_ref, bf16[4,3,36,32,128]{4,3,2,1,0:T(8,128)(2,1)S(1)} %get-tuple-element.35.traj_ref, bf16[3,36,64]{2,1,0:T(8,128)(2,1)S(1)} %copy-done.13), custom_call_target="tpu_custom_call" | custom-call | tf_op jit(solution)/shard_map/pallas_call | solution.py:43
  74.1 2.5 %shard_map.114 = (f32[3,36,32,128]{3,2,1,0:T(8,128)S(1)}, f32[1,3456]{1,0:T(1,128)S(1)}, f32[1,3456]{1,0:T(1,128)S(1)}, f32[108,128]{1,0:T(8,128)S(1)}, f32[108,...) custom-call(f32[3,36,32,128]{3,2,1,0:T(8,128)S(1)} %get-tuple-element.56.w_in, f32[1,3456]{1,0:T(1,128)S(1)} %collective-permute-done.8.west_in, ...), custom_call_target="tpu_custom_call" | custom-call | tf_op jit(solution)/shard_map/pallas_call | solution.py:43
  76.7 2.9 %collective-permute-start.15 = (f32[108,128]{1,0:T(8,128)S(1)}, f32[108,128]{1,0:T(8,128)S(1)}, u32[]{:S(2)}, u32[]{:S(2)}) collective-permute-start(f32[108,128]{1,0:T(8,128)S(1)} %get-tuple-element.66), channel_id=1, source_target_pairs={{16,0},{32,16},{48,32},{64,48},{80,64},{96,80},{112,96},{0,112},{1... | collective-permute-start | bytes 165896 | tf_op jit(solution)/shard_map/ppermute | solution.py:353
  79.6 5.3 %collective-permute-start.13 = (f32[1,3456]{1,0:T(1,128)S(1)}, f32[1,3456]{1,0:T(1,128)S(1)}, u32[]{:S(2)}, u32[]{:S(2)}) collective-permute-start(f32[1,3456]{1,0:T(1,128)S(1)} %get-tuple-element.64), channel_id=1, source_target_pairs={{1,0},{2,1},{3,2},{4,3},{5,4},{6,5},{7,6},{8,7},{9,8},{10,9},{11,1... | collective-permute-start | bytes 41480 | tf_op jit(solution)/shard_map/ppermute | solution.py:355
  85.0 1.7 %collective-permute-done.12.west_in = f32[1,3456]{1,0:T(1,128)S(1)} collective-permute-done((f32[1,3456]{1,0:T(1,128)S(1)}, f32[1,3456]{1,0:T(1,128)S(1)}, u32[]{:S(2)}, u32[]{:S(2)}) %collective-permute-start.12) | collective-permute-done | bytes 13856 | tf_op jit(solution)/shard_map/ppermute | solution.py:354
  86.7 2.4 %shard_map.115 = (f32[3,36,32,128]{3,2,1,0:T(8,128)}, f32[3,32,128]{2,1,0:T(8,128)}) custom-call(f32[3,36,32,128]{3,2,1,0:T(8,128)S(1)} %get-tuple-element.62.w_in, f32[1,3456]{1,0:T(1,128)S(1)} %collective-permute-done.12.west_in, f32[1,3456]{1,0:T(1,128)S(1)} %collective-permute-done.13.east_in, f32[108,128]{1,0:T(8,128)S(1)} %collective-permute-done.14.north_in, ...), custom_call_target="tpu_custom_call" | custom-call | tf_op jit(solution)/shard_map/pallas_call | solution.py:43
  (53 shorter events, 5.4 us)
Async XLA Ops:
  3.5 21.2 %all-to-all-start = ((f32[128,2,128]{2,1,0:T(2,128)}), f32[128,2,128]{2,1,0:T(2,128)}, u32[]{:S(2)}, u32[]{:S(2)}) async-start(f32[128,2,128]{2,1,0:T(2,128)} %shard_map.104), calls=%async_computation | async-start | bytes 262144 | tf_op jit(solution)/shard_map/all_to_all | solution.py:388
  18.8 1.6 %copy-start = (f32[5,36,32,128]{3,2,1,0:T(8,128)}, f32[5,36,32,128]{3,2,1,0:T(8,128)S(1)}, u32[]{:S(2)}) copy-start(f32[5,36,32,128]{3,2,1,0:T(8,128)S(1)} %get-tuple-element.40.refs_4_) | copy-start | bytes 8847364
  26.5 3.9 %copy-start.1 = (f32[5,36,32,128]{3,2,1,0:T(8,128)S(1)}, f32[5,36,32,128]{3,2,1,0:T(8,128)}, u32[]{:S(2)}) copy-start(f32[5,36,32,128]{3,2,1,0:T(8,128)} %copy-done) | copy-start | bytes 8847364
  26.5 3.9 %copy-start.3 = (f32[36,32,128]{2,1,0:T(8,128)S(1)}, f32[36,32,128]{2,1,0:T(8,128)}, u32[]{:S(2)}) copy-start(f32[36,32,128]{2,1,0:T(8,128)} %copy-done.2) | copy-start | bytes 1769476
  26.5 3.9 %copy-start.5 = (f32[35,32,128]{2,1,0:T(8,128)S(1)}, f32[35,32,128]{2,1,0:T(8,128)}, u32[]{:S(2)}) copy-start(f32[35,32,128]{2,1,0:T(8,128)} %copy-done.4) | copy-start | bytes 1720324
  26.5 3.9 %copy-start.7 = (f32[35,32,128]{2,1,0:T(8,128)S(1)}, f32[35,32,128]{2,1,0:T(8,128)}, u32[]{:S(2)}) copy-start(f32[35,32,128]{2,1,0:T(8,128)} %copy-done.6) | copy-start | bytes 1720324
  26.5 3.9 %copy-start.9 = (bf16[256,256]{1,0:T(8,128)(2,1)S(1)}, bf16[256,256]{1,0:T(8,128)(2,1)}, u32[]{:S(2)}) copy-start(bf16[256,256]{1,0:T(8,128)(2,1)} %copy-done.8) | copy-start | bytes 393220
  26.6 3.9 %copy-start.11 = (f32[2,36,128]{2,1,0:T(8,128)S(1)}, f32[2,36,128]{2,1,0:T(8,128)}, u32[]{:S(2)}) copy-start(f32[2,36,128]{2,1,0:T(8,128)} %copy-done.10) | copy-start | bytes 110596
  32.5 12.2 %collective-permute-start.2 = (f32[108,128]{1,0:T(8,128)S(1)}, f32[108,128]{1,0:T(8,128)S(1)}, u32[]{:S(2)}, u32[]{:S(2)}) collective-permute-start(f32[108,128]{1,0:T(8,128)S(1)} %get-tuple-element.48), channel_id=1, source_target_pairs={{0,16},{16,32},{32,48},{48,64},{64,80},{80,96},{96,112},{112,0},{1... | collective-permute-start | bytes 165896 | tf_op jit(solution)/shard_map/ppermute | solution.py:352
  32.5 12.2 %collective-permute-start.3 = (f32[108,128]{1,0:T(8,128)S(1)}, f32[108,128]{1,0:T(8,128)S(1)}, u32[]{:S(2)}, u32[]{:S(2)}) collective-permute-start(f32[108,128]{1,0:T(8,128)S(1)} %get-tuple-element.49), channel_id=1, source_target_pairs={{16,0},{32,16},{48,32},{64,48},{80,64},{96,80},{112,96},{0,112},{1... | collective-permute-start | bytes 165896 | tf_op jit(solution)/shard_map/ppermute | solution.py:353
  35.4 9.2 %collective-permute-start = (f32[1,3456]{1,0:T(1,128)S(1)}, f32[1,3456]{1,0:T(1,128)S(1)}, u32[]{:S(2)}, u32[]{:S(2)}) collective-permute-start(f32[1,3456]{1,0:T(1,128)S(1)} %get-tuple-element.46), channel_id=1, source_target_pairs={{0,1},{1,2},{2,3},{3,4},{4,5},{5,6},{6,7},{7,8},{8,9},{9,10},{10,1... | collective-permute-start | bytes 41480 | tf_op jit(solution)/shard_map/ppermute | solution.py:354
  36.5 8.2 %collective-permute-start.1 = (f32[1,3456]{1,0:T(1,128)S(1)}, f32[1,3456]{1,0:T(1,128)S(1)}, u32[]{:S(2)}, u32[]{:S(2)}) collective-permute-start(f32[1,3456]{1,0:T(1,128)S(1)} %get-tuple-element.47), channel_id=1, source_target_pairs={{1,0},{2,1},{3,2},{4,3},{5,4},{6,5},{7,6},{8,7},{9,8},{10,9},{11,1... | collective-permute-start | bytes 41480 | tf_op jit(solution)/shard_map/ppermute | solution.py:355
  47.2 12.2 %collective-permute-start.6 = (f32[108,128]{1,0:T(8,128)S(1)}, f32[108,128]{1,0:T(8,128)S(1)}, u32[]{:S(2)}, u32[]{:S(2)}) collective-permute-start(f32[108,128]{1,0:T(8,128)S(1)} %get-tuple-element.53), channel_id=1, source_target_pairs={{0,16},{16,32},{32,48},{48,64},{64,80},{80,96},{96,112},{112,0},{1... | collective-permute-start | bytes 165896 | tf_op jit(solution)/shard_map/ppermute | solution.py:352
  47.2 12.2 %collective-permute-start.7 = (f32[108,128]{1,0:T(8,128)S(1)}, f32[108,128]{1,0:T(8,128)S(1)}, u32[]{:S(2)}, u32[]{:S(2)}) collective-permute-start(f32[108,128]{1,0:T(8,128)S(1)} %get-tuple-element.54), channel_id=1, source_target_pairs={{16,0},{32,16},{48,32},{64,48},{80,64},{96,80},{112,96},{0,112},{1... | collective-permute-start | bytes 165896 | tf_op jit(solution)/shard_map/ppermute | solution.py:353
  50.2 9.2 %collective-permute-start.4 = (f32[1,3456]{1,0:T(1,128)S(1)}, f32[1,3456]{1,0:T(1,128)S(1)}, u32[]{:S(2)}, u32[]{:S(2)}) collective-permute-start(f32[1,3456]{1,0:T(1,128)S(1)} %get-tuple-element.51), channel_id=1, source_target_pairs={{0,1},{1,2},{2,3},{3,4},{4,5},{5,6},{6,7},{7,8},{8,9},{9,10},{10,1... | collective-permute-start | bytes 41480 | tf_op jit(solution)/shard_map/ppermute | solution.py:354
  50.2 9.2 %collective-permute-start.5 = (f32[1,3456]{1,0:T(1,128)S(1)}, f32[1,3456]{1,0:T(1,128)S(1)}, u32[]{:S(2)}, u32[]{:S(2)}) collective-permute-start(f32[1,3456]{1,0:T(1,128)S(1)} %get-tuple-element.52), channel_id=1, source_target_pairs={{1,0},{2,1},{3,2},{4,3},{5,4},{6,5},{7,6},{8,7},{9,8},{10,9},{11,1... | collective-permute-start | bytes 41480 | tf_op jit(solution)/shard_map/ppermute | solution.py:355
  61.9 12.2 %collective-permute-start.10 = (f32[108,128]{1,0:T(8,128)S(1)}, f32[108,128]{1,0:T(8,128)S(1)}, u32[]{:S(2)}, u32[]{:S(2)}) collective-permute-start(f32[108,128]{1,0:T(8,128)S(1)} %get-tuple-element.59), channel_id=1, source_target_pairs={{0,16},{16,32},{32,48},{48,64},{64,80},{80,96},{96,112},{112,0},{1... | collective-permute-start | bytes 165896 | tf_op jit(solution)/shard_map/ppermute | solution.py:352
  62.0 12.2 %collective-permute-start.11 = (f32[108,128]{1,0:T(8,128)S(1)}, f32[108,128]{1,0:T(8,128)S(1)}, u32[]{:S(2)}, u32[]{:S(2)}) collective-permute-start(f32[108,128]{1,0:T(8,128)S(1)} %get-tuple-element.60), channel_id=1, source_target_pairs={{16,0},{32,16},{48,32},{64,48},{80,64},{96,80},{112,96},{0,112},{1... | collective-permute-start | bytes 165896 | tf_op jit(solution)/shard_map/ppermute | solution.py:353
  64.9 9.2 %collective-permute-start.8 = (f32[1,3456]{1,0:T(1,128)S(1)}, f32[1,3456]{1,0:T(1,128)S(1)}, u32[]{:S(2)}, u32[]{:S(2)}) collective-permute-start(f32[1,3456]{1,0:T(1,128)S(1)} %get-tuple-element.57), channel_id=1, source_target_pairs={{0,1},{1,2},{2,3},{3,4},{4,5},{5,6},{6,7},{7,8},{8,9},{9,10},{10,1... | collective-permute-start | bytes 41480 | tf_op jit(solution)/shard_map/ppermute | solution.py:354
  64.9 9.2 %collective-permute-start.9 = (f32[1,3456]{1,0:T(1,128)S(1)}, f32[1,3456]{1,0:T(1,128)S(1)}, u32[]{:S(2)}, u32[]{:S(2)}) collective-permute-start(f32[1,3456]{1,0:T(1,128)S(1)} %get-tuple-element.58), channel_id=1, source_target_pairs={{1,0},{2,1},{3,2},{4,3},{5,4},{6,5},{7,6},{8,7},{9,8},{10,9},{11,1... | collective-permute-start | bytes 41480 | tf_op jit(solution)/shard_map/ppermute | solution.py:355
  76.7 10.0 %collective-permute-start.14 = (f32[108,128]{1,0:T(8,128)S(1)}, f32[108,128]{1,0:T(8,128)S(1)}, u32[]{:S(2)}, u32[]{:S(2)}) collective-permute-start(f32[108,128]{1,0:T(8,128)S(1)} %get-tuple-element.65), channel_id=1, source_target_pairs={{0,16},{16,32},{32,48},{48,64},{64,80},{80,96},{96,112},{112,0},{1... | collective-permute-start | bytes 165896 | tf_op jit(solution)/shard_map/ppermute | solution.py:352
  76.7 10.0 %collective-permute-start.15 = (f32[108,128]{1,0:T(8,128)S(1)}, f32[108,128]{1,0:T(8,128)S(1)}, u32[]{:S(2)}, u32[]{:S(2)}) collective-permute-start(f32[108,128]{1,0:T(8,128)S(1)} %get-tuple-element.66), channel_id=1, source_target_pairs={{16,0},{32,16},{48,32},{64,48},{80,64},{96,80},{112,96},{0,112},{1... | collective-permute-start | bytes 165896 | tf_op jit(solution)/shard_map/ppermute | solution.py:353
  79.6 7.0 %collective-permute-start.12 = (f32[1,3456]{1,0:T(1,128)S(1)}, f32[1,3456]{1,0:T(1,128)S(1)}, u32[]{:S(2)}, u32[]{:S(2)}) collective-permute-start(f32[1,3456]{1,0:T(1,128)S(1)} %get-tuple-element.63), channel_id=1, source_target_pairs={{0,1},{1,2},{2,3},{3,4},{4,5},{5,6},{6,7},{7,8},{8,9},{9,10},{10,1... | collective-permute-start | bytes 41480 | tf_op jit(solution)/shard_map/ppermute | solution.py:354
  79.6 7.0 %collective-permute-start.13 = (f32[1,3456]{1,0:T(1,128)S(1)}, f32[1,3456]{1,0:T(1,128)S(1)}, u32[]{:S(2)}, u32[]{:S(2)}) collective-permute-start(f32[1,3456]{1,0:T(1,128)S(1)} %get-tuple-element.64), channel_id=1, source_target_pairs={{1,0},{2,1},{3,2},{4,3},{5,4},{6,5},{7,6},{8,7},{9,8},{10,9},{11,1... | collective-permute-start | bytes 41480 | tf_op jit(solution)/shard_map/ppermute | solution.py:355
  (7 other events, 5.1 us)

commit v2 on v1

--- a/solution.py
+++ b/solution.py
@@ -214,47 +214,60 @@
         return 0
 
     lax.fori_loop(0, layers, coefs, 0, unroll=4)
-    lat_w[0] = tr_ref[3, :, 0, :] * mask_ref[0:1, :]
-    lat_w[1] = tr_ref[2, :, 31, :] * mask_ref[1:2, :]
+    to_north = tr_ref[3, :, 0, :] * mask_ref[0:1, :]
+    to_south = tr_ref[2, :, 31, :] * mask_ref[1:2, :]
+    odd = mask_ref[2:3, :]
+    lat_w[0] = odd * to_north
+    lat_w[1] = (1.0 - odd) * to_south
+    lat_w[2] = (1.0 - odd) * to_north
+    lat_w[3] = odd * to_south
+    odd = mask_ref[3:4, 0:1]
     for side in range(2):
         flat = None
         for part in split3(tr_ref[side].reshape(layers * 32, 128)):
             term = dot_t(ends[:, 0:128], part)
             flat = term if flat is None else flat + term
-        lon_w[side] = flat[side : side + 1, :]
+        flat = flat[side : side + 1, :]
+        lon_w[side] = flat * (odd if side else 1.0 - odd)
+        lon_w[2 + side] = flat * (1.0 - odd if side else odd)
     copies[2].wait()
     for i, part in enumerate(split3(table_ref[...])):
         parts_ref[i] = part
     copies[3].wait()
 
 
-def spread(west_ref, east_ref, halo):
+def spread(mask_ref, lon_a, lon_b, lat_a, lat_b, halo, lat_halo):
     tracers, layers, rows, cols = halo.shape
     size = layers * rows
+    odd = mask_ref[2:3, :] > 0.5
+    lat_halo[0] = jnp.where(odd, lat_a[...], lat_b[...])
+    lat_halo[1] = jnp.where(odd, lat_b[...], lat_a[...])
     row = lax.broadcasted_iota(jnp.int32, (4, cols), 0)
     lane = lax.broadcasted_iota(jnp.int32, (4, cols), 1)
-    place = ((row % 2 == 0) & (lane == 0)) | ((row % 2 == 1) & (lane == cols - 1))
-    place = jnp.where(place, 1.0, 0.0).astype(BF16)
+    other = (row % 2).astype(F32)
+    lon_odd = jnp.broadcast_to(mask_ref[3:4, :], (4, cols))
+    spot = (other * lon_odd + (1.0 - other) * (1.0 - lon_odd)) * (cols - 1)
+    place = jnp.where(lane.astype(F32) == spot, 1.0, 0.0).astype(BF16)
     for t in range(tracers):
         at = slice(t * size, (t + 1) * size)
-        hi, lo = split2(jnp.concatenate([west_ref[:, at], east_ref[:, at]], axis=0))
+        hi, lo = split2(jnp.concatenate([lon_a[:, at], lon_b[:, at]], axis=0))
         both = jnp.concatenate([hi, lo], axis=0)
         spot = lax.dot_general(both, place, (((0,), (0,)), ((), ())), preferred_element_type=F32)
         halo[t] = spot.reshape(layers, rows, cols)
 
 
-def received(w_ref, halo, north_ref, south_ref, t, k):
+def received(w_ref, halo, lat_halo, t, k):
     value = w_ref[t, k] + halo[t, k]
     row = lax.broadcasted_iota(jnp.int32, (8, 128), 0)
     at = pl.ds(t * w_ref.shape[1] + k, 1)
-    top = value[0:8] + jnp.where(row == 0, north_ref[at, :], 0.0)
-    low = value[24:32] + jnp.where(row == 7, south_ref[at, :], 0.0)
+    top = value[0:8] + jnp.where(row == 0, lat_halo[0, at, :], 0.0)
+    low = value[24:32] + jnp.where(row == 7, lat_halo[1, at, :], 0.0)
     return jnp.concatenate([top, value[8:24], low], axis=0)
 
 
 def step_body(base, force_ref, fixed, outs, v):
     mix_ref, inv_ref, up_ref, coef_ref, lat_w, lon_w, shift_ref, ends_ref = fixed
-    w_out, east_out, west_out, north_out, south_out = outs
+    w_out, lon_a, lon_b, lat_a, lat_b = outs
     tracers, layers, rows, cols = force_ref.shape
     d = tuple((force_ref[t, 0] + base(t, 0)) * inv_ref[0] for t in range(tracers))
     for t in range(tracers):
@@ -290,8 +303,8 @@
             ends = dot_t(ends_ref[...], both)
             to = pl.ds((t * layers + g) * rows, size)
             at = pl.ds(g * rows, size)
-            east_out[:, to] = ends[0:1, :] * lon_w[0, :, at]
-            west_out[:, to] = ends[1:2, :] * lon_w[1, :, at]
+            lon_a[:, to] = ends[0:1, :] * lon_w[0, :, at] + ends[1:2, :] * lon_w[1, :, at]
+            lon_b[:, to] = ends[0:1, :] * lon_w[2, :, at] + ends[1:2, :] * lon_w[3, :, at]
             c = [coef_ref[i, g : g + group].reshape(size, cols) for i in range(5)]
             down = jnp.stack([pltpu.roll(x[i], 1, axis=0) for i in range(group)])
             up = jnp.stack([pltpu.roll(x[i], rows - 1, axis=0) for i in range(group)])
@@ -301,20 +314,21 @@
 
     for t in range(tracers):
         at = slice(t * layers, (t + 1) * layers)
-        north_out[at, :] = v[t, :, 0, :] * lat_w[0]
-        south_out[at, :] = v[t, :, rows - 1, :] * lat_w[1]
+        top, low = v[t, :, 0, :], v[t, :, rows - 1, :]
+        lat_a[at, :] = top * lat_w[0] + low * lat_w[1]
+        lat_b[at, :] = top * lat_w[2] + low * lat_w[3]
 
 
 def first_step_kernel(*refs):
     step_body(lambda t, k: 0.0, refs[0], refs[1:9], refs[9:14], refs[14])
 
 
-def step_kernel(w_in, west_in, east_in, north_in, south_in, flux_in, *refs):
-    force_ref, fixed, outs, (flux_out, v, halo) = refs[0], refs[1:9], refs[9:14], refs[14:]
-    spread(west_in, east_in, halo)
+def step_kernel(mask_ref, w_in, lon_a, lon_b, lat_a, lat_b, flux_in, *refs):
+    force_ref, fixed, outs, (flux_out, v, halo, lat_halo) = refs[0], refs[1:9], refs[9:14], refs[14:]
+    spread(mask_ref, lon_a, lon_b, lat_a, lat_b, halo, lat_halo)
 
     def base(t, k):
-        value = received(w_in, halo, north_in, south_in, t, k)
+        value = received(w_in, halo, lat_halo, t, k)
         if isinstance(k, int):
             flux_out[t] = flux_in[t] + value
         return value
@@ -322,14 +336,16 @@
     step_body(base, force_ref, fixed, outs, v)
 
 
-def last_kernel(w_in, west_in, east_in, north_in, south_in, flux_in, adj_out, flux_out, halo, done, sems):
+def last_kernel(
+    mask_ref, w_in, lon_a, lon_b, lat_a, lat_b, flux_in, adj_out, flux_out, halo, lat_halo, done, sems
+):
     tracers, layers = w_in.shape[:2]
-    spread(west_in, east_in, halo)
+    spread(mask_ref, lon_a, lon_b, lat_a, lat_b, halo, lat_halo)
     copies = []
     for t in range(tracers):
 
         def finish(k, _):
-            done[t, k] = received(w_in, halo, north_in, south_in, t, k)
+            done[t, k] = received(w_in, halo, lat_halo, t, k)
             return 0
 
         lax.fori_loop(0, layers, finish, 0, unroll=4)
@@ -340,20 +356,20 @@
         copy.wait()
 
 
-def shifts(axis):
+def swaps(axis):
     peers = lax.axis_size(axis)
-    up = [(i, (i + 1) % peers) for i in range(peers)]
-    return up, [(b, a) for a, b in up]
-
-
-def exchange(east, west, north, south):
-    lat_up, lat_down = shifts("lat")
-    lon_up, lon_down = shifts("lon")
-    from_north = lax.ppermute(south, "lat", lat_up)
-    from_south = lax.ppermute(north, "lat", lat_down)
-    from_west = lax.ppermute(east, "lon", lon_up)
-    from_east = lax.ppermute(west, "lon", lon_down)
-    return from_west, from_east, from_north, from_south
+    near = [(i, i + 1 - 2 * (i % 2)) for i in range(peers)]
+    return near, [((i + 1) % peers, (j + 1) % peers) for i, j in near]
+
+
+def exchange(lon_a, lon_b, lat_a, lat_b):
+    lat_near, lat_far = swaps("lat")
+    lon_near, lon_far = swaps("lon")
+    lon_b = lax.ppermute(lon_b, "lon", lon_far)
+    lat_b = lax.ppermute(lat_b, "lat", lat_far)
+    lon_a = lax.ppermute(lon_a, "lon", lon_near)
+    lat_a = lax.ppermute(lat_a, "lat", lat_near)
+    return lon_a, lon_b, lat_a, lat_b
 
 
 def body(
@@ -386,9 +402,9 @@
         ),
     )
     got = lax.all_to_all(outgoing, ("lat", "lon"), split_axis=0, concat_axis=0, tiled=True)
-    lat = lax.axis_index("lat")
-    mask = jnp.stack([lat > 0, lat < lax.axis_size("lat") - 1]).astype(F32)
-    mask = jnp.broadcast_to(mask[:, None], (2, cols))
+    lat, lon = lax.axis_index("lat"), lax.axis_index("lon")
+    mask = jnp.stack([lat > 0, lat < lax.axis_size("lat") - 1, lat % 2 > 0, lon % 2 > 0]).astype(F32)
+    mask = jnp.broadcast_to(mask[:, None], (4, cols))
     *fixed, local, table = call(
         setup_kernel,
         (
@@ -396,8 +412,8 @@
             sds(layers, rows, cols),
             sds(*mixing.shape),
             sds(5, layers, rows, cols),
-            sds(2, layers, cols),
-            sds(2, 1, layers * rows),
+            sds(4, layers, cols),
+            sds(4, 1, layers * rows),
             sds(256, 256, dtype=BF16),
             sds(8, 256, dtype=BF16),
             sds(*trajectory.shape, dtype=BF16),
@@ -428,22 +444,32 @@
         )
 
     v = pltpu.VMEM(field.shape, F32)
+    lat_halo = pltpu.VMEM((2,) + lat_edge.shape, F32)
     moved = (field, lon_edge, lon_edge, lat_edge, lat_edge)
     w, *edges = call(first_step_kernel, moved, forcing(steps - 1), *fixed, scratch=(v,))
     flux = jnp.zeros((tracers, rows, cols), F32)
     for s in range(steps - 2, -1, -1):
         halos = exchange(*edges)
         w, *edges, flux = call(
-            step_kernel, moved + (plane,), w, *halos, flux, forcing(s), *fixed, scratch=(v, v)
+            step_kernel,
+            moved + (plane,),
+            mask,
+            w,
+            *halos,
+            flux,
+            forcing(s),
+            *fixed,
+            scratch=(v, v, lat_halo),
         )
     return call(
         last_kernel,
         (field, plane),
+        mask,
         w,
         *exchange(*edges),
         flux,
         hbm_out=(0,),
-        scratch=(v, v, pltpu.SemaphoreType.DMA((tracers,))),
+        scratch=(v, lat_halo, v, pltpu.SemaphoreType.DMA((tracers,))),
     )
 
 

time: 89.6 us -> 81.5 us (0.910)
  starting transfers between devices: 44.9 us -> 32 us
  waiting for transfers between devices: 1.73 us -> 5.67 us
    ppermute x16, starting transfers between devices: 33.2 us -> 20.3 us  [the longest x4 12.3 us: exchange(): lon_b = lax.ppermute(lon_b, 'lon', lon_far)]
    ppermute x16, waiting for transfers between devices: 1.72 us -> 5.67 us  [the longest x4 4.24 us: exchange(): lon_b = lax.ppermute(lon_b, 'lon', lon_far)]
    unnamed x28 -> x32, local copies, waits for them, and re-layouts: 6.66 us -> 7.25 us
  transfers between devices with their start and end apart: 17 -> 17, of which waited for: 1 -> 3; matrix products, arithmetic and copies ran while one was open for 0% -> 0% of each run, Pallas kernels for 17% -> 18%
where the time goes in v2:
time: 81.5 us; the launch traced here: 81.2 us
  Pallas kernels  35 us (43%)
  starting transfers between devices  32 us (39%)
  local copies, waits for them, and re-layouts  7.33 us (9%)
  waiting for transfers between devices  5.67 us (7%)
  between operations  1.11 us (1%)
    pallas_call x12, Pallas kernels, call(): pl.pallas_call(kernel, out_shape=outs, in_specs=[HBM if i in hbm else VME...  35 us
    ppermute x4, starting transfers between devices, exchange(): lon_b = lax.ppermute(lon_b, 'lon', lon_far)  12.3 us
    all_to_all x1, starting transfers between devices, body(): lax.all_to_all(outgoing, ('lat', 'lon'), split_axis=0, concat_axis=0, til...  11.7 us
    unnamed x32, local copies, waits for them, and re-layouts  7.25 us
    ppermute x4, starting transfers between devices, exchange(): lat_b = lax.ppermute(lat_b, 'lat', lat_far)  5.97 us
    ppermute x4, waiting for transfers between devices, exchange(): lon_b = lax.ppermute(lon_b, 'lon', lon_far)  4.24 us
    ppermute x4, starting transfers between devices, exchange(): lon_a = lax.ppermute(lon_a, 'lon', lon_near)  1.75 us
  transfers between devices with their start and end apart: 17, of which 3 were waited for; matrix products, arithmetic and copies ran while one was open for 0% of the time, Pallas kernels for 18%

profile of v2, /device:TPU:0, one launch (start us, length us, event | category | flops | bytes accessed | tf_op | source)
XLA Modules:
  0.0 81.2 jit_solution(10630197902019684666)
XLA Ops:
  0.6 2.8 %shard_map.104 = f32[128,2,128]{2,1,0:T(2,128)} custom-call(s32[4,1,512]{2,1,0:T(1,128)} %bitcast.9, s32[4,512]{1,0:T(4,128)} %cell_in.1, s32[4,512]{1,0:T(4,128)} %index_in.1, f32[3,4,512]{2,1,0:T(4,128)} %bitcast.7, f32[4,512]{1,0:T(4,128)} %prec_in.1), custom_call_target="tpu_custom_call" | custom-call | tf_op jit(solution)/shard_map/pallas_call | solution.py:43
  3.4 11.7 %all-to-all-start = ((f32[128,2,128]{2,1,0:T(2,128)}), f32[128,2,128]{2,1,0:T(2,128)}, u32[]{:S(2)}, u32[]{:S(2)}) async-start(f32[128,2,128]{2,1,0:T(2,128)} %shard_map.104), calls=%async_computation | async-start | bytes 262144 | tf_op jit(solution)/shard_map/all_to_all | solution.py:404
  15.3 3.5 %shard_map.106 = (f32[35,32,128]{2,1,0:T(8,128)S(1)}, f32[36,32,128]{2,1,0:T(8,128)S(1)}, f32[35,32,128]{2,1,0:T(8,128)S(1)}, f32[5,36,32,128]{3,2,1,0:T(8,128)S...) custom-call(f32[4,128]{1,0:T(4,128)S(1)} %broadcast_in_dim.4.mask_re, ...), custom_call_target="tpu_custom_call" | custom-call | tf_op jit(solution)/shard_map/pallas_call | solution.py:43
  18.8 1.6 %copy-done = f32[5,36,32,128]{3,2,1,0:T(8,128)} copy-done((f32[5,36,32,128]{3,2,1,0:T(8,128)}, f32[5,36,32,128]{3,2,1,0:T(8,128)S(1)}, u32[]{:S(2)}) %copy-start) | copy-done | bytes 2949144
  25.3 1.1 %shard_map.105.snd_ref = f32[4,8,1024]{2,1,0:T(8,128)S(1)} custom-call(f32[128,2,128]{2,1,0:T(2,128)} %all-to-all-done.got_ref), custom_call_target="tpu_custom_call" | custom-call | tf_op jit(solution)/shard_map/pallas_call | solution.py:43
  27.2 3.8 %shard_map.107.refs_0_ = f32[3,36,32,128]{3,2,1,0:T(8,128)S(1)} custom-call(f32[4,8,1024]{2,1,0:T(8,128)S(1)} %shard_map.105.snd_ref, bf16[4,3,36,32,128]{4,3,2,1,0:T(8,128)(2,1)S(1)} %get-tuple-element.35.traj_ref, bf16[3,36,64]{2,1,0:T(8,128)(2,1)S(1)} %copy-done.13), custom_call_target="tpu_custom_call" | custom-call | tf_op jit(solution)/shard_map/pallas_call | solution.py:43
  31.1 2.0 %shard_map.108 = (f32[3,36,32,128]{3,2,1,0:T(8,128)S(1)}, f32[1,3456]{1,0:T(1,128)S(1)}, f32[1,3456]{1,0:T(1,128)S(1)}, f32[108,128]{1,0:T(8,128)S(1)}, f32[108,128]{1,0:T(8,128)S(1)}) custom-call(f32[3,36,32,128]{3,2,1,0:T(8,128)S(1)} %shard_map.107.refs_0_, f32[35,32,128]{2,1,0:T(8,128)S(1)} %copy-done.5, f32[36,32,128]{2,1,0:T(8,128)S(1)} %copy-done.3, ...), custom_call_target="tpu_custom_call" | custom-call | tf_op jit(solution)/shard_map/pallas_call | solution.py:43
  33.2 2.3 %collective-permute-start.3 = (f32[108,128]{1,0:T(8,128)S(1)}, f32[108,128]{1,0:T(8,128)S(1)}, u32[]{:S(2)}, u32[]{:S(2)}) collective-permute-start(f32[108,128]{1,0:T(8,128)S(1)} %get-tuple-element.49), channel_id=1, source_target_pairs={{16,32},{32,16},{48,64},{64,48},{80,96},{96,80},{112,0},{0,112},{1... | collective-permute-start | bytes 165896 | tf_op jit(solution)/shard_map/ppermute | solution.py:369
  35.4 1.7 %collective-permute-start = (f32[1,3456]{1,0:T(1,128)S(1)}, f32[1,3456]{1,0:T(1,128)S(1)}, u32[]{:S(2)}, u32[]{:S(2)}) collective-permute-start(f32[1,3456]{1,0:T(1,128)S(1)} %get-tuple-element.46), channel_id=1, source_target_pairs={{0,1},{1,0},{2,3},{3,2},{4,5},{5,4},{6,7},{7,6},{8,9},{9,8},{10,11... | collective-permute-start | bytes 41480 | tf_op jit(solution)/shard_map/ppermute | solution.py:370
  37.2 4.5 %collective-permute-start.1 = (f32[1,3456]{1,0:T(1,128)S(1)}, f32[1,3456]{1,0:T(1,128)S(1)}, u32[]{:S(2)}, u32[]{:S(2)}) collective-permute-start(f32[1,3456]{1,0:T(1,128)S(1)} %get-tuple-element.47), channel_id=1, source_target_pairs={{1,2},{2,1},{3,4},{4,3},{5,6},{6,5},{7,8},{8,7},{9,10},{10,9},{11,... | collective-permute-start | bytes 41480 | tf_op jit(solution)/shard_map/ppermute | solution.py:368
  41.7 3.8 %shard_map.109.refs_0_ = f32[3,36,32,128]{3,2,1,0:T(8,128)S(1)} custom-call(f32[4,8,1024]{2,1,0:T(8,128)S(1)} %shard_map.105.snd_ref, bf16[4,3,36,32,128]{4,3,2,1,0:T(8,128)(2,1)S(1)} %get-tuple-element.35.traj_ref, bf16[3,36,64]{2,1,0:T(8,128)(2,1)S(1)} %copy-done.13), custom_call_target="tpu_custom_call" | custom-call | tf_op jit(solution)/shard_map/pallas_call | solution.py:43
  45.5 2.6 %shard_map.110 = (f32[3,36,32,128]{3,2,1,0:T(8,128)S(1)}, f32[1,3456]{1,0:T(1,128)S(1)}, f32[1,3456]{1,0:T(1,128)S(1)}, f32[108,128]{1,0:T(8,128)S(1)}, f32[108,...) custom-call(f32[4,128]{1,0:T(4,128)S(1)} %broadcast_in_dim.4.mask_ref, f32[3,36,32,128]{3,2,1,0:T(8,128)S(1)} %get-tuple-element.45.w_in, ...), custom_call_target="tpu_custom_call" | custom-call | tf_op jit(solution)/shard_map/pallas_call | solution.py:43
  48.3 0.9 %collective-permute-start.7 = (f32[108,128]{1,0:T(8,128)S(1)}, f32[108,128]{1,0:T(8,128)S(1)}, u32[]{:S(2)}, u32[]{:S(2)}) collective-permute-start(f32[108,128]{1,0:T(8,128)S(1)} %get-tuple-element.54), channel_id=1, source_target_pairs={{16,32},{32,16},{48,64},{64,48},{80,96},{96,80},{112,0},{0,112},{1... | collective-permute-start | bytes 165896 | tf_op jit(solution)/shard_map/ppermute | solution.py:369
  49.2 3.2 %collective-permute-start.5 = (f32[1,3456]{1,0:T(1,128)S(1)}, f32[1,3456]{1,0:T(1,128)S(1)}, u32[]{:S(2)}, u32[]{:S(2)}) collective-permute-start(f32[1,3456]{1,0:T(1,128)S(1)} %get-tuple-element.52), channel_id=1, source_target_pairs={{1,2},{2,1},{3,4},{4,3},{5,6},{6,5},{7,8},{8,7},{9,10},{10,9},{11,... | collective-permute-start | bytes 41480 | tf_op jit(solution)/shard_map/ppermute | solution.py:368
  52.3 3.8 %shard_map.111.refs_0_ = f32[3,36,32,128]{3,2,1,0:T(8,128)S(1)} custom-call(f32[4,8,1024]{2,1,0:T(8,128)S(1)} %shard_map.105.snd_ref, bf16[4,3,36,32,128]{4,3,2,1,0:T(8,128)(2,1)S(1)} %get-tuple-element.35.traj_ref, bf16[3,36,64]{2,1,0:T(8,128)(2,1)S(1)} %copy-done.13), custom_call_target="tpu_custom_call" | custom-call | tf_op jit(solution)/shard_map/pallas_call | solution.py:43
  56.2 2.6 %shard_map.112 = (f32[3,36,32,128]{3,2,1,0:T(8,128)S(1)}, f32[1,3456]{1,0:T(1,128)S(1)}, f32[1,3456]{1,0:T(1,128)S(1)}, f32[108,128]{1,0:T(8,128)S(1)}, f32[108,...) custom-call(f32[4,128]{1,0:T(4,128)S(1)} %broadcast_in_dim.4.mask_ref, f32[3,36,32,128]{3,2,1,0:T(8,128)S(1)} %get-tuple-element.50.w_in, ...), custom_call_target="tpu_custom_call" | custom-call | tf_op jit(solution)/shard_map/pallas_call | solution.py:43
  58.9 1.9 %collective-permute-start.11 = (f32[108,128]{1,0:T(8,128)S(1)}, f32[108,128]{1,0:T(8,128)S(1)}, u32[]{:S(2)}, u32[]{:S(2)}) collective-permute-start(f32[108,128]{1,0:T(8,128)S(1)} %get-tuple-element.60), channel_id=1, source_target_pairs={{16,32},{32,16},{48,64},{64,48},{80,96},{96,80},{112,0},{0,112},{1... | collective-permute-start | bytes 165896 | tf_op jit(solution)/shard_map/ppermute | solution.py:369
  60.9 2.3 %collective-permute-start.9 = (f32[1,3456]{1,0:T(1,128)S(1)}, f32[1,3456]{1,0:T(1,128)S(1)}, u32[]{:S(2)}, u32[]{:S(2)}) collective-permute-start(f32[1,3456]{1,0:T(1,128)S(1)} %get-tuple-element.58), channel_id=1, source_target_pairs={{1,2},{2,1},{3,4},{4,3},{5,6},{6,5},{7,8},{8,7},{9,10},{10,9},{11,... | collective-permute-start | bytes 41480 | tf_op jit(solution)/shard_map/ppermute | solution.py:368
  63.2 3.8 %shard_map.113.refs_0_ = f32[3,36,32,128]{3,2,1,0:T(8,128)S(1)} custom-call(f32[4,8,1024]{2,1,0:T(8,128)S(1)} %shard_map.105.snd_ref, bf16[4,3,36,32,128]{4,3,2,1,0:T(8,128)(2,1)S(1)} %get-tuple-element.35.traj_ref, bf16[3,36,64]{2,1,0:T(8,128)(2,1)S(1)} %copy-done.13), custom_call_target="tpu_custom_call" | custom-call | tf_op jit(solution)/shard_map/pallas_call | solution.py:43
  67.9 2.6 %shard_map.114 = (f32[3,36,32,128]{3,2,1,0:T(8,128)S(1)}, f32[1,3456]{1,0:T(1,128)S(1)}, f32[1,3456]{1,0:T(1,128)S(1)}, f32[108,128]{1,0:T(8,128)S(1)}, f32[108,...) custom-call(f32[4,128]{1,0:T(4,128)S(1)} %broadcast_in_dim.4.mask_ref, f32[3,36,32,128]{3,2,1,0:T(8,128)S(1)} %get-tuple-element.56.w_in, ...), custom_call_target="tpu_custom_call" | custom-call | tf_op jit(solution)/shard_map/pallas_call | solution.py:43
  71.6 2.3 %collective-permute-start.13 = (f32[1,3456]{1,0:T(1,128)S(1)}, f32[1,3456]{1,0:T(1,128)S(1)}, u32[]{:S(2)}, u32[]{:S(2)}) collective-permute-start(f32[1,3456]{1,0:T(1,128)S(1)} %get-tuple-element.64), channel_id=1, source_target_pairs={{1,2},{2,1},{3,4},{4,3},{5,6},{6,5},{7,8},{8,7},{9,10},{10,9},{11,... | collective-permute-start | bytes 41480 | tf_op jit(solution)/shard_map/ppermute | solution.py:368
  73.9 1.4 %collective-permute-done.12.lon_a = f32[1,3456]{1,0:T(1,128)S(1)} collective-permute-done((f32[1,3456]{1,0:T(1,128)S(1)}, f32[1,3456]{1,0:T(1,128)S(1)}, u32[]{:S(2)}, u32[]{:S(2)}) %collective-permute-start.12) | collective-permute-done | bytes 13856 | tf_op jit(solution)/shard_map/ppermute | solution.py:370
  75.3 3.3 %collective-permute-done.13.lon_b = f32[1,3456]{1,0:T(1,128)S(1)} collective-permute-done((f32[1,3456]{1,0:T(1,128)S(1)}, f32[1,3456]{1,0:T(1,128)S(1)}, u32[]{:S(2)}, u32[]{:S(2)}) %collective-permute-start.13) | collective-permute-done | bytes 13856 | tf_op jit(solution)/shard_map/ppermute | solution.py:368
  78.6 2.4 %shard_map.115 = (f32[3,36,32,128]{3,2,1,0:T(8,128)}, f32[3,32,128]{2,1,0:T(8,128)}) custom-call(f32[4,128]{1,0:T(4,128)S(1)} %broadcast_in_dim.4.mask_ref, f32[3,36,32,128]{3,2,1,0:T(8,128)S(1)} %get-tuple-element.62.w_in, f32[1,3456]{1,0:T(1,128)S(1)} %collective-permute-done.12.lon_a, f32[1,3456]{1,0:T(1,128)S(1)} %collective-permute-done.13.lon_b, ...), custom_call_target="tpu_custom_call" | custom-call | tf_op jit(solution)/shard_map/pallas_call | solution.py:43
  (57 shorter events, 8.0 us)
Async XLA Ops:
  3.4 21.8 %all-to-all-start = ((f32[128,2,128]{2,1,0:T(2,128)}), f32[128,2,128]{2,1,0:T(2,128)}, u32[]{:S(2)}, u32[]{:S(2)}) async-start(f32[128,2,128]{2,1,0:T(2,128)} %shard_map.104), calls=%async_computation | async-start | bytes 262144 | tf_op jit(solution)/shard_map/all_to_all | solution.py:404
  27.1 3.9 %copy-start.1 = (f32[5,36,32,128]{3,2,1,0:T(8,128)S(1)}, f32[5,36,32,128]{3,2,1,0:T(8,128)}, u32[]{:S(2)}) copy-start(f32[5,36,32,128]{3,2,1,0:T(8,128)} %copy-done) | copy-start | bytes 8847364
  27.1 3.9 %copy-start.3 = (f32[36,32,128]{2,1,0:T(8,128)S(1)}, f32[36,32,128]{2,1,0:T(8,128)}, u32[]{:S(2)}) copy-start(f32[36,32,128]{2,1,0:T(8,128)} %copy-done.2) | copy-start | bytes 1769476
  27.1 3.9 %copy-start.5 = (f32[35,32,128]{2,1,0:T(8,128)S(1)}, f32[35,32,128]{2,1,0:T(8,128)}, u32[]{:S(2)}) copy-start(f32[35,32,128]{2,1,0:T(8,128)} %copy-done.4) | copy-start | bytes 1720324
  27.1 3.9 %copy-start.7 = (f32[35,32,128]{2,1,0:T(8,128)S(1)}, f32[35,32,128]{2,1,0:T(8,128)}, u32[]{:S(2)}) copy-start(f32[35,32,128]{2,1,0:T(8,128)} %copy-done.6) | copy-start | bytes 1720324
  27.2 3.9 %copy-start.9 = (bf16[256,256]{1,0:T(8,128)(2,1)S(1)}, bf16[256,256]{1,0:T(8,128)(2,1)}, u32[]{:S(2)}) copy-start(bf16[256,256]{1,0:T(8,128)(2,1)} %copy-done.8) | copy-start | bytes 393220
  27.2 3.9 %copy-start.11 = (f32[4,36,128]{2,1,0:T(8,128)S(1)}, f32[4,36,128]{2,1,0:T(8,128)}, u32[]{:S(2)}) copy-start(f32[4,36,128]{2,1,0:T(8,128)} %copy-done.10) | copy-start | bytes 221188
  27.2 3.9 %copy-start.15 = (f32[4,1,1152]{2,1,0:T(1,128)S(1)}, f32[4,1,1152]{2,1,0:T(1,128)}, u32[]{:S(2)}) copy-start(f32[4,1,1152]{2,1,0:T(1,128)} %copy-done.14) | copy-start | bytes 55300
  33.1 12.4 %collective-permute-start.2 = (f32[108,128]{1,0:T(8,128)S(1)}, f32[108,128]{1,0:T(8,128)S(1)}, u32[]{:S(2)}, u32[]{:S(2)}) collective-permute-start(f32[108,128]{1,0:T(8,128)S(1)} %get-tuple-element.48), channel_id=1, source_target_pairs={{0,16},{16,0},{32,48},{48,32},{64,80},{80,64},{96,112},{112,96},{1... | collective-permute-start | bytes 165896 | tf_op jit(solution)/shard_map/ppermute | solution.py:371
  33.2 12.3 %collective-permute-start.3 = (f32[108,128]{1,0:T(8,128)S(1)}, f32[108,128]{1,0:T(8,128)S(1)}, u32[]{:S(2)}, u32[]{:S(2)}) collective-permute-start(f32[108,128]{1,0:T(8,128)S(1)} %get-tuple-element.49), channel_id=1, source_target_pairs={{16,32},{32,16},{48,64},{64,48},{80,96},{96,80},{112,0},{0,112},{1... | collective-permute-start | bytes 165896 | tf_op jit(solution)/shard_map/ppermute | solution.py:369
  35.4 10.1 %collective-permute-start = (f32[1,3456]{1,0:T(1,128)S(1)}, f32[1,3456]{1,0:T(1,128)S(1)}, u32[]{:S(2)}, u32[]{:S(2)}) collective-permute-start(f32[1,3456]{1,0:T(1,128)S(1)} %get-tuple-element.46), channel_id=1, source_target_pairs={{0,1},{1,0},{2,3},{3,2},{4,5},{5,4},{6,7},{7,6},{8,9},{9,8},{10,11... | collective-permute-start | bytes 41480 | tf_op jit(solution)/shard_map/ppermute | solution.py:370
  37.2 8.3 %collective-permute-start.1 = (f32[1,3456]{1,0:T(1,128)S(1)}, f32[1,3456]{1,0:T(1,128)S(1)}, u32[]{:S(2)}, u32[]{:S(2)}) collective-permute-start(f32[1,3456]{1,0:T(1,128)S(1)} %get-tuple-element.47), channel_id=1, source_target_pairs={{1,2},{2,1},{3,4},{4,3},{5,6},{6,5},{7,8},{8,7},{9,10},{10,9},{11,... | collective-permute-start | bytes 41480 | tf_op jit(solution)/shard_map/ppermute | solution.py:368
  48.2 8.0 %collective-permute-start.6 = (f32[108,128]{1,0:T(8,128)S(1)}, f32[108,128]{1,0:T(8,128)S(1)}, u32[]{:S(2)}, u32[]{:S(2)}) collective-permute-start(f32[108,128]{1,0:T(8,128)S(1)} %get-tuple-element.53), channel_id=1, source_target_pairs={{0,16},{16,0},{32,48},{48,32},{64,80},{80,64},{96,112},{112,96},{1... | collective-permute-start | bytes 165896 | tf_op jit(solution)/shard_map/ppermute | solution.py:371
  48.3 7.9 %collective-permute-start.7 = (f32[108,128]{1,0:T(8,128)S(1)}, f32[108,128]{1,0:T(8,128)S(1)}, u32[]{:S(2)}, u32[]{:S(2)}) collective-permute-start(f32[108,128]{1,0:T(8,128)S(1)} %get-tuple-element.54), channel_id=1, source_target_pairs={{16,32},{32,16},{48,64},{64,48},{80,96},{96,80},{112,0},{0,112},{1... | collective-permute-start | bytes 165896 | tf_op jit(solution)/shard_map/ppermute | solution.py:369
  49.2 7.0 %collective-permute-start.4 = (f32[1,3456]{1,0:T(1,128)S(1)}, f32[1,3456]{1,0:T(1,128)S(1)}, u32[]{:S(2)}, u32[]{:S(2)}) collective-permute-start(f32[1,3456]{1,0:T(1,128)S(1)} %get-tuple-element.51), channel_id=1, source_target_pairs={{0,1},{1,0},{2,3},{3,2},{4,5},{5,4},{6,7},{7,6},{8,9},{9,8},{10,11... | collective-permute-start | bytes 41480 | tf_op jit(solution)/shard_map/ppermute | solution.py:370
  49.2 7.0 %collective-permute-start.5 = (f32[1,3456]{1,0:T(1,128)S(1)}, f32[1,3456]{1,0:T(1,128)S(1)}, u32[]{:S(2)}, u32[]{:S(2)}) collective-permute-start(f32[1,3456]{1,0:T(1,128)S(1)} %get-tuple-element.52), channel_id=1, source_target_pairs={{1,2},{2,1},{3,4},{4,3},{5,6},{6,5},{7,8},{8,7},{9,10},{10,9},{11,... | collective-permute-start | bytes 41480 | tf_op jit(solution)/shard_map/ppermute | solution.py:368
  58.9 9.1 %collective-permute-start.10 = (f32[108,128]{1,0:T(8,128)S(1)}, f32[108,128]{1,0:T(8,128)S(1)}, u32[]{:S(2)}, u32[]{:S(2)}) collective-permute-start(f32[108,128]{1,0:T(8,128)S(1)} %get-tuple-element.59), channel_id=1, source_target_pairs={{0,16},{16,0},{32,48},{48,32},{64,80},{80,64},{96,112},{112,96},{1... | collective-permute-start | bytes 165896 | tf_op jit(solution)/shard_map/ppermute | solution.py:371
  58.9 9.0 %collective-permute-start.11 = (f32[108,128]{1,0:T(8,128)S(1)}, f32[108,128]{1,0:T(8,128)S(1)}, u32[]{:S(2)}, u32[]{:S(2)}) collective-permute-start(f32[108,128]{1,0:T(8,128)S(1)} %get-tuple-element.60), channel_id=1, source_target_pairs={{16,32},{32,16},{48,64},{64,48},{80,96},{96,80},{112,0},{0,112},{1... | collective-permute-start | bytes 165896 | tf_op jit(solution)/shard_map/ppermute | solution.py:369
  60.9 6.1 %collective-permute-start.8 = (f32[1,3456]{1,0:T(1,128)S(1)}, f32[1,3456]{1,0:T(1,128)S(1)}, u32[]{:S(2)}, u32[]{:S(2)}) collective-permute-start(f32[1,3456]{1,0:T(1,128)S(1)} %get-tuple-element.57), channel_id=1, source_target_pairs={{0,1},{1,0},{2,3},{3,2},{4,5},{5,4},{6,7},{7,6},{8,9},{9,8},{10,11... | collective-permute-start | bytes 41480 | tf_op jit(solution)/shard_map/ppermute | solution.py:370
  60.9 7.0 %collective-permute-start.9 = (f32[1,3456]{1,0:T(1,128)S(1)}, f32[1,3456]{1,0:T(1,128)S(1)}, u32[]{:S(2)}, u32[]{:S(2)}) collective-permute-start(f32[1,3456]{1,0:T(1,128)S(1)} %get-tuple-element.58), channel_id=1, source_target_pairs={{1,2},{2,1},{3,4},{4,3},{5,6},{6,5},{7,8},{8,7},{9,10},{10,9},{11,... | collective-permute-start | bytes 41480 | tf_op jit(solution)/shard_map/ppermute | solution.py:368
  70.6 8.0 %collective-permute-start.14 = (f32[108,128]{1,0:T(8,128)S(1)}, f32[108,128]{1,0:T(8,128)S(1)}, u32[]{:S(2)}, u32[]{:S(2)}) collective-permute-start(f32[108,128]{1,0:T(8,128)S(1)} %get-tuple-element.65), channel_id=1, source_target_pairs={{0,16},{16,0},{32,48},{48,32},{64,80},{80,64},{96,112},{112,96},{1... | collective-permute-start | bytes 165896 | tf_op jit(solution)/shard_map/ppermute | solution.py:371
  70.7 7.9 %collective-permute-start.15 = (f32[108,128]{1,0:T(8,128)S(1)}, f32[108,128]{1,0:T(8,128)S(1)}, u32[]{:S(2)}, u32[]{:S(2)}) collective-permute-start(f32[108,128]{1,0:T(8,128)S(1)} %get-tuple-element.66), channel_id=1, source_target_pairs={{16,32},{32,16},{48,64},{64,48},{80,96},{96,80},{112,0},{0,112},{1... | collective-permute-start | bytes 165896 | tf_op jit(solution)/shard_map/ppermute | solution.py:369
  71.6 3.7 %collective-permute-start.12 = (f32[1,3456]{1,0:T(1,128)S(1)}, f32[1,3456]{1,0:T(1,128)S(1)}, u32[]{:S(2)}, u32[]{:S(2)}) collective-permute-start(f32[1,3456]{1,0:T(1,128)S(1)} %get-tuple-element.63), channel_id=1, source_target_pairs={{0,1},{1,0},{2,3},{3,2},{4,5},{5,4},{6,7},{7,6},{8,9},{9,8},{10,11... | collective-permute-start | bytes 41480 | tf_op jit(solution)/shard_map/ppermute | solution.py:370
  71.6 7.0 %collective-permute-start.13 = (f32[1,3456]{1,0:T(1,128)S(1)}, f32[1,3456]{1,0:T(1,128)S(1)}, u32[]{:S(2)}, u32[]{:S(2)}) collective-permute-start(f32[1,3456]{1,0:T(1,128)S(1)} %get-tuple-element.64), channel_id=1, source_target_pairs={{1,2},{2,1},{3,4},{4,3},{5,6},{6,5},{7,8},{8,7},{9,10},{10,9},{11,... | collective-permute-start | bytes 41480 | tf_op jit(solution)/shard_map/ppermute | solution.py:368
  (9 other events, 7.2 us)

commit v3 on v2

--- a/solution.py
+++ b/solution.py
@@ -42,7 +42,7 @@
     args = [pltpu.with_memory_space_constraint(a, pltpu.HBM) if i in hbm else a for i, a in enumerate(args)]
     done = pl.pallas_call(
         kernel,
-        out_shape=outs,
+        out_shape=tuple(pltpu.HBM(o.shape, o.dtype) if i in hbm_out else o for i, o in enumerate(outs)),
         in_specs=[HBM if i in hbm else VMEM for i in range(len(args))],
         out_specs=tuple(HBM if i in hbm_out else VMEM for i in range(len(outs))),
         scratch_shapes=list(scratch),
@@ -128,19 +128,29 @@
             out_ref[s, 7:8, :] = jnp.zeros((1, CAP * ntiles), F32)
 
 
-def forcing_kernel(s, chunk, snd_ref, traj_ref, table_ref, out_ref, pick, weight):
+def forcing_kernel(s, chunk, snd_ref, traj_ref, table_in, out_ref, pick, weight, table_ref, sem):
+    copy = pltpu.make_async_copy(table_in, table_ref, sem)
+    copy.start()
+    forcing_body(s, chunk, snd_ref, traj_ref, copy, table_ref, out_ref, pick, weight)
+
+
+def forcing_body(s, chunk, snd_ref, traj_ref, copy, table_ref, out_ref, pick, weight):
     tracers, layers = out_ref.shape[:2]
     slots = snd_ref.shape[2]
-    nker = table_ref.shape[2]
+    nker = table_ref.shape[1]
     cell_ids = lax.broadcasted_iota(jnp.int32, (256, chunk), 0).astype(F32)
     low_ids = lax.broadcasted_iota(jnp.int32, (16, chunk), 0).astype(F32)
     ker_ids = lax.broadcasted_iota(jnp.int32, (nker, chunk), 0).astype(F32)
     for c in range(slots // chunk):
         at = pl.ds(c * chunk, chunk)
         pick[:, at] = jnp.where(cell_ids == snd_ref[s, 0:1, at], 1.0, 0.0).astype(BF16)
+    copy.wait()
+    table = split3(table_ref[...])
+    for c in range(slots // chunk):
+        at = pl.ds(c * chunk, chunk)
         low = jnp.where(low_ids == snd_ref[s, 1:2, at], 1.0, 0.0)
         ker = jnp.where(ker_ids == snd_ref[s, 2:3, at], 1.0, 0.0).astype(BF16)
-        w = dot(table_ref[0], ker) + dot(table_ref[1], ker) + dot(table_ref[2], ker)
+        w = dot(table[0], ker) + dot(table[1], ker) + dot(table[2], ker)
         for k in range(layers):
             weight[k, :, at] = w[k : k + 1, :] * low
     for t in range(tracers):
@@ -164,28 +174,44 @@
         out_ref[t, :, 16:32, :] = force[:, 128:256].reshape(layers, 16, 128)
 
 
+def end_rows():
+    row = lax.broadcasted_iota(jnp.int32, (8, 256), 0)
+    lane = lax.broadcasted_iota(jnp.int32, (8, 256), 1) % 128
+    ends = ((row == 0) & (lane == 127)) | ((row == 1) & (lane == 0))
+    return jnp.where(ends, 1.0, 0.0).astype(BF16)
+
+
+def lane_shifts():
+    src = lax.broadcasted_iota(jnp.int32, (256, 256), 0) % 128
+    dst = lax.broadcasted_iota(jnp.int32, (256, 256), 1)
+    dst = jnp.where(dst < 128, dst - 1, dst - 127)
+    return jnp.where(src == dst, 1.0, 0.0).astype(BF16)
+
+
+def views(planes_ref):
+    layers = (planes_ref.shape[0] + 1) // 7
+    part = [planes_ref.at[pl.ds(i * layers, layers)] for i in range(6)]
+    return part[5], planes_ref.at[pl.ds(6 * layers, layers - 1)], part[:5]
+
+
 def setup_kernel(
-    mask_ref, mix_in, tr_in, traj_in, table_in,
-    mix_ref, inv_ref, up_ref, coef_ref, lat_w, lon_w, shift_ref, ends_ref, traj_ref, parts_ref, tr_ref, table_ref, sems,
+    mask_ref, mix_in, tr_in, traj_in, planes_out, lat_out, lon_out, traj_ref,
+    mix_ref, tr_ref, planes_ref, lat_w, lon_w, in_sems, out_sems,
 ):
-    layers = inv_ref.shape[0]
+    layers = tr_ref.shape[1]
+    inv_ref, up_ref, coef_ref = views(planes_ref)
     copies = [
-        pltpu.make_async_copy(src, dst, sems.at[i])
-        for i, (src, dst) in enumerate(
-            ((mix_in, mix_ref), (tr_in, tr_ref), (table_in, table_ref), (traj_in, traj_ref))
-        )
+        pltpu.make_async_copy(src, dst, in_sems.at[i])
+        for i, (src, dst) in enumerate(((mix_in, mix_ref), (tr_in, tr_ref), (traj_in, traj_ref)))
     ]
     for copy in copies:
         copy.start()
-    src = lax.broadcasted_iota(jnp.int32, (256, 256), 0) % 128
-    dst = lax.broadcasted_iota(jnp.int32, (256, 256), 1)
-    dst = jnp.where(dst < 128, dst - 1, dst - 127)
-    shift_ref[...] = jnp.where(src == dst, 1.0, 0.0).astype(BF16)
-    end_row = lax.broadcasted_iota(jnp.int32, (8, 256), 0)
-    end_lane = lax.broadcasted_iota(jnp.int32, (8, 256), 1) % 128
-    ends = ((end_row == 0) & (end_lane == 127)) | ((end_row == 1) & (end_lane == 0))
-    ends = jnp.where(ends, 1.0, 0.0).astype(BF16)
-    ends_ref[...] = ends
+    sent = []
+
+    def send(src, dst):
+        sent.append(pltpu.make_async_copy(src, dst, out_sems.at[len(sent)]))
+        sent[-1].start()
+
     copies[0].wait()
     for k in range(layers):
         diag = jnp.ones_like(mix_ref[0])
@@ -200,20 +226,27 @@
         if k < layers - 1:
             up = -mix_ref[k] * inv
             up_ref[k] = up
+    at = pl.ds(5 * layers, 2 * layers - 1)
+    send(planes_ref.at[at], planes_out.at[at])
     copies[1].wait()
     lane = lax.broadcasted_iota(jnp.int32, (32, 128), 1)
     row = lax.broadcasted_iota(jnp.int32, (32, 128), 0)
 
     def coefs(k, _):
         te, tw, tn, ts = (tr_ref[i, k] for i in range(4))
-        coef_ref[0, k] = jnp.where(lane == 0, 0.0, pltpu.roll(te, 1, axis=1))
-        coef_ref[1, k] = jnp.where(lane == 127, 0.0, pltpu.roll(tw, 127, axis=1))
-        coef_ref[2, k] = jnp.where(row == 0, 0.0, pltpu.roll(tn, 1, axis=0))
-        coef_ref[3, k] = jnp.where(row == 31, 0.0, pltpu.roll(ts, 31, axis=0))
-        coef_ref[4, k] = 1.0 - te - tw - tn - ts
+        coef_ref[0][k] = jnp.where(lane == 0, 0.0, pltpu.roll(te, 1, axis=1))
+        coef_ref[1][k] = jnp.where(lane == 127, 0.0, pltpu.roll(tw, 127, axis=1))
+        coef_ref[2][k] = jnp.where(row == 0, 0.0, pltpu.roll(tn, 1, axis=0))
+        coef_ref[3][k] = jnp.where(row == 31, 0.0, pltpu.roll(ts, 31, axis=0))
+        coef_ref[4][k] = 1.0 - te - tw - tn - ts
         return 0
 
-    lax.fori_loop(0, layers, coefs, 0, unroll=4)
+    group = layers // 3
+    for g in range(3):
+        lax.fori_loop(g * group, (g + 1) * group, coefs, 0, unroll=4)
+        for i in range(5):
+            at = pl.ds(i * layers + g * group, group)
+            send(planes_ref.at[at], planes_out.at[at])
     to_north = tr_ref[3, :, 0, :] * mask_ref[0:1, :]
     to_south = tr_ref[2, :, 31, :] * mask_ref[1:2, :]
     odd = mask_ref[2:3, :]
@@ -221,19 +254,20 @@
     lat_w[1] = (1.0 - odd) * to_south
     lat_w[2] = (1.0 - odd) * to_north
     lat_w[3] = odd * to_south
+    send(lat_w, lat_out)
     odd = mask_ref[3:4, 0:1]
+    ends = end_rows()[:, 0:128]
     for side in range(2):
         flat = None
         for part in split3(tr_ref[side].reshape(layers * 32, 128)):
-            term = dot_t(ends[:, 0:128], part)
+            term = dot_t(ends, part)
             flat = term if flat is None else flat + term
         flat = flat[side : side + 1, :]
         lon_w[side] = flat * (odd if side else 1.0 - odd)
         lon_w[2 + side] = flat * (1.0 - odd if side else odd)
-    copies[2].wait()
-    for i, part in enumerate(split3(table_ref[...])):
-        parts_ref[i] = part
-    copies[3].wait()
+    send(lon_w, lon_out)
+    for copy in copies[2:] + sent:
+        copy.wait()
 
 
 def spread(mask_ref, lon_a, lon_b, lat_a, lat_b, halo, lat_halo):
@@ -266,7 +300,9 @@
 
 
 def step_body(base, force_ref, fixed, outs, v):
-    mix_ref, inv_ref, up_ref, coef_ref, lat_w, lon_w, shift_ref, ends_ref = fixed
+    mix_ref, planes_ref, lat_w, lon_w = fixed
+    inv_ref, up_ref, coef_ref = views(planes_ref)
+    shifts, end_lanes = lane_shifts(), end_rows()
     w_out, lon_a, lon_b, lat_a, lat_b = outs
     tracers, layers, rows, cols = force_ref.shape
     d = tuple((force_ref[t, 0] + base(t, 0)) * inv_ref[0] for t in range(tracers))
@@ -299,13 +335,13 @@
             x = v[t, g : g + group]
             hi, lo = split2(x.reshape(size, cols))
             both = jnp.concatenate([hi, lo], axis=1)
-            moved = dot(both, shift_ref[...])
-            ends = dot_t(ends_ref[...], both)
+            moved = dot(both, shifts)
+            ends = dot_t(end_lanes, both)
             to = pl.ds((t * layers + g) * rows, size)
             at = pl.ds(g * rows, size)
             lon_a[:, to] = ends[0:1, :] * lon_w[0, :, at] + ends[1:2, :] * lon_w[1, :, at]
             lon_b[:, to] = ends[0:1, :] * lon_w[2, :, at] + ends[1:2, :] * lon_w[3, :, at]
-            c = [coef_ref[i, g : g + group].reshape(size, cols) for i in range(5)]
+            c = [coef_ref[i][g : g + group].reshape(size, cols) for i in range(5)]
             down = jnp.stack([pltpu.roll(x[i], 1, axis=0) for i in range(group)])
             up = jnp.stack([pltpu.roll(x[i], rows - 1, axis=0) for i in range(group)])
             out = c[4] * x.reshape(size, cols) + c[0] * moved[:, :cols] + c[1] * moved[:, cols:]
@@ -319,12 +355,26 @@
         lat_b[at, :] = top * lat_w[2] + low * lat_w[3]
 
 
+def head_kernel(s, chunk, got_ref, traj_ref, table_in, *refs):
+    sources, (out_ref, snd_ref), held = refs[0:4], refs[4:6], refs[6:10]
+    pick, weight, table_ref, sem, sems = refs[10:]
+    copy = pltpu.make_async_copy(table_in, table_ref, sem)
+    copy.start()
+    copies = [pltpu.make_async_copy(a, b, sems.at[i]) for i, (a, b) in enumerate(zip(sources, held))]
+    for held_copy in copies:
+        held_copy.start()
+    unpack_kernel(got_ref, snd_ref)
+    forcing_body(s, chunk, snd_ref, traj_ref, copy, table_ref, out_ref, pick, weight)
+    for held_copy in copies:
+        held_copy.wait()
+
+
 def first_step_kernel(*refs):
-    step_body(lambda t, k: 0.0, refs[0], refs[1:9], refs[9:14], refs[14])
+    step_body(lambda t, k: 0.0, refs[0], refs[1:5], refs[5:10], refs[10])
 
 
 def step_kernel(mask_ref, w_in, lon_a, lon_b, lat_a, lat_b, flux_in, *refs):
-    force_ref, fixed, outs, (flux_out, v, halo, lat_halo) = refs[0], refs[1:9], refs[9:14], refs[14:]
+    force_ref, fixed, outs, (flux_out, v, halo, lat_halo) = refs[0], refs[1:5], refs[5:10], refs[10:]
     spread(mask_ref, lon_a, lon_b, lat_a, lat_b, halo, lat_halo)
 
     def base(t, k):
@@ -348,9 +398,12 @@
             done[t, k] = received(w_in, halo, lat_halo, t, k)
             return 0
 
-        lax.fori_loop(0, layers, finish, 0, unroll=4)
-        copies.append(pltpu.make_async_copy(done.at[t], adj_out.at[t], sems.at[t]))
-        copies[-1].start()
+        group = layers // 3
+        for g in range(3):
+            lax.fori_loop(g * group, (g + 1) * group, finish, 0, unroll=4)
+            at = (t, pl.ds(g * group, group))
+            copies.append(pltpu.make_async_copy(done.at[at], adj_out.at[at], sems.at[3 * t + g]))
+            copies[-1].start()
     flux_out[...] = flux_in[...] + done[:, 0]
     for copy in copies:
         copy.wait()
@@ -405,33 +458,28 @@
     lat, lon = lax.axis_index("lat"), lax.axis_index("lon")
     mask = jnp.stack([lat > 0, lat < lax.axis_size("lat") - 1, lat % 2 > 0, lon % 2 > 0]).astype(F32)
     mask = jnp.broadcast_to(mask[:, None], (4, cols))
-    *fixed, local, table = call(
+    planes = (sds(7 * layers - 1, rows, cols),)
+    weights = (sds(4, layers, cols), sds(4, 1, layers * rows))
+    *fixed, local = call(
         setup_kernel,
-        (
-            sds(*mixing.shape),
-            sds(layers, rows, cols),
-            sds(*mixing.shape),
-            sds(5, layers, rows, cols),
-            sds(4, layers, cols),
-            sds(4, 1, layers * rows),
-            sds(256, 256, dtype=BF16),
-            sds(8, 256, dtype=BF16),
-            sds(*trajectory.shape, dtype=BF16),
-            sds(3, layers, kernel_table.shape[0], dtype=BF16),
-        ),
+        planes + weights + (sds(*trajectory.shape, dtype=BF16),),
         mask,
         mixing,
         transport,
         trajectory,
-        kernel_table.T,
-        hbm=(1, 2, 3, 4),
-        scratch=(
-            pltpu.VMEM(transport.shape, F32),
-            pltpu.VMEM(kernel_table.shape[::-1], F32),
-            pltpu.SemaphoreType.DMA((4,)),
-        ),
+        hbm=(1, 2, 3),
+        hbm_out=range(3),
+        scratch=[pltpu.VMEM(x.shape, F32) for x in (mixing, transport) + planes + weights]
+        + [pltpu.SemaphoreType.DMA((3,)), pltpu.SemaphoreType.DMA((18,))],
     )
-    snd = call(unpack_kernel, sds(steps, 8, slots), got)
+    fixed = (mixing, *fixed)
+    table = kernel_table.T
+    work = (
+        pltpu.VMEM((256, slots), BF16),
+        pltpu.VMEM((layers, 16, slots), F32),
+        pltpu.VMEM(table.shape, F32),
+        pltpu.SemaphoreType.DMA,
+    )
 
     def forcing(s):
         return call(
@@ -440,13 +488,24 @@
             snd,
             local,
             table,
-            scratch=(pltpu.VMEM((256, slots), BF16), pltpu.VMEM((layers, 16, slots), F32)),
+            hbm=(2,),
+            scratch=work,
         )
 
+    force, snd, *fixed = call(
+        functools.partial(head_kernel, steps - 1, 512),
+        (field, sds(steps, 8, slots)) + tuple(sds(*x.shape) for x in fixed),
+        got,
+        local,
+        table,
+        *fixed,
+        hbm=range(2, 7),
+        scratch=work + (pltpu.SemaphoreType.DMA((4,)),),
+    )
     v = pltpu.VMEM(field.shape, F32)
     lat_halo = pltpu.VMEM((2,) + lat_edge.shape, F32)
     moved = (field, lon_edge, lon_edge, lat_edge, lat_edge)
-    w, *edges = call(first_step_kernel, moved, forcing(steps - 1), *fixed, scratch=(v,))
+    w, *edges = call(first_step_kernel, moved, force, *fixed, scratch=(v,))
     flux = jnp.zeros((tracers, rows, cols), F32)
     for s in range(steps - 2, -1, -1):
         halos = exchange(*edges)
@@ -469,7 +528,7 @@
         *exchange(*edges),
         flux,
         hbm_out=(0,),
-        scratch=(v, lat_halo, v, pltpu.SemaphoreType.DMA((tracers,))),
+        scratch=(v, lat_halo, v, pltpu.SemaphoreType.DMA((3 * tracers,))),
     )
 
 

time: 81.5 us -> 79.5 us (0.975)
  local copies, waits for them, and re-layouts: 7.33 us -> 0.08 us
  waiting for transfers between devices: 5.67 us -> 10.5 us
  Pallas kernels: 35 us -> 39.6 us
  starting transfers between devices: 32 us -> 27.8 us
    unnamed x32 -> x0, local copies, waits for them, and re-layouts: 7.25 us -> none
    all_to_all x1, waiting for transfers between devices: 0.01 us -> 5.14 us  [body(): lax.all_to_all(outgoing, ('lat', 'lon'), split_axis=0, concat_axis=0, til...]
    pallas_call x12 -> x11, Pallas kernels: 35 us -> 39.6 us  [call(): pl.pallas_call(kernel, out_shape=tuple((pltpu.HBM(o.shape, o.dtype) if i...]
    ppermute x4, starting transfers between devices: 12.3 us -> 10.4 us  [exchange(): lon_b = lax.ppermute(lon_b, 'lon', lon_far)]
    ppermute x4, starting transfers between devices: 5.97 us -> 4.52 us  [exchange(): lat_b = lax.ppermute(lat_b, 'lat', lat_far)]
    ppermute x4, starting transfers between devices: 1.75 us -> 0.84 us  [exchange(): lon_a = lax.ppermute(lon_a, 'lon', lon_near)]
  transfers between devices with their start and end apart: 17 -> 17, of which waited for: 3 -> 4; matrix products, arithmetic and copies ran while one was open for 0% -> 0% of each run, Pallas kernels for 18% -> 23%
where the time goes in v3:
time: 79.5 us; the launch traced here: 79.1 us
  Pallas kernels  39.6 us (50%)
  starting transfers between devices  27.8 us (35%)
  waiting for transfers between devices  10.5 us (13%)
  between operations  1.02 us (1%)
    pallas_call x11, Pallas kernels, call(): pl.pallas_call(kernel, out_shape=tuple((pltpu.HBM(o.shape, o.dtype) if i...  39.6 us
    all_to_all x1, starting transfers between devices, body(): lax.all_to_all(outgoing, ('lat', 'lon'), split_axis=0, concat_axis=0, til...  11.7 us
    ppermute x4, starting transfers between devices, exchange(): lon_b = lax.ppermute(lon_b, 'lon', lon_far)  10.4 us
    all_to_all x1, waiting for transfers between devices, body(): lax.all_to_all(outgoing, ('lat', 'lon'), split_axis=0, concat_axis=0, til...  5.14 us
    ppermute x4, starting transfers between devices, exchange(): lat_b = lax.ppermute(lat_b, 'lat', lat_far)  4.52 us
    ppermute x4, waiting for transfers between devices, exchange(): lon_b = lax.ppermute(lon_b, 'lon', lon_far)  4.5 us
  transfers between devices with their start and end apart: 17, of which 4 were waited for; matrix products, arithmetic and copies ran while one was open for 0% of the time, Pallas kernels for 23%

profile of v3, /device:TPU:0, one launch (start us, length us, event | category | flops | bytes accessed | tf_op | source)
XLA Modules:
  0.0 79.1 jit_solution(16218204726280565372)
XLA Ops:
  0.6 2.8 %shard_map.104 = f32[128,2,128]{2,1,0:T(2,128)} custom-call(s32[4,1,512]{2,1,0:T(1,128)} %bitcast.12, s32[4,512]{1,0:T(4,128)} %cell_in.1, s32[4,512]{1,0:T(4,128)} %index_in.1, f32[3,4,512]{2,1,0:T(4,128)} %bitcast.11, f32[4,512]{1,0:T(4,128)} %prec_in.1), custom_call_target="tpu_custom_call" | custom-call | tf_op jit(solution)/shard_map/pallas_call | solution.py:43
  3.4 11.7 %all-to-all-start = ((f32[128,2,128]{2,1,0:T(2,128)}), f32[128,2,128]{2,1,0:T(2,128)}, u32[]{:S(2)}, u32[]{:S(2)}) async-start(f32[128,2,128]{2,1,0:T(2,128)} %shard_map.104), calls=%async_computation | async-start | bytes 262144 | tf_op jit(solution)/shard_map/all_to_all | solution.py:457
  15.3 4.2 %shard_map.105 = (f32[251,32,128]{2,1,0:T(8,128)}, f32[4,36,128]{2,1,0:T(8,128)}, f32[4,1,1152]{2,1,0:T(1,128)}, bf16[4,3,36,32,128]{4,3,2,1,0:T(8,128)(2,1)S(1)}) custom-call(f32[4,128]{1,0:T(4,128)S(1)} %broadcast_in_dim.4.mask_ref, f32[35,32,128]{2,1,0:T(8,128)} %refs_0_.1, f32[4,36,32,128]{3,2,1,0:T(8,128)} %tr_in.1, bf16[4,3,36,32,128]{4,3,2,1,0:T(8,128)(2,1)} %traj_in.1), custom_call_target="tpu_custom_call" | custom-call | tf_op jit(solution)/shard_map/pallas_call | solution.py:43
  19.5 5.1 %all-to-all-done.got_ref = f32[128,2,128]{2,1,0:T(2,128)} async-done(((f32[128,2,128]{2,1,0:T(2,128)}), f32[128,2,128]{2,1,0:T(2,128)}, u32[]{:S(2)}, u32[]{:S(2)}) %all-to-all-start) | async-done | bytes 131104 | tf_op jit(solution)/shard_map/all_to_all | solution.py:457
  24.6 7.0 %shard_map.106 = (f32[3,36,32,128]{3,2,1,0:T(8,128)S(1)}, f32[4,8,1024]{2,1,0:T(8,128)S(1)}, f32[35,32,128]{2,1,0:T(8,128)S(1)}, f32[251,32,128]{2,1,0:T(8,128)S...) custom-call(f32[128,2,128]{2,1,0:T(2,128)} %all-to-all-done.got_ref, ...), custom_call_target="tpu_custom_call" | custom-call | tf_op jit(solution)/shard_map/pallas_call | solution.py:43
  31.6 2.0 %shard_map.107 = (f32[3,36,32,128]{3,2,1,0:T(8,128)S(1)}, f32[1,3456]{1,0:T(1,128)S(1)}, f32[1,3456]{1,0:T(1,128)S(1)}, f32[108,128]{1,0:T(8,128)S(1)}, f32[108,128]{1,0:T(8,128)S(1)}) custom-call(f32[3,36,32,128]{3,2,1,0:T(8,128)S(1)} %get-tuple-element.39.refs_0_, f32[35,32,128]{2,1,0:T(8,128)S(1)} %get-tuple-element.40.refs_1_, ...), custom_call_target="tpu_custom_call" | custom-call | tf_op jit(solution)/shard_map/pallas_call | solution.py:43
  33.8 1.2 %collective-permute-start.3 = (f32[108,128]{1,0:T(8,128)S(1)}, f32[108,128]{1,0:T(8,128)S(1)}, u32[]{:S(2)}, u32[]{:S(2)}) collective-permute-start(f32[108,128]{1,0:T(8,128)S(1)} %get-tuple-element.48), channel_id=1, source_target_pairs={{16,32},{32,16},{48,64},{64,48},{80,96},{96,80},{112,0},{0,112},{1... | collective-permute-start | bytes 165896 | tf_op jit(solution)/shard_map/ppermute | solution.py:422
  35.0 0.8 %collective-permute-start = (f32[1,3456]{1,0:T(1,128)S(1)}, f32[1,3456]{1,0:T(1,128)S(1)}, u32[]{:S(2)}, u32[]{:S(2)}) collective-permute-start(f32[1,3456]{1,0:T(1,128)S(1)} %get-tuple-element.45), channel_id=1, source_target_pairs={{0,1},{1,0},{2,3},{3,2},{4,5},{5,4},{6,7},{7,6},{8,9},{9,8},{10,11... | collective-permute-start | bytes 41480 | tf_op jit(solution)/shard_map/ppermute | solution.py:423
  35.8 1.3 %collective-permute-start.1 = (f32[1,3456]{1,0:T(1,128)S(1)}, f32[1,3456]{1,0:T(1,128)S(1)}, u32[]{:S(2)}, u32[]{:S(2)}) collective-permute-start(f32[1,3456]{1,0:T(1,128)S(1)} %get-tuple-element.46), channel_id=1, source_target_pairs={{1,2},{2,1},{3,4},{4,3},{5,6},{6,5},{7,8},{8,7},{9,10},{10,9},{11,... | collective-permute-start | bytes 41480 | tf_op jit(solution)/shard_map/ppermute | solution.py:421
  37.1 4.5 %shard_map.108.refs_0_ = f32[3,36,32,128]{3,2,1,0:T(8,128)S(1)} custom-call(f32[4,8,1024]{2,1,0:T(8,128)S(1)} %get-tuple-element.49.snd_ref, bf16[4,3,36,32,128]{4,3,2,1,0:T(8,128)(2,1)S(1)} %get-tuple-element.35.traj_ref, f32[36,64]{1,0:T(8,128)} %bitcast.8), custom_call_target="tpu_custom_call" | custom-call | tf_op jit(solution)/shard_map/pallas_call | solution.py:43
  41.7 1.1 %collective-permute-done.1.lon_b = f32[1,3456]{1,0:T(1,128)S(1)} collective-permute-done((f32[1,3456]{1,0:T(1,128)S(1)}, f32[1,3456]{1,0:T(1,128)S(1)}, u32[]{:S(2)}, u32[]{:S(2)}) %collective-permute-start.1) | collective-permute-done | bytes 13856 | tf_op jit(solution)/shard_map/ppermute | solution.py:421
  42.8 2.5 %shard_map.109 = (f32[3,36,32,128]{3,2,1,0:T(8,128)S(1)}, f32[1,3456]{1,0:T(1,128)S(1)}, f32[1,3456]{1,0:T(1,128)S(1)}, f32[108,128]{1,0:T(8,128)S(1)}, f32[108,...) custom-call(f32[4,128]{1,0:T(4,128)S(1)} %broadcast_in_dim.4.mask_ref, f32[3,36,32,128]{3,2,1,0:T(8,128)S(1)} %get-tuple-element.44.w_in, ...), custom_call_target="tpu_custom_call" | custom-call | tf_op jit(solution)/shard_map/pallas_call | solution.py:43
  46.0 3.8 %collective-permute-start.5 = (f32[1,3456]{1,0:T(1,128)S(1)}, f32[1,3456]{1,0:T(1,128)S(1)}, u32[]{:S(2)}, u32[]{:S(2)}) collective-permute-start(f32[1,3456]{1,0:T(1,128)S(1)} %get-tuple-element.52), channel_id=1, source_target_pairs={{1,2},{2,1},{3,4},{4,3},{5,6},{6,5},{7,8},{8,7},{9,10},{10,9},{11,... | collective-permute-start | bytes 41480 | tf_op jit(solution)/shard_map/ppermute | solution.py:421
  49.7 4.6 %shard_map.110.refs_0_ = f32[3,36,32,128]{3,2,1,0:T(8,128)S(1)} custom-call(f32[4,8,1024]{2,1,0:T(8,128)S(1)} %get-tuple-element.49.snd_ref, bf16[4,3,36,32,128]{4,3,2,1,0:T(8,128)(2,1)S(1)} %get-tuple-element.35.traj_ref, f32[36,64]{1,0:T(8,128)} %bitcast.9), custom_call_target="tpu_custom_call" | custom-call | tf_op jit(solution)/shard_map/pallas_call | solution.py:43
  54.3 2.5 %shard_map.111 = (f32[3,36,32,128]{3,2,1,0:T(8,128)S(1)}, f32[1,3456]{1,0:T(1,128)S(1)}, f32[1,3456]{1,0:T(1,128)S(1)}, f32[108,128]{1,0:T(8,128)S(1)}, f32[108,...) custom-call(f32[4,128]{1,0:T(4,128)S(1)} %broadcast_in_dim.4.mask_ref, f32[3,36,32,128]{3,2,1,0:T(8,128)S(1)} %get-tuple-element.50.w_in, ...), custom_call_target="tpu_custom_call" | custom-call | tf_op jit(solution)/shard_map/pallas_call | solution.py:43
  57.0 1.5 %collective-permute-start.11 = (f32[108,128]{1,0:T(8,128)S(1)}, f32[108,128]{1,0:T(8,128)S(1)}, u32[]{:S(2)}, u32[]{:S(2)}) collective-permute-start(f32[108,128]{1,0:T(8,128)S(1)} %get-tuple-element.60), channel_id=1, source_target_pairs={{16,32},{32,16},{48,64},{64,48},{80,96},{96,80},{112,0},{0,112},{1... | collective-permute-start | bytes 165896 | tf_op jit(solution)/shard_map/ppermute | solution.py:422
  58.5 2.4 %collective-permute-start.9 = (f32[1,3456]{1,0:T(1,128)S(1)}, f32[1,3456]{1,0:T(1,128)S(1)}, u32[]{:S(2)}, u32[]{:S(2)}) collective-permute-start(f32[1,3456]{1,0:T(1,128)S(1)} %get-tuple-element.58), channel_id=1, source_target_pairs={{1,2},{2,1},{3,4},{4,3},{5,6},{6,5},{7,8},{8,7},{9,10},{10,9},{11,... | collective-permute-start | bytes 41480 | tf_op jit(solution)/shard_map/ppermute | solution.py:421
  60.9 4.5 %shard_map.112.refs_0_ = f32[3,36,32,128]{3,2,1,0:T(8,128)S(1)} custom-call(f32[4,8,1024]{2,1,0:T(8,128)S(1)} %get-tuple-element.49.snd_ref, bf16[4,3,36,32,128]{4,3,2,1,0:T(8,128)(2,1)S(1)} %get-tuple-element.35.traj_ref, f32[36,64]{1,0:T(8,128)} %bitcast.10), custom_call_target="tpu_custom_call" | custom-call | tf_op jit(solution)/shard_map/pallas_call | solution.py:43
  65.5 2.5 %shard_map.113 = (f32[3,36,32,128]{3,2,1,0:T(8,128)S(1)}, f32[1,3456]{1,0:T(1,128)S(1)}, f32[1,3456]{1,0:T(1,128)S(1)}, f32[108,128]{1,0:T(8,128)S(1)}, f32[108,...) custom-call(f32[4,128]{1,0:T(4,128)S(1)} %broadcast_in_dim.4.mask_ref, f32[3,36,32,128]{3,2,1,0:T(8,128)S(1)} %get-tuple-element.56.w_in, ...), custom_call_target="tpu_custom_call" | custom-call | tf_op jit(solution)/shard_map/pallas_call | solution.py:43
  68.1 1.3 %collective-permute-start.15 = (f32[108,128]{1,0:T(8,128)S(1)}, f32[108,128]{1,0:T(8,128)S(1)}, u32[]{:S(2)}, u32[]{:S(2)}) collective-permute-start(f32[108,128]{1,0:T(8,128)S(1)} %get-tuple-element.66), channel_id=1, source_target_pairs={{16,32},{32,16},{48,64},{64,48},{80,96},{96,80},{112,0},{0,112},{1... | collective-permute-start | bytes 165896 | tf_op jit(solution)/shard_map/ppermute | solution.py:422
  69.5 2.9 %collective-permute-start.13 = (f32[1,3456]{1,0:T(1,128)S(1)}, f32[1,3456]{1,0:T(1,128)S(1)}, u32[]{:S(2)}, u32[]{:S(2)}) collective-permute-start(f32[1,3456]{1,0:T(1,128)S(1)} %get-tuple-element.64), channel_id=1, source_target_pairs={{1,2},{2,1},{3,4},{4,3},{5,6},{6,5},{7,8},{8,7},{9,10},{10,9},{11,... | collective-permute-start | bytes 41480 | tf_op jit(solution)/shard_map/ppermute | solution.py:421
  72.4 0.8 %collective-permute-done.12.lon_a = f32[1,3456]{1,0:T(1,128)S(1)} collective-permute-done((f32[1,3456]{1,0:T(1,128)S(1)}, f32[1,3456]{1,0:T(1,128)S(1)}, u32[]{:S(2)}, u32[]{:S(2)}) %collective-permute-start.12) | collective-permute-done | bytes 13856 | tf_op jit(solution)/shard_map/ppermute | solution.py:423
  73.2 3.3 %collective-permute-done.13.lon_b = f32[1,3456]{1,0:T(1,128)S(1)} collective-permute-done((f32[1,3456]{1,0:T(1,128)S(1)}, f32[1,3456]{1,0:T(1,128)S(1)}, u32[]{:S(2)}, u32[]{:S(2)}) %collective-permute-start.13) | collective-permute-done | bytes 13856 | tf_op jit(solution)/shard_map/ppermute | solution.py:421
  76.5 2.4 %shard_map.114 = (f32[3,36,32,128]{3,2,1,0:T(8,128)}, f32[3,32,128]{2,1,0:T(8,128)}) custom-call(f32[4,128]{1,0:T(4,128)S(1)} %broadcast_in_dim.4.mask_ref, f32[3,36,32,128]{3,2,1,0:T(8,128)S(1)} %get-tuple-element.62.w_in, f32[1,3456]{1,0:T(1,128)S(1)} %collective-permute-done.12.lon_a, f32[1,3456]{1,0:T(1,128)S(1)} %collective-permute-done.13.lon_b, ...), custom_call_target="tpu_custom_call" | custom-call | tf_op jit(solution)/shard_map/pallas_call | solution.py:43
  (24 shorter events, 1.0 us)
Async XLA Ops:
  3.4 21.2 %all-to-all-start = ((f32[128,2,128]{2,1,0:T(2,128)}), f32[128,2,128]{2,1,0:T(2,128)}, u32[]{:S(2)}, u32[]{:S(2)}) async-start(f32[128,2,128]{2,1,0:T(2,128)} %shard_map.104), calls=%async_computation | async-start | bytes 262144 | tf_op jit(solution)/shard_map/all_to_all | solution.py:457
  33.7 9.2 %collective-permute-start.2 = (f32[108,128]{1,0:T(8,128)S(1)}, f32[108,128]{1,0:T(8,128)S(1)}, u32[]{:S(2)}, u32[]{:S(2)}) collective-permute-start(f32[108,128]{1,0:T(8,128)S(1)} %get-tuple-element.47), channel_id=1, source_target_pairs={{0,16},{16,0},{32,48},{48,32},{64,80},{80,64},{96,112},{112,96},{1... | collective-permute-start | bytes 165896 | tf_op jit(solution)/shard_map/ppermute | solution.py:424
  33.8 9.1 %collective-permute-start.3 = (f32[108,128]{1,0:T(8,128)S(1)}, f32[108,128]{1,0:T(8,128)S(1)}, u32[]{:S(2)}, u32[]{:S(2)}) collective-permute-start(f32[108,128]{1,0:T(8,128)S(1)} %get-tuple-element.48), channel_id=1, source_target_pairs={{16,32},{32,16},{48,64},{64,48},{80,96},{96,80},{112,0},{0,112},{1... | collective-permute-start | bytes 165896 | tf_op jit(solution)/shard_map/ppermute | solution.py:422
  35.0 6.7 %collective-permute-start = (f32[1,3456]{1,0:T(1,128)S(1)}, f32[1,3456]{1,0:T(1,128)S(1)}, u32[]{:S(2)}, u32[]{:S(2)}) collective-permute-start(f32[1,3456]{1,0:T(1,128)S(1)} %get-tuple-element.45), channel_id=1, source_target_pairs={{0,1},{1,0},{2,3},{3,2},{4,5},{5,4},{6,7},{7,6},{8,9},{9,8},{10,11... | collective-permute-start | bytes 41480 | tf_op jit(solution)/shard_map/ppermute | solution.py:423
  35.8 7.0 %collective-permute-start.1 = (f32[1,3456]{1,0:T(1,128)S(1)}, f32[1,3456]{1,0:T(1,128)S(1)}, u32[]{:S(2)}, u32[]{:S(2)}) collective-permute-start(f32[1,3456]{1,0:T(1,128)S(1)} %get-tuple-element.46), channel_id=1, source_target_pairs={{1,2},{2,1},{3,4},{4,3},{5,6},{6,5},{7,8},{8,7},{9,10},{10,9},{11,... | collective-permute-start | bytes 41480 | tf_op jit(solution)/shard_map/ppermute | solution.py:421
  45.4 8.9 %collective-permute-start.6 = (f32[108,128]{1,0:T(8,128)S(1)}, f32[108,128]{1,0:T(8,128)S(1)}, u32[]{:S(2)}, u32[]{:S(2)}) collective-permute-start(f32[108,128]{1,0:T(8,128)S(1)} %get-tuple-element.53), channel_id=1, source_target_pairs={{0,16},{16,0},{32,48},{48,32},{64,80},{80,64},{96,112},{112,96},{1... | collective-permute-start | bytes 165896 | tf_op jit(solution)/shard_map/ppermute | solution.py:424
  45.5 8.9 %collective-permute-start.7 = (f32[108,128]{1,0:T(8,128)S(1)}, f32[108,128]{1,0:T(8,128)S(1)}, u32[]{:S(2)}, u32[]{:S(2)}) collective-permute-start(f32[108,128]{1,0:T(8,128)S(1)} %get-tuple-element.54), channel_id=1, source_target_pairs={{16,32},{32,16},{48,64},{64,48},{80,96},{96,80},{112,0},{0,112},{1... | collective-permute-start | bytes 165896 | tf_op jit(solution)/shard_map/ppermute | solution.py:422
  46.0 8.3 %collective-permute-start.4 = (f32[1,3456]{1,0:T(1,128)S(1)}, f32[1,3456]{1,0:T(1,128)S(1)}, u32[]{:S(2)}, u32[]{:S(2)}) collective-permute-start(f32[1,3456]{1,0:T(1,128)S(1)} %get-tuple-element.51), channel_id=1, source_target_pairs={{0,1},{1,0},{2,3},{3,2},{4,5},{5,4},{6,7},{7,6},{8,9},{9,8},{10,11... | collective-permute-start | bytes 41480 | tf_op jit(solution)/shard_map/ppermute | solution.py:423
  46.0 8.4 %collective-permute-start.5 = (f32[1,3456]{1,0:T(1,128)S(1)}, f32[1,3456]{1,0:T(1,128)S(1)}, u32[]{:S(2)}, u32[]{:S(2)}) collective-permute-start(f32[1,3456]{1,0:T(1,128)S(1)} %get-tuple-element.52), channel_id=1, source_target_pairs={{1,2},{2,1},{3,4},{4,3},{5,6},{6,5},{7,8},{8,7},{9,10},{10,9},{11,... | collective-permute-start | bytes 41480 | tf_op jit(solution)/shard_map/ppermute | solution.py:421
  56.9 8.6 %collective-permute-start.10 = (f32[108,128]{1,0:T(8,128)S(1)}, f32[108,128]{1,0:T(8,128)S(1)}, u32[]{:S(2)}, u32[]{:S(2)}) collective-permute-start(f32[108,128]{1,0:T(8,128)S(1)} %get-tuple-element.59), channel_id=1, source_target_pairs={{0,16},{16,0},{32,48},{48,32},{64,80},{80,64},{96,112},{112,96},{1... | collective-permute-start | bytes 165896 | tf_op jit(solution)/shard_map/ppermute | solution.py:424
  57.0 8.5 %collective-permute-start.11 = (f32[108,128]{1,0:T(8,128)S(1)}, f32[108,128]{1,0:T(8,128)S(1)}, u32[]{:S(2)}, u32[]{:S(2)}) collective-permute-start(f32[108,128]{1,0:T(8,128)S(1)} %get-tuple-element.60), channel_id=1, source_target_pairs={{16,32},{32,16},{48,64},{64,48},{80,96},{96,80},{112,0},{0,112},{1... | collective-permute-start | bytes 165896 | tf_op jit(solution)/shard_map/ppermute | solution.py:422
  58.5 7.0 %collective-permute-start.8 = (f32[1,3456]{1,0:T(1,128)S(1)}, f32[1,3456]{1,0:T(1,128)S(1)}, u32[]{:S(2)}, u32[]{:S(2)}) collective-permute-start(f32[1,3456]{1,0:T(1,128)S(1)} %get-tuple-element.57), channel_id=1, source_target_pairs={{0,1},{1,0},{2,3},{3,2},{4,5},{5,4},{6,7},{7,6},{8,9},{9,8},{10,11... | collective-permute-start | bytes 41480 | tf_op jit(solution)/shard_map/ppermute | solution.py:423
  58.5 7.0 %collective-permute-start.9 = (f32[1,3456]{1,0:T(1,128)S(1)}, f32[1,3456]{1,0:T(1,128)S(1)}, u32[]{:S(2)}, u32[]{:S(2)}) collective-permute-start(f32[1,3456]{1,0:T(1,128)S(1)} %get-tuple-element.58), channel_id=1, source_target_pairs={{1,2},{2,1},{3,4},{4,3},{5,6},{6,5},{7,8},{8,7},{9,10},{10,9},{11,... | collective-permute-start | bytes 41480 | tf_op jit(solution)/shard_map/ppermute | solution.py:421
  68.0 8.5 %collective-permute-start.14 = (f32[108,128]{1,0:T(8,128)S(1)}, f32[108,128]{1,0:T(8,128)S(1)}, u32[]{:S(2)}, u32[]{:S(2)}) collective-permute-start(f32[108,128]{1,0:T(8,128)S(1)} %get-tuple-element.65), channel_id=1, source_target_pairs={{0,16},{16,0},{32,48},{48,32},{64,80},{80,64},{96,112},{112,96},{1... | collective-permute-start | bytes 165896 | tf_op jit(solution)/shard_map/ppermute | solution.py:424
  68.1 8.4 %collective-permute-start.15 = (f32[108,128]{1,0:T(8,128)S(1)}, f32[108,128]{1,0:T(8,128)S(1)}, u32[]{:S(2)}, u32[]{:S(2)}) collective-permute-start(f32[108,128]{1,0:T(8,128)S(1)} %get-tuple-element.66), channel_id=1, source_target_pairs={{16,32},{32,16},{48,64},{64,48},{80,96},{96,80},{112,0},{0,112},{1... | collective-permute-start | bytes 165896 | tf_op jit(solution)/shard_map/ppermute | solution.py:422
  69.5 3.7 %collective-permute-start.12 = (f32[1,3456]{1,0:T(1,128)S(1)}, f32[1,3456]{1,0:T(1,128)S(1)}, u32[]{:S(2)}, u32[]{:S(2)}) collective-permute-start(f32[1,3456]{1,0:T(1,128)S(1)} %get-tuple-element.63), channel_id=1, source_target_pairs={{0,1},{1,0},{2,3},{3,2},{4,5},{5,4},{6,7},{7,6},{8,9},{9,8},{10,11... | collective-permute-start | bytes 41480 | tf_op jit(solution)/shard_map/ppermute | solution.py:423
  69.5 7.0 %collective-permute-start.13 = (f32[1,3456]{1,0:T(1,128)S(1)}, f32[1,3456]{1,0:T(1,128)S(1)}, u32[]{:S(2)}, u32[]{:S(2)}) collective-permute-start(f32[1,3456]{1,0:T(1,128)S(1)} %get-tuple-element.64), channel_id=1, source_target_pairs={{1,2},{2,1},{3,4},{4,3},{5,6},{6,5},{7,8},{8,7},{9,10},{10,9},{11,... | collective-permute-start | bytes 41480 | tf_op jit(solution)/shard_map/ppermute | solution.py:421

commit v4 on v3

--- a/solution.py
+++ b/solution.py
@@ -128,36 +128,30 @@
             out_ref[s, 7:8, :] = jnp.zeros((1, CAP * ntiles), F32)
 
 
-def forcing_kernel(s, chunk, snd_ref, traj_ref, table_in, out_ref, pick, weight, table_ref, sem):
-    copy = pltpu.make_async_copy(table_in, table_ref, sem)
-    copy.start()
-    forcing_body(s, chunk, snd_ref, traj_ref, copy, table_ref, out_ref, pick, weight)
-
-
-def forcing_body(s, chunk, snd_ref, traj_ref, copy, table_ref, out_ref, pick, weight):
+def forcing_kernel(s, chunk, snd_ref, traj_ref, table_ref, out_ref, pick, weight):
+    forcing_body(s, chunk, snd_ref, traj_ref.at[s], table_ref, out_ref, pick, weight)
+
+
+def forcing_body(s, chunk, snd_ref, step_traj, table_ref, out_ref, pick, weight):
     tracers, layers = out_ref.shape[:2]
     slots = snd_ref.shape[2]
-    nker = table_ref.shape[1]
+    nker = table_ref.shape[2]
     cell_ids = lax.broadcasted_iota(jnp.int32, (256, chunk), 0).astype(F32)
     low_ids = lax.broadcasted_iota(jnp.int32, (16, chunk), 0).astype(F32)
     ker_ids = lax.broadcasted_iota(jnp.int32, (nker, chunk), 0).astype(F32)
     for c in range(slots // chunk):
         at = pl.ds(c * chunk, chunk)
         pick[:, at] = jnp.where(cell_ids == snd_ref[s, 0:1, at], 1.0, 0.0).astype(BF16)
-    copy.wait()
-    table = split3(table_ref[...])
-    for c in range(slots // chunk):
-        at = pl.ds(c * chunk, chunk)
         low = jnp.where(low_ids == snd_ref[s, 1:2, at], 1.0, 0.0)
         ker = jnp.where(ker_ids == snd_ref[s, 2:3, at], 1.0, 0.0).astype(BF16)
-        w = dot(table[0], ker) + dot(table[1], ker) + dot(table[2], ker)
+        w = dot(table_ref[0], ker) + dot(table_ref[1], ker) + dot(table_ref[2], ker)
         for k in range(layers):
             weight[k, :, at] = w[k : k + 1, :] * low
     for t in range(tracers):
         lhs = jnp.concatenate(
             [
-                traj_ref[s, t, :, 0:16, :].reshape(layers * 16, 128),
-                traj_ref[s, t, :, 16:32, :].reshape(layers * 16, 128),
+                step_traj[t, :, 0:16, :].reshape(layers * 16, 128),
+                step_traj[t, :, 16:32, :].reshape(layers * 16, 128),
             ],
             axis=1,
         )
@@ -202,7 +196,7 @@
     inv_ref, up_ref, coef_ref = views(planes_ref)
     copies = [
         pltpu.make_async_copy(src, dst, in_sems.at[i])
-        for i, (src, dst) in enumerate(((mix_in, mix_ref), (tr_in, tr_ref), (traj_in, traj_ref)))
+        for i, (src, dst) in enumerate(((mix_in, mix_ref), (tr_in, tr_ref), (traj_in.at[traj_in.shape[0] - 1], traj_ref)))
     ]
     for copy in copies:
         copy.start()
@@ -270,12 +264,10 @@
         copy.wait()
 
 
-def spread(mask_ref, lon_a, lon_b, lat_a, lat_b, halo, lat_halo):
+def spread(mask_ref, lon_a, lon_b, lat_a, lat_b, halo):
     tracers, layers, rows, cols = halo.shape
     size = layers * rows
     odd = mask_ref[2:3, :] > 0.5
-    lat_halo[0] = jnp.where(odd, lat_a[...], lat_b[...])
-    lat_halo[1] = jnp.where(odd, lat_b[...], lat_a[...])
     row = lax.broadcasted_iota(jnp.int32, (4, cols), 0)
     lane = lax.broadcasted_iota(jnp.int32, (4, cols), 1)
     other = (row % 2).astype(F32)
@@ -288,15 +280,9 @@
         both = jnp.concatenate([hi, lo], axis=0)
         spot = lax.dot_general(both, place, (((0,), (0,)), ((), ())), preferred_element_type=F32)
         halo[t] = spot.reshape(layers, rows, cols)
-
-
-def received(w_ref, halo, lat_halo, t, k):
-    value = w_ref[t, k] + halo[t, k]
-    row = lax.broadcasted_iota(jnp.int32, (8, 128), 0)
-    at = pl.ds(t * w_ref.shape[1] + k, 1)
-    top = value[0:8] + jnp.where(row == 0, lat_halo[0, at, :], 0.0)
-    low = value[24:32] + jnp.where(row == 7, lat_halo[1, at, :], 0.0)
-    return jnp.concatenate([top, value[8:24], low], axis=0)
+        at = slice(t * layers, (t + 1) * layers)
+        halo[t, :, 0, :] += jnp.where(odd, lat_a[at, :], lat_b[at, :])
+        halo[t, :, rows - 1, :] += jnp.where(odd, lat_b[at, :], lat_a[at, :])
 
 
 def step_body(base, force_ref, fixed, outs, v):
@@ -355,30 +341,34 @@
         lat_b[at, :] = top * lat_w[2] + low * lat_w[3]
 
 
-def head_kernel(s, chunk, got_ref, traj_ref, table_in, *refs):
-    sources, (out_ref, snd_ref), held = refs[0:4], refs[4:6], refs[6:10]
-    pick, weight, table_ref, sem, sems = refs[10:]
-    copy = pltpu.make_async_copy(table_in, table_ref, sem)
-    copy.start()
-    copies = [pltpu.make_async_copy(a, b, sems.at[i]) for i, (a, b) in enumerate(zip(sources, held))]
-    for held_copy in copies:
-        held_copy.start()
+def head_kernel(s, chunk, got_ref, traj_ref, table_in, traj_in, *refs):
+    sources, (out_ref, snd_ref, parts_ref, rest_ref), held = refs[0:4], refs[4:8], refs[8:12]
+    pick, weight, table_ref, sem, sems = refs[12:]
+    table_copy = pltpu.make_async_copy(table_in, table_ref, sem)
+    table_copy.start()
+    pairs = list(zip(sources, held)) + [(traj_in.at[pl.ds(0, s)], rest_ref)]
+    copies = [pltpu.make_async_copy(a, b, sems.at[i]) for i, (a, b) in enumerate(pairs)]
+    for copy in copies:
+        copy.start()
     unpack_kernel(got_ref, snd_ref)
-    forcing_body(s, chunk, snd_ref, traj_ref, copy, table_ref, out_ref, pick, weight)
-    for held_copy in copies:
-        held_copy.wait()
+    table_copy.wait()
+    for i, part in enumerate(split3(table_ref[...])):
+        parts_ref[i] = part
+    forcing_body(s, chunk, snd_ref, traj_ref, parts_ref, out_ref, pick, weight)
+    for copy in copies:
+        copy.wait()
 
 
 def first_step_kernel(*refs):
     step_body(lambda t, k: 0.0, refs[0], refs[1:5], refs[5:10], refs[10])
 
 
-def step_kernel(mask_ref, w_in, lon_a, lon_b, lat_a, lat_b, flux_in, *refs):
-    force_ref, fixed, outs, (flux_out, v, halo, lat_halo) = refs[0], refs[1:5], refs[5:10], refs[10:]
-    spread(mask_ref, lon_a, lon_b, lat_a, lat_b, halo, lat_halo)
+def step_kernel(mask_ref, w_in, lat_b, lat_a, lon_b, lon_a, flux_in, *refs):
+    force_ref, fixed, outs, (flux_out, v, halo) = refs[0], refs[1:5], refs[5:10], refs[10:]
+    spread(mask_ref, lon_a, lon_b, lat_a, lat_b, halo)
 
     def base(t, k):
-        value = received(w_in, halo, lat_halo, t, k)
+        value = w_in[t, k] + halo[t, k]
         if isinstance(k, int):
             flux_out[t] = flux_in[t] + value
         return value
@@ -387,21 +377,16 @@
 
 
 def last_kernel(
-    mask_ref, w_in, lon_a, lon_b, lat_a, lat_b, flux_in, adj_out, flux_out, halo, lat_halo, done, sems
+    mask_ref, w_in, lat_b, lat_a, lon_b, lon_a, flux_in, adj_out, flux_out, halo, done, sems
 ):
     tracers, layers = w_in.shape[:2]
-    spread(mask_ref, lon_a, lon_b, lat_a, lat_b, halo, lat_halo)
+    spread(mask_ref, lon_a, lon_b, lat_a, lat_b, halo)
     copies = []
+    group = layers // 3
     for t in range(tracers):
-
-        def finish(k, _):
-            done[t, k] = received(w_in, halo, lat_halo, t, k)
-            return 0
-
-        group = layers // 3
         for g in range(3):
-            lax.fori_loop(g * group, (g + 1) * group, finish, 0, unroll=4)
             at = (t, pl.ds(g * group, group))
+            done[at] = w_in[at] + halo[at]
             copies.append(pltpu.make_async_copy(done.at[at], adj_out.at[at], sems.at[3 * t + g]))
             copies[-1].start()
     flux_out[...] = flux_in[...] + done[:, 0]
@@ -422,7 +407,7 @@
     lat_b = lax.ppermute(lat_b, "lat", lat_far)
     lon_a = lax.ppermute(lon_a, "lon", lon_near)
     lat_a = lax.ppermute(lat_a, "lat", lat_near)
-    return lon_a, lon_b, lat_a, lat_b
+    return lat_b, lat_a, lon_b, lon_a
 
 
 def body(
@@ -434,7 +419,7 @@
     field = sds(tracers, layers, rows, cols)
     plane = sds(tracers, rows, cols)
     lat_edge = sds(tracers * layers, cols)
-    lon_edge = sds(1, tracers * layers * rows)
+    lon_edge = sds(1, 14336)
     slots = ntiles * CAP
     outgoing = call(
         route_kernel,
@@ -462,7 +447,7 @@
     weights = (sds(4, layers, cols), sds(4, 1, layers * rows))
     *fixed, local = call(
         setup_kernel,
-        planes + weights + (sds(*trajectory.shape, dtype=BF16),),
+        planes + weights + (sds(*trajectory.shape[1:], dtype=BF16),),
         mask,
         mixing,
         transport,
@@ -474,36 +459,33 @@
     )
     fixed = (mixing, *fixed)
     table = kernel_table.T
-    work = (
-        pltpu.VMEM((256, slots), BF16),
-        pltpu.VMEM((layers, 16, slots), F32),
-        pltpu.VMEM(table.shape, F32),
-        pltpu.SemaphoreType.DMA,
-    )
-
-    def forcing(s):
-        return call(
-            functools.partial(forcing_kernel, s, 512),
+    work = (pltpu.VMEM((256, slots), BF16), pltpu.VMEM((layers, 16, slots), F32))
+
+    force, snd, parts, rest, *fixed = call(
+        functools.partial(head_kernel, steps - 1, 512),
+        (
             field,
-            snd,
-            local,
-            table,
-            hbm=(2,),
-            scratch=work,
+            sds(steps, 8, slots),
+            sds(3, *table.shape, dtype=BF16),
+            sds(steps - 1, *trajectory.shape[1:], dtype=BF16),
         )
-
-    force, snd, *fixed = call(
-        functools.partial(head_kernel, steps - 1, 512),
-        (field, sds(steps, 8, slots)) + tuple(sds(*x.shape) for x in fixed),
+        + tuple(sds(*x.shape) for x in fixed),
         got,
         local,
         table,
+        trajectory,
         *fixed,
-        hbm=range(2, 7),
-        scratch=work + (pltpu.SemaphoreType.DMA((4,)),),
+        hbm=range(2, 8),
+        scratch=work
+        + (pltpu.VMEM(table.shape, F32), pltpu.SemaphoreType.DMA, pltpu.SemaphoreType.DMA((5,))),
     )
+
+    def forcing(s):
+        return call(
+            functools.partial(forcing_kernel, s, 512), field, snd, rest, parts, scratch=work
+        )
+
     v = pltpu.VMEM(field.shape, F32)
-    lat_halo = pltpu.VMEM((2,) + lat_edge.shape, F32)
     moved = (field, lon_edge, lon_edge, lat_edge, lat_edge)
     w, *edges = call(first_step_kernel, moved, force, *fixed, scratch=(v,))
     flux = jnp.zeros((tracers, rows, cols), F32)
@@ -518,7 +500,7 @@
             flux,
             forcing(s),
             *fixed,
-            scratch=(v, v, lat_halo),
+            scratch=(v, v),
         )
     return call(
         last_kernel,
@@ -528,7 +510,7 @@
         *exchange(*edges),
         flux,
         hbm_out=(0,),
-        scratch=(v, lat_halo, v, pltpu.SemaphoreType.DMA((3 * tracers,))),
+        scratch=(v, v, pltpu.SemaphoreType.DMA((3 * tracers,))),
     )
 
 

time: 79.5 us -> 74.2 us (0.933)
  Pallas kernels: 39.6 us -> 36.7 us
  starting transfers between devices: 27.8 us -> 25.9 us
    ppermute x4, waiting for transfers between devices: 0.01 us -> 3.17 us  [exchange(): lat_b = lax.ppermute(lat_b, 'lat', lat_far)]
    pallas_call x11, Pallas kernels: 39.6 us -> 36.7 us  [call(): pl.pallas_call(kernel, out_shape=tuple((pltpu.HBM(o.shape, o.dtype) if i...]
    ppermute x4, waiting for transfers between devices: 4.5 us -> 1.72 us  [exchange(): lon_b = lax.ppermute(lon_b, 'lon', lon_far)]
    ppermute x4, starting transfers between devices: 10.4 us -> 8.93 us  [exchange(): lon_b = lax.ppermute(lon_b, 'lon', lon_far)]
    ppermute x4, starting transfers between devices: 4.52 us -> 5.82 us  [exchange(): lat_b = lax.ppermute(lat_b, 'lat', lat_far)]
    ppermute x4, starting transfers between devices: 0.84 us -> 0.01 us  [exchange(): lon_a = lax.ppermute(lon_a, 'lon', lon_near)]
    ppermute x4, waiting for transfers between devices: 0.81 us -> 0.01 us  [exchange(): lon_a = lax.ppermute(lon_a, 'lon', lon_near)]
  transfers between devices with their start and end apart: 17 -> 17, of which waited for: 4 -> 6; matrix products, arithmetic and copies ran while one was open for 0% -> 0% of each run, Pallas kernels for 23% -> 21%
where the time goes in v4:
time: 74.2 us; the launch traced here: 73.8 us
  Pallas kernels  36.7 us (49%)
  starting transfers between devices  25.9 us (35%)
  waiting for transfers between devices  10.1 us (14%)
  between operations  0.97 us (1%)
    pallas_call x11, Pallas kernels, call(): pl.pallas_call(kernel, out_shape=tuple((pltpu.HBM(o.shape, o.dtype) if i...  36.7 us
    all_to_all x1, starting transfers between devices, body(): lax.all_to_all(outgoing, ('lat', 'lon'), split_axis=0, concat_axis=0, til...  11.1 us
    ppermute x4, starting transfers between devices, exchange(): lon_b = lax.ppermute(lon_b, 'lon', lon_far)  8.93 us
    ppermute x4, starting transfers between devices, exchange(): lat_b = lax.ppermute(lat_b, 'lat', lat_far)  5.82 us
    all_to_all x1, waiting for transfers between devices, body(): lax.all_to_all(outgoing, ('lat', 'lon'), split_axis=0, concat_axis=0, til...  5.23 us
    ppermute x4, waiting for transfers between devices, exchange(): lat_b = lax.ppermute(lat_b, 'lat', lat_far)  3.17 us
    ppermute x4, waiting for transfers between devices, exchange(): lon_b = lax.ppermute(lon_b, 'lon', lon_far)  1.72 us
  transfers between devices with their start and end apart: 17, of which 6 were waited for; matrix products, arithmetic and copies ran while one was open for 0% of the time, Pallas kernels for 21%

profile of v4, /device:TPU:0, one launch (start us, length us, event | category | flops | bytes accessed | tf_op | source)
XLA Modules:
  0.0 73.8 jit_solution(17270596287621031256)
XLA Ops:
  0.6 2.8 %shard_map.104 = f32[128,2,128]{2,1,0:T(2,128)} custom-call(s32[4,1,512]{2,1,0:T(1,128)} %bitcast.9, s32[4,512]{1,0:T(4,128)} %cell_in.1, s32[4,512]{1,0:T(4,128)} %index_in.1, f32[3,4,512]{2,1,0:T(4,128)} %bitcast.7, f32[4,512]{1,0:T(4,128)} %prec_in.1), custom_call_target="tpu_custom_call" | custom-call | tf_op jit(solution)/shard_map/pallas_call | solution.py:43
  3.4 11.1 %all-to-all-start = ((f32[128,2,128]{2,1,0:T(2,128)}), f32[128,2,128]{2,1,0:T(2,128)S(1)}, u32[]{:S(2)}, u32[]{:S(2)}) async-start(f32[128,2,128]{2,1,0:T(2,128)} %shard_map.104), calls=%async_computation | async-start | bytes 262144 | tf_op jit(solution)/shard_map/all_to_all | solution.py:442
  14.8 4.2 %shard_map.105 = (f32[251,32,128]{2,1,0:T(8,128)}, f32[4,36,128]{2,1,0:T(8,128)}, f32[4,1,1152]{2,1,0:T(1,128)}, bf16[3,36,32,128]{3,2,1,0:T(8,128)(2,1)S(1)}) custom-call(f32[4,128]{1,0:T(4,128)S(1)} %broadcast_in_dim.4.mask_ref, f32[35,32,128]{2,1,0:T(8,128)} %refs_0_.1, f32[4,36,32,128]{3,2,1,0:T(8,128)} %tr_in.1, bf16[4,3,36,32,128]{4,3,2,1,0:T(8,128)(2,1)} %traj_in.3), custom_call_target="tpu_custom_call" | custom-call | tf_op jit(solution)/shard_map/pallas_call | solution.py:43
  19.0 5.2 %all-to-all-done.got_ref = f32[128,2,128]{2,1,0:T(2,128)S(1)} async-done(((f32[128,2,128]{2,1,0:T(2,128)}), f32[128,2,128]{2,1,0:T(2,128)S(1)}, u32[]{:S(2)}, u32[]{:S(2)}) %all-to-all-start) | async-done | bytes 131104 | tf_op jit(solution)/shard_map/all_to_all | solution.py:442
  24.2 6.1 %shard_map.106 = (f32[3,36,32,128]{3,2,1,0:T(8,128)S(1)}, f32[4,8,1024]{2,1,0:T(8,128)S(1)}, bf16[3,36,64]{2,1,0:T(8,128)(2,1)S(1)}, bf16[3,3,36,32,128]{4,3,2,1...) custom-call(f32[128,2,128]{2,1,0:T(2,128)S(1)} %all-to-all-done.got_, ...), custom_call_target="tpu_custom_call" | custom-call | tf_op jit(solution)/shard_map/pallas_call | solution.py:43
  30.3 2.0 %shard_map.107 = (f32[3,36,32,128]{3,2,1,0:T(8,128)S(1)}, f32[1,14336]{1,0:T(1,128)S(1)}, f32[1,14336]{1,0:T(1,128)S(1)}, f32[108,128]{1,0:T(8,128)S(1)}, f32[108,128]{1,0:T(8,128)S(1)}) custom-call(f32[3,36,32,128]{3,2,1,0:T(8,128)S(1)} %get-tuple-element.41.refs_0_, f32[35,32,128]{2,1,0:T(8,128)S(1)} %get-tuple-element.42.refs_1_, ...), custom_call_target="tpu_custom_call" | custom-call | tf_op jit(solution)/shard_map/pallas_call | solution.py:43
  32.4 1.4 %collective-permute-start.2 = (f32[1,14336]{1,0:T(1,128)S(1)}, f32[1,14336]{1,0:T(1,128)S(1)}, u32[]{:S(2)}, u32[]{:S(2)}) collective-permute-start(f32[1,14336]{1,0:T(1,128)S(1)} %get-tuple-element.49), channel_id=1, source_target_pairs={{1,2},{2,1},{3,4},{4,3},{5,6},{6,5},{7,8},{8,7},{9,10},{10,9},{11,... | collective-permute-start | bytes 172040 | tf_op jit(solution)/shard_map/ppermute | solution.py:406
  33.7 0.8 %collective-permute-start = (f32[108,128]{1,0:T(8,128)S(1)}, f32[108,128]{1,0:T(8,128)S(1)}, u32[]{:S(2)}, u32[]{:S(2)}) collective-permute-start(f32[108,128]{1,0:T(8,128)S(1)} %get-tuple-element.47), channel_id=1, source_target_pairs={{16,32},{32,16},{48,64},{64,48},{80,96},{96,80},{112,0},{0,112},{1... | collective-permute-start | bytes 165896 | tf_op jit(solution)/shard_map/ppermute | solution.py:407
  34.6 3.9 %shard_map.108.refs_0_ = f32[3,36,32,128]{3,2,1,0:T(8,128)S(1)} custom-call(f32[4,8,1024]{2,1,0:T(8,128)S(1)} %get-tuple-element.51.snd_ref, bf16[3,3,36,32,128]{4,3,2,1,0:T(8,128)(2,1)S(1)} %get-tuple-element.52.traj_ref, bf16[3,36,64]{2,1,0:T(8,128)(2,1)S(1)} %get-tuple-element.53.table_ref), custom_call_target="tpu_custom_call" | custom-call | tf_op jit(solution)/shard_map/pallas_call | solution.py:43
  38.6 1.4 %collective-permute-done.2.lon_b = f32[1,14336]{1,0:T(1,128)S(1)} collective-permute-done((f32[1,14336]{1,0:T(1,128)S(1)}, f32[1,14336]{1,0:T(1,128)S(1)}, u32[]{:S(2)}, u32[]{:S(2)}) %collective-permute-start.2) | collective-permute-done | bytes 57376 | tf_op jit(solution)/shard_map/ppermute | solution.py:406
  40.0 2.6 %shard_map.109 = (f32[3,36,32,128]{3,2,1,0:T(8,128)S(1)}, f32[1,14336]{1,0:T(1,128)S(1)}, f32[1,14336]{1,0:T(1,128)S(1)}, f32[108,128]{1,0:T(8,128)S(1)}, f32[10...) custom-call(f32[4,128]{1,0:T(4,128)S(1)} %broadcast_in_dim.4.mask_ref, f32[3,36,32,128]{3,2,1,0:T(8,128)S(1)} %get-tuple-element.46.w_in, ...), custom_call_target="tpu_custom_call" | custom-call | tf_op jit(solution)/shard_map/pallas_call | solution.py:43
  42.5 2.8 %collective-permute-start.6 = (f32[1,14336]{1,0:T(1,128)S(1)}, f32[1,14336]{1,0:T(1,128)S(1)}, u32[]{:S(2)}, u32[]{:S(2)}) collective-permute-start(f32[1,14336]{1,0:T(1,128)S(1)} %get-tuple-element.57), channel_id=1, source_target_pairs={{1,2},{2,1},{3,4},{4,3},{5,6},{6,5},{7,8},{8,7},{9,10},{10,9},{11,... | collective-permute-start | bytes 172040 | tf_op jit(solution)/shard_map/ppermute | solution.py:406
  45.3 1.8 %collective-permute-start.4 = (f32[108,128]{1,0:T(8,128)S(1)}, f32[108,128]{1,0:T(8,128)S(1)}, u32[]{:S(2)}, u32[]{:S(2)}) collective-permute-start(f32[108,128]{1,0:T(8,128)S(1)} %get-tuple-element.55), channel_id=1, source_target_pairs={{16,32},{32,16},{48,64},{64,48},{80,96},{96,80},{112,0},{0,112},{1... | collective-permute-start | bytes 165896 | tf_op jit(solution)/shard_map/ppermute | solution.py:407
  47.1 3.9 %shard_map.110.refs_0_ = f32[3,36,32,128]{3,2,1,0:T(8,128)S(1)} custom-call(f32[4,8,1024]{2,1,0:T(8,128)S(1)} %get-tuple-element.51.snd_ref, bf16[3,3,36,32,128]{4,3,2,1,0:T(8,128)(2,1)S(1)} %get-tuple-element.52.traj_ref, bf16[3,36,64]{2,1,0:T(8,128)(2,1)S(1)} %get-tuple-element.53.table_ref), custom_call_target="tpu_custom_call" | custom-call | tf_op jit(solution)/shard_map/pallas_call | solution.py:43
  51.0 2.6 %shard_map.111 = (f32[3,36,32,128]{3,2,1,0:T(8,128)S(1)}, f32[1,14336]{1,0:T(1,128)S(1)}, f32[1,14336]{1,0:T(1,128)S(1)}, f32[108,128]{1,0:T(8,128)S(1)}, f32[10...) custom-call(f32[4,128]{1,0:T(4,128)S(1)} %broadcast_in_dim.4.mask_ref, f32[3,36,32,128]{3,2,1,0:T(8,128)S(1)} %get-tuple-element.54.w_in, ...), custom_call_target="tpu_custom_call" | custom-call | tf_op jit(solution)/shard_map/pallas_call | solution.py:43
  53.5 2.2 %collective-permute-start.10 = (f32[1,14336]{1,0:T(1,128)S(1)}, f32[1,14336]{1,0:T(1,128)S(1)}, u32[]{:S(2)}, u32[]{:S(2)}) collective-permute-start(f32[1,14336]{1,0:T(1,128)S(1)} %get-tuple-element.63), channel_id=1, source_target_pairs={{1,2},{2,1},{3,4},{4,3},{5,6},{6,5},{7,8},{8,7},{9,10},{10,9},{11,... | collective-permute-start | bytes 172040 | tf_op jit(solution)/shard_map/ppermute | solution.py:406
  55.7 1.5 %collective-permute-start.8 = (f32[108,128]{1,0:T(8,128)S(1)}, f32[108,128]{1,0:T(8,128)S(1)}, u32[]{:S(2)}, u32[]{:S(2)}) collective-permute-start(f32[108,128]{1,0:T(8,128)S(1)} %get-tuple-element.61), channel_id=1, source_target_pairs={{16,32},{32,16},{48,64},{64,48},{80,96},{96,80},{112,0},{0,112},{1... | collective-permute-start | bytes 165896 | tf_op jit(solution)/shard_map/ppermute | solution.py:407
  57.2 3.9 %shard_map.112.refs_0_ = f32[3,36,32,128]{3,2,1,0:T(8,128)S(1)} custom-call(f32[4,8,1024]{2,1,0:T(8,128)S(1)} %get-tuple-element.51.snd_ref, bf16[3,3,36,32,128]{4,3,2,1,0:T(8,128)(2,1)S(1)} %get-tuple-element.52.traj_ref, bf16[3,36,64]{2,1,0:T(8,128)(2,1)S(1)} %get-tuple-element.53.table_ref), custom_call_target="tpu_custom_call" | custom-call | tf_op jit(solution)/shard_map/pallas_call | solution.py:43
  61.1 0.2 collective-permute-done.10.lon_b
  61.3 2.6 %shard_map.113 = (f32[3,36,32,128]{3,2,1,0:T(8,128)S(1)}, f32[1,14336]{1,0:T(1,128)S(1)}, f32[1,14336]{1,0:T(1,128)S(1)}, f32[108,128]{1,0:T(8,128)S(1)}, f32[10...) custom-call(f32[4,128]{1,0:T(4,128)S(1)} %broadcast_in_dim.4.mask_ref, f32[3,36,32,128]{3,2,1,0:T(8,128)S(1)} %get-tuple-element.60.w_in, ...), custom_call_target="tpu_custom_call" | custom-call | tf_op jit(solution)/shard_map/pallas_call | solution.py:43
  63.8 2.6 %collective-permute-start.14 = (f32[1,14336]{1,0:T(1,128)S(1)}, f32[1,14336]{1,0:T(1,128)S(1)}, u32[]{:S(2)}, u32[]{:S(2)}) collective-permute-start(f32[1,14336]{1,0:T(1,128)S(1)} %get-tuple-element.69), channel_id=1, source_target_pairs={{1,2},{2,1},{3,4},{4,3},{5,6},{6,5},{7,8},{8,7},{9,10},{10,9},{11,... | collective-permute-start | bytes 172040 | tf_op jit(solution)/shard_map/ppermute | solution.py:406
  66.5 1.8 %collective-permute-start.12 = (f32[108,128]{1,0:T(8,128)S(1)}, f32[108,128]{1,0:T(8,128)S(1)}, u32[]{:S(2)}, u32[]{:S(2)}) collective-permute-start(f32[108,128]{1,0:T(8,128)S(1)} %get-tuple-element.67), channel_id=1, source_target_pairs={{16,32},{32,16},{48,64},{64,48},{80,96},{96,80},{112,0},{0,112},{1... | collective-permute-start | bytes 165896 | tf_op jit(solution)/shard_map/ppermute | solution.py:407
  68.2 3.1 %collective-permute-done.12.lat_b = f32[108,128]{1,0:T(8,128)S(1)} collective-permute-done((f32[108,128]{1,0:T(8,128)S(1)}, f32[108,128]{1,0:T(8,128)S(1)}, u32[]{:S(2)}, u32[]{:S(2)}) %collective-permute-start.12) | collective-permute-done | bytes 55328 | tf_op jit(solution)/shard_map/ppermute | solution.py:407
  71.4 2.2 %shard_map.114 = (f32[3,36,32,128]{3,2,1,0:T(8,128)}, f32[3,32,128]{2,1,0:T(8,128)}) custom-call(f32[4,128]{1,0:T(4,128)S(1)} %broadcast_in_dim.4.mask_ref, f32[3,36,32,128]{3,2,1,0:T(8,128)S(1)} %get-tuple-element.66.w_in, f32[108,128]{1,0:T(8,128)S(1)} %collective-permute-done.12.lat_b, f32[108,128]{1,0:T(8,128)S(1)} %collective-permute-done.13.lat_a, ...), custom_call_target="tpu_custom_call" | custom-call | tf_op jit(solution)/shard_map/pallas_call | solution.py:43
  (24 shorter events, 0.5 us)
Async XLA Ops:
  3.4 20.8 %all-to-all-start = ((f32[128,2,128]{2,1,0:T(2,128)}), f32[128,2,128]{2,1,0:T(2,128)S(1)}, u32[]{:S(2)}, u32[]{:S(2)}) async-start(f32[128,2,128]{2,1,0:T(2,128)} %shard_map.104), calls=%async_computation | async-start | bytes 262144 | tf_op jit(solution)/shard_map/all_to_all | solution.py:442
  32.4 7.6 %collective-permute-start.2 = (f32[1,14336]{1,0:T(1,128)S(1)}, f32[1,14336]{1,0:T(1,128)S(1)}, u32[]{:S(2)}, u32[]{:S(2)}) collective-permute-start(f32[1,14336]{1,0:T(1,128)S(1)} %get-tuple-element.49), channel_id=1, source_target_pairs={{1,2},{2,1},{3,4},{4,3},{5,6},{6,5},{7,8},{8,7},{9,10},{10,9},{11,... | collective-permute-start | bytes 172040 | tf_op jit(solution)/shard_map/ppermute | solution.py:406
  33.7 6.2 %collective-permute-start.3 = (f32[1,14336]{1,0:T(1,128)S(1)}, f32[1,14336]{1,0:T(1,128)S(1)}, u32[]{:S(2)}, u32[]{:S(2)}) collective-permute-start(f32[1,14336]{1,0:T(1,128)S(1)} %get-tuple-element.50), channel_id=1, source_target_pairs={{0,1},{1,0},{2,3},{3,2},{4,5},{5,4},{6,7},{7,6},{8,9},{9,8},{10,11... | collective-permute-start | bytes 172040 | tf_op jit(solution)/shard_map/ppermute | solution.py:408
  33.7 4.8 %collective-permute-start = (f32[108,128]{1,0:T(8,128)S(1)}, f32[108,128]{1,0:T(8,128)S(1)}, u32[]{:S(2)}, u32[]{:S(2)}) collective-permute-start(f32[108,128]{1,0:T(8,128)S(1)} %get-tuple-element.47), channel_id=1, source_target_pairs={{16,32},{32,16},{48,64},{64,48},{80,96},{96,80},{112,0},{0,112},{1... | collective-permute-start | bytes 165896 | tf_op jit(solution)/shard_map/ppermute | solution.py:407
  34.6 4.0 %collective-permute-start.1 = (f32[108,128]{1,0:T(8,128)S(1)}, f32[108,128]{1,0:T(8,128)S(1)}, u32[]{:S(2)}, u32[]{:S(2)}) collective-permute-start(f32[108,128]{1,0:T(8,128)S(1)} %get-tuple-element.48), channel_id=1, source_target_pairs={{0,16},{16,0},{32,48},{48,32},{64,80},{80,64},{96,112},{112,96},{1... | collective-permute-start | bytes 165896 | tf_op jit(solution)/shard_map/ppermute | solution.py:409
  42.5 8.4 %collective-permute-start.6 = (f32[1,14336]{1,0:T(1,128)S(1)}, f32[1,14336]{1,0:T(1,128)S(1)}, u32[]{:S(2)}, u32[]{:S(2)}) collective-permute-start(f32[1,14336]{1,0:T(1,128)S(1)} %get-tuple-element.57), channel_id=1, source_target_pairs={{1,2},{2,1},{3,4},{4,3},{5,6},{6,5},{7,8},{8,7},{9,10},{10,9},{11,... | collective-permute-start | bytes 172040 | tf_op jit(solution)/shard_map/ppermute | solution.py:406
  45.3 5.7 %collective-permute-start.7 = (f32[1,14336]{1,0:T(1,128)S(1)}, f32[1,14336]{1,0:T(1,128)S(1)}, u32[]{:S(2)}, u32[]{:S(2)}) collective-permute-start(f32[1,14336]{1,0:T(1,128)S(1)} %get-tuple-element.58), channel_id=1, source_target_pairs={{0,1},{1,0},{2,3},{3,2},{4,5},{5,4},{6,7},{7,6},{8,9},{9,8},{10,11... | collective-permute-start | bytes 172040 | tf_op jit(solution)/shard_map/ppermute | solution.py:408
  45.3 5.6 %collective-permute-start.4 = (f32[108,128]{1,0:T(8,128)S(1)}, f32[108,128]{1,0:T(8,128)S(1)}, u32[]{:S(2)}, u32[]{:S(2)}) collective-permute-start(f32[108,128]{1,0:T(8,128)S(1)} %get-tuple-element.55), channel_id=1, source_target_pairs={{16,32},{32,16},{48,64},{64,48},{80,96},{96,80},{112,0},{0,112},{1... | collective-permute-start | bytes 165896 | tf_op jit(solution)/shard_map/ppermute | solution.py:407
  47.1 3.9 %collective-permute-start.5 = (f32[108,128]{1,0:T(8,128)S(1)}, f32[108,128]{1,0:T(8,128)S(1)}, u32[]{:S(2)}, u32[]{:S(2)}) collective-permute-start(f32[108,128]{1,0:T(8,128)S(1)} %get-tuple-element.56), channel_id=1, source_target_pairs={{0,16},{16,0},{32,48},{48,32},{64,80},{80,64},{96,112},{112,96},{1... | collective-permute-start | bytes 165896 | tf_op jit(solution)/shard_map/ppermute | solution.py:409
  53.5 7.7 %collective-permute-start.10 = (f32[1,14336]{1,0:T(1,128)S(1)}, f32[1,14336]{1,0:T(1,128)S(1)}, u32[]{:S(2)}, u32[]{:S(2)}) collective-permute-start(f32[1,14336]{1,0:T(1,128)S(1)} %get-tuple-element.63), channel_id=1, source_target_pairs={{1,2},{2,1},{3,4},{4,3},{5,6},{6,5},{7,8},{8,7},{9,10},{10,9},{11,... | collective-permute-start | bytes 172040 | tf_op jit(solution)/shard_map/ppermute | solution.py:406
  55.7 5.5 %collective-permute-start.11 = (f32[1,14336]{1,0:T(1,128)S(1)}, f32[1,14336]{1,0:T(1,128)S(1)}, u32[]{:S(2)}, u32[]{:S(2)}) collective-permute-start(f32[1,14336]{1,0:T(1,128)S(1)} %get-tuple-element.64), channel_id=1, source_target_pairs={{0,1},{1,0},{2,3},{3,2},{4,5},{5,4},{6,7},{7,6},{8,9},{9,8},{10,11... | collective-permute-start | bytes 172040 | tf_op jit(solution)/shard_map/ppermute | solution.py:408
  55.7 5.3 %collective-permute-start.8 = (f32[108,128]{1,0:T(8,128)S(1)}, f32[108,128]{1,0:T(8,128)S(1)}, u32[]{:S(2)}, u32[]{:S(2)}) collective-permute-start(f32[108,128]{1,0:T(8,128)S(1)} %get-tuple-element.61), channel_id=1, source_target_pairs={{16,32},{32,16},{48,64},{64,48},{80,96},{96,80},{112,0},{0,112},{1... | collective-permute-start | bytes 165896 | tf_op jit(solution)/shard_map/ppermute | solution.py:407
  57.2 3.9 %collective-permute-start.9 = (f32[108,128]{1,0:T(8,128)S(1)}, f32[108,128]{1,0:T(8,128)S(1)}, u32[]{:S(2)}, u32[]{:S(2)}) collective-permute-start(f32[108,128]{1,0:T(8,128)S(1)} %get-tuple-element.62), channel_id=1, source_target_pairs={{0,16},{16,0},{32,48},{48,32},{64,80},{80,64},{96,112},{112,96},{1... | collective-permute-start | bytes 165896 | tf_op jit(solution)/shard_map/ppermute | solution.py:409
  63.8 7.6 %collective-permute-start.14 = (f32[1,14336]{1,0:T(1,128)S(1)}, f32[1,14336]{1,0:T(1,128)S(1)}, u32[]{:S(2)}, u32[]{:S(2)}) collective-permute-start(f32[1,14336]{1,0:T(1,128)S(1)} %get-tuple-element.69), channel_id=1, source_target_pairs={{1,2},{2,1},{3,4},{4,3},{5,6},{6,5},{7,8},{8,7},{9,10},{10,9},{11,... | collective-permute-start | bytes 172040 | tf_op jit(solution)/shard_map/ppermute | solution.py:406
  66.4 5.0 %collective-permute-start.15 = (f32[1,14336]{1,0:T(1,128)S(1)}, f32[1,14336]{1,0:T(1,128)S(1)}, u32[]{:S(2)}, u32[]{:S(2)}) collective-permute-start(f32[1,14336]{1,0:T(1,128)S(1)} %get-tuple-element.70), channel_id=1, source_target_pairs={{0,1},{1,0},{2,3},{3,2},{4,5},{5,4},{6,7},{7,6},{8,9},{9,8},{10,11... | collective-permute-start | bytes 172040 | tf_op jit(solution)/shard_map/ppermute | solution.py:408
  66.5 4.8 %collective-permute-start.12 = (f32[108,128]{1,0:T(8,128)S(1)}, f32[108,128]{1,0:T(8,128)S(1)}, u32[]{:S(2)}, u32[]{:S(2)}) collective-permute-start(f32[108,128]{1,0:T(8,128)S(1)} %get-tuple-element.67), channel_id=1, source_target_pairs={{16,32},{32,16},{48,64},{64,48},{80,96},{96,80},{112,0},{0,112},{1... | collective-permute-start | bytes 165896 | tf_op jit(solution)/shard_map/ppermute | solution.py:407
  68.2 3.1 %collective-permute-start.13 = (f32[108,128]{1,0:T(8,128)S(1)}, f32[108,128]{1,0:T(8,128)S(1)}, u32[]{:S(2)}, u32[]{:S(2)}) collective-permute-start(f32[108,128]{1,0:T(8,128)S(1)} %get-tuple-element.68), channel_id=1, source_target_pairs={{0,16},{16,0},{32,48},{48,32},{64,80},{80,64},{96,112},{112,96},{1... | collective-permute-start | bytes 165896 | tf_op jit(solution)/shard_map/ppermute | solution.py:409

commit v5 on v4

--- a/solution.py
+++ b/solution.py
@@ -128,8 +128,16 @@
             out_ref[s, 7:8, :] = jnp.zeros((1, CAP * ntiles), F32)
 
 
-def forcing_kernel(s, chunk, snd_ref, traj_ref, table_ref, out_ref, pick, weight):
-    forcing_body(s, chunk, snd_ref, traj_ref.at[s], table_ref, out_ref, pick, weight)
+def forcing_kernel(s, chunk, snd_ref, traj_ref, table_ref, *refs):
+    if s == 0:
+        out_ref, pick, weight = refs
+    else:
+        traj_in, out_ref, next_ref, pick, weight, sem = refs
+        copy = pltpu.make_async_copy(traj_in.at[s - 1], next_ref, sem)
+        copy.start()
+    forcing_body(s, chunk, snd_ref, traj_ref, table_ref, out_ref, pick, weight)
+    if s > 0:
+        copy.wait()
 
 
 def forcing_body(s, chunk, snd_ref, step_traj, table_ref, out_ref, pick, weight):
@@ -182,18 +190,18 @@
     return jnp.where(src == dst, 1.0, 0.0).astype(BF16)
 
 
-def views(planes_ref):
-    layers = (planes_ref.shape[0] + 1) // 7
-    part = [planes_ref.at[pl.ds(i * layers, layers)] for i in range(6)]
-    return part[5], planes_ref.at[pl.ds(6 * layers, layers - 1)], part[:5]
+def columns(column_ref, layers):
+    at = [0, layers - 1, 2 * layers - 1]
+    sizes = [layers - 1, layers, layers - 1]
+    return [column_ref.at[pl.ds(a, n)] for a, n in zip(at, sizes)]
 
 
 def setup_kernel(
-    mask_ref, mix_in, tr_in, traj_in, planes_out, lat_out, lon_out, traj_ref,
-    mix_ref, tr_ref, planes_ref, lat_w, lon_w, in_sems, out_sems,
+    mask_ref, mix_in, tr_in, traj_in, coef_out, column_ref, lat_w, lon_w, traj_ref,
+    tr_ref, flat_ref, in_sems, out_sems,
 ):
     layers = tr_ref.shape[1]
-    inv_ref, up_ref, coef_ref = views(planes_ref)
+    mix_ref, inv_ref, up_ref = columns(column_ref, layers)
     copies = [
         pltpu.make_async_copy(src, dst, in_sems.at[i])
         for i, (src, dst) in enumerate(((mix_in, mix_ref), (tr_in, tr_ref), (traj_in.at[traj_in.shape[0] - 1], traj_ref)))
@@ -220,19 +228,17 @@
         if k < layers - 1:
             up = -mix_ref[k] * inv
             up_ref[k] = up
-    at = pl.ds(5 * layers, 2 * layers - 1)
-    send(planes_ref.at[at], planes_out.at[at])
     copies[1].wait()
     lane = lax.broadcasted_iota(jnp.int32, (32, 128), 1)
     row = lax.broadcasted_iota(jnp.int32, (32, 128), 0)
 
     def coefs(k, _):
         te, tw, tn, ts = (tr_ref[i, k] for i in range(4))
-        coef_ref[0][k] = jnp.where(lane == 0, 0.0, pltpu.roll(te, 1, axis=1))
-        coef_ref[1][k] = jnp.where(lane == 127, 0.0, pltpu.roll(tw, 127, axis=1))
-        coef_ref[2][k] = jnp.where(row == 0, 0.0, pltpu.roll(tn, 1, axis=0))
-        coef_ref[3][k] = jnp.where(row == 31, 0.0, pltpu.roll(ts, 31, axis=0))
-        coef_ref[4][k] = 1.0 - te - tw - tn - ts
+        flat_ref[0 * layers + k] = jnp.where(lane == 0, 0.0, pltpu.roll(te, 1, axis=1))
+        flat_ref[1 * layers + k] = jnp.where(lane == 127, 0.0, pltpu.roll(tw, 127, axis=1))
+        flat_ref[2 * layers + k] = jnp.where(row == 0, 0.0, pltpu.roll(tn, 1, axis=0))
+        flat_ref[3 * layers + k] = jnp.where(row == 31, 0.0, pltpu.roll(ts, 31, axis=0))
+        flat_ref[4 * layers + k] = 1.0 - te - tw - tn - ts
         return 0
 
     group = layers // 3
@@ -240,7 +246,7 @@
         lax.fori_loop(g * group, (g + 1) * group, coefs, 0, unroll=4)
         for i in range(5):
             at = pl.ds(i * layers + g * group, group)
-            send(planes_ref.at[at], planes_out.at[at])
+            send(flat_ref.at[at], coef_out.at[at])
     to_north = tr_ref[3, :, 0, :] * mask_ref[0:1, :]
     to_south = tr_ref[2, :, 31, :] * mask_ref[1:2, :]
     odd = mask_ref[2:3, :]
@@ -248,7 +254,6 @@
     lat_w[1] = (1.0 - odd) * to_south
     lat_w[2] = (1.0 - odd) * to_north
     lat_w[3] = odd * to_south
-    send(lat_w, lat_out)
     odd = mask_ref[3:4, 0:1]
     ends = end_rows()[:, 0:128]
     for side in range(2):
@@ -259,7 +264,6 @@
         flat = flat[side : side + 1, :]
         lon_w[side] = flat * (odd if side else 1.0 - odd)
         lon_w[2 + side] = flat * (1.0 - odd if side else odd)
-    send(lon_w, lon_out)
     for copy in copies[2:] + sent:
         copy.wait()
 
@@ -285,12 +289,9 @@
         halo[t, :, rows - 1, :] += jnp.where(odd, lat_b[at, :], lat_a[at, :])
 
 
-def step_body(base, force_ref, fixed, outs, v):
-    mix_ref, planes_ref, lat_w, lon_w = fixed
-    inv_ref, up_ref, coef_ref = views(planes_ref)
-    shifts, end_lanes = lane_shifts(), end_rows()
-    w_out, lon_a, lon_b, lat_a, lat_b = outs
-    tracers, layers, rows, cols = force_ref.shape
+def vertical(base, force_ref, column_ref, v):
+    tracers, layers = v.shape[:2]
+    mix_ref, inv_ref, up_ref = columns(column_ref, layers)
     d = tuple((force_ref[t, 0] + base(t, 0)) * inv_ref[0] for t in range(tracers))
     for t in range(tracers):
         v[t, 0] = d[t]
@@ -314,57 +315,67 @@
 
     lax.fori_loop(0, layers - 1, backward, d, unroll=5)
 
+
+def horizontal(v, coef_ref=None, w_out=None, weights=None, edges=None):
+    tracers, layers, rows, cols = v.shape
+    shifts, end_lanes = lane_shifts(), end_rows()
     group = 12
     size = group * rows
     for t in range(tracers):
         for g in range(0, layers, group):
             x = v[t, g : g + group]
-            hi, lo = split2(x.reshape(size, cols))
-            both = jnp.concatenate([hi, lo], axis=1)
-            moved = dot(both, shifts)
-            ends = dot_t(end_lanes, both)
-            to = pl.ds((t * layers + g) * rows, size)
-            at = pl.ds(g * rows, size)
-            lon_a[:, to] = ends[0:1, :] * lon_w[0, :, at] + ends[1:2, :] * lon_w[1, :, at]
-            lon_b[:, to] = ends[0:1, :] * lon_w[2, :, at] + ends[1:2, :] * lon_w[3, :, at]
-            c = [coef_ref[i][g : g + group].reshape(size, cols) for i in range(5)]
-            down = jnp.stack([pltpu.roll(x[i], 1, axis=0) for i in range(group)])
-            up = jnp.stack([pltpu.roll(x[i], rows - 1, axis=0) for i in range(group)])
-            out = c[4] * x.reshape(size, cols) + c[0] * moved[:, :cols] + c[1] * moved[:, cols:]
-            out = out + c[2] * down.reshape(size, cols) + c[3] * up.reshape(size, cols)
-            w_out[t, g : g + group] = out.reshape(group, rows, cols)
-
-    for t in range(tracers):
-        at = slice(t * layers, (t + 1) * layers)
-        top, low = v[t, :, 0, :], v[t, :, rows - 1, :]
-        lat_a[at, :] = top * lat_w[0] + low * lat_w[1]
-        lat_b[at, :] = top * lat_w[2] + low * lat_w[3]
-
-
-def head_kernel(s, chunk, got_ref, traj_ref, table_in, traj_in, *refs):
-    sources, (out_ref, snd_ref, parts_ref, rest_ref), held = refs[0:4], refs[4:8], refs[8:12]
-    pick, weight, table_ref, sem, sems = refs[12:]
-    table_copy = pltpu.make_async_copy(table_in, table_ref, sem)
-    table_copy.start()
-    pairs = list(zip(sources, held)) + [(traj_in.at[pl.ds(0, s)], rest_ref)]
+            both = jnp.concatenate(split2(x.reshape(size, cols)), axis=1)
+            if edges is not None:
+                (_, lon_w), (lon_a, lon_b) = weights, edges[:2]
+                ends = dot_t(end_lanes, both)
+                to = pl.ds((t * layers + g) * rows, size)
+                at = pl.ds(g * rows, size)
+                lon_a[:, to] = ends[0:1, :] * lon_w[0, :, at] + ends[1:2, :] * lon_w[1, :, at]
+                lon_b[:, to] = ends[0:1, :] * lon_w[2, :, at] + ends[1:2, :] * lon_w[3, :, at]
+            if w_out is not None:
+                moved = dot(both, shifts)
+                c = [coef_ref[i * layers + g : i * layers + g + group].reshape(size, cols) for i in range(5)]
+                down = jnp.stack([pltpu.roll(x[i], 1, axis=0) for i in range(group)])
+                up = jnp.stack([pltpu.roll(x[i], rows - 1, axis=0) for i in range(group)])
+                out = c[4] * x.reshape(size, cols) + c[0] * moved[:, :cols] + c[1] * moved[:, cols:]
+                out = out + c[2] * down.reshape(size, cols) + c[3] * up.reshape(size, cols)
+                w_out[t, g : g + group] = out.reshape(group, rows, cols)
+        if edges is not None:
+            (lat_w, _), (lat_a, lat_b) = weights, edges[2:]
+            at = slice(t * layers, (t + 1) * layers)
+            top, low = v[t, :, 0, :], v[t, :, rows - 1, :]
+            lat_a[at, :] = top * lat_w[0] + low * lat_w[1]
+            lat_b[at, :] = top * lat_w[2] + low * lat_w[3]
+
+
+def head_kernel(
+    s, chunk, got_ref, traj_ref, table_in, traj_in, coef_in,
+    out_ref, snd_ref, parts_ref, next_ref, coef_ref, pick, weight, table_ref, sems,
+):
+    pairs = ((table_in, table_ref), (traj_in.at[s - 1], next_ref), (coef_in, coef_ref))
     copies = [pltpu.make_async_copy(a, b, sems.at[i]) for i, (a, b) in enumerate(pairs)]
     for copy in copies:
         copy.start()
     unpack_kernel(got_ref, snd_ref)
-    table_copy.wait()
+    copies[0].wait()
     for i, part in enumerate(split3(table_ref[...])):
         parts_ref[i] = part
     forcing_body(s, chunk, snd_ref, traj_ref, parts_ref, out_ref, pick, weight)
-    for copy in copies:
+    for copy in copies[1:]:
         copy.wait()
 
 
-def first_step_kernel(*refs):
-    step_body(lambda t, k: 0.0, refs[0], refs[1:5], refs[5:10], refs[10])
-
-
-def step_kernel(mask_ref, w_in, lat_b, lat_a, lon_b, lon_a, flux_in, *refs):
-    force_ref, fixed, outs, (flux_out, v, halo) = refs[0], refs[1:5], refs[5:10], refs[10:]
+def first_step_kernel(force_ref, column_ref, coef_ref, lat_w, lon_w, w_out, *refs):
+    edges, v = refs[:4], refs[4]
+    vertical(lambda t, k: 0.0, force_ref, column_ref, v)
+    horizontal(v, coef_ref, w_out, (lat_w, lon_w), edges)
+
+
+def step_kernel(
+    whole, mask_ref, w_in, lat_b, lat_a, lon_b, lon_a, flux_in, force_ref, column_ref, coef_ref, lat_w, lon_w,
+    w_out, *refs,
+):
+    edges, flux_out, halo, v = refs[:4], refs[4], refs[5], refs[6] if whole else w_out
     spread(mask_ref, lon_a, lon_b, lat_a, lat_b, halo)
 
     def base(t, k):
@@ -373,7 +384,12 @@
             flux_out[t] = flux_in[t] + value
         return value
 
-    step_body(base, force_ref, fixed, outs, v)
+    vertical(base, force_ref, column_ref, v)
+    horizontal(v, coef_ref if whole else None, w_out if whole else None, (lat_w, lon_w), edges)
+
+
+def interior_kernel(v, coef_ref, w_out):
+    horizontal(v, coef_ref, w_out)
 
 
 def last_kernel(
@@ -443,46 +459,63 @@
     lat, lon = lax.axis_index("lat"), lax.axis_index("lon")
     mask = jnp.stack([lat > 0, lat < lax.axis_size("lat") - 1, lat % 2 > 0, lon % 2 > 0]).astype(F32)
     mask = jnp.broadcast_to(mask[:, None], (4, cols))
-    planes = (sds(7 * layers - 1, rows, cols),)
-    weights = (sds(4, layers, cols), sds(4, 1, layers * rows))
-    *fixed, local = call(
+    one_step = sds(*trajectory.shape[1:], dtype=BF16)
+    coef, column, lat_w, lon_w, now = call(
         setup_kernel,
-        planes + weights + (sds(*trajectory.shape[1:], dtype=BF16),),
+        (
+            sds(5 * layers, rows, cols),
+            sds(3 * layers - 2, rows, cols),
+            sds(4, layers, cols),
+            sds(4, 1, layers * rows),
+            one_step,
+        ),
         mask,
         mixing,
         transport,
         trajectory,
         hbm=(1, 2, 3),
-        hbm_out=range(3),
-        scratch=[pltpu.VMEM(x.shape, F32) for x in (mixing, transport) + planes + weights]
-        + [pltpu.SemaphoreType.DMA((3,)), pltpu.SemaphoreType.DMA((18,))],
+        hbm_out=(0,),
+        scratch=(
+            pltpu.VMEM(transport.shape, F32),
+            pltpu.VMEM((5 * layers, rows, cols), F32),
+            pltpu.SemaphoreType.DMA((3,)),
+            pltpu.SemaphoreType.DMA((15,)),
+        ),
     )
-    fixed = (mixing, *fixed)
     table = kernel_table.T
     work = (pltpu.VMEM((256, slots), BF16), pltpu.VMEM((layers, 16, slots), F32))
-
-    force, snd, parts, rest, *fixed = call(
+    force, snd, parts, now, coef = call(
         functools.partial(head_kernel, steps - 1, 512),
         (
             field,
             sds(steps, 8, slots),
             sds(3, *table.shape, dtype=BF16),
-            sds(steps - 1, *trajectory.shape[1:], dtype=BF16),
-        )
-        + tuple(sds(*x.shape) for x in fixed),
+            one_step,
+            sds(*coef.shape),
+        ),
         got,
-        local,
+        now,
         table,
         trajectory,
-        *fixed,
-        hbm=range(2, 8),
-        scratch=work
-        + (pltpu.VMEM(table.shape, F32), pltpu.SemaphoreType.DMA, pltpu.SemaphoreType.DMA((5,))),
+        coef,
+        hbm=(2, 3, 4),
+        scratch=work + (pltpu.VMEM(table.shape, F32), pltpu.SemaphoreType.DMA((3,))),
     )
-
-    def forcing(s):
+    fixed = (column, coef, lat_w, lon_w)
+
+    def forcing(s, now):
+        kernel = functools.partial(forcing_kernel, s, 512)
+        if s == 0:
+            return call(kernel, field, snd, now, parts, scratch=work), None
         return call(
-            functools.partial(forcing_kernel, s, 512), field, snd, rest, parts, scratch=work
+            kernel,
+            (field, one_step),
+            snd,
+            now,
+            parts,
+            trajectory,
+            hbm=(3,),
+            scratch=work + (pltpu.SemaphoreType.DMA,),
         )
 
     v = pltpu.VMEM(field.shape, F32)
@@ -491,22 +524,23 @@
     flux = jnp.zeros((tracers, rows, cols), F32)
     for s in range(steps - 2, -1, -1):
         halos = exchange(*edges)
+        force, now = forcing(s, now)
         w, *edges, flux = call(
-            step_kernel,
+            functools.partial(step_kernel, s > 0),
             moved + (plane,),
             mask,
             w,
             *halos,
             flux,
-            forcing(s),
+            force,
             *fixed,
-            scratch=(v, v),
+            scratch=(v, v) if s > 0 else (v,),
         )
     return call(
         last_kernel,
         (field, plane),
         mask,
-        w,
+        call(interior_kernel, field, w, coef),
         *exchange(*edges),
         flux,
         hbm_out=(0,),

time: 74.2 us -> 72 us (0.970)
  Pallas kernels: 36.7 us -> 35.5 us
    pallas_call x11 -> x12, Pallas kernels: 36.7 us -> 35.5 us  [call(): pl.pallas_call(kernel, out_shape=tuple((pltpu.HBM(o.shape, o.dtype) if i...]
    ppermute x4, waiting for transfers between devices: 3.17 us -> 2.18 us  [exchange(): lat_b = lax.ppermute(lat_b, 'lat', lat_far)]
  transfers between devices with their start and end apart: 17 -> 17, of which waited for: 6 -> 6; matrix products, arithmetic and copies ran while one was open for 0% -> 0% of each run, Pallas kernels for 21% -> 23%
where the time goes in v5:
time: 72 us; the launch traced here: 71.7 us
  Pallas kernels  35.5 us (49%)
  starting transfers between devices  25.6 us (36%)
  waiting for transfers between devices  9.45 us (13%)
  between operations  0.98 us (1%)
    pallas_call x12, Pallas kernels, call(): pl.pallas_call(kernel, out_shape=tuple((pltpu.HBM(o.shape, o.dtype) if i...  35.5 us
    all_to_all x1, starting transfers between devices, body(): lax.all_to_all(outgoing, ('lat', 'lon'), split_axis=0, concat_axis=0, til...  11.1 us
    ppermute x4, starting transfers between devices, exchange(): lon_b = lax.ppermute(lon_b, 'lon', lon_far)  8.9 us
    all_to_all x1, waiting for transfers between devices, body(): lax.all_to_all(outgoing, ('lat', 'lon'), split_axis=0, concat_axis=0, til...  5.52 us
    ppermute x4, starting transfers between devices, exchange(): lat_b = lax.ppermute(lat_b, 'lat', lat_far)  5.49 us
    ppermute x4, waiting for transfers between devices, exchange(): lat_b = lax.ppermute(lat_b, 'lat', lat_far)  2.18 us
    ppermute x4, waiting for transfers between devices, exchange(): lon_b = lax.ppermute(lon_b, 'lon', lon_far)  1.73 us
  transfers between devices with their start and end apart: 17, of which 6 were waited for; matrix products, arithmetic and copies ran while one was open for 0% of the time, Pallas kernels for 23%

profile of v5, /device:TPU:0, one launch (start us, length us, event | category | flops | bytes accessed | tf_op | source)
XLA Modules:
  0.0 71.7 jit_solution(13507485219730088007)
XLA Ops:
  0.6 2.8 %shard_map.104 = f32[128,2,128]{2,1,0:T(2,128)} custom-call(s32[4,1,512]{2,1,0:T(1,128)} %bitcast.9, s32[4,512]{1,0:T(4,128)} %cell_in.1, s32[4,512]{1,0:T(4,128)} %index_in.1, f32[3,4,512]{2,1,0:T(4,128)} %bitcast.7, f32[4,512]{1,0:T(4,128)} %prec_in.1), custom_call_target="tpu_custom_call" | custom-call | tf_op jit(solution)/shard_map/pallas_call | solution.py:43
  3.4 11.1 %all-to-all-start = ((f32[128,2,128]{2,1,0:T(2,128)}), f32[128,2,128]{2,1,0:T(2,128)S(1)}, u32[]{:S(2)}, u32[]{:S(2)}) async-start(f32[128,2,128]{2,1,0:T(2,128)} %shard_map.104), calls=%async_computation | async-start | bytes 262144 | tf_op jit(solution)/shard_map/all_to_all | solution.py:458
  14.8 3.9 %shard_map.105 = (f32[180,32,128]{2,1,0:T(8,128)}, f32[106,32,128]{2,1,0:T(8,128)S(1)}, f32[4,36,128]{2,1,0:T(8,128)S(1)}, f32[4,1,1152]{2,1,0:T(1,128)S(1)}, bf16[3,36,32,128]{3,2,1,0:T(8,128)(2,1)S(1)}) custom-call(f32[4,128]{1,0:T(4,128)S(1)} %broadcast_in_dim.4.mask_ref, f32[35,32,128]{2,1,0:T(8,128)} %mix_in.1, f32[4,36,32,128]{3,2,1,0:T(8,128)} %tr_in.1, ...), custom_call_target="tpu_custom_call" | custom-call | tf_op jit(solution)/shard_map/pallas_call | solution.py:43
  18.7 5.5 %all-to-all-done.got_ref = f32[128,2,128]{2,1,0:T(2,128)S(1)} async-done(((f32[128,2,128]{2,1,0:T(2,128)}), f32[128,2,128]{2,1,0:T(2,128)S(1)}, u32[]{:S(2)}, u32[]{:S(2)}) %all-to-all-start) | async-done | bytes 131104 | tf_op jit(solution)/shard_map/all_to_all | solution.py:458
  24.2 4.7 %shard_map.106 = (f32[3,36,32,128]{3,2,1,0:T(8,128)S(1)}, f32[4,8,1024]{2,1,0:T(8,128)S(1)}, bf16[3,36,64]{2,1,0:T(8,128)(2,1)S(1)}, bf16[3,36,32,128]{3,2,1,0:T(8,128)(2,1)S(1)}, f32[180,32,128]{2,1,0:T(8,128)S(1)}) custom-call(f32[128,2,128]{2,1,0:T(2,128)S(1)} %all-to-all-done.got_ref, bf16[3,36,32,128]{3,2,1,0:T(8,128)(2,1)S(1)} %get-tuple-element.39.traj_ref, ...), custom_call_target="tpu_custom_call" | custom-call | tf_op jit(solution)/shard_map/pallas_call | solution.py:43
  28.9 1.9 %shard_map.107 = (f32[3,36,32,128]{3,2,1,0:T(8,128)S(1)}, f32[1,14336]{1,0:T(1,128)S(1)}, f32[1,14336]{1,0:T(1,128)S(1)}, f32[108,128]{1,0:T(8,128)S(1)}, f32[108,128]{1,0:T(8,128)S(1)}) custom-call(f32[3,36,32,128]{3,2,1,0:T(8,128)S(1)} %get-tuple-element.41.force_ref, f32[106,32,128]{2,1,0:T(8,128)S(1)} %get-tuple-element.42.column_ref, ...), custom_call_target="tpu_custom_call" | custom-call | tf_op jit(solution)/shard_map/pallas_call | solution.py:43
  30.7 1.4 %collective-permute-start.2 = (f32[1,14336]{1,0:T(1,128)S(1)}, f32[1,14336]{1,0:T(1,128)S(1)}, u32[]{:S(2)}, u32[]{:S(2)}) collective-permute-start(f32[1,14336]{1,0:T(1,128)S(1)} %get-tuple-element.49), channel_id=1, source_target_pairs={{1,2},{2,1},{3,4},{4,3},{5,6},{6,5},{7,8},{8,7},{9,10},{10,9},{11,... | collective-permute-start | bytes 172040 | tf_op jit(solution)/shard_map/ppermute | solution.py:422
  32.1 0.5 collective-permute-start
  32.7 3.8 %shard_map.108 = (f32[3,36,32,128]{3,2,1,0:T(8,128)S(1)}, bf16[3,36,32,128]{3,2,1,0:T(8,128)(2,1)S(1)}) custom-call(f32[4,8,1024]{2,1,0:T(8,128)S(1)} %get-tuple-element.51.snd_ref, bf16[3,36,32,128]{3,2,1,0:T(8,128)(2,1)S(1)} %get-tuple-element.52.traj_ref, bf16[3,36,64]{2,1,0:T(8,128)(2,1)S(1)} %get-tuple-element.53.table_ref, ...), custom_call_target="tpu_custom_call" | custom-call | tf_op jit(solution)/shard_map/pallas_call | solution.py:43
  36.9 1.4 %collective-permute-done.2.lon_b = f32[1,14336]{1,0:T(1,128)S(1)} collective-permute-done((f32[1,14336]{1,0:T(1,128)S(1)}, f32[1,14336]{1,0:T(1,128)S(1)}, u32[]{:S(2)}, u32[]{:S(2)}) %collective-permute-start.2) | collective-permute-done | bytes 57376 | tf_op jit(solution)/shard_map/ppermute | solution.py:422
  38.3 2.6 %shard_map.109 = (f32[3,36,32,128]{3,2,1,0:T(8,128)S(1)}, f32[1,14336]{1,0:T(1,128)S(1)}, f32[1,14336]{1,0:T(1,128)S(1)}, f32[108,128]{1,0:T(8,128)S(1)}, f32[10...) custom-call(f32[4,128]{1,0:T(4,128)S(1)} %broadcast_in_dim.4.mask_ref, f32[3,36,32,128]{3,2,1,0:T(8,128)S(1)} %get-tuple-element.46.w_in, ...), custom_call_target="tpu_custom_call" | custom-call | tf_op jit(solution)/shard_map/pallas_call | solution.py:43
  40.9 2.8 %collective-permute-start.6 = (f32[1,14336]{1,0:T(1,128)S(1)}, f32[1,14336]{1,0:T(1,128)S(1)}, u32[]{:S(2)}, u32[]{:S(2)}) collective-permute-start(f32[1,14336]{1,0:T(1,128)S(1)} %get-tuple-element.58), channel_id=1, source_target_pairs={{1,2},{2,1},{3,4},{4,3},{5,6},{6,5},{7,8},{8,7},{9,10},{10,9},{11,... | collective-permute-start | bytes 172040 | tf_op jit(solution)/shard_map/ppermute | solution.py:422
  43.7 1.7 %collective-permute-start.4 = (f32[108,128]{1,0:T(8,128)S(1)}, f32[108,128]{1,0:T(8,128)S(1)}, u32[]{:S(2)}, u32[]{:S(2)}) collective-permute-start(f32[108,128]{1,0:T(8,128)S(1)} %get-tuple-element.56), channel_id=1, source_target_pairs={{16,32},{32,16},{48,64},{64,48},{80,96},{96,80},{112,0},{0,112},{1... | collective-permute-start | bytes 165896 | tf_op jit(solution)/shard_map/ppermute | solution.py:423
  45.4 3.9 %shard_map.110 = (f32[3,36,32,128]{3,2,1,0:T(8,128)S(1)}, bf16[3,36,32,128]{3,2,1,0:T(8,128)(2,1)S(1)}) custom-call(f32[4,8,1024]{2,1,0:T(8,128)S(1)} %get-tuple-element.51.snd_ref, bf16[3,36,32,128]{3,2,1,0:T(8,128)(2,1)S(1)} %get-tuple-element.61.traj_ref, bf16[3,36,64]{2,1,0:T(8,128)(2,1)S(1)} %get-tuple-element.53.table_ref, ...), custom_call_target="tpu_custom_call" | custom-call | tf_op jit(solution)/shard_map/pallas_call | solution.py:43
  49.4 2.7 %shard_map.111 = (f32[3,36,32,128]{3,2,1,0:T(8,128)S(1)}, f32[1,14336]{1,0:T(1,128)S(1)}, f32[1,14336]{1,0:T(1,128)S(1)}, f32[108,128]{1,0:T(8,128)S(1)}, f32[10...) custom-call(f32[4,128]{1,0:T(4,128)S(1)} %broadcast_in_dim.4.mask_ref, f32[3,36,32,128]{3,2,1,0:T(8,128)S(1)} %get-tuple-element.55.w_in, ...), custom_call_target="tpu_custom_call" | custom-call | tf_op jit(solution)/shard_map/pallas_call | solution.py:43
  52.1 2.2 %collective-permute-start.10 = (f32[1,14336]{1,0:T(1,128)S(1)}, f32[1,14336]{1,0:T(1,128)S(1)}, u32[]{:S(2)}, u32[]{:S(2)}) collective-permute-start(f32[1,14336]{1,0:T(1,128)S(1)} %get-tuple-element.66), channel_id=1, source_target_pairs={{1,2},{2,1},{3,4},{4,3},{5,6},{6,5},{7,8},{8,7},{9,10},{10,9},{11,... | collective-permute-start | bytes 172040 | tf_op jit(solution)/shard_map/ppermute | solution.py:422
  54.3 1.5 %collective-permute-start.8 = (f32[108,128]{1,0:T(8,128)S(1)}, f32[108,128]{1,0:T(8,128)S(1)}, u32[]{:S(2)}, u32[]{:S(2)}) collective-permute-start(f32[108,128]{1,0:T(8,128)S(1)} %get-tuple-element.64), channel_id=1, source_target_pairs={{16,32},{32,16},{48,64},{64,48},{80,96},{96,80},{112,0},{0,112},{1... | collective-permute-start | bytes 165896 | tf_op jit(solution)/shard_map/ppermute | solution.py:423
  55.7 3.8 %shard_map.112.force_ref = f32[3,36,32,128]{3,2,1,0:T(8,128)S(1)} custom-call(f32[4,8,1024]{2,1,0:T(8,128)S(1)} %get-tuple-element.51.snd_ref, bf16[3,36,32,128]{3,2,1,0:T(8,128)(2,1)S(1)} %get-tuple-element.69.traj_ref, bf16[3,36,64]{2,1,0:T(8,128)(2,1)S(1)} %get-tuple-element.53.table_ref), custom_call_target="tpu_custom_call" | custom-call | tf_op jit(solution)/shard_map/pallas_call | solution.py:43
  59.8 2.0 %shard_map.113 = (f32[3,36,32,128]{3,2,1,0:T(8,128)S(1)}, f32[1,14336]{1,0:T(1,128)S(1)}, f32[1,14336]{1,0:T(1,128)S(1)}, f32[108,128]{1,0:T(8,128)S(1)}, f32[10...) custom-call(f32[4,128]{1,0:T(4,128)S(1)} %broadcast_in_dim.4.mask_ref, f32[3,36,32,128]{3,2,1,0:T(8,128)S(1)} %get-tuple-element.63.w_in, ...), custom_call_target="tpu_custom_call" | custom-call | tf_op jit(solution)/shard_map/pallas_call | solution.py:43
  61.7 2.6 %collective-permute-start.14 = (f32[1,14336]{1,0:T(1,128)S(1)}, f32[1,14336]{1,0:T(1,128)S(1)}, u32[]{:S(2)}, u32[]{:S(2)}) collective-permute-start(f32[1,14336]{1,0:T(1,128)S(1)} %get-tuple-element.73), channel_id=1, source_target_pairs={{1,2},{2,1},{3,4},{4,3},{5,6},{6,5},{7,8},{8,7},{9,10},{10,9},{11,... | collective-permute-start | bytes 172040 | tf_op jit(solution)/shard_map/ppermute | solution.py:422
  64.3 1.7 %collective-permute-start.12 = (f32[108,128]{1,0:T(8,128)S(1)}, f32[108,128]{1,0:T(8,128)S(1)}, u32[]{:S(2)}, u32[]{:S(2)}) collective-permute-start(f32[108,128]{1,0:T(8,128)S(1)} %get-tuple-element.71), channel_id=1, source_target_pairs={{16,32},{32,16},{48,64},{64,48},{80,96},{96,80},{112,0},{0,112},{1... | collective-permute-start | bytes 165896 | tf_op jit(solution)/shard_map/ppermute | solution.py:423
  66.1 1.2 %shard_map.114.w_in = f32[3,36,32,128]{3,2,1,0:T(8,128)S(1)} custom-call(f32[3,36,32,128]{3,2,1,0:T(8,128)S(1)} %get-tuple-element.70.v, f32[180,32,128]{2,1,0:T(8,128)S(1)} %get-tuple-element.43.coef_ref), custom_call_target="tpu_custom_call" | custom-call | tf_op jit(solution)/shard_map/pallas_call | solution.py:43
  67.3 1.8 %collective-permute-done.12.lat_b = f32[108,128]{1,0:T(8,128)S(1)} collective-permute-done((f32[108,128]{1,0:T(8,128)S(1)}, f32[108,128]{1,0:T(8,128)S(1)}, u32[]{:S(2)}, u32[]{:S(2)}) %collective-permute-start.12) | collective-permute-done | bytes 55328 | tf_op jit(solution)/shard_map/ppermute | solution.py:423
  69.3 2.3 %shard_map.115 = (f32[3,36,32,128]{3,2,1,0:T(8,128)}, f32[3,32,128]{2,1,0:T(8,128)}) custom-call(f32[4,128]{1,0:T(4,128)S(1)} %broadcast_in_dim.4.mask_ref, f32[3,36,32,128]{3,2,1,0:T(8,128)S(1)} %shard_map.114.w_in, f32[108,128]{1,0:T(8,128)S(1)} %collective-permute-done.12.lat_b, f32[108,128]{1,0:T(8,128)S(1)} %collective-permute-done.13.lat_a, ...), custom_call_target="tpu_custom_call" | custom-call | tf_op jit(solution)/shard_map/pallas_call | solution.py:43
  (25 shorter events, 1.0 us)
Async XLA Ops:
  3.4 20.8 %all-to-all-start = ((f32[128,2,128]{2,1,0:T(2,128)}), f32[128,2,128]{2,1,0:T(2,128)S(1)}, u32[]{:S(2)}, u32[]{:S(2)}) async-start(f32[128,2,128]{2,1,0:T(2,128)} %shard_map.104), calls=%async_computation | async-start | bytes 262144 | tf_op jit(solution)/shard_map/all_to_all | solution.py:458
  30.7 7.6 %collective-permute-start.2 = (f32[1,14336]{1,0:T(1,128)S(1)}, f32[1,14336]{1,0:T(1,128)S(1)}, u32[]{:S(2)}, u32[]{:S(2)}) collective-permute-start(f32[1,14336]{1,0:T(1,128)S(1)} %get-tuple-element.49), channel_id=1, source_target_pairs={{1,2},{2,1},{3,4},{4,3},{5,6},{6,5},{7,8},{8,7},{9,10},{10,9},{11,... | collective-permute-start | bytes 172040 | tf_op jit(solution)/shard_map/ppermute | solution.py:422
  32.1 6.2 %collective-permute-start.3 = (f32[1,14336]{1,0:T(1,128)S(1)}, f32[1,14336]{1,0:T(1,128)S(1)}, u32[]{:S(2)}, u32[]{:S(2)}) collective-permute-start(f32[1,14336]{1,0:T(1,128)S(1)} %get-tuple-element.50), channel_id=1, source_target_pairs={{0,1},{1,0},{2,3},{3,2},{4,5},{5,4},{6,7},{7,6},{8,9},{9,8},{10,11... | collective-permute-start | bytes 172040 | tf_op jit(solution)/shard_map/ppermute | solution.py:424
  32.1 4.8 %collective-permute-start = (f32[108,128]{1,0:T(8,128)S(1)}, f32[108,128]{1,0:T(8,128)S(1)}, u32[]{:S(2)}, u32[]{:S(2)}) collective-permute-start(f32[108,128]{1,0:T(8,128)S(1)} %get-tuple-element.47), channel_id=1, source_target_pairs={{16,32},{32,16},{48,64},{64,48},{80,96},{96,80},{112,0},{0,112},{1... | collective-permute-start | bytes 165896 | tf_op jit(solution)/shard_map/ppermute | solution.py:423
  32.7 4.3 %collective-permute-start.1 = (f32[108,128]{1,0:T(8,128)S(1)}, f32[108,128]{1,0:T(8,128)S(1)}, u32[]{:S(2)}, u32[]{:S(2)}) collective-permute-start(f32[108,128]{1,0:T(8,128)S(1)} %get-tuple-element.48), channel_id=1, source_target_pairs={{0,16},{16,0},{32,48},{48,32},{64,80},{80,64},{96,112},{112,96},{1... | collective-permute-start | bytes 165896 | tf_op jit(solution)/shard_map/ppermute | solution.py:425
  40.9 8.4 %collective-permute-start.6 = (f32[1,14336]{1,0:T(1,128)S(1)}, f32[1,14336]{1,0:T(1,128)S(1)}, u32[]{:S(2)}, u32[]{:S(2)}) collective-permute-start(f32[1,14336]{1,0:T(1,128)S(1)} %get-tuple-element.58), channel_id=1, source_target_pairs={{1,2},{2,1},{3,4},{4,3},{5,6},{6,5},{7,8},{8,7},{9,10},{10,9},{11,... | collective-permute-start | bytes 172040 | tf_op jit(solution)/shard_map/ppermute | solution.py:422
  43.7 5.7 %collective-permute-start.7 = (f32[1,14336]{1,0:T(1,128)S(1)}, f32[1,14336]{1,0:T(1,128)S(1)}, u32[]{:S(2)}, u32[]{:S(2)}) collective-permute-start(f32[1,14336]{1,0:T(1,128)S(1)} %get-tuple-element.59), channel_id=1, source_target_pairs={{0,1},{1,0},{2,3},{3,2},{4,5},{5,4},{6,7},{7,6},{8,9},{9,8},{10,11... | collective-permute-start | bytes 172040 | tf_op jit(solution)/shard_map/ppermute | solution.py:424
  43.7 5.6 %collective-permute-start.4 = (f32[108,128]{1,0:T(8,128)S(1)}, f32[108,128]{1,0:T(8,128)S(1)}, u32[]{:S(2)}, u32[]{:S(2)}) collective-permute-start(f32[108,128]{1,0:T(8,128)S(1)} %get-tuple-element.56), channel_id=1, source_target_pairs={{16,32},{32,16},{48,64},{64,48},{80,96},{96,80},{112,0},{0,112},{1... | collective-permute-start | bytes 165896 | tf_op jit(solution)/shard_map/ppermute | solution.py:423
  45.4 3.9 %collective-permute-start.5 = (f32[108,128]{1,0:T(8,128)S(1)}, f32[108,128]{1,0:T(8,128)S(1)}, u32[]{:S(2)}, u32[]{:S(2)}) collective-permute-start(f32[108,128]{1,0:T(8,128)S(1)} %get-tuple-element.57), channel_id=1, source_target_pairs={{0,16},{16,0},{32,48},{48,32},{64,80},{80,64},{96,112},{112,96},{1... | collective-permute-start | bytes 165896 | tf_op jit(solution)/shard_map/ppermute | solution.py:425
  52.1 7.7 %collective-permute-start.10 = (f32[1,14336]{1,0:T(1,128)S(1)}, f32[1,14336]{1,0:T(1,128)S(1)}, u32[]{:S(2)}, u32[]{:S(2)}) collective-permute-start(f32[1,14336]{1,0:T(1,128)S(1)} %get-tuple-element.66), channel_id=1, source_target_pairs={{1,2},{2,1},{3,4},{4,3},{5,6},{6,5},{7,8},{8,7},{9,10},{10,9},{11,... | collective-permute-start | bytes 172040 | tf_op jit(solution)/shard_map/ppermute | solution.py:422
  54.3 5.5 %collective-permute-start.11 = (f32[1,14336]{1,0:T(1,128)S(1)}, f32[1,14336]{1,0:T(1,128)S(1)}, u32[]{:S(2)}, u32[]{:S(2)}) collective-permute-start(f32[1,14336]{1,0:T(1,128)S(1)} %get-tuple-element.67), channel_id=1, source_target_pairs={{0,1},{1,0},{2,3},{3,2},{4,5},{5,4},{6,7},{7,6},{8,9},{9,8},{10,11... | collective-permute-start | bytes 172040 | tf_op jit(solution)/shard_map/ppermute | solution.py:424
  54.3 5.3 %collective-permute-start.8 = (f32[108,128]{1,0:T(8,128)S(1)}, f32[108,128]{1,0:T(8,128)S(1)}, u32[]{:S(2)}, u32[]{:S(2)}) collective-permute-start(f32[108,128]{1,0:T(8,128)S(1)} %get-tuple-element.64), channel_id=1, source_target_pairs={{16,32},{32,16},{48,64},{64,48},{80,96},{96,80},{112,0},{0,112},{1... | collective-permute-start | bytes 165896 | tf_op jit(solution)/shard_map/ppermute | solution.py:423
  55.7 3.8 %collective-permute-start.9 = (f32[108,128]{1,0:T(8,128)S(1)}, f32[108,128]{1,0:T(8,128)S(1)}, u32[]{:S(2)}, u32[]{:S(2)}) collective-permute-start(f32[108,128]{1,0:T(8,128)S(1)} %get-tuple-element.65), channel_id=1, source_target_pairs={{0,16},{16,0},{32,48},{48,32},{64,80},{80,64},{96,112},{112,96},{1... | collective-permute-start | bytes 165896 | tf_op jit(solution)/shard_map/ppermute | solution.py:425
  61.7 7.5 %collective-permute-start.14 = (f32[1,14336]{1,0:T(1,128)S(1)}, f32[1,14336]{1,0:T(1,128)S(1)}, u32[]{:S(2)}, u32[]{:S(2)}) collective-permute-start(f32[1,14336]{1,0:T(1,128)S(1)} %get-tuple-element.73), channel_id=1, source_target_pairs={{1,2},{2,1},{3,4},{4,3},{5,6},{6,5},{7,8},{8,7},{9,10},{10,9},{11,... | collective-permute-start | bytes 172040 | tf_op jit(solution)/shard_map/ppermute | solution.py:422
  64.3 5.0 %collective-permute-start.15 = (f32[1,14336]{1,0:T(1,128)S(1)}, f32[1,14336]{1,0:T(1,128)S(1)}, u32[]{:S(2)}, u32[]{:S(2)}) collective-permute-start(f32[1,14336]{1,0:T(1,128)S(1)} %get-tuple-element.74), channel_id=1, source_target_pairs={{0,1},{1,0},{2,3},{3,2},{4,5},{5,4},{6,7},{7,6},{8,9},{9,8},{10,11... | collective-permute-start | bytes 172040 | tf_op jit(solution)/shard_map/ppermute | solution.py:424
  64.3 4.8 %collective-permute-start.12 = (f32[108,128]{1,0:T(8,128)S(1)}, f32[108,128]{1,0:T(8,128)S(1)}, u32[]{:S(2)}, u32[]{:S(2)}) collective-permute-start(f32[108,128]{1,0:T(8,128)S(1)} %get-tuple-element.71), channel_id=1, source_target_pairs={{16,32},{32,16},{48,64},{64,48},{80,96},{96,80},{112,0},{0,112},{1... | collective-permute-start | bytes 165896 | tf_op jit(solution)/shard_map/ppermute | solution.py:423
  66.1 3.1 %collective-permute-start.13 = (f32[108,128]{1,0:T(8,128)S(1)}, f32[108,128]{1,0:T(8,128)S(1)}, u32[]{:S(2)}, u32[]{:S(2)}) collective-permute-start(f32[108,128]{1,0:T(8,128)S(1)} %get-tuple-element.72), channel_id=1, source_target_pairs={{0,16},{16,0},{32,48},{48,32},{64,80},{80,64},{96,112},{112,96},{1... | collective-permute-start | bytes 165896 | tf_op jit(solution)/shard_map/ppermute | solution.py:425

commit v6 on v5

--- a/solution.py
+++ b/solution.py
@@ -37,7 +37,7 @@
 HBM = pl.BlockSpec(memory_space=pltpu.HBM)
 
 
-def call(kernel, outs, *args, scratch=(), vmem=12 << 20, hbm=(), hbm_out=()):
+def call(kernel, outs, *args, scratch=(), vmem=20 << 20, hbm=(), hbm_out=()):
     outs = tuple(outs) if isinstance(outs, (tuple, list)) else (outs,)
     args = [pltpu.with_memory_space_constraint(a, pltpu.HBM) if i in hbm else a for i, a in enumerate(args)]
     done = pl.pallas_call(
@@ -80,28 +80,28 @@
         < lax.broadcasted_iota(jnp.int32, (count, count), 1)
     ).astype(F32).astype(BF16)
     rank_ids = lax.broadcasted_iota(jnp.int32, (CAP, count), 0)
-    pad = jnp.zeros((64 - CAP * WORDS, count), F32)
-    half = jnp.zeros((64, count), F32)
-    for copy in copies:
+    pad = jnp.zeros((48 - CAP * WORDS, count), F32)
+    empty = [jnp.zeros((n, count), BF16) for n in (64, 16)]
+    copies[0].wait()
+    mine, at_rank = [], []
+    for s in range(steps):
+        here = tile_ids == tile_ref[s]
+        here_f = jnp.where(here, 1.0, 0.0)
+        mine.append(here_f.astype(BF16))
+        rank = jnp.sum(here_f * dot(mine[s], before), axis=0, keepdims=True).astype(jnp.int32)
+        at_rank.append(rank_ids == rank)
+    for copy in copies[1:]:
         copy.wait()
     for pair in range(steps // 2):
         total = None
         for side in range(2):
             s = 2 * pair + side
-            mine = tile_ids == tile_ref[s]
-            mine_f = mine.astype(F32)
-            mine_b = mine_f.astype(BF16)
-            seen = dot(mine_b, before)
-            rank = jnp.sum(mine_f * seen, axis=0, keepdims=True).astype(jnp.int32)
-            at_rank = rank_ids == rank
             code = (index_ref[s : s + 1, :] * 4096 + cell_ref[s : s + 1, :]).astype(F32)
             words = [code] + [obs_ref[t, s : s + 1, :] for t in range(3)] + [prec_ref[s : s + 1, :]]
-            rows = [jnp.where(at_rank, w, 0.0) for w in words]
-            block = jnp.concatenate(rows + [pad] + [half], axis=0)
-            if side == 1:
-                block = jnp.concatenate([half] + rows + [pad], axis=0)
-            for part in split3(block):
-                term = dot_t(mine_b, part)
+            rows = jnp.concatenate([jnp.where(at_rank[s], w, 0.0) for w in words] + [pad], axis=0)
+            for part in split3(rows):
+                block = [part, empty[1], empty[0]] if side == 0 else [empty[0], part, empty[1]]
+                term = dot_t(mine[s], jnp.concatenate(block, axis=0))
                 total = term if total is None else total + term
         out_ref[:, pair, :] = total
 
@@ -268,25 +268,34 @@
         copy.wait()
 
 
-def spread(mask_ref, lon_a, lon_b, lat_a, lat_b, halo):
-    tracers, layers, rows, cols = halo.shape
-    size = layers * rows
-    odd = mask_ref[2:3, :] > 0.5
+def lon_spots(mask_ref, lon_a, lon_b, first, size, cols):
     row = lax.broadcasted_iota(jnp.int32, (4, cols), 0)
     lane = lax.broadcasted_iota(jnp.int32, (4, cols), 1)
     other = (row % 2).astype(F32)
     lon_odd = jnp.broadcast_to(mask_ref[3:4, :], (4, cols))
     spot = (other * lon_odd + (1.0 - other) * (1.0 - lon_odd)) * (cols - 1)
     place = jnp.where(lane.astype(F32) == spot, 1.0, 0.0).astype(BF16)
+    at = slice(first, first + size)
+    hi, lo = split2(jnp.concatenate([lon_a[:, at], lon_b[:, at]], axis=0))
+    both = jnp.concatenate([hi, lo], axis=0)
+    return lax.dot_general(both, place, (((0,), (0,)), ((), ())), preferred_element_type=F32)
+
+
+def lat_rows(mask_ref, lat_a, lat_b, layers):
+    odd = mask_ref[2:3, :] > 0.5
+    a, b = lat_a[...].astype(F32), lat_b[...].astype(F32)
+    north, south = jnp.where(odd, a, b), jnp.where(odd, b, a)
+    return [(x[0:layers], x[layers : 2 * layers], x[2 * layers :]) for x in (north, south)]
+
+
+def spread(mask_ref, lon_a, lon_b, lat_a, lat_b, halo):
+    tracers, layers, rows, cols = halo.shape
+    size = layers * rows
+    north, south = lat_rows(mask_ref, lat_a, lat_b, layers)
     for t in range(tracers):
-        at = slice(t * size, (t + 1) * size)
-        hi, lo = split2(jnp.concatenate([lon_a[:, at], lon_b[:, at]], axis=0))
-        both = jnp.concatenate([hi, lo], axis=0)
-        spot = lax.dot_general(both, place, (((0,), (0,)), ((), ())), preferred_element_type=F32)
-        halo[t] = spot.reshape(layers, rows, cols)
-        at = slice(t * layers, (t + 1) * layers)
-        halo[t, :, 0, :] += jnp.where(odd, lat_a[at, :], lat_b[at, :])
-        halo[t, :, rows - 1, :] += jnp.where(odd, lat_b[at, :], lat_a[at, :])
+        halo[t] = lon_spots(mask_ref, lon_a, lon_b, t * size, size, cols).reshape(layers, rows, cols)
+        halo[t, :, 0, :] += north[t]
+        halo[t, :, rows - 1, :] += south[t]
 
 
 def vertical(base, force_ref, column_ref, v):
@@ -340,12 +349,13 @@
                 out = c[4] * x.reshape(size, cols) + c[0] * moved[:, :cols] + c[1] * moved[:, cols:]
                 out = out + c[2] * down.reshape(size, cols) + c[3] * up.reshape(size, cols)
                 w_out[t, g : g + group] = out.reshape(group, rows, cols)
-        if edges is not None:
-            (lat_w, _), (lat_a, lat_b) = weights, edges[2:]
-            at = slice(t * layers, (t + 1) * layers)
-            top, low = v[t, :, 0, :], v[t, :, rows - 1, :]
-            lat_a[at, :] = top * lat_w[0] + low * lat_w[1]
-            lat_b[at, :] = top * lat_w[2] + low * lat_w[3]
+    if edges is not None:
+        (lat_w, _), (lat_a, lat_b) = weights, edges[2:]
+        ends = [(v[t, :, 0, :], v[t, :, rows - 1, :]) for t in range(tracers)]
+        to_a = [top * lat_w[0] + low * lat_w[1] for top, low in ends]
+        to_b = [top * lat_w[2] + low * lat_w[3] for top, low in ends]
+        lat_a[...] = jnp.concatenate(to_a, axis=0).astype(BF16)
+        lat_b[...] = jnp.concatenate(to_b, axis=0).astype(BF16)
 
 
 def head_kernel(
@@ -393,16 +403,21 @@
 
 
 def last_kernel(
-    mask_ref, w_in, lat_b, lat_a, lon_b, lon_a, flux_in, adj_out, flux_out, halo, done, sems
+    mask_ref, w_in, lat_b, lat_a, lon_b, lon_a, flux_in, adj_out, flux_out, done, sems
 ):
-    tracers, layers = w_in.shape[:2]
-    spread(mask_ref, lon_a, lon_b, lat_a, lat_b, halo)
+    tracers, layers, rows, cols = w_in.shape
+    north, south = lat_rows(mask_ref, lat_a, lat_b, layers)
+    group = layers // 3
+    size = group * rows
     copies = []
-    group = layers // 3
     for t in range(tracers):
         for g in range(3):
+            first = t * layers * rows + g * size
             at = (t, pl.ds(g * group, group))
-            done[at] = w_in[at] + halo[at]
+            spots = lon_spots(mask_ref, lon_a, lon_b, first, size, cols)
+            done[at] = w_in[at] + spots.reshape(group, rows, cols)
+            done[t, g * group : (g + 1) * group, 0, :] += north[t][g * group : (g + 1) * group]
+            done[t, g * group : (g + 1) * group, rows - 1, :] += south[t][g * group : (g + 1) * group]
             copies.append(pltpu.make_async_copy(done.at[at], adj_out.at[at], sems.at[3 * t + g]))
             copies[-1].start()
     flux_out[...] = flux_in[...] + done[:, 0]
@@ -434,8 +449,8 @@
     count = sound_cell.shape[1]
     field = sds(tracers, layers, rows, cols)
     plane = sds(tracers, rows, cols)
-    lat_edge = sds(tracers * layers, cols)
-    lon_edge = sds(1, 14336)
+    lat_edge = sds(tracers * layers, cols, dtype=BF16)
+    lon_edge = sds(1, 7168)
     slots = ntiles * CAP
     outgoing = call(
         route_kernel,
@@ -485,7 +500,7 @@
     table = kernel_table.T
     work = (pltpu.VMEM((256, slots), BF16), pltpu.VMEM((layers, 16, slots), F32))
     force, snd, parts, now, coef = call(
-        functools.partial(head_kernel, steps - 1, 512),
+        functools.partial(head_kernel, steps - 1, slots),
         (
             field,
             sds(steps, 8, slots),
@@ -504,7 +519,7 @@
     fixed = (column, coef, lat_w, lon_w)
 
     def forcing(s, now):
-        kernel = functools.partial(forcing_kernel, s, 512)
+        kernel = functools.partial(forcing_kernel, s, slots)
         if s == 0:
             return call(kernel, field, snd, now, parts, scratch=work), None
         return call(
@@ -544,7 +559,7 @@
         *exchange(*edges),
         flux,
         hbm_out=(0,),
-        scratch=(v, v, pltpu.SemaphoreType.DMA((3 * tracers,))),
+        scratch=(v, pltpu.SemaphoreType.DMA((3 * tracers,))),
     )
 
 

time: 72 us -> 70 us (0.972)
  Pallas kernels: 35.5 us -> 33.7 us
    pallas_call x12, Pallas kernels: 35.5 us -> 33.7 us  [call(): pl.pallas_call(kernel, out_shape=tuple((pltpu.HBM(o.shape, o.dtype) if i...]
  transfers between devices with their start and end apart: 17 -> 17, of which waited for: 6 -> 4; matrix products, arithmetic and copies ran while one was open for 0% -> 0% of each run, Pallas kernels for 23% -> 23%
where the time goes in v6:
time: 70 us; the launch traced here: 69.5 us
  Pallas kernels  33.7 us (48%)
  starting transfers between devices  25.8 us (37%)
  waiting for transfers between devices  8.94 us (13%)
  between operations  0.99 us (1%)
    pallas_call x12, Pallas kernels, call(): pl.pallas_call(kernel, out_shape=tuple((pltpu.HBM(o.shape, o.dtype) if i...  33.7 us
    all_to_all x1, starting transfers between devices, body(): lax.all_to_all(outgoing, ('lat', 'lon'), split_axis=0, concat_axis=0, til...  11.1 us
    ppermute x4, starting transfers between devices, exchange(): lon_b = lax.ppermute(lon_b, 'lon', lon_far)  9.07 us
    all_to_all x1, waiting for transfers between devices, body(): lax.all_to_all(outgoing, ('lat', 'lon'), split_axis=0, concat_axis=0, til...  5.52 us
    ppermute x4, starting transfers between devices, exchange(): lat_b = lax.ppermute(lat_b, 'lat', lat_far)  5.47 us
    ppermute x4, waiting for transfers between devices, exchange(): lat_b = lax.ppermute(lat_b, 'lat', lat_far)  1.94 us
    ppermute x4, waiting for transfers between devices, exchange(): lon_b = lax.ppermute(lon_b, 'lon', lon_far)  1.45 us
  transfers between devices with their start and end apart: 17, of which 4 were waited for; matrix products, arithmetic and copies ran while one was open for 0% of the time, Pallas kernels for 23%

profile of v6, /device:TPU:0, one launch (start us, length us, event | category | flops | bytes accessed | tf_op | source)
XLA Modules:
  0.0 69.5 jit_solution(8962966704931777818)
XLA Ops:
  0.6 2.5 %shard_map.104 = f32[128,2,128]{2,1,0:T(2,128)} custom-call(s32[4,1,512]{2,1,0:T(1,128)} %bitcast.9, s32[4,512]{1,0:T(4,128)} %cell_in.1, s32[4,512]{1,0:T(4,128)} %index_in.1, f32[3,4,512]{2,1,0:T(4,128)} %bitcast.7, f32[4,512]{1,0:T(4,128)} %prec_in.1), custom_call_target="tpu_custom_call" | custom-call | tf_op jit(solution)/shard_map/pallas_call | solution.py:43
  3.1 11.1 %all-to-all-start = ((f32[128,2,128]{2,1,0:T(2,128)}), f32[128,2,128]{2,1,0:T(2,128)S(1)}, u32[]{:S(2)}, u32[]{:S(2)}) async-start(f32[128,2,128]{2,1,0:T(2,128)} %shard_map.104), calls=%async_computation | async-start | bytes 262144 | tf_op jit(solution)/shard_map/all_to_all | solution.py:473
  14.5 3.9 %shard_map.105 = (f32[180,32,128]{2,1,0:T(8,128)}, f32[106,32,128]{2,1,0:T(8,128)S(1)}, f32[4,36,128]{2,1,0:T(8,128)S(1)}, f32[4,1,1152]{2,1,0:T(1,128)S(1)}, bf16[3,36,32,128]{3,2,1,0:T(8,128)(2,1)S(1)}) custom-call(f32[4,128]{1,0:T(4,128)S(1)} %broadcast_in_dim.4.mask_ref, f32[35,32,128]{2,1,0:T(8,128)} %mix_in.1, f32[4,36,32,128]{3,2,1,0:T(8,128)} %tr_in.1, ...), custom_call_target="tpu_custom_call" | custom-call | tf_op jit(solution)/shard_map/pallas_call | solution.py:43
  18.4 5.5 %all-to-all-done.got_ref = f32[128,2,128]{2,1,0:T(2,128)S(1)} async-done(((f32[128,2,128]{2,1,0:T(2,128)}), f32[128,2,128]{2,1,0:T(2,128)S(1)}, u32[]{:S(2)}, u32[]{:S(2)}) %all-to-all-start) | async-done | bytes 131104 | tf_op jit(solution)/shard_map/all_to_all | solution.py:473
  23.9 4.3 %shard_map.106 = (f32[3,36,32,128]{3,2,1,0:T(8,128)S(1)}, f32[4,8,1024]{2,1,0:T(8,128)S(1)}, bf16[3,36,64]{2,1,0:T(8,128)(2,1)S(1)}, bf16[3,36,32,128]{3,2,1,0:T(8,128)(2,1)S(1)}, f32[180,32,128]{2,1,0:T(8,128)S(1)}) custom-call(f32[128,2,128]{2,1,0:T(2,128)S(1)} %all-to-all-done.got_ref, bf16[3,36,32,128]{3,2,1,0:T(8,128)(2,1)S(1)} %get-tuple-element.39.traj_ref, ...), custom_call_target="tpu_custom_call" | custom-call | tf_op jit(solution)/shard_map/pallas_call | solution.py:43
  28.2 1.8 %shard_map.107 = (f32[3,36,32,128]{3,2,1,0:T(8,128)S(1)}, f32[1,7168]{1,0:T(1,128)S(1)}, f32[1,7168]{1,0:T(1,128)S(1)}, bf16[108,128]{1,0:T(8,128)(2,1)S(1)}, bf16[108,128]{1,0:T(8,128)(2,1)S(1)}) custom-call(f32[3,36,32,128]{3,2,1,0:T(8,128)S(1)} %get-tuple-element.41.force_ref, f32[106,32,128]{2,1,0:T(8,128)S(1)} %get-tuple-element.42.column_ref, ...), custom_call_target="tpu_custom_call" | custom-call | tf_op jit(solution)/shard_map/pallas_call | solution.py:43
  30.0 1.4 %collective-permute-start.2 = (f32[1,7168]{1,0:T(1,128)S(1)}, f32[1,7168]{1,0:T(1,128)S(1)}, u32[]{:S(2)}, u32[]{:S(2)}) collective-permute-start(f32[1,7168]{1,0:T(1,128)S(1)} %get-tuple-element.49), channel_id=1, source_target_pairs={{1,2},{2,1},{3,4},{4,3},{5,6},{6,5},{7,8},{8,7},{9,10},{10,9},{11,... | collective-permute-start | bytes 86024 | tf_op jit(solution)/shard_map/ppermute | solution.py:437
  31.4 0.6 collective-permute-start
  32.0 3.5 %shard_map.108 = (f32[3,36,32,128]{3,2,1,0:T(8,128)S(1)}, bf16[3,36,32,128]{3,2,1,0:T(8,128)(2,1)S(1)}) custom-call(f32[4,8,1024]{2,1,0:T(8,128)S(1)} %get-tuple-element.51.snd_ref, bf16[3,36,32,128]{3,2,1,0:T(8,128)(2,1)S(1)} %get-tuple-element.52.traj_ref, bf16[3,36,64]{2,1,0:T(8,128)(2,1)S(1)} %get-tuple-element.53.table_ref, ...), custom_call_target="tpu_custom_call" | custom-call | tf_op jit(solution)/shard_map/pallas_call | solution.py:43
  35.9 1.4 %collective-permute-done.2.lon_b = f32[1,7168]{1,0:T(1,128)S(1)} collective-permute-done((f32[1,7168]{1,0:T(1,128)S(1)}, f32[1,7168]{1,0:T(1,128)S(1)}, u32[]{:S(2)}, u32[]{:S(2)}) %collective-permute-start.2) | collective-permute-done | bytes 28704 | tf_op jit(solution)/shard_map/ppermute | solution.py:437
  37.3 2.6 %shard_map.109 = (f32[3,36,32,128]{3,2,1,0:T(8,128)S(1)}, f32[1,7168]{1,0:T(1,128)S(1)}, f32[1,7168]{1,0:T(1,128)S(1)}, bf16[108,128]{1,0:T(8,128)(2,1)S(1)}, bf...) custom-call(f32[4,128]{1,0:T(4,128)S(1)} %broadcast_in_dim.4.mask_ref, ...), custom_call_target="tpu_custom_call" | custom-call | tf_op jit(solution)/shard_map/pallas_call | solution.py:43
  39.9 2.8 %collective-permute-start.6 = (f32[1,7168]{1,0:T(1,128)S(1)}, f32[1,7168]{1,0:T(1,128)S(1)}, u32[]{:S(2)}, u32[]{:S(2)}) collective-permute-start(f32[1,7168]{1,0:T(1,128)S(1)} %get-tuple-element.58), channel_id=1, source_target_pairs={{1,2},{2,1},{3,4},{4,3},{5,6},{6,5},{7,8},{8,7},{9,10},{10,9},{11,... | collective-permute-start | bytes 86024 | tf_op jit(solution)/shard_map/ppermute | solution.py:437
  42.7 1.7 %collective-permute-start.4 = (bf16[108,128]{1,0:T(8,128)(2,1)S(1)}, bf16[108,128]{1,0:T(8,128)(2,1)S(1)}, u32[]{:S(2)}, u32[]{:S(2)}) collective-permute-start(bf16[108,128]{1,0:T(8,128)(2,1)S(1)} %get-tuple-element.56), channel_id=1, source_target_pairs={{16,32},{32,16},{48,64},{64,48},{80,96},{96,80},{112,0},{0,112},{1... | collective-permute-start | bytes 82952 | tf_op jit(solution)/shard_map/ppermute | solution.py:438
  44.4 3.5 %shard_map.110 = (f32[3,36,32,128]{3,2,1,0:T(8,128)S(1)}, bf16[3,36,32,128]{3,2,1,0:T(8,128)(2,1)S(1)}) custom-call(f32[4,8,1024]{2,1,0:T(8,128)S(1)} %get-tuple-element.51.snd_ref, bf16[3,36,32,128]{3,2,1,0:T(8,128)(2,1)S(1)} %get-tuple-element.61.traj_ref, bf16[3,36,64]{2,1,0:T(8,128)(2,1)S(1)} %get-tuple-element.53.table_ref, ...), custom_call_target="tpu_custom_call" | custom-call | tf_op jit(solution)/shard_map/pallas_call | solution.py:43
  48.0 2.7 %shard_map.111 = (f32[3,36,32,128]{3,2,1,0:T(8,128)S(1)}, f32[1,7168]{1,0:T(1,128)S(1)}, f32[1,7168]{1,0:T(1,128)S(1)}, bf16[108,128]{1,0:T(8,128)(2,1)S(1)}, bf...) custom-call(f32[4,128]{1,0:T(4,128)S(1)} %broadcast_in_dim.4.mask_ref, ...), custom_call_target="tpu_custom_call" | custom-call | tf_op jit(solution)/shard_map/pallas_call | solution.py:43
  50.7 2.2 %collective-permute-start.10 = (f32[1,7168]{1,0:T(1,128)S(1)}, f32[1,7168]{1,0:T(1,128)S(1)}, u32[]{:S(2)}, u32[]{:S(2)}) collective-permute-start(f32[1,7168]{1,0:T(1,128)S(1)} %get-tuple-element.66), channel_id=1, source_target_pairs={{1,2},{2,1},{3,4},{4,3},{5,6},{6,5},{7,8},{8,7},{9,10},{10,9},{11,... | collective-permute-start | bytes 86024 | tf_op jit(solution)/shard_map/ppermute | solution.py:437
  52.9 1.5 %collective-permute-start.8 = (bf16[108,128]{1,0:T(8,128)(2,1)S(1)}, bf16[108,128]{1,0:T(8,128)(2,1)S(1)}, u32[]{:S(2)}, u32[]{:S(2)}) collective-permute-start(bf16[108,128]{1,0:T(8,128)(2,1)S(1)} %get-tuple-element.64), channel_id=1, source_target_pairs={{16,32},{32,16},{48,64},{64,48},{80,96},{96,80},{112,0},{0,112},{1... | collective-permute-start | bytes 82952 | tf_op jit(solution)/shard_map/ppermute | solution.py:438
  54.4 3.5 %shard_map.112.force_ref = f32[3,36,32,128]{3,2,1,0:T(8,128)S(1)} custom-call(f32[4,8,1024]{2,1,0:T(8,128)S(1)} %get-tuple-element.51.snd_ref, bf16[3,36,32,128]{3,2,1,0:T(8,128)(2,1)S(1)} %get-tuple-element.69.traj_ref, bf16[3,36,64]{2,1,0:T(8,128)(2,1)S(1)} %get-tuple-element.53.table_ref), custom_call_target="tpu_custom_call" | custom-call | tf_op jit(solution)/shard_map/pallas_call | solution.py:43
  57.9 2.0 %shard_map.113 = (f32[3,36,32,128]{3,2,1,0:T(8,128)S(1)}, f32[1,7168]{1,0:T(1,128)S(1)}, f32[1,7168]{1,0:T(1,128)S(1)}, bf16[108,128]{1,0:T(8,128)(2,1)S(1)}, bf...) custom-call(f32[4,128]{1,0:T(4,128)S(1)} %broadcast_in_dim.4.mask_ref, ...), custom_call_target="tpu_custom_call" | custom-call | tf_op jit(solution)/shard_map/pallas_call | solution.py:43
  59.9 2.8 %collective-permute-start.14 = (f32[1,7168]{1,0:T(1,128)S(1)}, f32[1,7168]{1,0:T(1,128)S(1)}, u32[]{:S(2)}, u32[]{:S(2)}) collective-permute-start(f32[1,7168]{1,0:T(1,128)S(1)} %get-tuple-element.73), channel_id=1, source_target_pairs={{1,2},{2,1},{3,4},{4,3},{5,6},{6,5},{7,8},{8,7},{9,10},{10,9},{11,... | collective-permute-start | bytes 86024 | tf_op jit(solution)/shard_map/ppermute | solution.py:437
  62.7 1.7 %collective-permute-start.12 = (bf16[108,128]{1,0:T(8,128)(2,1)S(1)}, bf16[108,128]{1,0:T(8,128)(2,1)S(1)}, u32[]{:S(2)}, u32[]{:S(2)}) collective-permute-start(bf16[108,128]{1,0:T(8,128)(2,1)S(1)} %get-tuple-element.71), channel_id=1, source_target_pairs={{16,32},{32,16},{48,64},{64,48},{80,96},{96,80},{112,0},{0,112},{1... | collective-permute-start | bytes 82952 | tf_op jit(solution)/shard_map/ppermute | solution.py:438
  64.4 1.2 %shard_map.114.w_in = f32[3,36,32,128]{3,2,1,0:T(8,128)S(1)} custom-call(f32[3,36,32,128]{3,2,1,0:T(8,128)S(1)} %get-tuple-element.70.v, f32[180,32,128]{2,1,0:T(8,128)S(1)} %get-tuple-element.43.coef_ref), custom_call_target="tpu_custom_call" | custom-call | tf_op jit(solution)/shard_map/pallas_call | solution.py:43
  65.6 1.6 %collective-permute-done.12.lat_b = bf16[108,128]{1,0:T(8,128)(2,1)S(1)} collective-permute-done((bf16[108,128]{1,0:T(8,128)(2,1)S(1)}, bf16[108,128]{1,0:T(8,128)(2,1)S(1)}, u32[]{:S(2)}, u32[]{:S(2)}) %collective-permute-start.12) | collective-permute-done | bytes 27680 | tf_op jit(solution)/shard_map/ppermute | solution.py:438
  67.2 2.1 %shard_map.115 = (f32[3,36,32,128]{3,2,1,0:T(8,128)}, f32[3,32,128]{2,1,0:T(8,128)}) custom-call(f32[4,128]{1,0:T(4,128)S(1)} %broadcast_in_dim.4.mask_ref, f32[3,36,32,128]{3,2,1,0:T(8,128)S(1)} %shard_map.114.w_in, bf16[108,128]{1,0:T(8,128)(2,1)S(1)} %collective-permute-done.12.lat_b, bf16[108,128]{1,0:T(8,128)(2,1)S(1)} %collective-permute-done.13.lat_a, ...), custom_call_target="tpu_custom_call" | custom-call | tf_op jit(solution)/shard_map/pallas_call | solution.py:43
  (25 shorter events, 0.7 us)
Async XLA Ops:
  3.1 20.8 %all-to-all-start = ((f32[128,2,128]{2,1,0:T(2,128)}), f32[128,2,128]{2,1,0:T(2,128)S(1)}, u32[]{:S(2)}, u32[]{:S(2)}) async-start(f32[128,2,128]{2,1,0:T(2,128)} %shard_map.104), calls=%async_computation | async-start | bytes 262144 | tf_op jit(solution)/shard_map/all_to_all | solution.py:473
  30.0 7.3 %collective-permute-start.2 = (f32[1,7168]{1,0:T(1,128)S(1)}, f32[1,7168]{1,0:T(1,128)S(1)}, u32[]{:S(2)}, u32[]{:S(2)}) collective-permute-start(f32[1,7168]{1,0:T(1,128)S(1)} %get-tuple-element.49), channel_id=1, source_target_pairs={{1,2},{2,1},{3,4},{4,3},{5,6},{6,5},{7,8},{8,7},{9,10},{10,9},{11,... | collective-permute-start | bytes 86024 | tf_op jit(solution)/shard_map/ppermute | solution.py:437
  31.4 5.9 %collective-permute-start.3 = (f32[1,7168]{1,0:T(1,128)S(1)}, f32[1,7168]{1,0:T(1,128)S(1)}, u32[]{:S(2)}, u32[]{:S(2)}) collective-permute-start(f32[1,7168]{1,0:T(1,128)S(1)} %get-tuple-element.50), channel_id=1, source_target_pairs={{0,1},{1,0},{2,3},{3,2},{4,5},{5,4},{6,7},{7,6},{8,9},{9,8},{10,11... | collective-permute-start | bytes 86024 | tf_op jit(solution)/shard_map/ppermute | solution.py:439
  31.4 4.5 %collective-permute-start = (bf16[108,128]{1,0:T(8,128)(2,1)S(1)}, bf16[108,128]{1,0:T(8,128)(2,1)S(1)}, u32[]{:S(2)}, u32[]{:S(2)}) collective-permute-start(bf16[108,128]{1,0:T(8,128)(2,1)S(1)} %get-tuple-element.47), channel_id=1, source_target_pairs={{16,32},{32,16},{48,64},{64,48},{80,96},{96,80},{112,0},{0,112},{1... | collective-permute-start | bytes 82952 | tf_op jit(solution)/shard_map/ppermute | solution.py:438
  32.0 4.0 %collective-permute-start.1 = (bf16[108,128]{1,0:T(8,128)(2,1)S(1)}, bf16[108,128]{1,0:T(8,128)(2,1)S(1)}, u32[]{:S(2)}, u32[]{:S(2)}) collective-permute-start(bf16[108,128]{1,0:T(8,128)(2,1)S(1)} %get-tuple-element.48), channel_id=1, source_target_pairs={{0,16},{16,0},{32,48},{48,32},{64,80},{80,64},{96,112},{112,96},{1... | collective-permute-start | bytes 82952 | tf_op jit(solution)/shard_map/ppermute | solution.py:440
  39.9 8.1 %collective-permute-start.6 = (f32[1,7168]{1,0:T(1,128)S(1)}, f32[1,7168]{1,0:T(1,128)S(1)}, u32[]{:S(2)}, u32[]{:S(2)}) collective-permute-start(f32[1,7168]{1,0:T(1,128)S(1)} %get-tuple-element.58), channel_id=1, source_target_pairs={{1,2},{2,1},{3,4},{4,3},{5,6},{6,5},{7,8},{8,7},{9,10},{10,9},{11,... | collective-permute-start | bytes 86024 | tf_op jit(solution)/shard_map/ppermute | solution.py:437
  42.7 5.3 %collective-permute-start.7 = (f32[1,7168]{1,0:T(1,128)S(1)}, f32[1,7168]{1,0:T(1,128)S(1)}, u32[]{:S(2)}, u32[]{:S(2)}) collective-permute-start(f32[1,7168]{1,0:T(1,128)S(1)} %get-tuple-element.59), channel_id=1, source_target_pairs={{0,1},{1,0},{2,3},{3,2},{4,5},{5,4},{6,7},{7,6},{8,9},{9,8},{10,11... | collective-permute-start | bytes 86024 | tf_op jit(solution)/shard_map/ppermute | solution.py:439
  42.7 5.3 %collective-permute-start.4 = (bf16[108,128]{1,0:T(8,128)(2,1)S(1)}, bf16[108,128]{1,0:T(8,128)(2,1)S(1)}, u32[]{:S(2)}, u32[]{:S(2)}) collective-permute-start(bf16[108,128]{1,0:T(8,128)(2,1)S(1)} %get-tuple-element.56), channel_id=1, source_target_pairs={{16,32},{32,16},{48,64},{64,48},{80,96},{96,80},{112,0},{0,112},{1... | collective-permute-start | bytes 82952 | tf_op jit(solution)/shard_map/ppermute | solution.py:438
  44.4 3.6 %collective-permute-start.5 = (bf16[108,128]{1,0:T(8,128)(2,1)S(1)}, bf16[108,128]{1,0:T(8,128)(2,1)S(1)}, u32[]{:S(2)}, u32[]{:S(2)}) collective-permute-start(bf16[108,128]{1,0:T(8,128)(2,1)S(1)} %get-tuple-element.57), channel_id=1, source_target_pairs={{0,16},{16,0},{32,48},{48,32},{64,80},{80,64},{96,112},{112,96},{1... | collective-permute-start | bytes 82952 | tf_op jit(solution)/shard_map/ppermute | solution.py:440
  50.7 7.3 %collective-permute-start.10 = (f32[1,7168]{1,0:T(1,128)S(1)}, f32[1,7168]{1,0:T(1,128)S(1)}, u32[]{:S(2)}, u32[]{:S(2)}) collective-permute-start(f32[1,7168]{1,0:T(1,128)S(1)} %get-tuple-element.66), channel_id=1, source_target_pairs={{1,2},{2,1},{3,4},{4,3},{5,6},{6,5},{7,8},{8,7},{9,10},{10,9},{11,... | collective-permute-start | bytes 86024 | tf_op jit(solution)/shard_map/ppermute | solution.py:437
  52.9 5.1 %collective-permute-start.11 = (f32[1,7168]{1,0:T(1,128)S(1)}, f32[1,7168]{1,0:T(1,128)S(1)}, u32[]{:S(2)}, u32[]{:S(2)}) collective-permute-start(f32[1,7168]{1,0:T(1,128)S(1)} %get-tuple-element.67), channel_id=1, source_target_pairs={{0,1},{1,0},{2,3},{3,2},{4,5},{5,4},{6,7},{7,6},{8,9},{9,8},{10,11... | collective-permute-start | bytes 86024 | tf_op jit(solution)/shard_map/ppermute | solution.py:439
  52.9 5.0 %collective-permute-start.8 = (bf16[108,128]{1,0:T(8,128)(2,1)S(1)}, bf16[108,128]{1,0:T(8,128)(2,1)S(1)}, u32[]{:S(2)}, u32[]{:S(2)}) collective-permute-start(bf16[108,128]{1,0:T(8,128)(2,1)S(1)} %get-tuple-element.64), channel_id=1, source_target_pairs={{16,32},{32,16},{48,64},{64,48},{80,96},{96,80},{112,0},{0,112},{1... | collective-permute-start | bytes 82952 | tf_op jit(solution)/shard_map/ppermute | solution.py:438
  54.4 3.5 %collective-permute-start.9 = (bf16[108,128]{1,0:T(8,128)(2,1)S(1)}, bf16[108,128]{1,0:T(8,128)(2,1)S(1)}, u32[]{:S(2)}, u32[]{:S(2)}) collective-permute-start(bf16[108,128]{1,0:T(8,128)(2,1)S(1)} %get-tuple-element.65), channel_id=1, source_target_pairs={{0,16},{16,0},{32,48},{48,32},{64,80},{80,64},{96,112},{112,96},{1... | collective-permute-start | bytes 82952 | tf_op jit(solution)/shard_map/ppermute | solution.py:440
  59.9 7.3 %collective-permute-start.14 = (f32[1,7168]{1,0:T(1,128)S(1)}, f32[1,7168]{1,0:T(1,128)S(1)}, u32[]{:S(2)}, u32[]{:S(2)}) collective-permute-start(f32[1,7168]{1,0:T(1,128)S(1)} %get-tuple-element.73), channel_id=1, source_target_pairs={{1,2},{2,1},{3,4},{4,3},{5,6},{6,5},{7,8},{8,7},{9,10},{10,9},{11,... | collective-permute-start | bytes 86024 | tf_op jit(solution)/shard_map/ppermute | solution.py:437
  62.7 4.5 %collective-permute-start.15 = (f32[1,7168]{1,0:T(1,128)S(1)}, f32[1,7168]{1,0:T(1,128)S(1)}, u32[]{:S(2)}, u32[]{:S(2)}) collective-permute-start(f32[1,7168]{1,0:T(1,128)S(1)} %get-tuple-element.74), channel_id=1, source_target_pairs={{0,1},{1,0},{2,3},{3,2},{4,5},{5,4},{6,7},{7,6},{8,9},{9,8},{10,11... | collective-permute-start | bytes 86024 | tf_op jit(solution)/shard_map/ppermute | solution.py:439
  62.7 4.5 %collective-permute-start.12 = (bf16[108,128]{1,0:T(8,128)(2,1)S(1)}, bf16[108,128]{1,0:T(8,128)(2,1)S(1)}, u32[]{:S(2)}, u32[]{:S(2)}) collective-permute-start(bf16[108,128]{1,0:T(8,128)(2,1)S(1)} %get-tuple-element.71), channel_id=1, source_target_pairs={{16,32},{32,16},{48,64},{64,48},{80,96},{96,80},{112,0},{0,112},{1... | collective-permute-start | bytes 82952 | tf_op jit(solution)/shard_map/ppermute | solution.py:438
  64.4 2.8 %collective-permute-start.13 = (bf16[108,128]{1,0:T(8,128)(2,1)S(1)}, bf16[108,128]{1,0:T(8,128)(2,1)S(1)}, u32[]{:S(2)}, u32[]{:S(2)}) collective-permute-start(bf16[108,128]{1,0:T(8,128)(2,1)S(1)} %get-tuple-element.72), channel_id=1, source_target_pairs={{0,16},{16,0},{32,48},{48,32},{64,80},{80,64},{96,112},{112,96},{1... | collective-permute-start | bytes 82952 | tf_op jit(solution)/shard_map/ppermute | solution.py:440

commit v7 on v6

--- a/solution.py
+++ b/solution.py
@@ -11,6 +11,8 @@
 WORDS = 5
 F32 = jnp.float32
 BF16 = jnp.bfloat16
+F8 = jnp.float8_e4m3fn
+LOW = 256.0
 
 
 def split3(x):
@@ -130,17 +132,17 @@
 
 def forcing_kernel(s, chunk, snd_ref, traj_ref, table_ref, *refs):
     if s == 0:
-        out_ref, pick, weight = refs
+        out_ref, pick, pick8, weight = refs
     else:
-        traj_in, out_ref, next_ref, pick, weight, sem = refs
+        traj_in, out_ref, next_ref, pick, pick8, weight, sem = refs
         copy = pltpu.make_async_copy(traj_in.at[s - 1], next_ref, sem)
         copy.start()
-    forcing_body(s, chunk, snd_ref, traj_ref, table_ref, out_ref, pick, weight)
+    forcing_body(s, chunk, snd_ref, traj_ref, table_ref, out_ref, pick, pick8, weight)
     if s > 0:
         copy.wait()
 
 
-def forcing_body(s, chunk, snd_ref, step_traj, table_ref, out_ref, pick, weight):
+def forcing_body(s, chunk, snd_ref, step_traj, table_ref, out_ref, pick, pick8, weight):
     tracers, layers = out_ref.shape[:2]
     slots = snd_ref.shape[2]
     nker = table_ref.shape[2]
@@ -149,7 +151,9 @@
     ker_ids = lax.broadcasted_iota(jnp.int32, (nker, chunk), 0).astype(F32)
     for c in range(slots // chunk):
         at = pl.ds(c * chunk, chunk)
-        pick[:, at] = jnp.where(cell_ids == snd_ref[s, 0:1, at], 1.0, 0.0).astype(BF16)
+        here = jnp.where(cell_ids == snd_ref[s, 0:1, at], 1.0, 0.0)
+        pick[:, at] = here.astype(BF16)
+        pick8[:, at] = here.astype(F8)
         low = jnp.where(low_ids == snd_ref[s, 1:2, at], 1.0, 0.0)
         ker = jnp.where(ker_ids == snd_ref[s, 2:3, at], 1.0, 0.0).astype(BF16)
         w = dot(table_ref[0], ker) + dot(table_ref[1], ker) + dot(table_ref[2], ker)
@@ -169,8 +173,10 @@
             sampled = dot(lhs, pick[:, at]).reshape(layers, 16, chunk)
             model = jnp.sum(jnp.sum(sampled * weight[:, :, at], axis=0), axis=0, keepdims=True)
             sc = (model - snd_ref[s, 3 + t : 4 + t, at]) * snd_ref[s, 6:7, at]
-            hi, lo = split2((weight[:, :, at] * sc).reshape(layers * 16, chunk))
-            term = dot_t(hi, pick[:, at]) + dot_t(lo, pick[:, at])
+            value = (weight[:, :, at] * sc).reshape(layers * 16, chunk)
+            hi = value.astype(BF16)
+            lo = ((value - hi.astype(F32)) * LOW).astype(F8)
+            term = dot_t(hi, pick[:, at]) + dot_t(lo, pick8[:, at]) * (1.0 / LOW)
             force = term if force is None else force + term
         out_ref[t, :, 0:16, :] = force[:, 0:128].reshape(layers, 16, 128)
         out_ref[t, :, 16:32, :] = force[:, 128:256].reshape(layers, 16, 128)
@@ -283,9 +289,8 @@
 
 def lat_rows(mask_ref, lat_a, lat_b, layers):
     odd = mask_ref[2:3, :] > 0.5
-    a, b = lat_a[...].astype(F32), lat_b[...].astype(F32)
-    north, south = jnp.where(odd, a, b), jnp.where(odd, b, a)
-    return [(x[0:layers], x[layers : 2 * layers], x[2 * layers :]) for x in (north, south)]
+    rows = [(lat_a[at, :], lat_b[at, :]) for at in (slice(t * layers, (t + 1) * layers) for t in range(3))]
+    return [jnp.where(odd, a, b) for a, b in rows], [jnp.where(odd, b, a) for a, b in rows]
 
 
 def spread(mask_ref, lon_a, lon_b, lat_a, lat_b, halo):
@@ -354,13 +359,15 @@
         ends = [(v[t, :, 0, :], v[t, :, rows - 1, :]) for t in range(tracers)]
         to_a = [top * lat_w[0] + low * lat_w[1] for top, low in ends]
         to_b = [top * lat_w[2] + low * lat_w[3] for top, low in ends]
-        lat_a[...] = jnp.concatenate(to_a, axis=0).astype(BF16)
-        lat_b[...] = jnp.concatenate(to_b, axis=0).astype(BF16)
+        for t in range(tracers):
+            at = slice(t * layers, (t + 1) * layers)
+            lat_a[at, :] = to_a[t]
+            lat_b[at, :] = to_b[t]
 
 
 def head_kernel(
     s, chunk, got_ref, traj_ref, table_in, traj_in, coef_in,
-    out_ref, snd_ref, parts_ref, next_ref, coef_ref, pick, weight, table_ref, sems,
+    out_ref, snd_ref, parts_ref, next_ref, coef_ref, pick, pick8, weight, table_ref, sems,
 ):
     pairs = ((table_in, table_ref), (traj_in.at[s - 1], next_ref), (coef_in, coef_ref))
     copies = [pltpu.make_async_copy(a, b, sems.at[i]) for i, (a, b) in enumerate(pairs)]
@@ -370,7 +377,7 @@
     copies[0].wait()
     for i, part in enumerate(split3(table_ref[...])):
         parts_ref[i] = part
-    forcing_body(s, chunk, snd_ref, traj_ref, parts_ref, out_ref, pick, weight)
+    forcing_body(s, chunk, snd_ref, traj_ref, parts_ref, out_ref, pick, pick8, weight)
     for copy in copies[1:]:
         copy.wait()
 
@@ -382,16 +389,18 @@
 
 
 def step_kernel(
-    whole, mask_ref, w_in, lat_b, lat_a, lon_b, lon_a, flux_in, force_ref, column_ref, coef_ref, lat_w, lon_w,
-    w_out, *refs,
+    start, whole, mask_ref, w_in, lat_b, lat_a, lon_b, lon_a, *refs
 ):
+    flux_in, refs = (None, refs) if start else (refs[0], refs[1:])
+    force_ref, column_ref, coef_ref, lat_w, lon_w, w_out = refs[:6]
+    refs = refs[6:]
     edges, flux_out, halo, v = refs[:4], refs[4], refs[5], refs[6] if whole else w_out
     spread(mask_ref, lon_a, lon_b, lat_a, lat_b, halo)
 
     def base(t, k):
         value = w_in[t, k] + halo[t, k]
         if isinstance(k, int):
-            flux_out[t] = flux_in[t] + value
+            flux_out[t] = value if start else flux_in[t] + value
         return value
 
     vertical(base, force_ref, column_ref, v)
@@ -449,8 +458,8 @@
     count = sound_cell.shape[1]
     field = sds(tracers, layers, rows, cols)
     plane = sds(tracers, rows, cols)
-    lat_edge = sds(tracers * layers, cols, dtype=BF16)
-    lon_edge = sds(1, 7168)
+    lat_edge = sds(tracers * layers, cols)
+    lon_edge = sds(1, 14336)
     slots = ntiles * CAP
     outgoing = call(
         route_kernel,
@@ -498,7 +507,11 @@
         ),
     )
     table = kernel_table.T
-    work = (pltpu.VMEM((256, slots), BF16), pltpu.VMEM((layers, 16, slots), F32))
+    work = (
+        pltpu.VMEM((256, slots), BF16),
+        pltpu.VMEM((256, slots), F8),
+        pltpu.VMEM((layers, 16, slots), F32),
+    )
     force, snd, parts, now, coef = call(
         functools.partial(head_kernel, steps - 1, slots),
         (
@@ -536,28 +549,29 @@
     v = pltpu.VMEM(field.shape, F32)
     moved = (field, lon_edge, lon_edge, lat_edge, lat_edge)
     w, *edges = call(first_step_kernel, moved, force, *fixed, scratch=(v,))
-    flux = jnp.zeros((tracers, rows, cols), F32)
+    flux = []
     for s in range(steps - 2, -1, -1):
         halos = exchange(*edges)
         force, now = forcing(s, now)
-        w, *edges, flux = call(
-            functools.partial(step_kernel, s > 0),
+        *done, flux = call(
+            functools.partial(step_kernel, s == steps - 2, s > 0),
             moved + (plane,),
             mask,
             w,
             *halos,
-            flux,
+            *flux,
             force,
             *fixed,
             scratch=(v, v) if s > 0 else (v,),
         )
+        (w, *edges), flux = done, [flux]
     return call(
         last_kernel,
         (field, plane),
         mask,
         call(interior_kernel, field, w, coef),
         *exchange(*edges),
-        flux,
+        *flux,
         hbm_out=(0,),
         scratch=(v, pltpu.SemaphoreType.DMA((3 * tracers,))),
     )

time: 70 us -> 69.9 us (level)
  waiting for transfers between devices: 8.94 us -> 11.6 us
  Pallas kernels: 33.7 us -> 32.4 us
  starting transfers between devices: 25.8 us -> 24.6 us
    ppermute x4, waiting for transfers between devices: 1.94 us -> 4.67 us  [exchange(): lat_b = lax.ppermute(lat_b, 'lat', lat_far)]
    ppermute x4, starting transfers between devices: 5.47 us -> 3.75 us  [exchange(): lat_b = lax.ppermute(lat_b, 'lat', lat_far)]
    pallas_call x12, Pallas kernels: 33.7 us -> 32.4 us  [call(): pl.pallas_call(kernel, out_shape=tuple((pltpu.HBM(o.shape, o.dtype) if i...]
  transfers between devices with their start and end apart: 17 -> 17, of which waited for: 4 -> 6; matrix products, arithmetic and copies ran while one was open for 0% -> 0% of each run, Pallas kernels for 23% -> 21%
where the time goes in v7:
time: 69.9 us; the launch traced here: 69.7 us
  Pallas kernels  32.4 us (46%)
  starting transfers between devices  24.6 us (35%)
  waiting for transfers between devices  11.6 us (17%)
  between operations  0.95 us (1%)
    pallas_call x12, Pallas kernels, call(): pl.pallas_call(kernel, out_shape=tuple((pltpu.HBM(o.shape, o.dtype) if i...  32.4 us
    all_to_all x1, starting transfers between devices, body(): lax.all_to_all(outgoing, ('lat', 'lon'), split_axis=0, concat_axis=0, til...  11.1 us
    ppermute x4, starting transfers between devices, exchange(): lon_b = lax.ppermute(lon_b, 'lon', lon_far)  9.61 us
    all_to_all x1, waiting for transfers between devices, body(): lax.all_to_all(outgoing, ('lat', 'lon'), split_axis=0, concat_axis=0, til...  5.52 us
    ppermute x4, waiting for transfers between devices, exchange(): lat_b = lax.ppermute(lat_b, 'lat', lat_far)  4.67 us
    ppermute x4, starting transfers between devices, exchange(): lat_b = lax.ppermute(lat_b, 'lat', lat_far)  3.75 us
    ppermute x4, waiting for transfers between devices, exchange(): lon_b = lax.ppermute(lon_b, 'lon', lon_far)  1.42 us
  transfers between devices with their start and end apart: 17, of which 6 were waited for; matrix products, arithmetic and copies ran while one was open for 0% of the time, Pallas kernels for 21%

profile of v7, /device:TPU:0, one launch (start us, length us, event | category | flops | bytes accessed | tf_op | source)
XLA Modules:
  0.0 69.7 jit_solution(1279350196443883743)
XLA Ops:
  0.6 2.5 %shard_map.104 = f32[128,2,128]{2,1,0:T(2,128)} custom-call(s32[4,1,512]{2,1,0:T(1,128)} %bitcast.9, s32[4,512]{1,0:T(4,128)} %cell_in.1, s32[4,512]{1,0:T(4,128)} %index_in.1, f32[3,4,512]{2,1,0:T(4,128)} %bitcast.7, f32[4,512]{1,0:T(4,128)} %prec_in.1), custom_call_target="tpu_custom_call" | custom-call | tf_op jit(solution)/shard_map/pallas_call | solution.py:45
  3.1 11.1 %all-to-all-start = ((f32[128,2,128]{2,1,0:T(2,128)}), f32[128,2,128]{2,1,0:T(2,128)S(1)}, u32[]{:S(2)}, u32[]{:S(2)}) async-start(f32[128,2,128]{2,1,0:T(2,128)} %shard_map.104), calls=%async_computation | async-start | bytes 262144 | tf_op jit(solution)/shard_map/all_to_all | solution.py:482
  14.5 3.9 %shard_map.105 = (f32[180,32,128]{2,1,0:T(8,128)}, f32[106,32,128]{2,1,0:T(8,128)S(1)}, f32[4,36,128]{2,1,0:T(8,128)S(1)}, f32[4,1,1152]{2,1,0:T(1,128)S(1)}, bf16[3,36,32,128]{3,2,1,0:T(8,128)(2,1)S(1)}) custom-call(f32[4,128]{1,0:T(4,128)S(1)} %broadcast_in_dim.2.mask_ref, f32[35,32,128]{2,1,0:T(8,128)} %mix_in.1, f32[4,36,32,128]{3,2,1,0:T(8,128)} %tr_in.1, ...), custom_call_target="tpu_custom_call" | custom-call | tf_op jit(solution)/shard_map/pallas_call | solution.py:45
  18.4 5.5 %all-to-all-done.got_ref = f32[128,2,128]{2,1,0:T(2,128)S(1)} async-done(((f32[128,2,128]{2,1,0:T(2,128)}), f32[128,2,128]{2,1,0:T(2,128)S(1)}, u32[]{:S(2)}, u32[]{:S(2)}) %all-to-all-start) | async-done | bytes 131104 | tf_op jit(solution)/shard_map/all_to_all | solution.py:482
  23.9 3.9 %shard_map.106 = (f32[3,36,32,128]{3,2,1,0:T(8,128)S(1)}, f32[4,8,1024]{2,1,0:T(8,128)S(1)}, bf16[3,36,64]{2,1,0:T(8,128)(2,1)S(1)}, bf16[3,36,32,128]{3,2,1,0:T(8,128)(2,1)S(1)}, f32[180,32,128]{2,1,0:T(8,128)S(1)}) custom-call(f32[128,2,128]{2,1,0:T(2,128)S(1)} %all-to-all-done.got_ref, bf16[3,36,32,128]{3,2,1,0:T(8,128)(2,1)S(1)} %get-tuple-element.39.traj_ref, ...), custom_call_target="tpu_custom_call" | custom-call | tf_op jit(solution)/shard_map/pallas_call | solution.py:45
  27.8 1.8 %shard_map.107 = (f32[3,36,32,128]{3,2,1,0:T(8,128)S(1)}, f32[1,14336]{1,0:T(1,128)S(1)}, f32[1,14336]{1,0:T(1,128)S(1)}, f32[108,128]{1,0:T(8,128)S(1)}, f32[108,128]{1,0:T(8,128)S(1)}) custom-call(f32[3,36,32,128]{3,2,1,0:T(8,128)S(1)} %get-tuple-element.41.force_ref, f32[106,32,128]{2,1,0:T(8,128)S(1)} %get-tuple-element.42.column_ref.refs_1_.refs_2_, ...), custom_call_target="tpu_custom_call" | custom-call | tf_op jit(solution)/shard_map/pallas_call | solution.py:45
  29.7 1.4 %collective-permute-start.2 = (f32[1,14336]{1,0:T(1,128)S(1)}, f32[1,14336]{1,0:T(1,128)S(1)}, u32[]{:S(2)}, u32[]{:S(2)}) collective-permute-start(f32[1,14336]{1,0:T(1,128)S(1)} %get-tuple-element.49), channel_id=1, source_target_pairs={{1,2},{2,1},{3,4},{4,3},{5,6},{6,5},{7,8},{8,7},{9,10},{10,9},{11,... | collective-permute-start | bytes 172040 | tf_op jit(solution)/shard_map/ppermute | solution.py:446
  31.7 3.2 %shard_map.108 = (f32[3,36,32,128]{3,2,1,0:T(8,128)S(1)}, bf16[3,36,32,128]{3,2,1,0:T(8,128)(2,1)S(1)}) custom-call(f32[4,8,1024]{2,1,0:T(8,128)S(1)} %get-tuple-element.51.snd_ref, bf16[3,36,32,128]{3,2,1,0:T(8,128)(2,1)S(1)} %get-tuple-element.52.traj_ref, bf16[3,36,64]{2,1,0:T(8,128)(2,1)S(1)} %get-tuple-element.53.table_ref, ...), custom_call_target="tpu_custom_call" | custom-call | tf_op jit(solution)/shard_map/pallas_call | solution.py:45
  34.9 1.0 %collective-permute-done.lat_b = f32[108,128]{1,0:T(8,128)S(1)} collective-permute-done((f32[108,128]{1,0:T(8,128)S(1)}, f32[108,128]{1,0:T(8,128)S(1)}, u32[]{:S(2)}, u32[]{:S(2)}) %collective-permute-start) | collective-permute-done | bytes 55328 | tf_op jit(solution)/shard_map/ppermute | solution.py:447
  35.8 1.4 %collective-permute-done.2.lon_b = f32[1,14336]{1,0:T(1,128)S(1)} collective-permute-done((f32[1,14336]{1,0:T(1,128)S(1)}, f32[1,14336]{1,0:T(1,128)S(1)}, u32[]{:S(2)}, u32[]{:S(2)}) %collective-permute-start.2) | collective-permute-done | bytes 57376 | tf_op jit(solution)/shard_map/ppermute | solution.py:446
  37.2 2.7 %shard_map.109 = (f32[3,36,32,128]{3,2,1,0:T(8,128)S(1)}, f32[1,14336]{1,0:T(1,128)S(1)}, f32[1,14336]{1,0:T(1,128)S(1)}, f32[108,128]{1,0:T(8,128)S(1)}, f32[10...) custom-call(f32[4,128]{1,0:T(4,128)S(1)} %broadcast_in_dim.2.mask_ref, f32[3,36,32,128]{3,2,1,0:T(8,128)S(1)} %get-tuple-element.46.w_in, ...), custom_call_target="tpu_custom_call" | custom-call | tf_op jit(solution)/shard_map/pallas_call | solution.py:45
  39.9 2.8 %collective-permute-start.6 = (f32[1,14336]{1,0:T(1,128)S(1)}, f32[1,14336]{1,0:T(1,128)S(1)}, u32[]{:S(2)}, u32[]{:S(2)}) collective-permute-start(f32[1,14336]{1,0:T(1,128)S(1)} %get-tuple-element.58), channel_id=1, source_target_pairs={{1,2},{2,1},{3,4},{4,3},{5,6},{6,5},{7,8},{8,7},{9,10},{10,9},{11,... | collective-permute-start | bytes 172040 | tf_op jit(solution)/shard_map/ppermute | solution.py:446
  42.7 1.1 %collective-permute-start.4 = (f32[108,128]{1,0:T(8,128)S(1)}, f32[108,128]{1,0:T(8,128)S(1)}, u32[]{:S(2)}, u32[]{:S(2)}) collective-permute-start(f32[108,128]{1,0:T(8,128)S(1)} %get-tuple-element.56), channel_id=1, source_target_pairs={{16,32},{32,16},{48,64},{64,48},{80,96},{96,80},{112,0},{0,112},{1... | collective-permute-start | bytes 165896 | tf_op jit(solution)/shard_map/ppermute | solution.py:447
  43.8 3.1 %shard_map.110 = (f32[3,36,32,128]{3,2,1,0:T(8,128)S(1)}, bf16[3,36,32,128]{3,2,1,0:T(8,128)(2,1)S(1)}) custom-call(f32[4,8,1024]{2,1,0:T(8,128)S(1)} %get-tuple-element.51.snd_ref, bf16[3,36,32,128]{3,2,1,0:T(8,128)(2,1)S(1)} %get-tuple-element.61.traj_ref, bf16[3,36,64]{2,1,0:T(8,128)(2,1)S(1)} %get-tuple-element.53.table_ref, ...), custom_call_target="tpu_custom_call" | custom-call | tf_op jit(solution)/shard_map/pallas_call | solution.py:45
  47.5 2.7 %shard_map.111 = (f32[3,36,32,128]{3,2,1,0:T(8,128)S(1)}, f32[1,14336]{1,0:T(1,128)S(1)}, f32[1,14336]{1,0:T(1,128)S(1)}, f32[108,128]{1,0:T(8,128)S(1)}, f32[10...) custom-call(f32[4,128]{1,0:T(4,128)S(1)} %broadcast_in_dim.2.mask_ref, f32[3,36,32,128]{3,2,1,0:T(8,128)S(1)} %get-tuple-element.55.w_in, ...), custom_call_target="tpu_custom_call" | custom-call | tf_op jit(solution)/shard_map/pallas_call | solution.py:45
  50.2 2.7 %collective-permute-start.10 = (f32[1,14336]{1,0:T(1,128)S(1)}, f32[1,14336]{1,0:T(1,128)S(1)}, u32[]{:S(2)}, u32[]{:S(2)}) collective-permute-start(f32[1,14336]{1,0:T(1,128)S(1)} %get-tuple-element.66), channel_id=1, source_target_pairs={{1,2},{2,1},{3,4},{4,3},{5,6},{6,5},{7,8},{8,7},{9,10},{10,9},{11,... | collective-permute-start | bytes 172040 | tf_op jit(solution)/shard_map/ppermute | solution.py:446
  53.0 1.0 %collective-permute-start.8 = (f32[108,128]{1,0:T(8,128)S(1)}, f32[108,128]{1,0:T(8,128)S(1)}, u32[]{:S(2)}, u32[]{:S(2)}) collective-permute-start(f32[108,128]{1,0:T(8,128)S(1)} %get-tuple-element.64), channel_id=1, source_target_pairs={{16,32},{32,16},{48,64},{64,48},{80,96},{96,80},{112,0},{0,112},{1... | collective-permute-start | bytes 165896 | tf_op jit(solution)/shard_map/ppermute | solution.py:447
  54.0 3.2 %shard_map.112.refs_1_ = f32[3,36,32,128]{3,2,1,0:T(8,128)S(1)} custom-call(f32[4,8,1024]{2,1,0:T(8,128)S(1)} %get-tuple-element.51.snd_ref, bf16[3,36,32,128]{3,2,1,0:T(8,128)(2,1)S(1)} %get-tuple-element.69.traj_ref, bf16[3,36,64]{2,1,0:T(8,128)(2,1)S(1)} %get-tuple-element.53.table_ref), custom_call_target="tpu_custom_call" | custom-call | tf_op jit(solution)/shard_map/pallas_call | solution.py:45
  57.8 2.0 %shard_map.113 = (f32[3,36,32,128]{3,2,1,0:T(8,128)S(1)}, f32[1,14336]{1,0:T(1,128)S(1)}, f32[1,14336]{1,0:T(1,128)S(1)}, f32[108,128]{1,0:T(8,128)S(1)}, f32[10...) custom-call(f32[4,128]{1,0:T(4,128)S(1)} %broadcast_in_dim.2.mask_ref, f32[3,36,32,128]{3,2,1,0:T(8,128)S(1)} %get-tuple-element.63.w_in, ...), custom_call_target="tpu_custom_call" | custom-call | tf_op jit(solution)/shard_map/pallas_call | solution.py:45
  59.8 2.8 %collective-permute-start.14 = (f32[1,14336]{1,0:T(1,128)S(1)}, f32[1,14336]{1,0:T(1,128)S(1)}, u32[]{:S(2)}, u32[]{:S(2)}) collective-permute-start(f32[1,14336]{1,0:T(1,128)S(1)} %get-tuple-element.73), channel_id=1, source_target_pairs={{1,2},{2,1},{3,4},{4,3},{5,6},{6,5},{7,8},{8,7},{9,10},{10,9},{11,... | collective-permute-start | bytes 172040 | tf_op jit(solution)/shard_map/ppermute | solution.py:446
  62.5 1.1 %collective-permute-start.12 = (f32[108,128]{1,0:T(8,128)S(1)}, f32[108,128]{1,0:T(8,128)S(1)}, u32[]{:S(2)}, u32[]{:S(2)}) collective-permute-start(f32[108,128]{1,0:T(8,128)S(1)} %get-tuple-element.71), channel_id=1, source_target_pairs={{16,32},{32,16},{48,64},{64,48},{80,96},{96,80},{112,0},{0,112},{1... | collective-permute-start | bytes 165896 | tf_op jit(solution)/shard_map/ppermute | solution.py:447
  63.6 1.2 %shard_map.114.w_in = f32[3,36,32,128]{3,2,1,0:T(8,128)S(1)} custom-call(f32[3,36,32,128]{3,2,1,0:T(8,128)S(1)} %get-tuple-element.70.v, f32[180,32,128]{2,1,0:T(8,128)S(1)} %get-tuple-element.43.coef_ref.refs_2_.refs_3_), custom_call_target="tpu_custom_call" | custom-call | tf_op jit(solution)/shard_map/pallas_call | solution.py:45
  64.9 2.5 %collective-permute-done.12.lat_b = f32[108,128]{1,0:T(8,128)S(1)} collective-permute-done((f32[108,128]{1,0:T(8,128)S(1)}, f32[108,128]{1,0:T(8,128)S(1)}, u32[]{:S(2)}, u32[]{:S(2)}) %collective-permute-start.12) | collective-permute-done | bytes 55328 | tf_op jit(solution)/shard_map/ppermute | solution.py:447
  67.4 2.1 %shard_map.115 = (f32[3,36,32,128]{3,2,1,0:T(8,128)}, f32[3,32,128]{2,1,0:T(8,128)}) custom-call(f32[4,128]{1,0:T(4,128)S(1)} %broadcast_in_dim.2.mask_ref, f32[3,36,32,128]{3,2,1,0:T(8,128)S(1)} %shard_map.114.w_in, f32[108,128]{1,0:T(8,128)S(1)} %collective-permute-done.12.lat_b, f32[108,128]{1,0:T(8,128)S(1)} %collective-permute-done.13.lat_a, ...), custom_call_target="tpu_custom_call" | custom-call | tf_op jit(solution)/shard_map/pallas_call | solution.py:45
  (24 shorter events, 2.0 us)
Async XLA Ops:
  3.1 20.8 %all-to-all-start = ((f32[128,2,128]{2,1,0:T(2,128)}), f32[128,2,128]{2,1,0:T(2,128)S(1)}, u32[]{:S(2)}, u32[]{:S(2)}) async-start(f32[128,2,128]{2,1,0:T(2,128)} %shard_map.104), calls=%async_computation | async-start | bytes 262144 | tf_op jit(solution)/shard_map/all_to_all | solution.py:482
  29.7 7.6 %collective-permute-start.2 = (f32[1,14336]{1,0:T(1,128)S(1)}, f32[1,14336]{1,0:T(1,128)S(1)}, u32[]{:S(2)}, u32[]{:S(2)}) collective-permute-start(f32[1,14336]{1,0:T(1,128)S(1)} %get-tuple-element.49), channel_id=1, source_target_pairs={{1,2},{2,1},{3,4},{4,3},{5,6},{6,5},{7,8},{8,7},{9,10},{10,9},{11,... | collective-permute-start | bytes 172040 | tf_op jit(solution)/shard_map/ppermute | solution.py:446
  31.0 6.2 %collective-permute-start.3 = (f32[1,14336]{1,0:T(1,128)S(1)}, f32[1,14336]{1,0:T(1,128)S(1)}, u32[]{:S(2)}, u32[]{:S(2)}) collective-permute-start(f32[1,14336]{1,0:T(1,128)S(1)} %get-tuple-element.50), channel_id=1, source_target_pairs={{0,1},{1,0},{2,3},{3,2},{4,5},{5,4},{6,7},{7,6},{8,9},{9,8},{10,11... | collective-permute-start | bytes 172040 | tf_op jit(solution)/shard_map/ppermute | solution.py:448
  31.0 4.8 %collective-permute-start = (f32[108,128]{1,0:T(8,128)S(1)}, f32[108,128]{1,0:T(8,128)S(1)}, u32[]{:S(2)}, u32[]{:S(2)}) collective-permute-start(f32[108,128]{1,0:T(8,128)S(1)} %get-tuple-element.47), channel_id=1, source_target_pairs={{16,32},{32,16},{48,64},{64,48},{80,96},{96,80},{112,0},{0,112},{1... | collective-permute-start | bytes 165896 | tf_op jit(solution)/shard_map/ppermute | solution.py:447
  31.6 4.3 %collective-permute-start.1 = (f32[108,128]{1,0:T(8,128)S(1)}, f32[108,128]{1,0:T(8,128)S(1)}, u32[]{:S(2)}, u32[]{:S(2)}) collective-permute-start(f32[108,128]{1,0:T(8,128)S(1)} %get-tuple-element.48), channel_id=1, source_target_pairs={{0,16},{16,0},{32,48},{48,32},{64,80},{80,64},{96,112},{112,96},{1... | collective-permute-start | bytes 165896 | tf_op jit(solution)/shard_map/ppermute | solution.py:449
  39.9 7.6 %collective-permute-start.6 = (f32[1,14336]{1,0:T(1,128)S(1)}, f32[1,14336]{1,0:T(1,128)S(1)}, u32[]{:S(2)}, u32[]{:S(2)}) collective-permute-start(f32[1,14336]{1,0:T(1,128)S(1)} %get-tuple-element.58), channel_id=1, source_target_pairs={{1,2},{2,1},{3,4},{4,3},{5,6},{6,5},{7,8},{8,7},{9,10},{10,9},{11,... | collective-permute-start | bytes 172040 | tf_op jit(solution)/shard_map/ppermute | solution.py:446
  42.7 4.8 %collective-permute-start.7 = (f32[1,14336]{1,0:T(1,128)S(1)}, f32[1,14336]{1,0:T(1,128)S(1)}, u32[]{:S(2)}, u32[]{:S(2)}) collective-permute-start(f32[1,14336]{1,0:T(1,128)S(1)} %get-tuple-element.59), channel_id=1, source_target_pairs={{0,1},{1,0},{2,3},{3,2},{4,5},{5,4},{6,7},{7,6},{8,9},{9,8},{10,11... | collective-permute-start | bytes 172040 | tf_op jit(solution)/shard_map/ppermute | solution.py:448
  42.7 4.8 %collective-permute-start.4 = (f32[108,128]{1,0:T(8,128)S(1)}, f32[108,128]{1,0:T(8,128)S(1)}, u32[]{:S(2)}, u32[]{:S(2)}) collective-permute-start(f32[108,128]{1,0:T(8,128)S(1)} %get-tuple-element.56), channel_id=1, source_target_pairs={{16,32},{32,16},{48,64},{64,48},{80,96},{96,80},{112,0},{0,112},{1... | collective-permute-start | bytes 165896 | tf_op jit(solution)/shard_map/ppermute | solution.py:447
  43.8 3.7 %collective-permute-start.5 = (f32[108,128]{1,0:T(8,128)S(1)}, f32[108,128]{1,0:T(8,128)S(1)}, u32[]{:S(2)}, u32[]{:S(2)}) collective-permute-start(f32[108,128]{1,0:T(8,128)S(1)} %get-tuple-element.57), channel_id=1, source_target_pairs={{0,16},{16,0},{32,48},{48,32},{64,80},{80,64},{96,112},{112,96},{1... | collective-permute-start | bytes 165896 | tf_op jit(solution)/shard_map/ppermute | solution.py:449
  50.2 7.6 %collective-permute-start.10 = (f32[1,14336]{1,0:T(1,128)S(1)}, f32[1,14336]{1,0:T(1,128)S(1)}, u32[]{:S(2)}, u32[]{:S(2)}) collective-permute-start(f32[1,14336]{1,0:T(1,128)S(1)} %get-tuple-element.66), channel_id=1, source_target_pairs={{1,2},{2,1},{3,4},{4,3},{5,6},{6,5},{7,8},{8,7},{9,10},{10,9},{11,... | collective-permute-start | bytes 172040 | tf_op jit(solution)/shard_map/ppermute | solution.py:446
  53.0 4.8 %collective-permute-start.11 = (f32[1,14336]{1,0:T(1,128)S(1)}, f32[1,14336]{1,0:T(1,128)S(1)}, u32[]{:S(2)}, u32[]{:S(2)}) collective-permute-start(f32[1,14336]{1,0:T(1,128)S(1)} %get-tuple-element.67), channel_id=1, source_target_pairs={{0,1},{1,0},{2,3},{3,2},{4,5},{5,4},{6,7},{7,6},{8,9},{9,8},{10,11... | collective-permute-start | bytes 172040 | tf_op jit(solution)/shard_map/ppermute | solution.py:448
  53.0 4.8 %collective-permute-start.8 = (f32[108,128]{1,0:T(8,128)S(1)}, f32[108,128]{1,0:T(8,128)S(1)}, u32[]{:S(2)}, u32[]{:S(2)}) collective-permute-start(f32[108,128]{1,0:T(8,128)S(1)} %get-tuple-element.64), channel_id=1, source_target_pairs={{16,32},{32,16},{48,64},{64,48},{80,96},{96,80},{112,0},{0,112},{1... | collective-permute-start | bytes 165896 | tf_op jit(solution)/shard_map/ppermute | solution.py:447
  54.0 3.8 %collective-permute-start.9 = (f32[108,128]{1,0:T(8,128)S(1)}, f32[108,128]{1,0:T(8,128)S(1)}, u32[]{:S(2)}, u32[]{:S(2)}) collective-permute-start(f32[108,128]{1,0:T(8,128)S(1)} %get-tuple-element.65), channel_id=1, source_target_pairs={{0,16},{16,0},{32,48},{48,32},{64,80},{80,64},{96,112},{112,96},{1... | collective-permute-start | bytes 165896 | tf_op jit(solution)/shard_map/ppermute | solution.py:449
  59.8 7.6 %collective-permute-start.14 = (f32[1,14336]{1,0:T(1,128)S(1)}, f32[1,14336]{1,0:T(1,128)S(1)}, u32[]{:S(2)}, u32[]{:S(2)}) collective-permute-start(f32[1,14336]{1,0:T(1,128)S(1)} %get-tuple-element.73), channel_id=1, source_target_pairs={{1,2},{2,1},{3,4},{4,3},{5,6},{6,5},{7,8},{8,7},{9,10},{10,9},{11,... | collective-permute-start | bytes 172040 | tf_op jit(solution)/shard_map/ppermute | solution.py:446
  62.5 4.8 %collective-permute-start.15 = (f32[1,14336]{1,0:T(1,128)S(1)}, f32[1,14336]{1,0:T(1,128)S(1)}, u32[]{:S(2)}, u32[]{:S(2)}) collective-permute-start(f32[1,14336]{1,0:T(1,128)S(1)} %get-tuple-element.74), channel_id=1, source_target_pairs={{0,1},{1,0},{2,3},{3,2},{4,5},{5,4},{6,7},{7,6},{8,9},{9,8},{10,11... | collective-permute-start | bytes 172040 | tf_op jit(solution)/shard_map/ppermute | solution.py:448
  62.5 4.8 %collective-permute-start.12 = (f32[108,128]{1,0:T(8,128)S(1)}, f32[108,128]{1,0:T(8,128)S(1)}, u32[]{:S(2)}, u32[]{:S(2)}) collective-permute-start(f32[108,128]{1,0:T(8,128)S(1)} %get-tuple-element.71), channel_id=1, source_target_pairs={{16,32},{32,16},{48,64},{64,48},{80,96},{96,80},{112,0},{0,112},{1... | collective-permute-start | bytes 165896 | tf_op jit(solution)/shard_map/ppermute | solution.py:447
  63.6 3.7 %collective-permute-start.13 = (f32[108,128]{1,0:T(8,128)S(1)}, f32[108,128]{1,0:T(8,128)S(1)}, u32[]{:S(2)}, u32[]{:S(2)}) collective-permute-start(f32[108,128]{1,0:T(8,128)S(1)} %get-tuple-element.72), channel_id=1, source_target_pairs={{0,16},{16,0},{32,48},{48,32},{64,80},{80,64},{96,112},{112,96},{1... | collective-permute-start | bytes 165896 | tf_op jit(solution)/shard_map/ppermute | solution.py:449

commit v8 on v7

--- a/solution.py
+++ b/solution.py
@@ -289,8 +289,9 @@
 
 def lat_rows(mask_ref, lat_a, lat_b, layers):
     odd = mask_ref[2:3, :] > 0.5
-    rows = [(lat_a[at, :], lat_b[at, :]) for at in (slice(t * layers, (t + 1) * layers) for t in range(3))]
-    return [jnp.where(odd, a, b) for a, b in rows], [jnp.where(odd, b, a) for a, b in rows]
+    a, b = lat_a[...].astype(F32), lat_b[...].astype(F32)
+    north, south = jnp.where(odd, a, b), jnp.where(odd, b, a)
+    return [(x[0:layers], x[layers : 2 * layers], x[2 * layers :]) for x in (north, south)]
 
 
 def spread(mask_ref, lon_a, lon_b, lat_a, lat_b, halo):
@@ -359,10 +360,8 @@
         ends = [(v[t, :, 0, :], v[t, :, rows - 1, :]) for t in range(tracers)]
         to_a = [top * lat_w[0] + low * lat_w[1] for top, low in ends]
         to_b = [top * lat_w[2] + low * lat_w[3] for top, low in ends]
-        for t in range(tracers):
-            at = slice(t * layers, (t + 1) * layers)
-            lat_a[at, :] = to_a[t]
-            lat_b[at, :] = to_b[t]
+        lat_a[...] = jnp.concatenate(to_a, axis=0).astype(BF16)
+        lat_b[...] = jnp.concatenate(to_b, axis=0).astype(BF16)
 
 
 def head_kernel(
@@ -458,8 +457,8 @@
     count = sound_cell.shape[1]
     field = sds(tracers, layers, rows, cols)
     plane = sds(tracers, rows, cols)
-    lat_edge = sds(tracers * layers, cols)
-    lon_edge = sds(1, 14336)
+    lat_edge = sds(tracers * layers, cols, dtype=BF16)
+    lon_edge = sds(1, 7168)
     slots = ntiles * CAP
     outgoing = call(
         route_kernel,

time: 69.9 us -> 69 us (0.987)
  waiting for transfers between devices: 11.6 us -> 9.55 us
  starting transfers between devices: 24.6 us -> 25.5 us
    ppermute x4, waiting for transfers between devices: 4.67 us -> 2.57 us  [exchange(): lat_b = lax.ppermute(lat_b, 'lat', lat_far)]
    ppermute x4, starting transfers between devices: 3.75 us -> 4.66 us  [exchange(): lat_b = lax.ppermute(lat_b, 'lat', lat_far)]
  transfers between devices with their start and end apart: 17 -> 17, of which waited for: 6 -> 4; matrix products, arithmetic and copies ran while one was open for 0% -> 0% of each run, Pallas kernels for 21% -> 21%
where the time goes in v8:
time: 69 us; the launch traced here: 68.5 us
  Pallas kernels  32.3 us (47%)
  starting transfers between devices  25.5 us (37%)
  waiting for transfers between devices  9.55 us (14%)
  between operations  0.99 us (1%)
    pallas_call x12, Pallas kernels, call(): pl.pallas_call(kernel, out_shape=tuple((pltpu.HBM(o.shape, o.dtype) if i...  32.3 us
    all_to_all x1, starting transfers between devices, body(): lax.all_to_all(outgoing, ('lat', 'lon'), split_axis=0, concat_axis=0, til...  11.1 us
    ppermute x4, starting transfers between devices, exchange(): lon_b = lax.ppermute(lon_b, 'lon', lon_far)  9.58 us
    all_to_all x1, waiting for transfers between devices, body(): lax.all_to_all(outgoing, ('lat', 'lon'), split_axis=0, concat_axis=0, til...  5.52 us
    ppermute x4, starting transfers between devices, exchange(): lat_b = lax.ppermute(lat_b, 'lat', lat_far)  4.66 us
    ppermute x4, waiting for transfers between devices, exchange(): lat_b = lax.ppermute(lat_b, 'lat', lat_far)  2.57 us
    ppermute x4, waiting for transfers between devices, exchange(): lon_b = lax.ppermute(lon_b, 'lon', lon_far)  1.44 us
  transfers between devices with their start and end apart: 17, of which 4 were waited for; matrix products, arithmetic and copies ran while one was open for 0% of the time, Pallas kernels for 21%

profile of v8, /device:TPU:0, one launch (start us, length us, event | category | flops | bytes accessed | tf_op | source)
XLA Modules:
  0.0 68.5 jit_solution(9759254383312864050)
XLA Ops:
  0.6 2.5 %shard_map.104 = f32[128,2,128]{2,1,0:T(2,128)} custom-call(s32[4,1,512]{2,1,0:T(1,128)} %bitcast.9, s32[4,512]{1,0:T(4,128)} %cell_in.1, s32[4,512]{1,0:T(4,128)} %index_in.1, f32[3,4,512]{2,1,0:T(4,128)} %bitcast.7, f32[4,512]{1,0:T(4,128)} %prec_in.1), custom_call_target="tpu_custom_call" | custom-call | tf_op jit(solution)/shard_map/pallas_call | solution.py:45
  3.1 11.1 %all-to-all-start = ((f32[128,2,128]{2,1,0:T(2,128)}), f32[128,2,128]{2,1,0:T(2,128)S(1)}, u32[]{:S(2)}, u32[]{:S(2)}) async-start(f32[128,2,128]{2,1,0:T(2,128)} %shard_map.104), calls=%async_computation | async-start | bytes 262144 | tf_op jit(solution)/shard_map/all_to_all | solution.py:481
  14.5 3.9 %shard_map.105 = (f32[180,32,128]{2,1,0:T(8,128)}, f32[106,32,128]{2,1,0:T(8,128)S(1)}, f32[4,36,128]{2,1,0:T(8,128)S(1)}, f32[4,1,1152]{2,1,0:T(1,128)S(1)}, bf16[3,36,32,128]{3,2,1,0:T(8,128)(2,1)S(1)}) custom-call(f32[4,128]{1,0:T(4,128)S(1)} %broadcast_in_dim.2.mask_ref, f32[35,32,128]{2,1,0:T(8,128)} %mix_in.1, f32[4,36,32,128]{3,2,1,0:T(8,128)} %tr_in.1, ...), custom_call_target="tpu_custom_call" | custom-call | tf_op jit(solution)/shard_map/pallas_call | solution.py:45
  18.4 5.5 %all-to-all-done.got_ref = f32[128,2,128]{2,1,0:T(2,128)S(1)} async-done(((f32[128,2,128]{2,1,0:T(2,128)}), f32[128,2,128]{2,1,0:T(2,128)S(1)}, u32[]{:S(2)}, u32[]{:S(2)}) %all-to-all-start) | async-done | bytes 131104 | tf_op jit(solution)/shard_map/all_to_all | solution.py:481
  23.9 3.9 %shard_map.106 = (f32[3,36,32,128]{3,2,1,0:T(8,128)S(1)}, f32[4,8,1024]{2,1,0:T(8,128)S(1)}, bf16[3,36,64]{2,1,0:T(8,128)(2,1)S(1)}, bf16[3,36,32,128]{3,2,1,0:T(8,128)(2,1)S(1)}, f32[180,32,128]{2,1,0:T(8,128)S(1)}) custom-call(f32[128,2,128]{2,1,0:T(2,128)S(1)} %all-to-all-done.got_ref, bf16[3,36,32,128]{3,2,1,0:T(8,128)(2,1)S(1)} %get-tuple-element.39.traj_ref, ...), custom_call_target="tpu_custom_call" | custom-call | tf_op jit(solution)/shard_map/pallas_call | solution.py:45
  27.8 1.8 %shard_map.107 = (f32[3,36,32,128]{3,2,1,0:T(8,128)S(1)}, f32[1,7168]{1,0:T(1,128)S(1)}, f32[1,7168]{1,0:T(1,128)S(1)}, bf16[108,128]{1,0:T(8,128)(2,1)S(1)}, bf16[108,128]{1,0:T(8,128)(2,1)S(1)}) custom-call(f32[3,36,32,128]{3,2,1,0:T(8,128)S(1)} %get-tuple-element.41.force_ref, f32[106,32,128]{2,1,0:T(8,128)S(1)} %get-tuple-element.42.column_ref.refs_1_.refs_2_, ...), custom_call_target="tpu_custom_call" | custom-call | tf_op jit(solution)/shard_map/pallas_call | solution.py:45
  29.7 1.4 %collective-permute-start.2 = (f32[1,7168]{1,0:T(1,128)S(1)}, f32[1,7168]{1,0:T(1,128)S(1)}, u32[]{:S(2)}, u32[]{:S(2)}) collective-permute-start(f32[1,7168]{1,0:T(1,128)S(1)} %get-tuple-element.49), channel_id=1, source_target_pairs={{1,2},{2,1},{3,4},{4,3},{5,6},{6,5},{7,8},{8,7},{9,10},{10,9},{11,... | collective-permute-start | bytes 86024 | tf_op jit(solution)/shard_map/ppermute | solution.py:445
  31.7 3.2 %shard_map.108 = (f32[3,36,32,128]{3,2,1,0:T(8,128)S(1)}, bf16[3,36,32,128]{3,2,1,0:T(8,128)(2,1)S(1)}) custom-call(f32[4,8,1024]{2,1,0:T(8,128)S(1)} %get-tuple-element.51.snd_ref, bf16[3,36,32,128]{3,2,1,0:T(8,128)(2,1)S(1)} %get-tuple-element.52.traj_ref, bf16[3,36,64]{2,1,0:T(8,128)(2,1)S(1)} %get-tuple-element.53.table_ref, ...), custom_call_target="tpu_custom_call" | custom-call | tf_op jit(solution)/shard_map/pallas_call | solution.py:45
  34.9 0.7 collective-permute-done.lat_b
  35.5 1.4 %collective-permute-done.2.lon_b = f32[1,7168]{1,0:T(1,128)S(1)} collective-permute-done((f32[1,7168]{1,0:T(1,128)S(1)}, f32[1,7168]{1,0:T(1,128)S(1)}, u32[]{:S(2)}, u32[]{:S(2)}) %collective-permute-start.2) | collective-permute-done | bytes 28704 | tf_op jit(solution)/shard_map/ppermute | solution.py:445
  36.9 2.7 %shard_map.109 = (f32[3,36,32,128]{3,2,1,0:T(8,128)S(1)}, f32[1,7168]{1,0:T(1,128)S(1)}, f32[1,7168]{1,0:T(1,128)S(1)}, bf16[108,128]{1,0:T(8,128)(2,1)S(1)}, bf...) custom-call(f32[4,128]{1,0:T(4,128)S(1)} %broadcast_in_dim.2.mask_ref, ...), custom_call_target="tpu_custom_call" | custom-call | tf_op jit(solution)/shard_map/pallas_call | solution.py:45
  39.6 2.8 %collective-permute-start.6 = (f32[1,7168]{1,0:T(1,128)S(1)}, f32[1,7168]{1,0:T(1,128)S(1)}, u32[]{:S(2)}, u32[]{:S(2)}) collective-permute-start(f32[1,7168]{1,0:T(1,128)S(1)} %get-tuple-element.58), channel_id=1, source_target_pairs={{1,2},{2,1},{3,4},{4,3},{5,6},{6,5},{7,8},{8,7},{9,10},{10,9},{11,... | collective-permute-start | bytes 86024 | tf_op jit(solution)/shard_map/ppermute | solution.py:445
  42.4 1.4 %collective-permute-start.4 = (bf16[108,128]{1,0:T(8,128)(2,1)S(1)}, bf16[108,128]{1,0:T(8,128)(2,1)S(1)}, u32[]{:S(2)}, u32[]{:S(2)}) collective-permute-start(bf16[108,128]{1,0:T(8,128)(2,1)S(1)} %get-tuple-element.56), channel_id=1, source_target_pairs={{16,32},{32,16},{48,64},{64,48},{80,96},{96,80},{112,0},{0,112},{1... | collective-permute-start | bytes 82952 | tf_op jit(solution)/shard_map/ppermute | solution.py:446
  43.8 3.1 %shard_map.110 = (f32[3,36,32,128]{3,2,1,0:T(8,128)S(1)}, bf16[3,36,32,128]{3,2,1,0:T(8,128)(2,1)S(1)}) custom-call(f32[4,8,1024]{2,1,0:T(8,128)S(1)} %get-tuple-element.51.snd_ref, bf16[3,36,32,128]{3,2,1,0:T(8,128)(2,1)S(1)} %get-tuple-element.61.traj_ref, bf16[3,36,64]{2,1,0:T(8,128)(2,1)S(1)} %get-tuple-element.53.table_ref, ...), custom_call_target="tpu_custom_call" | custom-call | tf_op jit(solution)/shard_map/pallas_call | solution.py:45
  46.9 2.7 %shard_map.111 = (f32[3,36,32,128]{3,2,1,0:T(8,128)S(1)}, f32[1,7168]{1,0:T(1,128)S(1)}, f32[1,7168]{1,0:T(1,128)S(1)}, bf16[108,128]{1,0:T(8,128)(2,1)S(1)}, bf...) custom-call(f32[4,128]{1,0:T(4,128)S(1)} %broadcast_in_dim.2.mask_ref, ...), custom_call_target="tpu_custom_call" | custom-call | tf_op jit(solution)/shard_map/pallas_call | solution.py:45
  49.6 2.7 %collective-permute-start.10 = (f32[1,7168]{1,0:T(1,128)S(1)}, f32[1,7168]{1,0:T(1,128)S(1)}, u32[]{:S(2)}, u32[]{:S(2)}) collective-permute-start(f32[1,7168]{1,0:T(1,128)S(1)} %get-tuple-element.66), channel_id=1, source_target_pairs={{1,2},{2,1},{3,4},{4,3},{5,6},{6,5},{7,8},{8,7},{9,10},{10,9},{11,... | collective-permute-start | bytes 86024 | tf_op jit(solution)/shard_map/ppermute | solution.py:445
  52.3 1.3 %collective-permute-start.8 = (bf16[108,128]{1,0:T(8,128)(2,1)S(1)}, bf16[108,128]{1,0:T(8,128)(2,1)S(1)}, u32[]{:S(2)}, u32[]{:S(2)}) collective-permute-start(bf16[108,128]{1,0:T(8,128)(2,1)S(1)} %get-tuple-element.64), channel_id=1, source_target_pairs={{16,32},{32,16},{48,64},{64,48},{80,96},{96,80},{112,0},{0,112},{1... | collective-permute-start | bytes 82952 | tf_op jit(solution)/shard_map/ppermute | solution.py:446
  53.7 3.2 %shard_map.112.refs_1_ = f32[3,36,32,128]{3,2,1,0:T(8,128)S(1)} custom-call(f32[4,8,1024]{2,1,0:T(8,128)S(1)} %get-tuple-element.51.snd_ref, bf16[3,36,32,128]{3,2,1,0:T(8,128)(2,1)S(1)} %get-tuple-element.69.traj_ref, bf16[3,36,64]{2,1,0:T(8,128)(2,1)S(1)} %get-tuple-element.53.table_ref), custom_call_target="tpu_custom_call" | custom-call | tf_op jit(solution)/shard_map/pallas_call | solution.py:45
  56.9 2.0 %shard_map.113 = (f32[3,36,32,128]{3,2,1,0:T(8,128)S(1)}, f32[1,7168]{1,0:T(1,128)S(1)}, f32[1,7168]{1,0:T(1,128)S(1)}, bf16[108,128]{1,0:T(8,128)(2,1)S(1)}, bf...) custom-call(f32[4,128]{1,0:T(4,128)S(1)} %broadcast_in_dim.2.mask_ref, ...), custom_call_target="tpu_custom_call" | custom-call | tf_op jit(solution)/shard_map/pallas_call | solution.py:45
  58.9 2.8 %collective-permute-start.14 = (f32[1,7168]{1,0:T(1,128)S(1)}, f32[1,7168]{1,0:T(1,128)S(1)}, u32[]{:S(2)}, u32[]{:S(2)}) collective-permute-start(f32[1,7168]{1,0:T(1,128)S(1)} %get-tuple-element.73), channel_id=1, source_target_pairs={{1,2},{2,1},{3,4},{4,3},{5,6},{6,5},{7,8},{8,7},{9,10},{10,9},{11,... | collective-permute-start | bytes 86024 | tf_op jit(solution)/shard_map/ppermute | solution.py:445
  61.7 1.4 %collective-permute-start.12 = (bf16[108,128]{1,0:T(8,128)(2,1)S(1)}, bf16[108,128]{1,0:T(8,128)(2,1)S(1)}, u32[]{:S(2)}, u32[]{:S(2)}) collective-permute-start(bf16[108,128]{1,0:T(8,128)(2,1)S(1)} %get-tuple-element.71), channel_id=1, source_target_pairs={{16,32},{32,16},{48,64},{64,48},{80,96},{96,80},{112,0},{0,112},{1... | collective-permute-start | bytes 82952 | tf_op jit(solution)/shard_map/ppermute | solution.py:446
  63.1 1.2 %shard_map.114.w_in = f32[3,36,32,128]{3,2,1,0:T(8,128)S(1)} custom-call(f32[3,36,32,128]{3,2,1,0:T(8,128)S(1)} %get-tuple-element.70.v, f32[180,32,128]{2,1,0:T(8,128)S(1)} %get-tuple-element.43.coef_ref.refs_2_.refs_3_), custom_call_target="tpu_custom_call" | custom-call | tf_op jit(solution)/shard_map/pallas_call | solution.py:45
  64.3 1.9 %collective-permute-done.12.lat_b = bf16[108,128]{1,0:T(8,128)(2,1)S(1)} collective-permute-done((bf16[108,128]{1,0:T(8,128)(2,1)S(1)}, bf16[108,128]{1,0:T(8,128)(2,1)S(1)}, u32[]{:S(2)}, u32[]{:S(2)}) %collective-permute-start.12) | collective-permute-done | bytes 27680 | tf_op jit(solution)/shard_map/ppermute | solution.py:446
  66.2 2.1 %shard_map.115 = (f32[3,36,32,128]{3,2,1,0:T(8,128)}, f32[3,32,128]{2,1,0:T(8,128)}) custom-call(f32[4,128]{1,0:T(4,128)S(1)} %broadcast_in_dim.2.mask_ref, f32[3,36,32,128]{3,2,1,0:T(8,128)S(1)} %shard_map.114.w_in, bf16[108,128]{1,0:T(8,128)(2,1)S(1)} %collective-permute-done.12.lat_b, bf16[108,128]{1,0:T(8,128)(2,1)S(1)} %collective-permute-done.13.lat_a, ...), custom_call_target="tpu_custom_call" | custom-call | tf_op jit(solution)/shard_map/pallas_call | solution.py:45
  (24 shorter events, 0.9 us)
Async XLA Ops:
  3.1 20.8 %all-to-all-start = ((f32[128,2,128]{2,1,0:T(2,128)}), f32[128,2,128]{2,1,0:T(2,128)S(1)}, u32[]{:S(2)}, u32[]{:S(2)}) async-start(f32[128,2,128]{2,1,0:T(2,128)} %shard_map.104), calls=%async_computation | async-start | bytes 262144 | tf_op jit(solution)/shard_map/all_to_all | solution.py:481
  29.7 7.3 %collective-permute-start.2 = (f32[1,7168]{1,0:T(1,128)S(1)}, f32[1,7168]{1,0:T(1,128)S(1)}, u32[]{:S(2)}, u32[]{:S(2)}) collective-permute-start(f32[1,7168]{1,0:T(1,128)S(1)} %get-tuple-element.49), channel_id=1, source_target_pairs={{1,2},{2,1},{3,4},{4,3},{5,6},{6,5},{7,8},{8,7},{9,10},{10,9},{11,... | collective-permute-start | bytes 86024 | tf_op jit(solution)/shard_map/ppermute | solution.py:445
  31.0 5.9 %collective-permute-start.3 = (f32[1,7168]{1,0:T(1,128)S(1)}, f32[1,7168]{1,0:T(1,128)S(1)}, u32[]{:S(2)}, u32[]{:S(2)}) collective-permute-start(f32[1,7168]{1,0:T(1,128)S(1)} %get-tuple-element.50), channel_id=1, source_target_pairs={{0,1},{1,0},{2,3},{3,2},{4,5},{5,4},{6,7},{7,6},{8,9},{9,8},{10,11... | collective-permute-start | bytes 86024 | tf_op jit(solution)/shard_map/ppermute | solution.py:447
  31.0 4.5 %collective-permute-start = (bf16[108,128]{1,0:T(8,128)(2,1)S(1)}, bf16[108,128]{1,0:T(8,128)(2,1)S(1)}, u32[]{:S(2)}, u32[]{:S(2)}) collective-permute-start(bf16[108,128]{1,0:T(8,128)(2,1)S(1)} %get-tuple-element.47), channel_id=1, source_target_pairs={{16,32},{32,16},{48,64},{64,48},{80,96},{96,80},{112,0},{0,112},{1... | collective-permute-start | bytes 82952 | tf_op jit(solution)/shard_map/ppermute | solution.py:446
  31.6 3.9 %collective-permute-start.1 = (bf16[108,128]{1,0:T(8,128)(2,1)S(1)}, bf16[108,128]{1,0:T(8,128)(2,1)S(1)}, u32[]{:S(2)}, u32[]{:S(2)}) collective-permute-start(bf16[108,128]{1,0:T(8,128)(2,1)S(1)} %get-tuple-element.48), channel_id=1, source_target_pairs={{0,16},{16,0},{32,48},{48,32},{64,80},{80,64},{96,112},{112,96},{1... | collective-permute-start | bytes 82952 | tf_op jit(solution)/shard_map/ppermute | solution.py:448
  39.6 7.3 %collective-permute-start.6 = (f32[1,7168]{1,0:T(1,128)S(1)}, f32[1,7168]{1,0:T(1,128)S(1)}, u32[]{:S(2)}, u32[]{:S(2)}) collective-permute-start(f32[1,7168]{1,0:T(1,128)S(1)} %get-tuple-element.58), channel_id=1, source_target_pairs={{1,2},{2,1},{3,4},{4,3},{5,6},{6,5},{7,8},{8,7},{9,10},{10,9},{11,... | collective-permute-start | bytes 86024 | tf_op jit(solution)/shard_map/ppermute | solution.py:445
  42.4 4.6 %collective-permute-start.7 = (f32[1,7168]{1,0:T(1,128)S(1)}, f32[1,7168]{1,0:T(1,128)S(1)}, u32[]{:S(2)}, u32[]{:S(2)}) collective-permute-start(f32[1,7168]{1,0:T(1,128)S(1)} %get-tuple-element.59), channel_id=1, source_target_pairs={{0,1},{1,0},{2,3},{3,2},{4,5},{5,4},{6,7},{7,6},{8,9},{9,8},{10,11... | collective-permute-start | bytes 86024 | tf_op jit(solution)/shard_map/ppermute | solution.py:447
  42.4 4.5 %collective-permute-start.4 = (bf16[108,128]{1,0:T(8,128)(2,1)S(1)}, bf16[108,128]{1,0:T(8,128)(2,1)S(1)}, u32[]{:S(2)}, u32[]{:S(2)}) collective-permute-start(bf16[108,128]{1,0:T(8,128)(2,1)S(1)} %get-tuple-element.56), channel_id=1, source_target_pairs={{16,32},{32,16},{48,64},{64,48},{80,96},{96,80},{112,0},{0,112},{1... | collective-permute-start | bytes 82952 | tf_op jit(solution)/shard_map/ppermute | solution.py:446
  43.8 3.2 %collective-permute-start.5 = (bf16[108,128]{1,0:T(8,128)(2,1)S(1)}, bf16[108,128]{1,0:T(8,128)(2,1)S(1)}, u32[]{:S(2)}, u32[]{:S(2)}) collective-permute-start(bf16[108,128]{1,0:T(8,128)(2,1)S(1)} %get-tuple-element.57), channel_id=1, source_target_pairs={{0,16},{16,0},{32,48},{48,32},{64,80},{80,64},{96,112},{112,96},{1... | collective-permute-start | bytes 82952 | tf_op jit(solution)/shard_map/ppermute | solution.py:448
  49.6 7.3 %collective-permute-start.10 = (f32[1,7168]{1,0:T(1,128)S(1)}, f32[1,7168]{1,0:T(1,128)S(1)}, u32[]{:S(2)}, u32[]{:S(2)}) collective-permute-start(f32[1,7168]{1,0:T(1,128)S(1)} %get-tuple-element.66), channel_id=1, source_target_pairs={{1,2},{2,1},{3,4},{4,3},{5,6},{6,5},{7,8},{8,7},{9,10},{10,9},{11,... | collective-permute-start | bytes 86024 | tf_op jit(solution)/shard_map/ppermute | solution.py:445
  52.3 4.6 %collective-permute-start.11 = (f32[1,7168]{1,0:T(1,128)S(1)}, f32[1,7168]{1,0:T(1,128)S(1)}, u32[]{:S(2)}, u32[]{:S(2)}) collective-permute-start(f32[1,7168]{1,0:T(1,128)S(1)} %get-tuple-element.67), channel_id=1, source_target_pairs={{0,1},{1,0},{2,3},{3,2},{4,5},{5,4},{6,7},{7,6},{8,9},{9,8},{10,11... | collective-permute-start | bytes 86024 | tf_op jit(solution)/shard_map/ppermute | solution.py:447
  52.3 4.5 %collective-permute-start.8 = (bf16[108,128]{1,0:T(8,128)(2,1)S(1)}, bf16[108,128]{1,0:T(8,128)(2,1)S(1)}, u32[]{:S(2)}, u32[]{:S(2)}) collective-permute-start(bf16[108,128]{1,0:T(8,128)(2,1)S(1)} %get-tuple-element.64), channel_id=1, source_target_pairs={{16,32},{32,16},{48,64},{64,48},{80,96},{96,80},{112,0},{0,112},{1... | collective-permute-start | bytes 82952 | tf_op jit(solution)/shard_map/ppermute | solution.py:446
  53.7 3.2 %collective-permute-start.9 = (bf16[108,128]{1,0:T(8,128)(2,1)S(1)}, bf16[108,128]{1,0:T(8,128)(2,1)S(1)}, u32[]{:S(2)}, u32[]{:S(2)}) collective-permute-start(bf16[108,128]{1,0:T(8,128)(2,1)S(1)} %get-tuple-element.65), channel_id=1, source_target_pairs={{0,16},{16,0},{32,48},{48,32},{64,80},{80,64},{96,112},{112,96},{1... | collective-permute-start | bytes 82952 | tf_op jit(solution)/shard_map/ppermute | solution.py:448
  58.9 7.3 %collective-permute-start.14 = (f32[1,7168]{1,0:T(1,128)S(1)}, f32[1,7168]{1,0:T(1,128)S(1)}, u32[]{:S(2)}, u32[]{:S(2)}) collective-permute-start(f32[1,7168]{1,0:T(1,128)S(1)} %get-tuple-element.73), channel_id=1, source_target_pairs={{1,2},{2,1},{3,4},{4,3},{5,6},{6,5},{7,8},{8,7},{9,10},{10,9},{11,... | collective-permute-start | bytes 86024 | tf_op jit(solution)/shard_map/ppermute | solution.py:445
  61.7 4.5 %collective-permute-start.15 = (f32[1,7168]{1,0:T(1,128)S(1)}, f32[1,7168]{1,0:T(1,128)S(1)}, u32[]{:S(2)}, u32[]{:S(2)}) collective-permute-start(f32[1,7168]{1,0:T(1,128)S(1)} %get-tuple-element.74), channel_id=1, source_target_pairs={{0,1},{1,0},{2,3},{3,2},{4,5},{5,4},{6,7},{7,6},{8,9},{9,8},{10,11... | collective-permute-start | bytes 86024 | tf_op jit(solution)/shard_map/ppermute | solution.py:447
  61.7 4.5 %collective-permute-start.12 = (bf16[108,128]{1,0:T(8,128)(2,1)S(1)}, bf16[108,128]{1,0:T(8,128)(2,1)S(1)}, u32[]{:S(2)}, u32[]{:S(2)}) collective-permute-start(bf16[108,128]{1,0:T(8,128)(2,1)S(1)} %get-tuple-element.71), channel_id=1, source_target_pairs={{16,32},{32,16},{48,64},{64,48},{80,96},{96,80},{112,0},{0,112},{1... | collective-permute-start | bytes 82952 | tf_op jit(solution)/shard_map/ppermute | solution.py:446
  63.0 3.1 %collective-permute-start.13 = (bf16[108,128]{1,0:T(8,128)(2,1)S(1)}, bf16[108,128]{1,0:T(8,128)(2,1)S(1)}, u32[]{:S(2)}, u32[]{:S(2)}) collective-permute-start(bf16[108,128]{1,0:T(8,128)(2,1)S(1)} %get-tuple-element.72), channel_id=1, source_target_pairs={{0,16},{16,0},{32,48},{48,32},{64,80},{80,64},{96,112},{112,96},{1... | collective-permute-start | bytes 82952 | tf_op jit(solution)/shard_map/ppermute | solution.py:448

commit v9 on v8

--- a/solution.py
+++ b/solution.py
@@ -381,10 +381,9 @@
         copy.wait()
 
 
-def first_step_kernel(force_ref, column_ref, coef_ref, lat_w, lon_w, w_out, *refs):
-    edges, v = refs[:4], refs[4]
+def first_step_kernel(force_ref, column_ref, lat_w, lon_w, v, *edges):
     vertical(lambda t, k: 0.0, force_ref, column_ref, v)
-    horizontal(v, coef_ref, w_out, (lat_w, lon_w), edges)
+    horizontal(v, None, None, (lat_w, lon_w), edges)
 
 
 def step_kernel(
@@ -547,11 +546,13 @@
 
     v = pltpu.VMEM(field.shape, F32)
     moved = (field, lon_edge, lon_edge, lat_edge, lat_edge)
-    w, *edges = call(first_step_kernel, moved, force, *fixed, scratch=(v,))
+    w, *edges = call(first_step_kernel, moved, force, column, lat_w, lon_w)
     flux = []
     for s in range(steps - 2, -1, -1):
         halos = exchange(*edges)
         force, now = forcing(s, now)
+        if s == steps - 2:
+            w = call(interior_kernel, field, w, coef)
         *done, flux = call(
             functools.partial(step_kernel, s == steps - 2, s > 0),
             moved + (plane,),

time: 69 us -> 69.3 us (level)
  waiting for transfers between devices: 9.55 us -> 8.81 us
  starting transfers between devices: 25.5 us -> 26.2 us
    pallas_call x12 -> x13, Pallas kernels: 32.3 us -> 32.9 us  [call(): pl.pallas_call(kernel, out_shape=tuple((pltpu.HBM(o.shape, o.dtype) if i...]
  transfers between devices with their start and end apart: 17 -> 17, of which waited for: 4 -> 4; matrix products, arithmetic and copies ran while one was open for 0% -> 0% of each run, Pallas kernels for 21% -> 23%
where the time goes in v9:
time: 69.3 us; the launch traced here: 69.1 us
  Pallas kernels  32.9 us (47%)
  starting transfers between devices  26.2 us (38%)
  waiting for transfers between devices  8.81 us (13%)
  between operations  1 us (1%)
    pallas_call x13, Pallas kernels, call(): pl.pallas_call(kernel, out_shape=tuple((pltpu.HBM(o.shape, o.dtype) if i...  32.9 us
    all_to_all x1, starting transfers between devices, body(): lax.all_to_all(outgoing, ('lat', 'lon'), split_axis=0, concat_axis=0, til...  11.1 us
    ppermute x4, starting transfers between devices, exchange(): lon_b = lax.ppermute(lon_b, 'lon', lon_far)  9.8 us
    all_to_all x1, waiting for transfers between devices, body(): lax.all_to_all(outgoing, ('lat', 'lon'), split_axis=0, concat_axis=0, til...  5.52 us
    ppermute x4, starting transfers between devices, exchange(): lat_b = lax.ppermute(lat_b, 'lat', lat_far)  5.15 us
    ppermute x4, waiting for transfers between devices, exchange(): lat_b = lax.ppermute(lat_b, 'lat', lat_far)  1.92 us
  transfers between devices with their start and end apart: 17, of which 4 were waited for; matrix products, arithmetic and copies ran while one was open for 0% of the time, Pallas kernels for 23%

profile of v9, /device:TPU:0, one launch (start us, length us, event | category | flops | bytes accessed | tf_op | source)
XLA Modules:
  0.0 69.1 jit_solution(12105813617207398988)
XLA Ops:
  0.6 2.5 %shard_map.104 = f32[128,2,128]{2,1,0:T(2,128)} custom-call(s32[4,1,512]{2,1,0:T(1,128)} %bitcast.9, s32[4,512]{1,0:T(4,128)} %cell_in.1, s32[4,512]{1,0:T(4,128)} %index_in.1, f32[3,4,512]{2,1,0:T(4,128)} %bitcast.7, f32[4,512]{1,0:T(4,128)} %prec_in.1), custom_call_target="tpu_custom_call" | custom-call | tf_op jit(solution)/shard_map/pallas_call | solution.py:45
  3.1 11.1 %all-to-all-start = ((f32[128,2,128]{2,1,0:T(2,128)}), f32[128,2,128]{2,1,0:T(2,128)S(1)}, u32[]{:S(2)}, u32[]{:S(2)}) async-start(f32[128,2,128]{2,1,0:T(2,128)} %shard_map.104), calls=%async_computation | async-start | bytes 262144 | tf_op jit(solution)/shard_map/all_to_all | solution.py:480
  14.5 3.9 %shard_map.105 = (f32[180,32,128]{2,1,0:T(8,128)}, f32[106,32,128]{2,1,0:T(8,128)S(1)}, f32[4,36,128]{2,1,0:T(8,128)S(1)}, f32[4,1,1152]{2,1,0:T(1,128)S(1)}, bf16[3,36,32,128]{3,2,1,0:T(8,128)(2,1)S(1)}) custom-call(f32[4,128]{1,0:T(4,128)S(1)} %broadcast_in_dim.2.mask_ref, f32[35,32,128]{2,1,0:T(8,128)} %mix_in.1, f32[4,36,32,128]{3,2,1,0:T(8,128)} %tr_in.1, ...), custom_call_target="tpu_custom_call" | custom-call | tf_op jit(solution)/shard_map/pallas_call | solution.py:45
  18.4 5.5 %all-to-all-done.got_ref = f32[128,2,128]{2,1,0:T(2,128)S(1)} async-done(((f32[128,2,128]{2,1,0:T(2,128)}), f32[128,2,128]{2,1,0:T(2,128)S(1)}, u32[]{:S(2)}, u32[]{:S(2)}) %all-to-all-start) | async-done | bytes 131104 | tf_op jit(solution)/shard_map/all_to_all | solution.py:480
  23.9 3.9 %shard_map.106 = (f32[3,36,32,128]{3,2,1,0:T(8,128)S(1)}, f32[4,8,1024]{2,1,0:T(8,128)S(1)}, bf16[3,36,64]{2,1,0:T(8,128)(2,1)S(1)}, bf16[3,36,32,128]{3,2,1,0:T(8,128)(2,1)S(1)}, f32[180,32,128]{2,1,0:T(8,128)S(1)}) custom-call(f32[128,2,128]{2,1,0:T(2,128)S(1)} %all-to-all-done.got_ref, bf16[3,36,32,128]{3,2,1,0:T(8,128)(2,1)S(1)} %get-tuple-element.39.traj_ref, ...), custom_call_target="tpu_custom_call" | custom-call | tf_op jit(solution)/shard_map/pallas_call | solution.py:45
  27.8 1.1 %shard_map.107 = (f32[3,36,32,128]{3,2,1,0:T(8,128)S(1)}, f32[1,7168]{1,0:T(1,128)S(1)}, f32[1,7168]{1,0:T(1,128)S(1)}, bf16[108,128]{1,0:T(8,128)(2,1)S(1)}, bf16[108,128]{1,0:T(8,128)(2,1)S(1)}) custom-call(f32[3,36,32,128]{3,2,1,0:T(8,128)S(1)} %get-tuple-element.41.force_ref, f32[106,32,128]{2,1,0:T(8,128)S(1)} %get-tuple-element.42.column_ref.refs_1_.refs_2_, ...), custom_call_target="tpu_custom_call" | custom-call | tf_op jit(solution)/shard_map/pallas_call | solution.py:45
  28.9 1.4 %collective-permute-start.2 = (f32[1,7168]{1,0:T(1,128)S(1)}, f32[1,7168]{1,0:T(1,128)S(1)}, u32[]{:S(2)}, u32[]{:S(2)}) collective-permute-start(f32[1,7168]{1,0:T(1,128)S(1)} %get-tuple-element.49), channel_id=1, source_target_pairs={{1,2},{2,1},{3,4},{4,3},{5,6},{6,5},{7,8},{8,7},{9,10},{10,9},{11,... | collective-permute-start | bytes 86024 | tf_op jit(solution)/shard_map/ppermute | solution.py:444
  30.9 1.3 %shard_map.108.w_in = f32[3,36,32,128]{3,2,1,0:T(8,128)S(1)} custom-call(f32[3,36,32,128]{3,2,1,0:T(8,128)S(1)} %get-tuple-element.45.v, f32[180,32,128]{2,1,0:T(8,128)S(1)} %get-tuple-element.46.coef_ref.refs_2_.refs_3_), custom_call_target="tpu_custom_call" | custom-call | tf_op jit(solution)/shard_map/pallas_call | solution.py:45
  32.2 3.1 %shard_map.109 = (f32[3,36,32,128]{3,2,1,0:T(8,128)S(1)}, bf16[3,36,32,128]{3,2,1,0:T(8,128)(2,1)S(1)}) custom-call(f32[4,8,1024]{2,1,0:T(8,128)S(1)} %get-tuple-element.51.snd_ref, bf16[3,36,32,128]{3,2,1,0:T(8,128)(2,1)S(1)} %get-tuple-element.52.traj_ref, bf16[3,36,64]{2,1,0:T(8,128)(2,1)S(1)} %get-tuple-element.53.table_ref, ...), custom_call_target="tpu_custom_call" | custom-call | tf_op jit(solution)/shard_map/pallas_call | solution.py:45
  35.4 0.8 %collective-permute-done.2.lon_b = f32[1,7168]{1,0:T(1,128)S(1)} collective-permute-done((f32[1,7168]{1,0:T(1,128)S(1)}, f32[1,7168]{1,0:T(1,128)S(1)}, u32[]{:S(2)}, u32[]{:S(2)}) %collective-permute-start.2) | collective-permute-done | bytes 28704 | tf_op jit(solution)/shard_map/ppermute | solution.py:444
  36.2 2.7 %shard_map.110 = (f32[3,36,32,128]{3,2,1,0:T(8,128)S(1)}, f32[1,7168]{1,0:T(1,128)S(1)}, f32[1,7168]{1,0:T(1,128)S(1)}, bf16[108,128]{1,0:T(8,128)(2,1)S(1)}, bf...) custom-call(f32[4,128]{1,0:T(4,128)S(1)} %broadcast_in_dim.2.mask_ref, f32[3,36,32,128]{3,2,1,0:T(8,128)S(1)} %shard_map.108.w_in, ...), custom_call_target="tpu_custom_call" | custom-call | tf_op jit(solution)/shard_map/pallas_call | solution.py:45
  38.9 3.5 %collective-permute-start.6 = (f32[1,7168]{1,0:T(1,128)S(1)}, f32[1,7168]{1,0:T(1,128)S(1)}, u32[]{:S(2)}, u32[]{:S(2)}) collective-permute-start(f32[1,7168]{1,0:T(1,128)S(1)} %get-tuple-element.58), channel_id=1, source_target_pairs={{1,2},{2,1},{3,4},{4,3},{5,6},{6,5},{7,8},{8,7},{9,10},{10,9},{11,... | collective-permute-start | bytes 86024 | tf_op jit(solution)/shard_map/ppermute | solution.py:444
  42.3 1.9 %collective-permute-start.4 = (bf16[108,128]{1,0:T(8,128)(2,1)S(1)}, bf16[108,128]{1,0:T(8,128)(2,1)S(1)}, u32[]{:S(2)}, u32[]{:S(2)}) collective-permute-start(bf16[108,128]{1,0:T(8,128)(2,1)S(1)} %get-tuple-element.56), channel_id=1, source_target_pairs={{16,32},{32,16},{48,64},{64,48},{80,96},{96,80},{112,0},{0,112},{1... | collective-permute-start | bytes 82952 | tf_op jit(solution)/shard_map/ppermute | solution.py:445
  44.3 3.2 %shard_map.111 = (f32[3,36,32,128]{3,2,1,0:T(8,128)S(1)}, bf16[3,36,32,128]{3,2,1,0:T(8,128)(2,1)S(1)}) custom-call(f32[4,8,1024]{2,1,0:T(8,128)S(1)} %get-tuple-element.51.snd_ref, bf16[3,36,32,128]{3,2,1,0:T(8,128)(2,1)S(1)} %get-tuple-element.61.traj_ref, bf16[3,36,64]{2,1,0:T(8,128)(2,1)S(1)} %get-tuple-element.53.table_ref, ...), custom_call_target="tpu_custom_call" | custom-call | tf_op jit(solution)/shard_map/pallas_call | solution.py:45
  47.5 2.7 %shard_map.112 = (f32[3,36,32,128]{3,2,1,0:T(8,128)S(1)}, f32[1,7168]{1,0:T(1,128)S(1)}, f32[1,7168]{1,0:T(1,128)S(1)}, bf16[108,128]{1,0:T(8,128)(2,1)S(1)}, bf...) custom-call(f32[4,128]{1,0:T(4,128)S(1)} %broadcast_in_dim.2.mask_ref, ...), custom_call_target="tpu_custom_call" | custom-call | tf_op jit(solution)/shard_map/pallas_call | solution.py:45
  50.2 2.2 %collective-permute-start.10 = (f32[1,7168]{1,0:T(1,128)S(1)}, f32[1,7168]{1,0:T(1,128)S(1)}, u32[]{:S(2)}, u32[]{:S(2)}) collective-permute-start(f32[1,7168]{1,0:T(1,128)S(1)} %get-tuple-element.66), channel_id=1, source_target_pairs={{1,2},{2,1},{3,4},{4,3},{5,6},{6,5},{7,8},{8,7},{9,10},{10,9},{11,... | collective-permute-start | bytes 86024 | tf_op jit(solution)/shard_map/ppermute | solution.py:444
  52.4 1.3 %collective-permute-start.8 = (bf16[108,128]{1,0:T(8,128)(2,1)S(1)}, bf16[108,128]{1,0:T(8,128)(2,1)S(1)}, u32[]{:S(2)}, u32[]{:S(2)}) collective-permute-start(bf16[108,128]{1,0:T(8,128)(2,1)S(1)} %get-tuple-element.64), channel_id=1, source_target_pairs={{16,32},{32,16},{48,64},{64,48},{80,96},{96,80},{112,0},{0,112},{1... | collective-permute-start | bytes 82952 | tf_op jit(solution)/shard_map/ppermute | solution.py:445
  53.7 3.2 %shard_map.113.refs_1_ = f32[3,36,32,128]{3,2,1,0:T(8,128)S(1)} custom-call(f32[4,8,1024]{2,1,0:T(8,128)S(1)} %get-tuple-element.51.snd_ref, bf16[3,36,32,128]{3,2,1,0:T(8,128)(2,1)S(1)} %get-tuple-element.69.traj_ref, bf16[3,36,64]{2,1,0:T(8,128)(2,1)S(1)} %get-tuple-element.53.table_ref), custom_call_target="tpu_custom_call" | custom-call | tf_op jit(solution)/shard_map/pallas_call | solution.py:45
  57.5 2.0 %shard_map.114 = (f32[3,36,32,128]{3,2,1,0:T(8,128)S(1)}, f32[1,7168]{1,0:T(1,128)S(1)}, f32[1,7168]{1,0:T(1,128)S(1)}, bf16[108,128]{1,0:T(8,128)(2,1)S(1)}, bf...) custom-call(f32[4,128]{1,0:T(4,128)S(1)} %broadcast_in_dim.2.mask_ref, ...), custom_call_target="tpu_custom_call" | custom-call | tf_op jit(solution)/shard_map/pallas_call | solution.py:45
  59.5 2.8 %collective-permute-start.14 = (f32[1,7168]{1,0:T(1,128)S(1)}, f32[1,7168]{1,0:T(1,128)S(1)}, u32[]{:S(2)}, u32[]{:S(2)}) collective-permute-start(f32[1,7168]{1,0:T(1,128)S(1)} %get-tuple-element.73), channel_id=1, source_target_pairs={{1,2},{2,1},{3,4},{4,3},{5,6},{6,5},{7,8},{8,7},{9,10},{10,9},{11,... | collective-permute-start | bytes 86024 | tf_op jit(solution)/shard_map/ppermute | solution.py:444
  62.2 1.4 %collective-permute-start.12 = (bf16[108,128]{1,0:T(8,128)(2,1)S(1)}, bf16[108,128]{1,0:T(8,128)(2,1)S(1)}, u32[]{:S(2)}, u32[]{:S(2)}) collective-permute-start(bf16[108,128]{1,0:T(8,128)(2,1)S(1)} %get-tuple-element.71), channel_id=1, source_target_pairs={{16,32},{32,16},{48,64},{64,48},{80,96},{96,80},{112,0},{0,112},{1... | collective-permute-start | bytes 82952 | tf_op jit(solution)/shard_map/ppermute | solution.py:445
  63.6 1.2 %shard_map.115.w_in = f32[3,36,32,128]{3,2,1,0:T(8,128)S(1)} custom-call(f32[3,36,32,128]{3,2,1,0:T(8,128)S(1)} %get-tuple-element.70.v, f32[180,32,128]{2,1,0:T(8,128)S(1)} %get-tuple-element.46.coef_ref.refs_2_.refs_3_), custom_call_target="tpu_custom_call" | custom-call | tf_op jit(solution)/shard_map/pallas_call | solution.py:45
  64.9 1.9 %collective-permute-done.12.lat_b = bf16[108,128]{1,0:T(8,128)(2,1)S(1)} collective-permute-done((bf16[108,128]{1,0:T(8,128)(2,1)S(1)}, bf16[108,128]{1,0:T(8,128)(2,1)S(1)}, u32[]{:S(2)}, u32[]{:S(2)}) %collective-permute-start.12) | collective-permute-done | bytes 27680 | tf_op jit(solution)/shard_map/ppermute | solution.py:445
  66.8 2.1 %shard_map.116 = (f32[3,36,32,128]{3,2,1,0:T(8,128)}, f32[3,32,128]{2,1,0:T(8,128)}) custom-call(f32[4,128]{1,0:T(4,128)S(1)} %broadcast_in_dim.2.mask_ref, f32[3,36,32,128]{3,2,1,0:T(8,128)S(1)} %shard_map.115.w_in, bf16[108,128]{1,0:T(8,128)(2,1)S(1)} %collective-permute-done.12.lat_b, bf16[108,128]{1,0:T(8,128)(2,1)S(1)} %collective-permute-done.13.lat_a, ...), custom_call_target="tpu_custom_call" | custom-call | tf_op jit(solution)/shard_map/pallas_call | solution.py:45
  (25 shorter events, 1.4 us)
Async XLA Ops:
  3.1 20.8 %all-to-all-start = ((f32[128,2,128]{2,1,0:T(2,128)}), f32[128,2,128]{2,1,0:T(2,128)S(1)}, u32[]{:S(2)}, u32[]{:S(2)}) async-start(f32[128,2,128]{2,1,0:T(2,128)} %shard_map.104), calls=%async_computation | async-start | bytes 262144 | tf_op jit(solution)/shard_map/all_to_all | solution.py:480
  28.9 7.3 %collective-permute-start.2 = (f32[1,7168]{1,0:T(1,128)S(1)}, f32[1,7168]{1,0:T(1,128)S(1)}, u32[]{:S(2)}, u32[]{:S(2)}) collective-permute-start(f32[1,7168]{1,0:T(1,128)S(1)} %get-tuple-element.49), channel_id=1, source_target_pairs={{1,2},{2,1},{3,4},{4,3},{5,6},{6,5},{7,8},{8,7},{9,10},{10,9},{11,... | collective-permute-start | bytes 86024 | tf_op jit(solution)/shard_map/ppermute | solution.py:444
  30.3 5.9 %collective-permute-start.3 = (f32[1,7168]{1,0:T(1,128)S(1)}, f32[1,7168]{1,0:T(1,128)S(1)}, u32[]{:S(2)}, u32[]{:S(2)}) collective-permute-start(f32[1,7168]{1,0:T(1,128)S(1)} %get-tuple-element.50), channel_id=1, source_target_pairs={{0,1},{1,0},{2,3},{3,2},{4,5},{5,4},{6,7},{7,6},{8,9},{9,8},{10,11... | collective-permute-start | bytes 86024 | tf_op jit(solution)/shard_map/ppermute | solution.py:446
  30.3 5.1 %collective-permute-start = (bf16[108,128]{1,0:T(8,128)(2,1)S(1)}, bf16[108,128]{1,0:T(8,128)(2,1)S(1)}, u32[]{:S(2)}, u32[]{:S(2)}) collective-permute-start(bf16[108,128]{1,0:T(8,128)(2,1)S(1)} %get-tuple-element.47), channel_id=1, source_target_pairs={{16,32},{32,16},{48,64},{64,48},{80,96},{96,80},{112,0},{0,112},{1... | collective-permute-start | bytes 82952 | tf_op jit(solution)/shard_map/ppermute | solution.py:445
  30.8 4.6 %collective-permute-start.1 = (bf16[108,128]{1,0:T(8,128)(2,1)S(1)}, bf16[108,128]{1,0:T(8,128)(2,1)S(1)}, u32[]{:S(2)}, u32[]{:S(2)}) collective-permute-start(bf16[108,128]{1,0:T(8,128)(2,1)S(1)} %get-tuple-element.48), channel_id=1, source_target_pairs={{0,16},{16,0},{32,48},{48,32},{64,80},{80,64},{96,112},{112,96},{1... | collective-permute-start | bytes 82952 | tf_op jit(solution)/shard_map/ppermute | solution.py:447
  38.9 8.6 %collective-permute-start.6 = (f32[1,7168]{1,0:T(1,128)S(1)}, f32[1,7168]{1,0:T(1,128)S(1)}, u32[]{:S(2)}, u32[]{:S(2)}) collective-permute-start(f32[1,7168]{1,0:T(1,128)S(1)} %get-tuple-element.58), channel_id=1, source_target_pairs={{1,2},{2,1},{3,4},{4,3},{5,6},{6,5},{7,8},{8,7},{9,10},{10,9},{11,... | collective-permute-start | bytes 86024 | tf_op jit(solution)/shard_map/ppermute | solution.py:444
  42.3 5.2 %collective-permute-start.7 = (f32[1,7168]{1,0:T(1,128)S(1)}, f32[1,7168]{1,0:T(1,128)S(1)}, u32[]{:S(2)}, u32[]{:S(2)}) collective-permute-start(f32[1,7168]{1,0:T(1,128)S(1)} %get-tuple-element.59), channel_id=1, source_target_pairs={{0,1},{1,0},{2,3},{3,2},{4,5},{5,4},{6,7},{7,6},{8,9},{9,8},{10,11... | collective-permute-start | bytes 86024 | tf_op jit(solution)/shard_map/ppermute | solution.py:446
  42.3 5.1 %collective-permute-start.4 = (bf16[108,128]{1,0:T(8,128)(2,1)S(1)}, bf16[108,128]{1,0:T(8,128)(2,1)S(1)}, u32[]{:S(2)}, u32[]{:S(2)}) collective-permute-start(bf16[108,128]{1,0:T(8,128)(2,1)S(1)} %get-tuple-element.56), channel_id=1, source_target_pairs={{16,32},{32,16},{48,64},{64,48},{80,96},{96,80},{112,0},{0,112},{1... | collective-permute-start | bytes 82952 | tf_op jit(solution)/shard_map/ppermute | solution.py:445
  44.3 3.2 %collective-permute-start.5 = (bf16[108,128]{1,0:T(8,128)(2,1)S(1)}, bf16[108,128]{1,0:T(8,128)(2,1)S(1)}, u32[]{:S(2)}, u32[]{:S(2)}) collective-permute-start(bf16[108,128]{1,0:T(8,128)(2,1)S(1)} %get-tuple-element.57), channel_id=1, source_target_pairs={{0,16},{16,0},{32,48},{48,32},{64,80},{80,64},{96,112},{112,96},{1... | collective-permute-start | bytes 82952 | tf_op jit(solution)/shard_map/ppermute | solution.py:447
  50.2 7.3 %collective-permute-start.10 = (f32[1,7168]{1,0:T(1,128)S(1)}, f32[1,7168]{1,0:T(1,128)S(1)}, u32[]{:S(2)}, u32[]{:S(2)}) collective-permute-start(f32[1,7168]{1,0:T(1,128)S(1)} %get-tuple-element.66), channel_id=1, source_target_pairs={{1,2},{2,1},{3,4},{4,3},{5,6},{6,5},{7,8},{8,7},{9,10},{10,9},{11,... | collective-permute-start | bytes 86024 | tf_op jit(solution)/shard_map/ppermute | solution.py:444
  52.4 5.1 %collective-permute-start.11 = (f32[1,7168]{1,0:T(1,128)S(1)}, f32[1,7168]{1,0:T(1,128)S(1)}, u32[]{:S(2)}, u32[]{:S(2)}) collective-permute-start(f32[1,7168]{1,0:T(1,128)S(1)} %get-tuple-element.67), channel_id=1, source_target_pairs={{0,1},{1,0},{2,3},{3,2},{4,5},{5,4},{6,7},{7,6},{8,9},{9,8},{10,11... | collective-permute-start | bytes 86024 | tf_op jit(solution)/shard_map/ppermute | solution.py:446
  52.4 4.5 %collective-permute-start.8 = (bf16[108,128]{1,0:T(8,128)(2,1)S(1)}, bf16[108,128]{1,0:T(8,128)(2,1)S(1)}, u32[]{:S(2)}, u32[]{:S(2)}) collective-permute-start(bf16[108,128]{1,0:T(8,128)(2,1)S(1)} %get-tuple-element.64), channel_id=1, source_target_pairs={{16,32},{32,16},{48,64},{64,48},{80,96},{96,80},{112,0},{0,112},{1... | collective-permute-start | bytes 82952 | tf_op jit(solution)/shard_map/ppermute | solution.py:445
  53.7 3.2 %collective-permute-start.9 = (bf16[108,128]{1,0:T(8,128)(2,1)S(1)}, bf16[108,128]{1,0:T(8,128)(2,1)S(1)}, u32[]{:S(2)}, u32[]{:S(2)}) collective-permute-start(bf16[108,128]{1,0:T(8,128)(2,1)S(1)} %get-tuple-element.65), channel_id=1, source_target_pairs={{0,16},{16,0},{32,48},{48,32},{64,80},{80,64},{96,112},{112,96},{1... | collective-permute-start | bytes 82952 | tf_op jit(solution)/shard_map/ppermute | solution.py:447
  59.5 7.3 %collective-permute-start.14 = (f32[1,7168]{1,0:T(1,128)S(1)}, f32[1,7168]{1,0:T(1,128)S(1)}, u32[]{:S(2)}, u32[]{:S(2)}) collective-permute-start(f32[1,7168]{1,0:T(1,128)S(1)} %get-tuple-element.73), channel_id=1, source_target_pairs={{1,2},{2,1},{3,4},{4,3},{5,6},{6,5},{7,8},{8,7},{9,10},{10,9},{11,... | collective-permute-start | bytes 86024 | tf_op jit(solution)/shard_map/ppermute | solution.py:444
  62.2 4.5 %collective-permute-start.15 = (f32[1,7168]{1,0:T(1,128)S(1)}, f32[1,7168]{1,0:T(1,128)S(1)}, u32[]{:S(2)}, u32[]{:S(2)}) collective-permute-start(f32[1,7168]{1,0:T(1,128)S(1)} %get-tuple-element.74), channel_id=1, source_target_pairs={{0,1},{1,0},{2,3},{3,2},{4,5},{5,4},{6,7},{7,6},{8,9},{9,8},{10,11... | collective-permute-start | bytes 86024 | tf_op jit(solution)/shard_map/ppermute | solution.py:446
  62.2 4.5 %collective-permute-start.12 = (bf16[108,128]{1,0:T(8,128)(2,1)S(1)}, bf16[108,128]{1,0:T(8,128)(2,1)S(1)}, u32[]{:S(2)}, u32[]{:S(2)}) collective-permute-start(bf16[108,128]{1,0:T(8,128)(2,1)S(1)} %get-tuple-element.71), channel_id=1, source_target_pairs={{16,32},{32,16},{48,64},{64,48},{80,96},{96,80},{112,0},{0,112},{1... | collective-permute-start | bytes 82952 | tf_op jit(solution)/shard_map/ppermute | solution.py:445
  63.6 3.1 %collective-permute-start.13 = (bf16[108,128]{1,0:T(8,128)(2,1)S(1)}, bf16[108,128]{1,0:T(8,128)(2,1)S(1)}, u32[]{:S(2)}, u32[]{:S(2)}) collective-permute-start(bf16[108,128]{1,0:T(8,128)(2,1)S(1)} %get-tuple-element.72), channel_id=1, source_target_pairs={{0,16},{16,0},{32,48},{48,32},{64,80},{80,64},{96,112},{112,96},{1... | collective-permute-start | bytes 82952 | tf_op jit(solution)/shard_map/ppermute | solution.py:447

commit v10 on v8

--- a/solution.py
+++ b/solution.py
@@ -203,14 +203,21 @@
 
 
 def setup_kernel(
-    mask_ref, mix_in, tr_in, traj_in, coef_out, column_ref, lat_w, lon_w, traj_ref,
-    tr_ref, flat_ref, in_sems, out_sems,
+    mask_ref, mix_in, tr_in, traj_in, table_in, coef_out, column_ref, lat_w, lon_w, traj_ref, parts_ref,
+    tr_ref, flat_ref, table_ref, in_sems, out_sems,
 ):
     layers = tr_ref.shape[1]
     mix_ref, inv_ref, up_ref = columns(column_ref, layers)
     copies = [
         pltpu.make_async_copy(src, dst, in_sems.at[i])
-        for i, (src, dst) in enumerate(((mix_in, mix_ref), (tr_in, tr_ref), (traj_in.at[traj_in.shape[0] - 1], traj_ref)))
+        for i, (src, dst) in enumerate(
+            (
+                (mix_in, mix_ref),
+                (tr_in, tr_ref),
+                (table_in, table_ref),
+                (traj_in.at[traj_in.shape[0] - 1], traj_ref),
+            )
+        )
     ]
     for copy in copies:
         copy.start()
@@ -270,7 +277,10 @@
         flat = flat[side : side + 1, :]
         lon_w[side] = flat * (odd if side else 1.0 - odd)
         lon_w[2 + side] = flat * (1.0 - odd if side else odd)
-    for copy in copies[2:] + sent:
+    copies[2].wait()
+    for i, part in enumerate(split3(table_ref[...])):
+        parts_ref[i] = part
+    for copy in copies[3:] + sent:
         copy.wait()
 
 
@@ -365,19 +375,16 @@
 
 
 def head_kernel(
-    s, chunk, got_ref, traj_ref, table_in, traj_in, coef_in,
-    out_ref, snd_ref, parts_ref, next_ref, coef_ref, pick, pick8, weight, table_ref, sems,
+    s, chunk, got_ref, traj_ref, parts_ref, traj_in, coef_in,
+    out_ref, snd_ref, next_ref, coef_ref, pick, pick8, weight, sems,
 ):
-    pairs = ((table_in, table_ref), (traj_in.at[s - 1], next_ref), (coef_in, coef_ref))
+    pairs = ((traj_in.at[s - 1], next_ref), (coef_in, coef_ref))
     copies = [pltpu.make_async_copy(a, b, sems.at[i]) for i, (a, b) in enumerate(pairs)]
     for copy in copies:
         copy.start()
     unpack_kernel(got_ref, snd_ref)
-    copies[0].wait()
-    for i, part in enumerate(split3(table_ref[...])):
-        parts_ref[i] = part
     forcing_body(s, chunk, snd_ref, traj_ref, parts_ref, out_ref, pick, pick8, weight)
-    for copy in copies[1:]:
+    for copy in copies:
         copy.wait()
 
 
@@ -483,7 +490,8 @@
     mask = jnp.stack([lat > 0, lat < lax.axis_size("lat") - 1, lat % 2 > 0, lon % 2 > 0]).astype(F32)
     mask = jnp.broadcast_to(mask[:, None], (4, cols))
     one_step = sds(*trajectory.shape[1:], dtype=BF16)
-    coef, column, lat_w, lon_w, now = call(
+    table = kernel_table.T
+    coef, column, lat_w, lon_w, now, parts = call(
         setup_kernel,
         (
             sds(5 * layers, rows, cols),
@@ -491,42 +499,43 @@
             sds(4, layers, cols),
             sds(4, 1, layers * rows),
             one_step,
+            sds(3, *table.shape, dtype=BF16),
         ),
         mask,
         mixing,
         transport,
         trajectory,
-        hbm=(1, 2, 3),
+        table,
+        hbm=(1, 2, 3, 4),
         hbm_out=(0,),
         scratch=(
             pltpu.VMEM(transport.shape, F32),
             pltpu.VMEM((5 * layers, rows, cols), F32),
-            pltpu.SemaphoreType.DMA((3,)),
+            pltpu.VMEM(table.shape, F32),
+            pltpu.SemaphoreType.DMA((4,)),
             pltpu.SemaphoreType.DMA((15,)),
         ),
     )
-    table = kernel_table.T
     work = (
         pltpu.VMEM((256, slots), BF16),
         pltpu.VMEM((256, slots), F8),
         pltpu.VMEM((layers, 16, slots), F32),
     )
-    force, snd, parts, now, coef = call(
+    force, snd, now, coef = call(
         functools.partial(head_kernel, steps - 1, slots),
         (
             field,
             sds(steps, 8, slots),
-            sds(3, *table.shape, dtype=BF16),
             one_step,
             sds(*coef.shape),
         ),
         got,
         now,
-        table,
+        parts,
         trajectory,
         coef,
-        hbm=(2, 3, 4),
-        scratch=work + (pltpu.VMEM(table.shape, F32), pltpu.SemaphoreType.DMA((3,))),
+        hbm=(3, 4),
+        scratch=work + (pltpu.SemaphoreType.DMA((2,)),),
     )
     fixed = (column, coef, lat_w, lon_w)
 

time: 69 us -> 69.8 us (1.012)
  Pallas kernels: 32.3 us -> 33.1 us
    pallas_call x12, Pallas kernels: 32.3 us -> 33.1 us  [call(): pl.pallas_call(kernel, out_shape=tuple((pltpu.HBM(o.shape, o.dtype) if i...]
where the time goes in v10:
time: 69.8 us; the launch traced here: 69.3 us
  Pallas kernels  33.1 us (47%)
  starting transfers between devices  25.5 us (37%)
  waiting for transfers between devices  9.53 us (14%)
  between operations  0.99 us (1%)
    pallas_call x12, Pallas kernels, call(): pl.pallas_call(kernel, out_shape=tuple((pltpu.HBM(o.shape, o.dtype) if i...  33.1 us
    all_to_all x1, starting transfers between devices, body(): lax.all_to_all(outgoing, ('lat', 'lon'), split_axis=0, concat_axis=0, til...  11.1 us
    ppermute x4, starting transfers between devices, exchange(): lon_b = lax.ppermute(lon_b, 'lon', lon_far)  9.57 us
    all_to_all x1, waiting for transfers between devices, body(): lax.all_to_all(outgoing, ('lat', 'lon'), split_axis=0, concat_axis=0, til...  5.51 us
    ppermute x4, starting transfers between devices, exchange(): lat_b = lax.ppermute(lat_b, 'lat', lat_far)  4.67 us
    ppermute x4, waiting for transfers between devices, exchange(): lat_b = lax.ppermute(lat_b, 'lat', lat_far)  2.57 us
    ppermute x4, waiting for transfers between devices, exchange(): lon_b = lax.ppermute(lon_b, 'lon', lon_far)  1.42 us
  transfers between devices with their start and end apart: 17, of which 4 were waited for; matrix products, arithmetic and copies ran while one was open for 0% of the time, Pallas kernels for 21%

profile of v10, /device:TPU:0, one launch (start us, length us, event | category | flops | bytes accessed | tf_op | source)
XLA Modules:
  0.0 69.3 jit_solution(16732341119934371637)
XLA Ops:
  0.6 2.5 %shard_map.104 = f32[128,2,128]{2,1,0:T(2,128)} custom-call(s32[4,1,512]{2,1,0:T(1,128)} %bitcast.9, s32[4,512]{1,0:T(4,128)} %cell_in.1, s32[4,512]{1,0:T(4,128)} %index_in.1, f32[3,4,512]{2,1,0:T(4,128)} %bitcast.7, f32[4,512]{1,0:T(4,128)} %prec_in.1), custom_call_target="tpu_custom_call" | custom-call | tf_op jit(solution)/shard_map/pallas_call | solution.py:45
  3.1 11.1 %all-to-all-start = ((f32[128,2,128]{2,1,0:T(2,128)}), f32[128,2,128]{2,1,0:T(2,128)S(1)}, u32[]{:S(2)}, u32[]{:S(2)}) async-start(f32[128,2,128]{2,1,0:T(2,128)} %shard_map.104), calls=%async_computation | async-start | bytes 262144 | tf_op jit(solution)/shard_map/all_to_all | solution.py:488
  14.5 3.9 %shard_map.105 = (f32[180,32,128]{2,1,0:T(8,128)}, f32[106,32,128]{2,1,0:T(8,128)S(1)}, f32[4,36,128]{2,1,0:T(8,128)S(1)}, f32[4,1,1152]{2,1,0:T(1,128)S(1)}, bf...) custom-call(f32[4,128]{1,0:T(4,128)S(1)} %broadcast_in_dim.2.mask_ref, f32[35,32,128]{2,1,0:T(8,128)} %mix_in.1, ...), custom_call_target="tpu_custom_call" | custom-call | tf_op jit(solution)/shard_map/pallas_call | solution.py:45
  18.4 5.5 %all-to-all-done.got_ref = f32[128,2,128]{2,1,0:T(2,128)S(1)} async-done(((f32[128,2,128]{2,1,0:T(2,128)}), f32[128,2,128]{2,1,0:T(2,128)S(1)}, u32[]{:S(2)}, u32[]{:S(2)}) %all-to-all-start) | async-done | bytes 131104 | tf_op jit(solution)/shard_map/all_to_all | solution.py:488
  23.9 4.7 %shard_map.106 = (f32[3,36,32,128]{3,2,1,0:T(8,128)S(1)}, f32[4,8,1024]{2,1,0:T(8,128)S(1)}, bf16[3,36,32,128]{3,2,1,0:T(8,128)(2,1)S(1)}, f32[180,32,128]{2,1,0:T(8,128)S(1)}) custom-call(f32[128,2,128]{2,1,0:T(2,128)S(1)} %all-to-all-done.got_ref, bf16[3,36,32,128]{3,2,1,0:T(8,128)(2,1)S(1)} %get-tuple-element.39.traj_ref, ...), custom_call_target="tpu_custom_call" | custom-call | tf_op jit(solution)/shard_map/pallas_call | solution.py:45
  28.6 1.8 %shard_map.107 = (f32[3,36,32,128]{3,2,1,0:T(8,128)S(1)}, f32[1,7168]{1,0:T(1,128)S(1)}, f32[1,7168]{1,0:T(1,128)S(1)}, bf16[108,128]{1,0:T(8,128)(2,1)S(1)}, bf16[108,128]{1,0:T(8,128)(2,1)S(1)}) custom-call(f32[3,36,32,128]{3,2,1,0:T(8,128)S(1)} %get-tuple-element.42.force_ref, f32[106,32,128]{2,1,0:T(8,128)S(1)} %get-tuple-element.43.column_ref.refs_1_.refs_2_, ...), custom_call_target="tpu_custom_call" | custom-call | tf_op jit(solution)/shard_map/pallas_call | solution.py:45
  30.4 1.4 %collective-permute-start.2 = (f32[1,7168]{1,0:T(1,128)S(1)}, f32[1,7168]{1,0:T(1,128)S(1)}, u32[]{:S(2)}, u32[]{:S(2)}) collective-permute-start(f32[1,7168]{1,0:T(1,128)S(1)} %get-tuple-element.50), channel_id=1, source_target_pairs={{1,2},{2,1},{3,4},{4,3},{5,6},{6,5},{7,8},{8,7},{9,10},{10,9},{11,... | collective-permute-start | bytes 86024 | tf_op jit(solution)/shard_map/ppermute | solution.py:452
  32.4 3.2 %shard_map.108 = (f32[3,36,32,128]{3,2,1,0:T(8,128)S(1)}, bf16[3,36,32,128]{3,2,1,0:T(8,128)(2,1)S(1)}) custom-call(f32[4,8,1024]{2,1,0:T(8,128)S(1)} %get-tuple-element.52.snd_ref, bf16[3,36,32,128]{3,2,1,0:T(8,128)(2,1)S(1)} %get-tuple-element.53.traj_ref, bf16[3,36,64]{2,1,0:T(8,128)(2,1)S(1)} %get-tuple-element.40.parts_ref.table_ref, ...), custom_call_target="tpu_custom_call" | custom-call | tf_op jit(solution)/shard_map/pallas_call | solution.py:45
  35.6 0.7 collective-permute-done.lat_b
  36.3 1.4 %collective-permute-done.2.lon_b = f32[1,7168]{1,0:T(1,128)S(1)} collective-permute-done((f32[1,7168]{1,0:T(1,128)S(1)}, f32[1,7168]{1,0:T(1,128)S(1)}, u32[]{:S(2)}, u32[]{:S(2)}) %collective-permute-start.2) | collective-permute-done | bytes 28704 | tf_op jit(solution)/shard_map/ppermute | solution.py:452
  37.7 2.7 %shard_map.109 = (f32[3,36,32,128]{3,2,1,0:T(8,128)S(1)}, f32[1,7168]{1,0:T(1,128)S(1)}, f32[1,7168]{1,0:T(1,128)S(1)}, bf16[108,128]{1,0:T(8,128)(2,1)S(1)}, bf...) custom-call(f32[4,128]{1,0:T(4,128)S(1)} %broadcast_in_dim.2.mask_ref, ...), custom_call_target="tpu_custom_call" | custom-call | tf_op jit(solution)/shard_map/pallas_call | solution.py:45
  40.4 2.8 %collective-permute-start.6 = (f32[1,7168]{1,0:T(1,128)S(1)}, f32[1,7168]{1,0:T(1,128)S(1)}, u32[]{:S(2)}, u32[]{:S(2)}) collective-permute-start(f32[1,7168]{1,0:T(1,128)S(1)} %get-tuple-element.58), channel_id=1, source_target_pairs={{1,2},{2,1},{3,4},{4,3},{5,6},{6,5},{7,8},{8,7},{9,10},{10,9},{11,... | collective-permute-start | bytes 86024 | tf_op jit(solution)/shard_map/ppermute | solution.py:452
  43.1 1.4 %collective-permute-start.4 = (bf16[108,128]{1,0:T(8,128)(2,1)S(1)}, bf16[108,128]{1,0:T(8,128)(2,1)S(1)}, u32[]{:S(2)}, u32[]{:S(2)}) collective-permute-start(bf16[108,128]{1,0:T(8,128)(2,1)S(1)} %get-tuple-element.56), channel_id=1, source_target_pairs={{16,32},{32,16},{48,64},{64,48},{80,96},{96,80},{112,0},{0,112},{1... | collective-permute-start | bytes 82952 | tf_op jit(solution)/shard_map/ppermute | solution.py:453
  44.5 3.1 %shard_map.110 = (f32[3,36,32,128]{3,2,1,0:T(8,128)S(1)}, bf16[3,36,32,128]{3,2,1,0:T(8,128)(2,1)S(1)}) custom-call(f32[4,8,1024]{2,1,0:T(8,128)S(1)} %get-tuple-element.52.snd_ref, bf16[3,36,32,128]{3,2,1,0:T(8,128)(2,1)S(1)} %get-tuple-element.61.traj_ref, bf16[3,36,64]{2,1,0:T(8,128)(2,1)S(1)} %get-tuple-element.40.parts_ref.table_ref, ...), custom_call_target="tpu_custom_call" | custom-call | tf_op jit(solution)/shard_map/pallas_call | solution.py:45
  47.7 2.7 %shard_map.111 = (f32[3,36,32,128]{3,2,1,0:T(8,128)S(1)}, f32[1,7168]{1,0:T(1,128)S(1)}, f32[1,7168]{1,0:T(1,128)S(1)}, bf16[108,128]{1,0:T(8,128)(2,1)S(1)}, bf...) custom-call(f32[4,128]{1,0:T(4,128)S(1)} %broadcast_in_dim.2.mask_ref, ...), custom_call_target="tpu_custom_call" | custom-call | tf_op jit(solution)/shard_map/pallas_call | solution.py:45
  50.4 2.7 %collective-permute-start.10 = (f32[1,7168]{1,0:T(1,128)S(1)}, f32[1,7168]{1,0:T(1,128)S(1)}, u32[]{:S(2)}, u32[]{:S(2)}) collective-permute-start(f32[1,7168]{1,0:T(1,128)S(1)} %get-tuple-element.66), channel_id=1, source_target_pairs={{1,2},{2,1},{3,4},{4,3},{5,6},{6,5},{7,8},{8,7},{9,10},{10,9},{11,... | collective-permute-start | bytes 86024 | tf_op jit(solution)/shard_map/ppermute | solution.py:452
  53.1 1.3 %collective-permute-start.8 = (bf16[108,128]{1,0:T(8,128)(2,1)S(1)}, bf16[108,128]{1,0:T(8,128)(2,1)S(1)}, u32[]{:S(2)}, u32[]{:S(2)}) collective-permute-start(bf16[108,128]{1,0:T(8,128)(2,1)S(1)} %get-tuple-element.64), channel_id=1, source_target_pairs={{16,32},{32,16},{48,64},{64,48},{80,96},{96,80},{112,0},{0,112},{1... | collective-permute-start | bytes 82952 | tf_op jit(solution)/shard_map/ppermute | solution.py:453
  54.5 3.2 %shard_map.112.refs_1_ = f32[3,36,32,128]{3,2,1,0:T(8,128)S(1)} custom-call(f32[4,8,1024]{2,1,0:T(8,128)S(1)} %get-tuple-element.52.snd_ref, bf16[3,36,32,128]{3,2,1,0:T(8,128)(2,1)S(1)} %get-tuple-element.69.traj_ref, bf16[3,36,64]{2,1,0:T(8,128)(2,1)S(1)} %get-tuple-element.40.parts_ref.table_ref), custom_call_target="tpu_custom_call" | custom-call | tf_op jit(solution)/shard_map/pallas_call | solution.py:45
  57.7 2.0 %shard_map.113 = (f32[3,36,32,128]{3,2,1,0:T(8,128)S(1)}, f32[1,7168]{1,0:T(1,128)S(1)}, f32[1,7168]{1,0:T(1,128)S(1)}, bf16[108,128]{1,0:T(8,128)(2,1)S(1)}, bf...) custom-call(f32[4,128]{1,0:T(4,128)S(1)} %broadcast_in_dim.2.mask_ref, ...), custom_call_target="tpu_custom_call" | custom-call | tf_op jit(solution)/shard_map/pallas_call | solution.py:45
  59.7 2.8 %collective-permute-start.14 = (f32[1,7168]{1,0:T(1,128)S(1)}, f32[1,7168]{1,0:T(1,128)S(1)}, u32[]{:S(2)}, u32[]{:S(2)}) collective-permute-start(f32[1,7168]{1,0:T(1,128)S(1)} %get-tuple-element.73), channel_id=1, source_target_pairs={{1,2},{2,1},{3,4},{4,3},{5,6},{6,5},{7,8},{8,7},{9,10},{10,9},{11,... | collective-permute-start | bytes 86024 | tf_op jit(solution)/shard_map/ppermute | solution.py:452
  62.4 1.4 %collective-permute-start.12 = (bf16[108,128]{1,0:T(8,128)(2,1)S(1)}, bf16[108,128]{1,0:T(8,128)(2,1)S(1)}, u32[]{:S(2)}, u32[]{:S(2)}) collective-permute-start(bf16[108,128]{1,0:T(8,128)(2,1)S(1)} %get-tuple-element.71), channel_id=1, source_target_pairs={{16,32},{32,16},{48,64},{64,48},{80,96},{96,80},{112,0},{0,112},{1... | collective-permute-start | bytes 82952 | tf_op jit(solution)/shard_map/ppermute | solution.py:453
  63.8 1.2 %shard_map.114.w_in = f32[3,36,32,128]{3,2,1,0:T(8,128)S(1)} custom-call(f32[3,36,32,128]{3,2,1,0:T(8,128)S(1)} %get-tuple-element.70.v, f32[180,32,128]{2,1,0:T(8,128)S(1)} %get-tuple-element.44.coef_ref.refs_2_.refs_3_), custom_call_target="tpu_custom_call" | custom-call | tf_op jit(solution)/shard_map/pallas_call | solution.py:45
  65.1 1.9 %collective-permute-done.12.lat_b = bf16[108,128]{1,0:T(8,128)(2,1)S(1)} collective-permute-done((bf16[108,128]{1,0:T(8,128)(2,1)S(1)}, bf16[108,128]{1,0:T(8,128)(2,1)S(1)}, u32[]{:S(2)}, u32[]{:S(2)}) %collective-permute-start.12) | collective-permute-done | bytes 27680 | tf_op jit(solution)/shard_map/ppermute | solution.py:453
  67.0 2.1 %shard_map.115 = (f32[3,36,32,128]{3,2,1,0:T(8,128)}, f32[3,32,128]{2,1,0:T(8,128)}) custom-call(f32[4,128]{1,0:T(4,128)S(1)} %broadcast_in_dim.2.mask_ref, f32[3,36,32,128]{3,2,1,0:T(8,128)S(1)} %shard_map.114.w_in, bf16[108,128]{1,0:T(8,128)(2,1)S(1)} %collective-permute-done.12.lat_b, bf16[108,128]{1,0:T(8,128)(2,1)S(1)} %collective-permute-done.13.lat_a, ...), custom_call_target="tpu_custom_call" | custom-call | tf_op jit(solution)/shard_map/pallas_call | solution.py:45
  (24 shorter events, 0.9 us)
Async XLA Ops:
  3.1 20.8 %all-to-all-start = ((f32[128,2,128]{2,1,0:T(2,128)}), f32[128,2,128]{2,1,0:T(2,128)S(1)}, u32[]{:S(2)}, u32[]{:S(2)}) async-start(f32[128,2,128]{2,1,0:T(2,128)} %shard_map.104), calls=%async_computation | async-start | bytes 262144 | tf_op jit(solution)/shard_map/all_to_all | solution.py:488
  30.4 7.3 %collective-permute-start.2 = (f32[1,7168]{1,0:T(1,128)S(1)}, f32[1,7168]{1,0:T(1,128)S(1)}, u32[]{:S(2)}, u32[]{:S(2)}) collective-permute-start(f32[1,7168]{1,0:T(1,128)S(1)} %get-tuple-element.50), channel_id=1, source_target_pairs={{1,2},{2,1},{3,4},{4,3},{5,6},{6,5},{7,8},{8,7},{9,10},{10,9},{11,... | collective-permute-start | bytes 86024 | tf_op jit(solution)/shard_map/ppermute | solution.py:452
  31.8 5.9 %collective-permute-start.3 = (f32[1,7168]{1,0:T(1,128)S(1)}, f32[1,7168]{1,0:T(1,128)S(1)}, u32[]{:S(2)}, u32[]{:S(2)}) collective-permute-start(f32[1,7168]{1,0:T(1,128)S(1)} %get-tuple-element.51), channel_id=1, source_target_pairs={{0,1},{1,0},{2,3},{3,2},{4,5},{5,4},{6,7},{7,6},{8,9},{9,8},{10,11... | collective-permute-start | bytes 86024 | tf_op jit(solution)/shard_map/ppermute | solution.py:454
  31.8 4.5 %collective-permute-start = (bf16[108,128]{1,0:T(8,128)(2,1)S(1)}, bf16[108,128]{1,0:T(8,128)(2,1)S(1)}, u32[]{:S(2)}, u32[]{:S(2)}) collective-permute-start(bf16[108,128]{1,0:T(8,128)(2,1)S(1)} %get-tuple-element.48), channel_id=1, source_target_pairs={{16,32},{32,16},{48,64},{64,48},{80,96},{96,80},{112,0},{0,112},{1... | collective-permute-start | bytes 82952 | tf_op jit(solution)/shard_map/ppermute | solution.py:453
  32.4 3.9 %collective-permute-start.1 = (bf16[108,128]{1,0:T(8,128)(2,1)S(1)}, bf16[108,128]{1,0:T(8,128)(2,1)S(1)}, u32[]{:S(2)}, u32[]{:S(2)}) collective-permute-start(bf16[108,128]{1,0:T(8,128)(2,1)S(1)} %get-tuple-element.49), channel_id=1, source_target_pairs={{0,16},{16,0},{32,48},{48,32},{64,80},{80,64},{96,112},{112,96},{1... | collective-permute-start | bytes 82952 | tf_op jit(solution)/shard_map/ppermute | solution.py:455
  40.4 7.3 %collective-permute-start.6 = (f32[1,7168]{1,0:T(1,128)S(1)}, f32[1,7168]{1,0:T(1,128)S(1)}, u32[]{:S(2)}, u32[]{:S(2)}) collective-permute-start(f32[1,7168]{1,0:T(1,128)S(1)} %get-tuple-element.58), channel_id=1, source_target_pairs={{1,2},{2,1},{3,4},{4,3},{5,6},{6,5},{7,8},{8,7},{9,10},{10,9},{11,... | collective-permute-start | bytes 86024 | tf_op jit(solution)/shard_map/ppermute | solution.py:452
  43.1 4.6 %collective-permute-start.7 = (f32[1,7168]{1,0:T(1,128)S(1)}, f32[1,7168]{1,0:T(1,128)S(1)}, u32[]{:S(2)}, u32[]{:S(2)}) collective-permute-start(f32[1,7168]{1,0:T(1,128)S(1)} %get-tuple-element.59), channel_id=1, source_target_pairs={{0,1},{1,0},{2,3},{3,2},{4,5},{5,4},{6,7},{7,6},{8,9},{9,8},{10,11... | collective-permute-start | bytes 86024 | tf_op jit(solution)/shard_map/ppermute | solution.py:454
  43.1 4.5 %collective-permute-start.4 = (bf16[108,128]{1,0:T(8,128)(2,1)S(1)}, bf16[108,128]{1,0:T(8,128)(2,1)S(1)}, u32[]{:S(2)}, u32[]{:S(2)}) collective-permute-start(bf16[108,128]{1,0:T(8,128)(2,1)S(1)} %get-tuple-element.56), channel_id=1, source_target_pairs={{16,32},{32,16},{48,64},{64,48},{80,96},{96,80},{112,0},{0,112},{1... | collective-permute-start | bytes 82952 | tf_op jit(solution)/shard_map/ppermute | solution.py:453
  44.5 3.2 %collective-permute-start.5 = (bf16[108,128]{1,0:T(8,128)(2,1)S(1)}, bf16[108,128]{1,0:T(8,128)(2,1)S(1)}, u32[]{:S(2)}, u32[]{:S(2)}) collective-permute-start(bf16[108,128]{1,0:T(8,128)(2,1)S(1)} %get-tuple-element.57), channel_id=1, source_target_pairs={{0,16},{16,0},{32,48},{48,32},{64,80},{80,64},{96,112},{112,96},{1... | collective-permute-start | bytes 82952 | tf_op jit(solution)/shard_map/ppermute | solution.py:455
  50.4 7.3 %collective-permute-start.10 = (f32[1,7168]{1,0:T(1,128)S(1)}, f32[1,7168]{1,0:T(1,128)S(1)}, u32[]{:S(2)}, u32[]{:S(2)}) collective-permute-start(f32[1,7168]{1,0:T(1,128)S(1)} %get-tuple-element.66), channel_id=1, source_target_pairs={{1,2},{2,1},{3,4},{4,3},{5,6},{6,5},{7,8},{8,7},{9,10},{10,9},{11,... | collective-permute-start | bytes 86024 | tf_op jit(solution)/shard_map/ppermute | solution.py:452
  53.1 4.6 %collective-permute-start.11 = (f32[1,7168]{1,0:T(1,128)S(1)}, f32[1,7168]{1,0:T(1,128)S(1)}, u32[]{:S(2)}, u32[]{:S(2)}) collective-permute-start(f32[1,7168]{1,0:T(1,128)S(1)} %get-tuple-element.67), channel_id=1, source_target_pairs={{0,1},{1,0},{2,3},{3,2},{4,5},{5,4},{6,7},{7,6},{8,9},{9,8},{10,11... | collective-permute-start | bytes 86024 | tf_op jit(solution)/shard_map/ppermute | solution.py:454
  53.1 4.5 %collective-permute-start.8 = (bf16[108,128]{1,0:T(8,128)(2,1)S(1)}, bf16[108,128]{1,0:T(8,128)(2,1)S(1)}, u32[]{:S(2)}, u32[]{:S(2)}) collective-permute-start(bf16[108,128]{1,0:T(8,128)(2,1)S(1)} %get-tuple-element.64), channel_id=1, source_target_pairs={{16,32},{32,16},{48,64},{64,48},{80,96},{96,80},{112,0},{0,112},{1... | collective-permute-start | bytes 82952 | tf_op jit(solution)/shard_map/ppermute | solution.py:453
  54.5 3.2 %collective-permute-start.9 = (bf16[108,128]{1,0:T(8,128)(2,1)S(1)}, bf16[108,128]{1,0:T(8,128)(2,1)S(1)}, u32[]{:S(2)}, u32[]{:S(2)}) collective-permute-start(bf16[108,128]{1,0:T(8,128)(2,1)S(1)} %get-tuple-element.65), channel_id=1, source_target_pairs={{0,16},{16,0},{32,48},{48,32},{64,80},{80,64},{96,112},{112,96},{1... | collective-permute-start | bytes 82952 | tf_op jit(solution)/shard_map/ppermute | solution.py:455
  59.7 7.3 %collective-permute-start.14 = (f32[1,7168]{1,0:T(1,128)S(1)}, f32[1,7168]{1,0:T(1,128)S(1)}, u32[]{:S(2)}, u32[]{:S(2)}) collective-permute-start(f32[1,7168]{1,0:T(1,128)S(1)} %get-tuple-element.73), channel_id=1, source_target_pairs={{1,2},{2,1},{3,4},{4,3},{5,6},{6,5},{7,8},{8,7},{9,10},{10,9},{11,... | collective-permute-start | bytes 86024 | tf_op jit(solution)/shard_map/ppermute | solution.py:452
  62.4 4.5 %collective-permute-start.15 = (f32[1,7168]{1,0:T(1,128)S(1)}, f32[1,7168]{1,0:T(1,128)S(1)}, u32[]{:S(2)}, u32[]{:S(2)}) collective-permute-start(f32[1,7168]{1,0:T(1,128)S(1)} %get-tuple-element.74), channel_id=1, source_target_pairs={{0,1},{1,0},{2,3},{3,2},{4,5},{5,4},{6,7},{7,6},{8,9},{9,8},{10,11... | collective-permute-start | bytes 86024 | tf_op jit(solution)/shard_map/ppermute | solution.py:454
  62.4 4.5 %collective-permute-start.12 = (bf16[108,128]{1,0:T(8,128)(2,1)S(1)}, bf16[108,128]{1,0:T(8,128)(2,1)S(1)}, u32[]{:S(2)}, u32[]{:S(2)}) collective-permute-start(bf16[108,128]{1,0:T(8,128)(2,1)S(1)} %get-tuple-element.71), channel_id=1, source_target_pairs={{16,32},{32,16},{48,64},{64,48},{80,96},{96,80},{112,0},{0,112},{1... | collective-permute-start | bytes 82952 | tf_op jit(solution)/shard_map/ppermute | solution.py:453
  63.8 3.1 %collective-permute-start.13 = (bf16[108,128]{1,0:T(8,128)(2,1)S(1)}, bf16[108,128]{1,0:T(8,128)(2,1)S(1)}, u32[]{:S(2)}, u32[]{:S(2)}) collective-permute-start(bf16[108,128]{1,0:T(8,128)(2,1)S(1)} %get-tuple-element.72), channel_id=1, source_target_pairs={{0,16},{16,0},{32,48},{48,32},{64,80},{80,64},{96,112},{112,96},{1... | collective-permute-start | bytes 82952 | tf_op jit(solution)/shard_map/ppermute | solution.py:455

commit v11 on v8

--- a/solution.py
+++ b/solution.py
@@ -318,7 +318,7 @@
             v[t, k] = d[t]
         return d
 
-    d = lax.fori_loop(1, layers, forward, d, unroll=5)
+    d = lax.fori_loop(1, layers, forward, d, unroll=35)
 
     def backward(i, x):
         k = layers - 2 - i
@@ -328,7 +328,7 @@
             v[t, k] = x[t]
         return x
 
-    lax.fori_loop(0, layers - 1, backward, d, unroll=5)
+    lax.fori_loop(0, layers - 1, backward, d, unroll=35)
 
 
 def horizontal(v, coef_ref=None, w_out=None, weights=None, edges=None):

time: 69 us -> 68.3 us (0.990)
  transfers between devices with their start and end apart: 17 -> 17, of which waited for: 4 -> 4; matrix products, arithmetic and copies ran while one was open for 0% -> 0% of each run, Pallas kernels for 21% -> 22%
where the time goes in v11:
time: 68.3 us; the launch traced here: 67.8 us
  Pallas kernels  31.7 us (46%)
  starting transfers between devices  25.4 us (37%)
  waiting for transfers between devices  9.55 us (14%)
  between operations  0.98 us (1%)
    pallas_call x12, Pallas kernels, call(): pl.pallas_call(kernel, out_shape=tuple((pltpu.HBM(o.shape, o.dtype) if i...  31.7 us
    all_to_all x1, starting transfers between devices, body(): lax.all_to_all(outgoing, ('lat', 'lon'), split_axis=0, concat_axis=0, til...  11.1 us
    ppermute x4, starting transfers between devices, exchange(): lon_b = lax.ppermute(lon_b, 'lon', lon_far)  9.54 us
    all_to_all x1, waiting for transfers between devices, body(): lax.all_to_all(outgoing, ('lat', 'lon'), split_axis=0, concat_axis=0, til...  5.52 us
    ppermute x4, starting transfers between devices, exchange(): lat_b = lax.ppermute(lat_b, 'lat', lat_far)  4.65 us
    ppermute x4, waiting for transfers between devices, exchange(): lat_b = lax.ppermute(lat_b, 'lat', lat_far)  2.58 us
    ppermute x4, waiting for transfers between devices, exchange(): lon_b = lax.ppermute(lon_b, 'lon', lon_far)  1.43 us
  transfers between devices with their start and end apart: 17, of which 4 were waited for; matrix products, arithmetic and copies ran while one was open for 0% of the time, Pallas kernels for 22%

profile of v11, /device:TPU:0, one launch (start us, length us, event | category | flops | bytes accessed | tf_op | source)
XLA Modules:
  0.0 67.8 jit_solution(5163556392116345631)
XLA Ops:
  0.6 2.5 %shard_map.104 = f32[128,2,128]{2,1,0:T(2,128)} custom-call(s32[4,1,512]{2,1,0:T(1,128)} %bitcast.9, s32[4,512]{1,0:T(4,128)} %cell_in.1, s32[4,512]{1,0:T(4,128)} %index_in.1, f32[3,4,512]{2,1,0:T(4,128)} %bitcast.7, f32[4,512]{1,0:T(4,128)} %prec_in.1), custom_call_target="tpu_custom_call" | custom-call | tf_op jit(solution)/shard_map/pallas_call | solution.py:45
  3.1 11.1 %all-to-all-start = ((f32[128,2,128]{2,1,0:T(2,128)}), f32[128,2,128]{2,1,0:T(2,128)S(1)}, u32[]{:S(2)}, u32[]{:S(2)}) async-start(f32[128,2,128]{2,1,0:T(2,128)} %shard_map.104), calls=%async_computation | async-start | bytes 262144 | tf_op jit(solution)/shard_map/all_to_all | solution.py:481
  14.5 3.9 %shard_map.105 = (f32[180,32,128]{2,1,0:T(8,128)}, f32[106,32,128]{2,1,0:T(8,128)S(1)}, f32[4,36,128]{2,1,0:T(8,128)S(1)}, f32[4,1,1152]{2,1,0:T(1,128)S(1)}, bf16[3,36,32,128]{3,2,1,0:T(8,128)(2,1)S(1)}) custom-call(f32[4,128]{1,0:T(4,128)S(1)} %broadcast_in_dim.2.mask_ref, f32[35,32,128]{2,1,0:T(8,128)} %mix_in.1, f32[4,36,32,128]{3,2,1,0:T(8,128)} %tr_in.1, ...), custom_call_target="tpu_custom_call" | custom-call | tf_op jit(solution)/shard_map/pallas_call | solution.py:45
  18.4 5.5 %all-to-all-done.got_ref = f32[128,2,128]{2,1,0:T(2,128)S(1)} async-done(((f32[128,2,128]{2,1,0:T(2,128)}), f32[128,2,128]{2,1,0:T(2,128)S(1)}, u32[]{:S(2)}, u32[]{:S(2)}) %all-to-all-start) | async-done | bytes 131104 | tf_op jit(solution)/shard_map/all_to_all | solution.py:481
  23.9 3.9 %shard_map.106 = (f32[3,36,32,128]{3,2,1,0:T(8,128)S(1)}, f32[4,8,1024]{2,1,0:T(8,128)S(1)}, bf16[3,36,64]{2,1,0:T(8,128)(2,1)S(1)}, bf16[3,36,32,128]{3,2,1,0:T(8,128)(2,1)S(1)}, f32[180,32,128]{2,1,0:T(8,128)S(1)}) custom-call(f32[128,2,128]{2,1,0:T(2,128)S(1)} %all-to-all-done.got_ref, bf16[3,36,32,128]{3,2,1,0:T(8,128)(2,1)S(1)} %get-tuple-element.39.traj_ref, ...), custom_call_target="tpu_custom_call" | custom-call | tf_op jit(solution)/shard_map/pallas_call | solution.py:45
  27.8 2.1 %shard_map.107 = (f32[3,36,32,128]{3,2,1,0:T(8,128)S(1)}, f32[1,7168]{1,0:T(1,128)S(1)}, f32[1,7168]{1,0:T(1,128)S(1)}, bf16[108,128]{1,0:T(8,128)(2,1)S(1)}, bf16[108,128]{1,0:T(8,128)(2,1)S(1)}) custom-call(f32[3,36,32,128]{3,2,1,0:T(8,128)S(1)} %get-tuple-element.41.force_ref, f32[106,32,128]{2,1,0:T(8,128)S(1)} %get-tuple-element.42.column_ref.refs_1_.refs_2_, ...), custom_call_target="tpu_custom_call" | custom-call | tf_op jit(solution)/shard_map/pallas_call | solution.py:45
  29.9 1.4 %collective-permute-start.2 = (f32[1,7168]{1,0:T(1,128)S(1)}, f32[1,7168]{1,0:T(1,128)S(1)}, u32[]{:S(2)}, u32[]{:S(2)}) collective-permute-start(f32[1,7168]{1,0:T(1,128)S(1)} %get-tuple-element.49), channel_id=1, source_target_pairs={{1,2},{2,1},{3,4},{4,3},{5,6},{6,5},{7,8},{8,7},{9,10},{10,9},{11,... | collective-permute-start | bytes 86024 | tf_op jit(solution)/shard_map/ppermute | solution.py:445
  31.9 3.2 %shard_map.108 = (f32[3,36,32,128]{3,2,1,0:T(8,128)S(1)}, bf16[3,36,32,128]{3,2,1,0:T(8,128)(2,1)S(1)}) custom-call(f32[4,8,1024]{2,1,0:T(8,128)S(1)} %get-tuple-element.51.snd_ref, bf16[3,36,32,128]{3,2,1,0:T(8,128)(2,1)S(1)} %get-tuple-element.52.traj_ref, bf16[3,36,64]{2,1,0:T(8,128)(2,1)S(1)} %get-tuple-element.53.table_ref, ...), custom_call_target="tpu_custom_call" | custom-call | tf_op jit(solution)/shard_map/pallas_call | solution.py:45
  35.1 0.7 %collective-permute-done.lat_b = bf16[108,128]{1,0:T(8,128)(2,1)S(1)} collective-permute-done((bf16[108,128]{1,0:T(8,128)(2,1)S(1)}, bf16[108,128]{1,0:T(8,128)(2,1)S(1)}, u32[]{:S(2)}, u32[]{:S(2)}) %collective-permute-start) | collective-permute-done | bytes 27680 | tf_op jit(solution)/shard_map/ppermute | solution.py:446
  35.8 1.4 %collective-permute-done.2.lon_b = f32[1,7168]{1,0:T(1,128)S(1)} collective-permute-done((f32[1,7168]{1,0:T(1,128)S(1)}, f32[1,7168]{1,0:T(1,128)S(1)}, u32[]{:S(2)}, u32[]{:S(2)}) %collective-permute-start.2) | collective-permute-done | bytes 28704 | tf_op jit(solution)/shard_map/ppermute | solution.py:445
  37.2 2.4 %shard_map.109 = (f32[3,36,32,128]{3,2,1,0:T(8,128)S(1)}, f32[1,7168]{1,0:T(1,128)S(1)}, f32[1,7168]{1,0:T(1,128)S(1)}, bf16[108,128]{1,0:T(8,128)(2,1)S(1)}, bf...) custom-call(f32[4,128]{1,0:T(4,128)S(1)} %broadcast_in_dim.2.mask_ref, ...), custom_call_target="tpu_custom_call" | custom-call | tf_op jit(solution)/shard_map/pallas_call | solution.py:45
  39.5 2.8 %collective-permute-start.6 = (f32[1,7168]{1,0:T(1,128)S(1)}, f32[1,7168]{1,0:T(1,128)S(1)}, u32[]{:S(2)}, u32[]{:S(2)}) collective-permute-start(f32[1,7168]{1,0:T(1,128)S(1)} %get-tuple-element.58), channel_id=1, source_target_pairs={{1,2},{2,1},{3,4},{4,3},{5,6},{6,5},{7,8},{8,7},{9,10},{10,9},{11,... | collective-permute-start | bytes 86024 | tf_op jit(solution)/shard_map/ppermute | solution.py:445
  42.3 1.4 %collective-permute-start.4 = (bf16[108,128]{1,0:T(8,128)(2,1)S(1)}, bf16[108,128]{1,0:T(8,128)(2,1)S(1)}, u32[]{:S(2)}, u32[]{:S(2)}) collective-permute-start(bf16[108,128]{1,0:T(8,128)(2,1)S(1)} %get-tuple-element.56), channel_id=1, source_target_pairs={{16,32},{32,16},{48,64},{64,48},{80,96},{96,80},{112,0},{0,112},{1... | collective-permute-start | bytes 82952 | tf_op jit(solution)/shard_map/ppermute | solution.py:446
  43.7 3.1 %shard_map.110 = (f32[3,36,32,128]{3,2,1,0:T(8,128)S(1)}, bf16[3,36,32,128]{3,2,1,0:T(8,128)(2,1)S(1)}) custom-call(f32[4,8,1024]{2,1,0:T(8,128)S(1)} %get-tuple-element.51.snd_ref, bf16[3,36,32,128]{3,2,1,0:T(8,128)(2,1)S(1)} %get-tuple-element.61.traj_ref, bf16[3,36,64]{2,1,0:T(8,128)(2,1)S(1)} %get-tuple-element.53.table_ref, ...), custom_call_target="tpu_custom_call" | custom-call | tf_op jit(solution)/shard_map/pallas_call | solution.py:45
  46.9 2.4 %shard_map.111 = (f32[3,36,32,128]{3,2,1,0:T(8,128)S(1)}, f32[1,7168]{1,0:T(1,128)S(1)}, f32[1,7168]{1,0:T(1,128)S(1)}, bf16[108,128]{1,0:T(8,128)(2,1)S(1)}, bf...) custom-call(f32[4,128]{1,0:T(4,128)S(1)} %broadcast_in_dim.2.mask_ref, ...), custom_call_target="tpu_custom_call" | custom-call | tf_op jit(solution)/shard_map/pallas_call | solution.py:45
  49.3 2.7 %collective-permute-start.10 = (f32[1,7168]{1,0:T(1,128)S(1)}, f32[1,7168]{1,0:T(1,128)S(1)}, u32[]{:S(2)}, u32[]{:S(2)}) collective-permute-start(f32[1,7168]{1,0:T(1,128)S(1)} %get-tuple-element.66), channel_id=1, source_target_pairs={{1,2},{2,1},{3,4},{4,3},{5,6},{6,5},{7,8},{8,7},{9,10},{10,9},{11,... | collective-permute-start | bytes 86024 | tf_op jit(solution)/shard_map/ppermute | solution.py:445
  52.0 1.3 %collective-permute-start.8 = (bf16[108,128]{1,0:T(8,128)(2,1)S(1)}, bf16[108,128]{1,0:T(8,128)(2,1)S(1)}, u32[]{:S(2)}, u32[]{:S(2)}) collective-permute-start(bf16[108,128]{1,0:T(8,128)(2,1)S(1)} %get-tuple-element.64), channel_id=1, source_target_pairs={{16,32},{32,16},{48,64},{64,48},{80,96},{96,80},{112,0},{0,112},{1... | collective-permute-start | bytes 82952 | tf_op jit(solution)/shard_map/ppermute | solution.py:446
  53.3 3.2 %shard_map.112.refs_1_ = f32[3,36,32,128]{3,2,1,0:T(8,128)S(1)} custom-call(f32[4,8,1024]{2,1,0:T(8,128)S(1)} %get-tuple-element.51.snd_ref, bf16[3,36,32,128]{3,2,1,0:T(8,128)(2,1)S(1)} %get-tuple-element.69.traj_ref, bf16[3,36,64]{2,1,0:T(8,128)(2,1)S(1)} %get-tuple-element.53.table_ref), custom_call_target="tpu_custom_call" | custom-call | tf_op jit(solution)/shard_map/pallas_call | solution.py:45
  56.6 1.7 %shard_map.113 = (f32[3,36,32,128]{3,2,1,0:T(8,128)S(1)}, f32[1,7168]{1,0:T(1,128)S(1)}, f32[1,7168]{1,0:T(1,128)S(1)}, bf16[108,128]{1,0:T(8,128)(2,1)S(1)}, bf...) custom-call(f32[4,128]{1,0:T(4,128)S(1)} %broadcast_in_dim.2.mask_ref, ...), custom_call_target="tpu_custom_call" | custom-call | tf_op jit(solution)/shard_map/pallas_call | solution.py:45
  58.2 2.7 %collective-permute-start.14 = (f32[1,7168]{1,0:T(1,128)S(1)}, f32[1,7168]{1,0:T(1,128)S(1)}, u32[]{:S(2)}, u32[]{:S(2)}) collective-permute-start(f32[1,7168]{1,0:T(1,128)S(1)} %get-tuple-element.73), channel_id=1, source_target_pairs={{1,2},{2,1},{3,4},{4,3},{5,6},{6,5},{7,8},{8,7},{9,10},{10,9},{11,... | collective-permute-start | bytes 86024 | tf_op jit(solution)/shard_map/ppermute | solution.py:445
  61.0 1.4 %collective-permute-start.12 = (bf16[108,128]{1,0:T(8,128)(2,1)S(1)}, bf16[108,128]{1,0:T(8,128)(2,1)S(1)}, u32[]{:S(2)}, u32[]{:S(2)}) collective-permute-start(bf16[108,128]{1,0:T(8,128)(2,1)S(1)} %get-tuple-element.71), channel_id=1, source_target_pairs={{16,32},{32,16},{48,64},{64,48},{80,96},{96,80},{112,0},{0,112},{1... | collective-permute-start | bytes 82952 | tf_op jit(solution)/shard_map/ppermute | solution.py:446
  62.3 1.2 %shard_map.114.w_in = f32[3,36,32,128]{3,2,1,0:T(8,128)S(1)} custom-call(f32[3,36,32,128]{3,2,1,0:T(8,128)S(1)} %get-tuple-element.70.v, f32[180,32,128]{2,1,0:T(8,128)S(1)} %get-tuple-element.43.coef_ref.refs_2_.refs_3_), custom_call_target="tpu_custom_call" | custom-call | tf_op jit(solution)/shard_map/pallas_call | solution.py:45
  63.6 1.9 %collective-permute-done.12.lat_b = bf16[108,128]{1,0:T(8,128)(2,1)S(1)} collective-permute-done((bf16[108,128]{1,0:T(8,128)(2,1)S(1)}, bf16[108,128]{1,0:T(8,128)(2,1)S(1)}, u32[]{:S(2)}, u32[]{:S(2)}) %collective-permute-start.12) | collective-permute-done | bytes 27680 | tf_op jit(solution)/shard_map/ppermute | solution.py:446
  65.5 2.1 %shard_map.115 = (f32[3,36,32,128]{3,2,1,0:T(8,128)}, f32[3,32,128]{2,1,0:T(8,128)}) custom-call(f32[4,128]{1,0:T(4,128)S(1)} %broadcast_in_dim.2.mask_ref, f32[3,36,32,128]{3,2,1,0:T(8,128)S(1)} %shard_map.114.w_in, bf16[108,128]{1,0:T(8,128)(2,1)S(1)} %collective-permute-done.12.lat_b, bf16[108,128]{1,0:T(8,128)(2,1)S(1)} %collective-permute-done.13.lat_a, ...), custom_call_target="tpu_custom_call" | custom-call | tf_op jit(solution)/shard_map/pallas_call | solution.py:45
  (24 shorter events, 0.9 us)
Async XLA Ops:
  3.1 20.8 %all-to-all-start = ((f32[128,2,128]{2,1,0:T(2,128)}), f32[128,2,128]{2,1,0:T(2,128)S(1)}, u32[]{:S(2)}, u32[]{:S(2)}) async-start(f32[128,2,128]{2,1,0:T(2,128)} %shard_map.104), calls=%async_computation | async-start | bytes 262144 | tf_op jit(solution)/shard_map/all_to_all | solution.py:481
  29.9 7.3 %collective-permute-start.2 = (f32[1,7168]{1,0:T(1,128)S(1)}, f32[1,7168]{1,0:T(1,128)S(1)}, u32[]{:S(2)}, u32[]{:S(2)}) collective-permute-start(f32[1,7168]{1,0:T(1,128)S(1)} %get-tuple-element.49), channel_id=1, source_target_pairs={{1,2},{2,1},{3,4},{4,3},{5,6},{6,5},{7,8},{8,7},{9,10},{10,9},{11,... | collective-permute-start | bytes 86024 | tf_op jit(solution)/shard_map/ppermute | solution.py:445
  31.2 5.9 %collective-permute-start.3 = (f32[1,7168]{1,0:T(1,128)S(1)}, f32[1,7168]{1,0:T(1,128)S(1)}, u32[]{:S(2)}, u32[]{:S(2)}) collective-permute-start(f32[1,7168]{1,0:T(1,128)S(1)} %get-tuple-element.50), channel_id=1, source_target_pairs={{0,1},{1,0},{2,3},{3,2},{4,5},{5,4},{6,7},{7,6},{8,9},{9,8},{10,11... | collective-permute-start | bytes 86024 | tf_op jit(solution)/shard_map/ppermute | solution.py:447
  31.2 4.5 %collective-permute-start = (bf16[108,128]{1,0:T(8,128)(2,1)S(1)}, bf16[108,128]{1,0:T(8,128)(2,1)S(1)}, u32[]{:S(2)}, u32[]{:S(2)}) collective-permute-start(bf16[108,128]{1,0:T(8,128)(2,1)S(1)} %get-tuple-element.47), channel_id=1, source_target_pairs={{16,32},{32,16},{48,64},{64,48},{80,96},{96,80},{112,0},{0,112},{1... | collective-permute-start | bytes 82952 | tf_op jit(solution)/shard_map/ppermute | solution.py:446
  31.8 3.9 %collective-permute-start.1 = (bf16[108,128]{1,0:T(8,128)(2,1)S(1)}, bf16[108,128]{1,0:T(8,128)(2,1)S(1)}, u32[]{:S(2)}, u32[]{:S(2)}) collective-permute-start(bf16[108,128]{1,0:T(8,128)(2,1)S(1)} %get-tuple-element.48), channel_id=1, source_target_pairs={{0,16},{16,0},{32,48},{48,32},{64,80},{80,64},{96,112},{112,96},{1... | collective-permute-start | bytes 82952 | tf_op jit(solution)/shard_map/ppermute | solution.py:448
  39.5 7.3 %collective-permute-start.6 = (f32[1,7168]{1,0:T(1,128)S(1)}, f32[1,7168]{1,0:T(1,128)S(1)}, u32[]{:S(2)}, u32[]{:S(2)}) collective-permute-start(f32[1,7168]{1,0:T(1,128)S(1)} %get-tuple-element.58), channel_id=1, source_target_pairs={{1,2},{2,1},{3,4},{4,3},{5,6},{6,5},{7,8},{8,7},{9,10},{10,9},{11,... | collective-permute-start | bytes 86024 | tf_op jit(solution)/shard_map/ppermute | solution.py:445
  42.3 4.6 %collective-permute-start.7 = (f32[1,7168]{1,0:T(1,128)S(1)}, f32[1,7168]{1,0:T(1,128)S(1)}, u32[]{:S(2)}, u32[]{:S(2)}) collective-permute-start(f32[1,7168]{1,0:T(1,128)S(1)} %get-tuple-element.59), channel_id=1, source_target_pairs={{0,1},{1,0},{2,3},{3,2},{4,5},{5,4},{6,7},{7,6},{8,9},{9,8},{10,11... | collective-permute-start | bytes 86024 | tf_op jit(solution)/shard_map/ppermute | solution.py:447
  42.3 4.5 %collective-permute-start.4 = (bf16[108,128]{1,0:T(8,128)(2,1)S(1)}, bf16[108,128]{1,0:T(8,128)(2,1)S(1)}, u32[]{:S(2)}, u32[]{:S(2)}) collective-permute-start(bf16[108,128]{1,0:T(8,128)(2,1)S(1)} %get-tuple-element.56), channel_id=1, source_target_pairs={{16,32},{32,16},{48,64},{64,48},{80,96},{96,80},{112,0},{0,112},{1... | collective-permute-start | bytes 82952 | tf_op jit(solution)/shard_map/ppermute | solution.py:446
  43.7 3.2 %collective-permute-start.5 = (bf16[108,128]{1,0:T(8,128)(2,1)S(1)}, bf16[108,128]{1,0:T(8,128)(2,1)S(1)}, u32[]{:S(2)}, u32[]{:S(2)}) collective-permute-start(bf16[108,128]{1,0:T(8,128)(2,1)S(1)} %get-tuple-element.57), channel_id=1, source_target_pairs={{0,16},{16,0},{32,48},{48,32},{64,80},{80,64},{96,112},{112,96},{1... | collective-permute-start | bytes 82952 | tf_op jit(solution)/shard_map/ppermute | solution.py:448
  49.3 7.3 %collective-permute-start.10 = (f32[1,7168]{1,0:T(1,128)S(1)}, f32[1,7168]{1,0:T(1,128)S(1)}, u32[]{:S(2)}, u32[]{:S(2)}) collective-permute-start(f32[1,7168]{1,0:T(1,128)S(1)} %get-tuple-element.66), channel_id=1, source_target_pairs={{1,2},{2,1},{3,4},{4,3},{5,6},{6,5},{7,8},{8,7},{9,10},{10,9},{11,... | collective-permute-start | bytes 86024 | tf_op jit(solution)/shard_map/ppermute | solution.py:445
  52.0 4.6 %collective-permute-start.11 = (f32[1,7168]{1,0:T(1,128)S(1)}, f32[1,7168]{1,0:T(1,128)S(1)}, u32[]{:S(2)}, u32[]{:S(2)}) collective-permute-start(f32[1,7168]{1,0:T(1,128)S(1)} %get-tuple-element.67), channel_id=1, source_target_pairs={{0,1},{1,0},{2,3},{3,2},{4,5},{5,4},{6,7},{7,6},{8,9},{9,8},{10,11... | collective-permute-start | bytes 86024 | tf_op jit(solution)/shard_map/ppermute | solution.py:447
  52.0 4.5 %collective-permute-start.8 = (bf16[108,128]{1,0:T(8,128)(2,1)S(1)}, bf16[108,128]{1,0:T(8,128)(2,1)S(1)}, u32[]{:S(2)}, u32[]{:S(2)}) collective-permute-start(bf16[108,128]{1,0:T(8,128)(2,1)S(1)} %get-tuple-element.64), channel_id=1, source_target_pairs={{16,32},{32,16},{48,64},{64,48},{80,96},{96,80},{112,0},{0,112},{1... | collective-permute-start | bytes 82952 | tf_op jit(solution)/shard_map/ppermute | solution.py:446
  53.3 3.2 %collective-permute-start.9 = (bf16[108,128]{1,0:T(8,128)(2,1)S(1)}, bf16[108,128]{1,0:T(8,128)(2,1)S(1)}, u32[]{:S(2)}, u32[]{:S(2)}) collective-permute-start(bf16[108,128]{1,0:T(8,128)(2,1)S(1)} %get-tuple-element.65), channel_id=1, source_target_pairs={{0,16},{16,0},{32,48},{48,32},{64,80},{80,64},{96,112},{112,96},{1... | collective-permute-start | bytes 82952 | tf_op jit(solution)/shard_map/ppermute | solution.py:448
  58.2 7.2 %collective-permute-start.14 = (f32[1,7168]{1,0:T(1,128)S(1)}, f32[1,7168]{1,0:T(1,128)S(1)}, u32[]{:S(2)}, u32[]{:S(2)}) collective-permute-start(f32[1,7168]{1,0:T(1,128)S(1)} %get-tuple-element.73), channel_id=1, source_target_pairs={{1,2},{2,1},{3,4},{4,3},{5,6},{6,5},{7,8},{8,7},{9,10},{10,9},{11,... | collective-permute-start | bytes 86024 | tf_op jit(solution)/shard_map/ppermute | solution.py:445
  61.0 4.5 %collective-permute-start.15 = (f32[1,7168]{1,0:T(1,128)S(1)}, f32[1,7168]{1,0:T(1,128)S(1)}, u32[]{:S(2)}, u32[]{:S(2)}) collective-permute-start(f32[1,7168]{1,0:T(1,128)S(1)} %get-tuple-element.74), channel_id=1, source_target_pairs={{0,1},{1,0},{2,3},{3,2},{4,5},{5,4},{6,7},{7,6},{8,9},{9,8},{10,11... | collective-permute-start | bytes 86024 | tf_op jit(solution)/shard_map/ppermute | solution.py:447
  61.0 4.5 %collective-permute-start.12 = (bf16[108,128]{1,0:T(8,128)(2,1)S(1)}, bf16[108,128]{1,0:T(8,128)(2,1)S(1)}, u32[]{:S(2)}, u32[]{:S(2)}) collective-permute-start(bf16[108,128]{1,0:T(8,128)(2,1)S(1)} %get-tuple-element.71), channel_id=1, source_target_pairs={{16,32},{32,16},{48,64},{64,48},{80,96},{96,80},{112,0},{0,112},{1... | collective-permute-start | bytes 82952 | tf_op jit(solution)/shard_map/ppermute | solution.py:446
  62.3 3.1 %collective-permute-start.13 = (bf16[108,128]{1,0:T(8,128)(2,1)S(1)}, bf16[108,128]{1,0:T(8,128)(2,1)S(1)}, u32[]{:S(2)}, u32[]{:S(2)}) collective-permute-start(bf16[108,128]{1,0:T(8,128)(2,1)S(1)} %get-tuple-element.72), channel_id=1, source_target_pairs={{0,16},{16,0},{32,48},{48,32},{64,80},{80,64},{96,112},{112,96},{1... | collective-permute-start | bytes 82952 | tf_op jit(solution)/shard_map/ppermute | solution.py:448
